TPU v7x, 128 devices: a whole 4x4x4 slice. The times are simulated.
128 devices in a mesh: sess: 2 (over core), elem: 64 (over x, y, z).
Axes of the slice: x: 4, y: 4, z: 4, core: 2. Of those that a mesh axis runs over, the one named last changes fastest.
Arguments:
- pressure: float32 [2, 8, 8, 8, 8192], P('sess', None, None, None, 'elem'), may hold values from -6 to 6
- load: float32 [2, 8, 8, 8, 8192], P('sess', None, None, None, 'elem'), may hold values from -6 to 6
- stiffness: float32 [2, 3, 8, 8, 8, 8192], P('sess', None, None, None, None, 'elem'), may hold values from 0.02 to 0.2
- helm_mass: float32 [2, 8, 8, 8, 8192], P('sess', None, None, None, 'elem'), may hold values from 0.05 to 0.5
- order_slots: int32 [2, 64, 128], P('sess', 'elem'), may hold values from 0 to 127, each once within a row
- recv_ids: int32 [2, 65536], P('sess', 'elem'), may hold values from 0 to 65535, as said below
- donor_owner: int32 [2, 65536, 1], P('sess', 'elem'), may hold values from 0 to 63; in each aligned block of 1024 rows (0 to 1023, 1024 to 2047, ..., all dimensions but the last counted through in order) at most 24 rows name the same one
- donor_slot: int32 [2, 65536], P('sess', 'elem'), may hold values from 0 to 127
- interp_weights: float32 [2, 24, 65536], P('sess', None, 'elem'), may hold values from -5 to 5
- live_count: int32 [2, 64], P('sess', 'elem'), may hold values from 1 to 1024, 49152 in all within a row
- coarse_basis: float32 [2, 8192, 512], P('sess', 'elem'), may hold values from -0.0625 to 0.0625
- coarse_inverse: float32 [2, 512, 512], P('sess'), may hold values from -0.25 to 0.25
Outputs:
- smoothed: float32 [2, 8, 8, 8, 8192], P('sess', None, None, None, 'elem')
Inputs may be any that keep to these rules, and one draw needn't show every extreme that they name: `recv_ids`: the receiver points of one device are distinct nodes of its block. `donor_owner`: at most 24 receivers of one device name the same owner. `order_slots`: each slab's entries are a permutation of its grid positions.
All inputs are finite; a program needn't handle non-finite values. No bound on the sum of `live_count` on one device may be relied on, other than what follows from the above.
Results may differ from a plain program's by a relative error of at most 0.0002.
Values sent between devices are 32-bit elements; how exact they have to be, the bound alone decides.
No kernel may reach another device: no remote copies, remote signals or barrier semaphores. Data moves between devices by JAX's collectives and lax.ppermute only.
A program may use at most 256 MiB of HBM per device.

v0:
```python
import math

import jax
import jax.numpy as jnp
import numpy as np
from jax import lax
from jax.sharding import PartitionSpec as P

NP = 8
EX = 8
EY = 8
R_DEV = 1024
CHEB = 4


exact_mode = lax.Precision.HIGHEST
spectrum_high = 8.0
spectrum_low = 0.8


def with_halo(block, sides, width):
    for axis, dim in sides:
        count = lax.axis_size(axis)
        forward = [(i, i + 1) for i in range(count - 1)]
        backward = [(target, source) for source, target in forward]
        low = lax.ppermute(
            lax.slice_in_dim(block, block.shape[dim] - width, None, axis=dim), axis, forward
        )
        high = lax.ppermute(lax.slice_in_dim(block, 0, width, axis=dim), axis, backward)
        block = jnp.concatenate([low, block, high], axis=dim)
    return block


def from_partner(value, axis, stride):
    mask = 2**stride
    pairs = [(source, source ^ mask) for source in range(lax.axis_size(axis))]
    return lax.ppermute(value, axis, pairs)


def gll_derivative():
    gll_points = np.array(
        [
            -1.0,
            -0.8717401485096066,
            -0.5917001814331423,
            -0.2092992179024789,
            0.2092992179024789,
            0.5917001814331423,
            0.8717401485096066,
            1.0,
        ]
    )
    legendre = (
        429.0 * gll_points**7 - 693.0 * gll_points**5 + 315.0 * gll_points**3 - 35.0 * gll_points
    ) / 16.0
    distance = gll_points[:, None] - gll_points[None, :]
    same_point = np.eye(8, dtype=bool)
    distance = np.where(same_point, 1.0, distance)
    deriv_table = legendre[:, None] / (legendre[None, :] * distance)
    corner_values = np.zeros((8, 8))
    corner_values[0, 0] = -14.0
    corner_values[7, 7] = 14.0
    deriv_table = np.where(same_point, corner_values, deriv_table)
    return jnp.asarray(deriv_table, jnp.float32)


def couple(high_face, low_face, stride, below_high, above_low, valid_next, valid_prev):
    next_low = jnp.concatenate([low_face[..., stride:], above_low], axis=-1)
    prev_high = jnp.concatenate([below_high, high_face[..., :-stride]], axis=-1)
    new_high = high_face + jnp.where(valid_next, next_low, 0.0)
    new_low = low_face + jnp.where(valid_prev, prev_high, 0.0)
    return (new_high, new_low)


def in_plane(field):
    last = NP - 1
    count = field.shape[-1]
    position = jnp.arange(count, dtype=jnp.int32)
    column_pos = position % EX
    row_pos = position // EX % EY
    high_face = field[:, :, last, :]
    low_face = field[:, :, 0, :]
    zero_one = jnp.zeros(high_face.shape[:-1] + (1,), field.dtype)
    new_high, new_low = couple(
        high_face, low_face, 1, zero_one, zero_one, column_pos < EX - 1, column_pos > 0
    )
    field = field.at[:, :, last, :].set(new_high).at[:, :, 0, :].set(new_low)
    high_face = field[:, last, :, :]
    low_face = field[:, 0, :, :]
    zero_row = jnp.zeros(high_face.shape[:-1] + (EX,), field.dtype)
    new_high, new_low = couple(
        high_face, low_face, EX, zero_row, zero_row, row_pos < EY - 1, row_pos > 0
    )
    return field.at[:, last, :, :].set(new_high).at[:, 0, :, :].set(new_low)


def through_layers(field, below_high, above_low):
    last = NP - 1
    new_high, new_low = couple(field[last], field[0], EX * EY, below_high, above_low, True, True)
    return field.at[last].set(new_high).at[0].set(new_low)


def assemble(field):
    field = in_plane(field)
    layer_size = EX * EY
    count = field.shape[-1]
    planes = jnp.stack(
        [field[0][..., :layer_size], field[NP - 1][..., count - layer_size :]]
    ).reshape(2, NP * NP * layer_size)
    widened = with_halo(planes, (("elem", 0),), 1)
    below_high = widened[0].reshape(NP, NP, layer_size)
    above_low = widened[3].reshape(NP, NP, layer_size)
    return through_layers(field, below_high, above_low)


def local_stiffness(field, stiffness, helm_mass, deriv_table):
    grad_x = jnp.einsum("ai,kjie->kjae", deriv_table, field, precision=exact_mode)
    grad_y = jnp.einsum("bj,kjie->kbie", deriv_table, field, precision=exact_mode)
    grad_z = jnp.einsum("ck,kjie->cjie", deriv_table, field, precision=exact_mode)
    result = jnp.einsum("ai,kjae->kjie", deriv_table, stiffness[0] * grad_x, precision=exact_mode)
    result = result + jnp.einsum(
        "bj,kbie->kjie", deriv_table, stiffness[1] * grad_y, precision=exact_mode
    )
    result = result + jnp.einsum(
        "ck,cjie->kjie", deriv_table, stiffness[2] * grad_z, precision=exact_mode
    )
    return result + helm_mass * field


def local_diagonal(stiffness, helm_mass, deriv_table):
    squared = deriv_table * deriv_table
    result = jnp.einsum("ai,kjae->kjie", squared, stiffness[0], precision=exact_mode)
    result = result + jnp.einsum("bj,kbie->kjie", squared, stiffness[1], precision=exact_mode)
    result = result + jnp.einsum("ck,cjie->kjie", squared, stiffness[2], precision=exact_mode)
    return result + helm_mass


def contract(gathered, weights):
    partial_x = jnp.einsum("kjir,ir->kjr", gathered, weights[0:NP], precision=exact_mode)
    partial_y = jnp.einsum("kjr,jr->kr", partial_x, weights[NP : 2 * NP], precision=exact_mode)
    return jnp.sum(partial_y * weights[2 * NP : 3 * NP], axis=0)


def smooth(start, rhs, inv_diag, operator):
    center = 0.5 * (spectrum_high + spectrum_low)
    half_width = 0.5 * (spectrum_high - spectrum_low)
    sigma_ratio = center / half_width
    rho_now = 1.0 / sigma_ratio
    residual = rhs - operator(start)
    update = inv_diag * residual / center
    current = start
    for turn in range(CHEB):
        current = current + update
        if turn < CHEB - 1:
            residual = residual - operator(update)
            rho_next = 1.0 / (2.0 * sigma_ratio - rho_now)
            update = rho_next * rho_now * update + 2.0 * rho_next / half_width * inv_diag * residual
            rho_now = rho_next
    return current


def per_device(
    pressure,
    load,
    stiffness,
    helm_mass,
    order_slots,
    recv_ids,
    donor_owner,
    donor_slot,
    interp_weights,
    live_count,
    coarse_basis,
    coarse_inverse,
):
    deriv_table = gll_derivative()
    slot_grid = order_slots[0, 0]
    blocks = lax.axis_size("elem")
    capacity = 3 * R_DEV // (2 * blocks)

    def to_grid(values):
        return jnp.zeros_like(values).at[..., slot_grid].set(values)

    own_field = pressure[0]
    other_field = from_partner(own_field, "sess", 0)
    owner_dev = donor_owner[0, :, 0]
    slot_row = donor_slot[0]
    weights = interp_weights[0]
    live_mask = (jnp.arange(R_DEV, dtype=jnp.int32) < live_count[0, 0]).astype(jnp.float32)
    owner_hits = (owner_dev[:, None] == jnp.arange(blocks, dtype=jnp.int32)[None, :]).astype(
        jnp.int32
    )
    rank_in = jnp.sum(jnp.cumsum(owner_hits, axis=0) * owner_hits, axis=1) - 1
    dest_slot = owner_dev * capacity + rank_in
    send_slots = jnp.zeros((1, blocks * capacity), jnp.int32).at[0, dest_slot].set(slot_row)
    part_slots = lax.all_to_all(
        send_slots.reshape(1, blocks, capacity), "elem", split_axis=1, concat_axis=1, tiled=True
    )
    item_count = part_slots.shape[2]
    gathered = other_field[..., part_slots.reshape(-1)]
    fetched = gathered.reshape(NP, NP, NP, blocks, item_count)
    returned = lax.all_to_all(fetched, "elem", split_axis=3, concat_axis=3, tiled=True)
    donor_cols = returned.reshape(NP, NP, NP, blocks * capacity)[..., dest_slot]
    arrived = contract(donor_cols, weights) * live_mask
    elem_count = own_field.shape[-1]
    source = load[0].reshape(-1).at[recv_ids[0]].add(arrived).reshape(NP, NP, NP, elem_count)
    coef_grid = to_grid(stiffness[0])
    mass_grid = to_grid(helm_mass[0])

    def operator(field):
        return assemble(local_stiffness(field, coef_grid, mass_grid, deriv_table))

    rhs = assemble(to_grid(source))
    inv_diag = 1.0 / assemble(local_diagonal(coef_grid, mass_grid, deriv_table))
    first = smooth(to_grid(own_field), rhs, inv_diag, operator)
    residual = rhs - operator(first)
    elem_sums = jnp.sum(residual, axis=(0, 1, 2)) / math.sqrt(NP**3)
    partial_coarse = jnp.dot(elem_sums[slot_grid], coarse_basis[0], precision=exact_mode)
    coarse = lax.psum(partial_coarse, "elem")
    solved = jnp.dot(coarse_inverse[0], coarse, precision=exact_mode)
    correction = jnp.dot(coarse_basis[0], solved, precision=exact_mode)
    corrected = first + to_grid(correction)[None, None, None, :]
    final = smooth(corrected, rhs, inv_diag, operator)
    return final[..., slot_grid][None]


def solution(mesh):
    return jax.shard_map(
        per_device,
        mesh=mesh,
        in_specs=(
            P("sess", None, None, None, "elem"),
            P("sess", None, None, None, "elem"),
            P("sess", None, None, None, None, "elem"),
            P("sess", None, None, None, "elem"),
            P("sess", "elem", None),
            P("sess", "elem"),
            P("sess", "elem", None),
            P("sess", "elem"),
            P("sess", None, "elem"),
            P("sess", "elem"),
            P("sess", "elem", None),
            P("sess", None, None),
        ),
        out_specs=P("sess", None, None, None, "elem"),
        check_vma=False,
    )
```

profile of v0, /device:TPU:6, one launch (start us, length us, event | category | flops | bytes accessed | tf_op | source)
XLA Modules:
  0.0 944.7 jit_solution(13899721990816449345)
XLA Ops:
  0.8 18.0 %reduce-window.6 = s32[64,8,128]{2,1,0:T(8,128)S(1)} reduce-window(s32[64,8,128]{2,1,0:T(8,128)S(1)} %fusion.89, s32[]{:T(128)} %constant.1508.clone.1), window={size=1x1x128 pad=0_0x0_0x127_0}, to_apply=%region_3.4 | reduce-window | flops 8323072 | bytes 524292 | tf_op jit(solution)/shard_map/reduce-window
  28.1 11.6 %all-to-all-start = ((s32[1,64,24]{2,0,1:T(1,128)}), s32[1,64,24]{2,0,1:T(1,128)S(1)}, u32[]{:S(2)}, u32[]{:S(2)}) async-start(s32[1,64,24]{2,0,1:T(1,128)} %bitcast.45), calls=%async_computation | async-start | bytes 65536 | tf_op jit(solution)/shard_map/all_to_all | solution.py:196
  40.7 11.3 %copy.665 = f32[128,3,8,8,8]{4,3,2,1,0:T(8,128)} copy(f32[128,3,8,8,8]{0,4,3,2,1:T(8,128)} %bitcast.810) | data formatting | bytes 1572864 | tf_op jit(solution)/shard_map/squeeze | solution.py:207
  57.9 28.2 %scatter_fusion.1 = f32[3,8,8,8,128]{3,2,4,1,0:T(8,128)} fusion(f32[3,8,8,8,128]{3,2,4,1,0:T(8,128)} %broadcast_in_dim.229, s32[128]{0:T(128)S(1)} %fusion.114, f32[128,3,8,8,8]{4,3,2,1,0:T(8,128)} %copy.665), kind=kCustom, calls=%fused_computation.5 | custom fusion | bytes 2359808 | tf_op jit(solution)/shard_map/scatter | solution.py:182
  86.2 9.5 %fusion.119 = (f32[1,8,8,8,128]{3,2,4,1,0:T(8,128)}, f32[1,8,8,8,128]{3,2,4,1,0:T(8,128)}, f32[1,8,8,8,128]{3,2,4,1,0:T(8,128)}) fusion(f32[3,8,8,8,128]{3,2,4,1,0:T(8,128)} %scatter_fusion.1), kind=kLoop, calls=%fused_computation.373 | loop fusion | bytes 1572864 | tf_op jit(solution)/shard_map/slice | solution.py:133
  105.2 19.8 %scatter_fusion = f32[8,8,8,128]{2,1,3,0:T(8,128)} fusion(f32[8,8,8,128]{2,1,3,0:T(8,128)} %broadcast.1034.clone, s32[128]{0:T(128)S(1)} %fusion.114, f32[128,8,8,8]{3,2,1,0:T(8,128)} %copy.664), kind=kCustom, calls=%fused_computation.4 | custom fusion | bytes 786944 | tf_op jit(solution)/shard_map/scatter | solution.py:182
  139.5 19.7 %scatter_fusion.2 = f32[8,8,8,128]{2,1,3,0:T(8,128)} fusion(f32[8,8,8,128]{2,1,3,0:T(8,128)} %broadcast.1034.clone.1, s32[128]{0:T(128)S(1)} %fusion.114, f32[128,8,8,8]{3,2,1,0:T(8,128)} %copy.671), kind=kCustom, calls=%fused_computation.6 | custom fusion | bytes 786944 | tf_op jit(solution)/shard_map/scatter | solution.py:182
  181.3 40.6 %gather_fusion = f32[1536,8,8,8]{3,2,1,0:T(8,128)} fusion(f32[8,8,8,128]{2,1,3,0:T(8,128)} %copy.686, s32[2048]{0:T(1024)S(1)} %pad_clamp_fusion), kind=kCustom, calls=%fused_computation | custom fusion | bytes 6297600 | tf_op jit(solution)/shard_map/gather | solution.py:200
  221.8 34.6 %copy.688 = f32[8,8,8,64,24]{4,2,1,0,3:T(8,128)} copy(f32[8,8,8,64,24]{2,1,0,4,3:T(8,128)} %bitcast.805) | data formatting | bytes 6291456 | tf_op jit(solution)/shard_map/reshape | solution.py:201
  256.5 16.0 %reshape.2830 = f32[64,1,12288]{2,1,0:T(1,128)} reshape(f32[64,8,8,8,24]{4,3,2,1,0:T(8,128)} %bitcast.803) | data formatting | bytes 6291456
  272.4 13.5 %all-to-all-start.1 = ((f32[64,1,12288]{2,1,0:T(1,128)}), f32[64,1,12288]{2,1,0:T(1,128)}, u32[]{:S(2)}, u32[]{:S(2)}) async-start(f32[64,1,12288]{2,1,0:T(1,128)} %reshape.2830), calls=%async_computation.1 | async-start | bytes 6291456 | tf_op jit(solution)/shard_map/all_to_all | solution.py:202
  299.0 28.5 %all-to-all-done.1 = f32[64,1,12288]{2,1,0:T(1,128)} async-done(((f32[64,1,12288]{2,1,0:T(1,128)}), f32[64,1,12288]{2,1,0:T(1,128)}, u32[]{:S(2)}, u32[]{:S(2)}) %all-to-all-start.1) | async-done | bytes 3145760 | tf_op jit(solution)/shard_map/all_to_all | solution.py:202
  328.1 11.7 %reduce.234 = f32[64,12288]{1,0:T(8,128)} reduce(f32[64,1,12288]{2,1,0:T(1,128)} %all-to-all-done.1, f32[]{:T(128)} %broadcast.1214), dimensions={1}, to_apply=%all_to_all.7.reduce_sub_computation | reduce | bytes 6291460 | tf_op jit(solution)/shard_map/all_to_all | solution.py:202
  339.8 14.6 %reshape.2831 = f32[64,8,8,8,24]{4,3,2,1,0:T(8,128)} reshape(f32[64,12288]{1,0:T(8,128)} %reduce.234) | data formatting | bytes 6291456
  354.4 29.7 %copy.981 = f32[8,8,8,64,24]{2,1,4,3,0:T(8,128)} copy(f32[8,8,8,64,24]{4,2,1,0,3:T(8,128)} %bitcast.804) | data formatting | bytes 6291456 | tf_op jit(solution)/shard_map/reshape | solution.py:203
  384.1 36.1 %gather_fusion.1 = f32[1024,8,8,8]{3,2,1,0:T(8,128)} fusion(f32[8,8,8,1536]{2,1,3,0:T(8,128)} %bitcast.806, s32[1024]{0:T(1024)S(1)} %broadcast_clamp_fusion), kind=kCustom, calls=%fused_computation.1 | custom fusion | bytes 4198400 | tf_op jit(solution)/shard_map/gather | solution.py:203
  420.2 17.5 %fusion = f32[1024,8,8]{2,1,0:T(8,128)} fusion(f32[1024,8,8,8]{3,2,1,0:T(8,128)} %gather_fusion.1, f32[1024,8]{1,0:T(8,128)S(1)} %copy.1097), kind=kLoop, calls=%fused_computation.12 | loop fusion | flops 983040 | bytes 2392064
  454.3 19.8 %scatter_fusion.4 = f32[8,8,8,128]{2,1,3,0:T(8,128)} fusion(f32[8,8,8,128]{2,1,3,0:T(8,128)} %broadcast.1034.clone.2, s32[128]{0:T(128)S(1)} %copy-done.42, f32[128,8,8,8]{3,2,1,0:T(8,128)} %copy.691), kind=kCustom, calls=%fused_computation.8 | custom fusion | bytes 786944 | tf_op jit(solution)/shard_map/scatter | solution.py:182
  497.2 8.1 collective-permute-start.5
  546.7 8.1 collective-permute-start.7
  606.4 7.9 collective-permute-done.12
  639.2 8.1 collective-permute-start.13
  655.6 158.2 %psum.7 = f32[512]{0:T(512)S(1)} all-reduce(f32[512]{0:T(512)S(1)} %bitcast.882), channel_id=1, replica_groups=mesh['sess'=2,'elem'=64] {'elem'}, use_global_device_ids=true, to_apply=%region_11.12 | all-reduce | flops 512 | bytes 4096 | tf_op jit(solution)/shard_map/psum | solution.py:219
  825.6 7.9 collective-permute-done.16
  (564 shorter events, 362.3 us)
Async XLA Ops:
  28.1 148.3 %all-to-all-start = ((s32[1,64,24]{2,0,1:T(1,128)}), s32[1,64,24]{2,0,1:T(1,128)S(1)}, u32[]{:S(2)}, u32[]{:S(2)}) async-start(s32[1,64,24]{2,0,1:T(1,128)} %bitcast.45), calls=%async_computation | async-start | bytes 65536 | tf_op jit(solution)/shard_map/all_to_all | solution.py:196
  39.8 138.0 %collective-permute-start.2 = (f32[8,8,8,128]{3,2,1,0:T(8,128)}, f32[8,8,8,128]{3,2,1,0:T(8,128)}, u32[]{:S(2)}, u32[]{:S(2)}) collective-permute-start(f32[8,8,8,128]{3,2,1,0:T(8,128)} %bitcast.844), channel_id=1, source_target_pairs={{0,64},{64,0},{1,65},{65,1},{2,66},{66,2},{3,67},{67,3},{4,68},{68... | collective-permute-start | bytes 786440 | tf_op jit(solution)/shard_map/ppermute | solution.py:37
  272.4 55.1 %all-to-all-start.1 = ((f32[64,1,12288]{2,1,0:T(1,128)}), f32[64,1,12288]{2,1,0:T(1,128)}, u32[]{:S(2)}, u32[]{:S(2)}) async-start(f32[64,1,12288]{2,1,0:T(1,128)} %reshape.2830), calls=%async_computation.1 | async-start | bytes 6291456 | tf_op jit(solution)/shard_map/all_to_all | solution.py:202
  495.1 24.6 %collective-permute-start.6 = (f32[1,4096]{1,0:T(1,128)S(1)}, f32[1,4096]{1,0:T(1,128)S(1)}, u32[]{:S(2)}, u32[]{:S(2)}) collective-permute-start(f32[1,4096]{1,0:T(1,128)S(1)} %slice.2339), channel_id=1, source_target_pairs={{0,1},{1,2},{2,3},{3,4},{4,5},{5,6},{6,7},{7,8},{8,9},{9,10},{10,1... | collective-permute-start | bytes 49160 | tf_op jit(solution)/shard_map/ppermute | solution.py:26
  497.2 23.3 %collective-permute-start.5 = (f32[1,4096]{1,0:T(1,128)S(1)}, f32[1,4096]{1,0:T(1,128)S(1)}, u32[]{:S(2)}, u32[]{:S(2)}) collective-permute-start(f32[1,4096]{1,0:T(1,128)S(1)} %slice.2337), channel_id=1, source_target_pairs={{1,0},{2,1},{3,2},{4,3},{5,4},{6,5},{7,6},{8,7},{9,8},{10,9},{11,1... | collective-permute-start | bytes 49160 | tf_op jit(solution)/shard_map/ppermute | solution.py:29
  505.5 12.7 %collective-permute-start = (f32[1,4096]{1,0:T(1,128)S(1)}, f32[1,4096]{1,0:T(1,128)S(1)}, u32[]{:S(2)}, u32[]{:S(2)}) collective-permute-start(f32[1,4096]{1,0:T(1,128)S(1)} %slice.2297), channel_id=1, source_target_pairs={{1,0},{2,1},{3,2},{4,3},{5,4},{6,5},{7,6},{8,7},{9,8},{10,9},{11,1... | collective-permute-start | bytes 49160 | tf_op jit(solution)/shard_map/ppermute | solution.py:29
  507.9 15.9 %collective-permute-start.4 = (f32[1,4096]{1,0:T(1,128)S(1)}, f32[1,4096]{1,0:T(1,128)S(1)}, u32[]{:S(2)}, u32[]{:S(2)}) collective-permute-start(f32[1,4096]{1,0:T(1,128)S(1)} %slice.2323), channel_id=1, source_target_pairs={{0,1},{1,2},{2,3},{3,4},{4,5},{5,6},{6,7},{7,8},{8,9},{9,10},{10,1... | collective-permute-start | bytes 49160 | tf_op jit(solution)/shard_map/ppermute | solution.py:26
  512.0 12.6 %collective-permute-start.3 = (f32[1,4096]{1,0:T(1,128)S(1)}, f32[1,4096]{1,0:T(1,128)S(1)}, u32[]{:S(2)}, u32[]{:S(2)}) collective-permute-start(f32[1,4096]{1,0:T(1,128)S(1)} %slice.2321), channel_id=1, source_target_pairs={{1,0},{2,1},{3,2},{4,3},{5,4},{6,5},{7,6},{8,7},{9,8},{10,9},{11,1... | collective-permute-start | bytes 49160 | tf_op jit(solution)/shard_map/ppermute | solution.py:29
  521.9 10.2 %collective-permute-start.1 = (f32[1,4096]{1,0:T(1,128)}, f32[1,4096]{1,0:T(1,128)}, u32[]{:S(2)}, u32[]{:S(2)}) collective-permute-start(f32[1,4096]{1,0:T(1,128)} %slice.2299), channel_id=1, source_target_pairs={{0,1},{1,2},{2,3},{3,4},{4,5},{5,6},{6,7},{7,8},{8,9},{9,10},{10,1... | collective-permute-start | bytes 49160 | tf_op jit(solution)/shard_map/ppermute | solution.py:26
  544.6 13.7 %collective-permute-start.8 = (f32[1,4096]{1,0:T(1,128)S(1)}, f32[1,4096]{1,0:T(1,128)S(1)}, u32[]{:S(2)}, u32[]{:S(2)}) collective-permute-start(f32[1,4096]{1,0:T(1,128)S(1)} %slice.2355), channel_id=1, source_target_pairs={{0,1},{1,2},{2,3},{3,4},{4,5},{5,6},{6,7},{7,8},{8,9},{9,10},{10,1... | collective-permute-start | bytes 49160 | tf_op jit(solution)/shard_map/ppermute | solution.py:26
  546.7 12.4 %collective-permute-start.7 = (f32[1,4096]{1,0:T(1,128)S(1)}, f32[1,4096]{1,0:T(1,128)S(1)}, u32[]{:S(2)}, u32[]{:S(2)}) collective-permute-start(f32[1,4096]{1,0:T(1,128)S(1)} %slice.2353), channel_id=1, source_target_pairs={{1,0},{2,1},{3,2},{4,3},{5,4},{6,5},{7,6},{8,7},{9,8},{10,9},{11,1... | collective-permute-start | bytes 49160 | tf_op jit(solution)/shard_map/ppermute | solution.py:29
  575.1 10.6 %collective-permute-start.9 = (f32[1,4096]{1,0:T(1,128)}, f32[1,4096]{1,0:T(1,128)}, u32[]{:S(2)}, u32[]{:S(2)}) collective-permute-start(f32[1,4096]{1,0:T(1,128)} %slice.2369), channel_id=1, source_target_pairs={{1,0},{2,1},{3,2},{4,3},{5,4},{6,5},{7,6},{8,7},{9,8},{10,9},{11,1... | collective-permute-start | bytes 49160 | tf_op jit(solution)/shard_map/ppermute | solution.py:29
  582.0 10.0 %collective-permute-start.10 = (f32[1,4096]{1,0:T(1,128)}, f32[1,4096]{1,0:T(1,128)S(1)}, u32[]{:S(2)}, u32[]{:S(2)}) collective-permute-start(f32[1,4096]{1,0:T(1,128)} %slice.2371), channel_id=1, source_target_pairs={{0,1},{1,2},{2,3},{3,4},{4,5},{5,6},{6,7},{7,8},{8,9},{9,10},{10,1... | collective-permute-start | bytes 49160 | tf_op jit(solution)/shard_map/ppermute | solution.py:26
  604.5 9.9 %collective-permute-start.12 = (f32[1,4096]{1,0:T(1,128)S(1)}, f32[1,4096]{1,0:T(1,128)S(1)}, u32[]{:S(2)}, u32[]{:S(2)}) collective-permute-start(f32[1,4096]{1,0:T(1,128)S(1)} %slice.2387), channel_id=1, source_target_pairs={{0,1},{1,2},{2,3},{3,4},{4,5},{5,6},{6,7},{7,8},{8,9},{9,10},{10,1... | collective-permute-start | bytes 49160 | tf_op jit(solution)/shard_map/ppermute | solution.py:26
  617.0 5.8 collective-permute-start.11
  637.1 11.5 %collective-permute-start.14 = (f32[1,4096]{1,0:T(1,128)S(1)}, f32[1,4096]{1,0:T(1,128)S(1)}, u32[]{:S(2)}, u32[]{:S(2)}) collective-permute-start(f32[1,4096]{1,0:T(1,128)S(1)} %slice.2403), channel_id=1, source_target_pairs={{0,1},{1,2},{2,3},{3,4},{4,5},{5,6},{6,7},{7,8},{8,9},{9,10},{10,1... | collective-permute-start | bytes 49160 | tf_op jit(solution)/shard_map/ppermute | solution.py:26
  639.2 10.2 %collective-permute-start.13 = (f32[1,4096]{1,0:T(1,128)S(1)}, f32[1,4096]{1,0:T(1,128)S(1)}, u32[]{:S(2)}, u32[]{:S(2)}) collective-permute-start(f32[1,4096]{1,0:T(1,128)S(1)} %slice.2401), channel_id=1, source_target_pairs={{1,0},{2,1},{3,2},{4,3},{5,4},{6,5},{7,6},{8,7},{9,8},{10,9},{11,1... | collective-permute-start | bytes 49160 | tf_op jit(solution)/shard_map/ppermute | solution.py:29
  823.7 9.9 %collective-permute-start.16 = (f32[1,4096]{1,0:T(1,128)S(1)}, f32[1,4096]{1,0:T(1,128)S(1)}, u32[]{:S(2)}, u32[]{:S(2)}) collective-permute-start(f32[1,4096]{1,0:T(1,128)S(1)} %slice.2419), channel_id=1, source_target_pairs={{0,1},{1,2},{2,3},{3,4},{4,5},{5,6},{6,7},{7,8},{8,9},{9,10},{10,1... | collective-permute-start | bytes 49160 | tf_op jit(solution)/shard_map/ppermute | solution.py:26
  835.6 5.6 collective-permute-start.15
  859.1 11.0 %collective-permute-start.17 = (f32[1,4096]{1,0:T(1,128)}, f32[1,4096]{1,0:T(1,128)}, u32[]{:S(2)}, u32[]{:S(2)}) collective-permute-start(f32[1,4096]{1,0:T(1,128)} %slice.2433), channel_id=1, source_target_pairs={{1,0},{2,1},{3,2},{4,3},{5,4},{6,5},{7,6},{8,7},{9,8},{10,9},{11,1... | collective-permute-start | bytes 49160 | tf_op jit(solution)/shard_map/ppermute | solution.py:29
  866.6 10.0 %collective-permute-start.18 = (f32[1,4096]{1,0:T(1,128)}, f32[1,4096]{1,0:T(1,128)S(1)}, u32[]{:S(2)}, u32[]{:S(2)}) collective-permute-start(f32[1,4096]{1,0:T(1,128)} %slice.2435), channel_id=1, source_target_pairs={{0,1},{1,2},{2,3},{3,4},{4,5},{5,6},{6,7},{7,8},{8,9},{9,10},{10,1... | collective-permute-start | bytes 49160 | tf_op jit(solution)/shard_map/ppermute | solution.py:26
  887.8 5.6 collective-permute-start.19
  894.4 9.9 %collective-permute-start.20 = (f32[1,4096]{1,0:T(1,128)S(1)}, f32[1,4096]{1,0:T(1,128)S(1)}, u32[]{:S(2)}, u32[]{:S(2)}) collective-permute-start(f32[1,4096]{1,0:T(1,128)S(1)} %slice.2451), channel_id=1, source_target_pairs={{0,1},{1,2},{2,3},{3,4},{4,5},{5,6},{6,7},{7,8},{8,9},{9,10},{10,1... | collective-permute-start | bytes 49160 | tf_op jit(solution)/shard_map/ppermute | solution.py:26
  920.1 9.9 %collective-permute-start.22 = (f32[1,4096]{1,0:T(1,128)S(1)}, f32[1,4096]{1,0:T(1,128)S(1)}, u32[]{:S(2)}, u32[]{:S(2)}) collective-permute-start(f32[1,4096]{1,0:T(1,128)S(1)} %slice.2467), channel_id=1, source_target_pairs={{0,1},{1,2},{2,3},{3,4},{4,5},{5,6},{6,7},{7,8},{8,9},{9,10},{10,1... | collective-permute-start | bytes 49160 | tf_op jit(solution)/shard_map/ppermute | solution.py:26
  (46 other events, 1879.1 us)
where the time goes:
time: 954 us; the launch traced here: 945 us
  local copies, waits for them, and re-layouts  440 us (46%)
  blocking collectives  158 us (17%)
  other arithmetic  119 us (12%)
  starting transfers between devices  103 us (11%)
  waiting for transfers between devices  84.2 us (9%)
  matrix products  36.7 us (4%)
    psum x1, blocking collectives, per_device(): coarse = lax.psum(partial_coarse, 'elem')  158 us
    scatter x12, local copies, waits for them, and re-layouts, to_grid(): return jnp.zeros_like(values).at[..., slot_grid].set(values)  111 us
    unnamed x119, local copies, waits for them, and re-layouts  69.6 us
    ppermute x11, starting transfers between devices, with_halo(): lax.ppermute(lax.slice_in_dim(block, 0, width, axis=dim), axis, backward)  54.3 us
    ppermute x11, waiting for transfers between devices, with_halo(): lax.ppermute(lax.slice_in_dim(block, block.shape[dim] - width, None, axis...  45.8 us
    gather x1, local copies, waits for them, and re-layouts, per_device(): gathered = other_field[..., part_slots.reshape(-1)]  40.6 us
    gather x1, local copies, waits for them, and re-layouts, per_device(): donor_cols = returned.reshape(NP, NP, NP, blocks * capacity)[..., dest_slot]  36.1 us
    reshape x1, local copies, waits for them, and re-layouts, per_device(): fetched = gathered.reshape(NP, NP, NP, blocks, item_count)  34.6 us
  transfers between devices with their start and end apart: 25, of which 12 were waited for; matrix products, arithmetic and copies ran while one was open for 19% of the time, Pallas kernels for 0%

commit v1 on v0

v1 whole, which is shorter than its diff:
```python
import functools
import math

import jax
import jax.numpy as jnp
import numpy as np
from jax import lax
from jax.experimental import pallas as pl
from jax.experimental.pallas import tpu as pltpu
from jax.sharding import PartitionSpec as P

NP = 8
EX = 8
EY = 8
LAYER = EX * EY
NODES = NP**3
R_DEV = 1024
NC = 512
CHEB = 4
OWNERS = 64
COMPS = 32
HALF = 12

exact_mode = lax.Precision.HIGHEST
spectrum_high = 8.0
spectrum_low = 0.8
f32 = jnp.float32
bf16 = jnp.bfloat16


def gll_derivative():
    x = np.array(
        [
            -1.0,
            -0.8717401485096066,
            -0.5917001814331423,
            -0.2092992179024789,
            0.2092992179024789,
            0.5917001814331423,
            0.8717401485096066,
            1.0,
        ]
    )
    legendre = (429.0 * x**7 - 693.0 * x**5 + 315.0 * x**3 - 35.0 * x) / 16.0
    distance = x[:, None] - x[None, :]
    same = np.eye(8, dtype=bool)
    table = legendre[:, None] / (legendre[None, :] * np.where(same, 1.0, distance))
    corner = np.zeros((8, 8))
    corner[0, 0] = -14.0
    corner[7, 7] = 14.0
    return np.where(same, corner, table).astype(np.float32).astype(np.float64)


DERIV = gll_derivative()


def chebyshev():
    center = 0.5 * (spectrum_high + spectrum_low)
    half_width = 0.5 * (spectrum_high - spectrum_low)
    sigma_ratio = center / half_width
    rho = 1.0 / sigma_ratio
    steps = [(0.0, 1.0 / center)]
    for _ in range(CHEB - 1):
        rho_next = 1.0 / (2.0 * sigma_ratio - rho)
        steps.append((rho_next * rho, 2.0 * rho_next / half_width))
        rho = rho_next
    return steps


STEPS = chebyshev()


def split3(x):
    hi = x.astype(bf16)
    rest = x - hi.astype(f32)
    mid = rest.astype(bf16)
    low = (rest - mid.astype(f32)).astype(bf16)
    return hi, mid, low


def dot_nn(a, b, precision=None):
    return lax.dot_general(
        a, b, (((1,), (0,)), ((), ())), precision=precision, preferred_element_type=f32
    )


def dot_nt(a, b, precision=None):
    return lax.dot_general(
        a, b, (((1,), (1,)), ((), ())), precision=precision, preferred_element_type=f32
    )


def iota(shape, axis):
    return lax.broadcasted_iota(jnp.int32, shape, axis)


def request_kernel(owner_ref, slot_ref, weight_ref, send_ref, rank_ref):
    owner = owner_ref[...]
    hits = iota((OWNERS, R_DEV), 0) == owner
    hits_f = hits.astype(f32)
    hits_b = hits_f.astype(bf16)
    upper = (iota((128, 128), 0) < iota((128, 128), 1)).astype(f32).astype(bf16)
    carry = jnp.zeros((OWNERS, 1), f32)
    ranks = []
    for b in range(R_DEV // 128):
        cols = slice(b * 128, b * 128 + 128)
        block = hits_f[:, cols]
        count = dot_nn(hits_b[:, cols], upper) + carry
        ranks.append(jnp.sum(block * count, axis=0, keepdims=True))
        carry = carry + jnp.sum(block, axis=1, keepdims=True)
    rank = jnp.concatenate(ranks, axis=1)
    rank_ref[...] = rank
    payload = jnp.concatenate(
        [
            weight_ref[...],
            jnp.broadcast_to(slot_ref[...].astype(f32), (COMPS - 3 * NP, R_DEV)),
        ],
        axis=0,
    )
    pieces = split3(payload)
    total = None
    for piece in pieces:
        rows = [
            piece * (rank == float(m)).astype(f32).astype(bf16) for m in range(2 * HALF)
        ]
        part = dot_nt(hits_b, jnp.concatenate(rows, axis=0))
        total = part if total is None else total + part
    send_ref[...] = total


def owner_kernel(recv_ref, field_ref, ret_ref):
    width = HALF * COMPS
    packed = jnp.concatenate([recv_ref[:, :width], recv_ref[:, width:]], axis=0)
    comps = packed.T
    pieces = jnp.concatenate(split3(field_ref[...]), axis=1)
    rows = []
    for pair in range(HALF // 2):
        a = comps[(2 * pair) * COMPS : (2 * pair + 1) * COMPS]
        b = comps[(2 * pair + 1) * COMPS : (2 * pair + 2) * COMPS]
        both = jnp.concatenate([a, b], axis=1)
        slot = both[3 * NP : 3 * NP + 1].astype(jnp.int32)
        pick = (iota((128, 256), 0) == slot).astype(f32).astype(bf16)
        gathered = dot_nn(pieces, jnp.concatenate([pick, pick, pick], axis=0))
        wx = both[0:NP]
        wy = both[NP : 2 * NP]
        wz = both[2 * NP : 3 * NP]
        acc = None
        for k in range(NP):
            line = None
            for j in range(NP):
                row = (k * NP + j) * NP
                term = gathered[row : row + NP] * wy[j : j + 1]
                line = term if line is None else line + term
            line = line * wz[k : k + 1]
            acc = line if acc is None else acc + line
        value = jnp.sum(acc * wx, axis=0, keepdims=True)
        rows.append(value[:, :128])
        rows.append(value[:, 128:])
    rows.append(jnp.zeros((128 - HALF, 128), f32))
    turned = jnp.concatenate(rows, axis=0).T
    ret_ref[...] = turned[:OWNERS] + pltpu.roll(turned[OWNERS:], 16, 1)


def deriv8(table, v):
    plus = [v[m] + v[7 - m] for m in range(4)]
    minus = [v[m] - v[7 - m] for m in range(4)]
    out = [None] * 8
    for a in range(4):
        even = odd = None
        for m in range(4):
            ce = 0.5 * (table[a, m] + table[a, 7 - m])
            co = 0.5 * (table[a, m] - table[a, 7 - m])
            te = plus[m] * float(ce)
            to = minus[m] * float(co)
            even = te if even is None else even + te
            odd = to if odd is None else odd + to
        out[a] = odd + even
        out[7 - a] = odd - even
    return out


def apply_line(v, coef):
    grad = deriv8(DERIV, v)
    return deriv8(DERIV.T, [grad[a] * coef(a) for a in range(8)])


def stiff_apply(v_ref, coef_ref, mass_ref, out_ref):
    def per_k(k, carry):
        base = pl.multiple_of(k * 64, 64)
        lines = [v_ref[pl.ds(base + i, 8, stride=8), :] for i in range(8)]
        res = apply_line(lines, lambda a: coef_ref[pl.ds(base + a * 8, 8), :])
        for i in range(8):
            out_ref[pl.ds(base + i, 8, stride=8), :] = res[i]
        rows = [v_ref[pl.ds(base + j * 8, 8), :] for j in range(8)]
        res = apply_line(rows, lambda b: coef_ref[pl.ds(512 + base + b * 8, 8), :])
        for j in range(8):
            at = pl.ds(base + j * 8, 8)
            out_ref[at, :] = out_ref[at, :] + res[j] + mass_ref[at, :] * rows[j]
        return carry

    lax.fori_loop(0, 8, per_k, 0)

    def per_j(j, carry):
        base = pl.multiple_of(j * 8, 8)
        cols = [v_ref[pl.ds(base + k * 64, 8), :] for k in range(8)]
        res = apply_line(cols, lambda c: coef_ref[pl.ds(1024 + base + c * 64, 8), :])
        for k in range(8):
            at = pl.ds(base + k * 64, 8)
            out_ref[at, :] = out_ref[at, :] + res[k]
        return carry

    lax.fori_loop(0, 8, per_j, 0)


def couple(high, low, shift, pos, count):
    lanes = high.shape[-1]
    next_low = pltpu.roll(low, lanes - shift, high.ndim - 1)
    prev_high = pltpu.roll(high, shift, high.ndim - 1)
    new_high = high + jnp.where(pos < count - 1, next_low, 0.0)
    new_low = low + jnp.where(pos > 0, prev_high, 0.0)
    return new_high, new_low


def in_plane(ref, count=NP):
    rows = count * NP
    col = iota((rows, 128), 1) % EX
    high, low = couple(
        ref[pl.ds(7, rows, stride=8), :], ref[pl.ds(0, rows, stride=8), :], 1, col, EX
    )
    ref[pl.ds(7, rows, stride=8), :] = high
    ref[pl.ds(0, rows, stride=8), :] = low
    line = (iota((8, 128), 1) // EX) % EY
    for k in range(count):
        high, low = couple(
            ref[k * 64 + 56 : k * 64 + 64], ref[k * 64 : k * 64 + 8], EX, line, EY
        )
        ref[k * 64 + 56 : k * 64 + 64] = high
        ref[k * 64 : k * 64 + 8] = low


def through(bottom, top, below, above):
    first = iota(bottom.shape, 1) < LAYER
    new_bottom = bottom + pltpu.roll(jnp.where(first, top, below), LAYER, 1)
    new_top = top + pltpu.roll(jnp.where(first, above, bottom), LAYER, 1)
    return new_bottom, new_top


def plain8(table, v):
    out = []
    for i in range(8):
        total = None
        for a in range(8):
            if table[a, i] == 0.0:
                continue
            term = v[a] * float(table[a, i])
            total = term if total is None else total + term
        out.append(total)
    return out


def take_lanes(x, index):
    return jnp.take_along_axis(
        x, jnp.broadcast_to(index, x.shape), axis=1, mode="promise_in_bounds"
    )


def setup_kernel(
    order_ref,
    stiff_ref,
    mass_ref,
    field_ref,
    basis_ref,
    inverse_ref,
    coef_ref,
    mass_out_ref,
    start_ref,
    diag_ref,
    inv_ref,
    basis_out_ref,
    solve_ref,
    pack_up_ref,
    pack_down_ref,
    tmp_ref,
):
    order = order_ref[...]
    match = (iota((128, 128), 0) == order).astype(f32)
    inv = jnp.sum(match.T * iota((128, 128), 0).astype(f32), axis=0, keepdims=True)
    inv = inv.astype(jnp.int32)
    inv_ref[...] = inv
    tmp_ref[...] = take_lanes(stiff_ref[0:512, :], inv)
    for k in range(8):
        for i in range(8):
            coef_ref[k * 64 + i * 8 : k * 64 + i * 8 + 8, :] = tmp_ref[
                pl.ds(k * 64 + i, 8, stride=8), :
            ]
    coef_ref[512:1536, :] = take_lanes(stiff_ref[512:1536, :], inv)
    mass_out_ref[...] = take_lanes(mass_ref[...], inv)
    start_ref[...] = take_lanes(field_ref[...], inv)
    basis = dot_nn(match, basis_ref[...], exact_mode)
    basis_out_ref[...] = basis
    solve = dot_nn(basis, inverse_ref[...], exact_mode)
    solve_ref[...] = solve
    squared = DERIV * DERIV

    def per_k(k, carry):
        base = pl.multiple_of(k * 64, 64)
        res = plain8(squared, [coef_ref[pl.ds(base + a * 8, 8), :] for a in range(8)])
        for i in range(8):
            diag_ref[pl.ds(base + i, 8, stride=8), :] = res[i]
        res = plain8(squared, [coef_ref[pl.ds(512 + base + b * 8, 8), :] for b in range(8)])
        for j in range(8):
            at = pl.ds(base + j * 8, 8)
            diag_ref[at, :] = diag_ref[at, :] + res[j] + mass_out_ref[at, :]
        return carry

    lax.fori_loop(0, 8, per_k, 0)

    def per_j(j, carry):
        base = pl.multiple_of(j * 8, 8)
        res = plain8(squared, [coef_ref[pl.ds(1024 + base + c * 64, 8), :] for c in range(8)])
        for k in range(8):
            at = pl.ds(base + k * 64, 8)
            diag_ref[at, :] = diag_ref[at, :] + res[k]
        return carry

    lax.fori_loop(0, 8, per_j, 0)
    in_plane(diag_ref)
    pack_up_ref[:, 0:512] = basis[LAYER:]
    pack_up_ref[:, 512:1024] = solve[LAYER:]
    pack_up_ref[:, 1024:1152] = mass_out_ref[448:512, :]
    pack_down_ref[:, 0:512] = basis[:LAYER]
    pack_down_ref[:, 512:1024] = solve[:LAYER]
    pack_down_ref[:, 1024:1152] = mass_out_ref[0:64, :]


def source_kernel(
    ret_ref,
    owner_ref,
    rank_ref,
    ids_ref,
    live_ref,
    load_ref,
    inv_ref,
    start_ref,
    coef_ref,
    mass_ref,
    diag_ref,
    out_ref,
    up_ref,
    down_ref,
):
    hits = (iota((OWNERS, R_DEV), 0) == owner_ref[...]).astype(f32)
    picked = dot_nn(ret_ref[...].T, hits, exact_mode)[0:32]
    rank = rank_ref[...].astype(jnp.int32)
    place = rank + jnp.where(rank >= HALF, 16 - HALF, 0)
    value = jnp.sum(
        jnp.where(iota((32, R_DEV), 0) == place, picked, 0.0), axis=0, keepdims=True
    )
    value = jnp.where(iota((1, R_DEV), 1) < live_ref[0, 0], value, 0.0)
    ids = ids_ref[...]
    node = lax.shift_right_logical(ids, 7)
    elem = jnp.bitwise_and(ids, 127)
    at_node = (iota((NODES, R_DEV), 0) == node).astype(f32).astype(bf16)
    at_elem = (iota((128, R_DEV), 0) == elem).astype(f32).astype(bf16)
    spread = jnp.concatenate([at_elem * piece for piece in split3(value)], axis=0)
    landed = dot_nt(at_node, spread)
    source = load_ref[...] + (landed[:, 0:128] + landed[:, 128:256] + landed[:, 256:384])
    source = take_lanes(source, inv_ref[...])
    stiff_apply(start_ref, coef_ref, mass_ref, out_ref)
    out_ref[...] = source - out_ref[...]
    in_plane(out_ref)
    up_ref[0:64] = out_ref[448:512]
    up_ref[64:128] = diag_ref[448:512]
    down_ref[0:64] = out_ref[0:64]
    down_ref[64:128] = diag_ref[0:64]


def finish_through(w_ref, below, above):
    bottom, top = through(w_ref[0:64], w_ref[448:512], below, above)
    return jnp.concatenate([bottom, w_ref[64:448], top], axis=0)


def emit(update_ref, coef_ref, mass_ref, w_ref, up_ref, down_ref):
    stiff_apply(update_ref, coef_ref, mass_ref, w_ref)
    in_plane(w_ref)
    up_ref[...] = w_ref[448:512]
    down_ref[...] = w_ref[0:64]


def first_step_kernel(
    w_ref,
    diag_ref,
    start_ref,
    below_ref,
    above_ref,
    coef_ref,
    mass_ref,
    res_ref,
    upd_ref,
    cur_ref,
    invd_ref,
    w_out_ref,
    up_ref,
    down_ref,
):
    residual = finish_through(w_ref, below_ref[0:64], above_ref[0:64])
    diag = finish_through(diag_ref, below_ref[64:128], above_ref[64:128])
    invd = 1.0 / diag
    invd_ref[...] = invd
    res_ref[...] = residual
    update = residual * invd * STEPS[0][1]
    upd_ref[...] = update
    cur_ref[...] = start_ref[...] + update
    emit(upd_ref, coef_ref, mass_ref, w_out_ref, up_ref, down_ref)


def step_kernel(
    turn,
    send,
    w_ref,
    res_in_ref,
    upd_in_ref,
    cur_in_ref,
    invd_ref,
    below_ref,
    above_ref,
    coef_ref,
    mass_ref,
    res_ref,
    upd_ref,
    cur_ref,
    *out_refs,
):
    alpha, beta = STEPS[turn]
    residual = res_in_ref[...] - finish_through(w_ref, below_ref[...], above_ref[...])
    res_ref[...] = residual
    update = alpha * upd_in_ref[...] + beta * invd_ref[...] * residual
    upd_ref[...] = update
    cur_ref[...] = cur_in_ref[...] + update
    if send:
        emit(upd_ref, coef_ref, mass_ref, *out_refs)


def coarse_kernel(res_ref, w_ref, basis_ref, from_below_ref, from_above_ref, out_ref):
    zeros = jnp.zeros((64, 128), f32)
    local = res_ref[...] - finish_through(w_ref, zeros, zeros)
    sums = jnp.sum(local, axis=0, keepdims=True)
    bottom = -jnp.sum(w_ref[0:64], axis=0, keepdims=True)
    top = -jnp.sum(w_ref[448:512], axis=0, keepdims=True)
    outer = jnp.where(iota((1, 128), 1) < LAYER, bottom, top)
    outer_basis = jnp.concatenate(
        [from_below_ref[:, 0:512], from_above_ref[:, 0:512]], axis=0
    )
    left = jnp.broadcast_to(jnp.concatenate([sums, outer], axis=1), (8, 256))
    right = jnp.concatenate([basis_ref[...], outer_basis], axis=0)
    part = dot_nn(left, right, exact_mode) * (1.0 / math.sqrt(NODES))
    out_ref[...] = jnp.broadcast_to(part[0:1], (OWNERS, NC))


def restart_kernel(
    parts_ref,
    solve_ref,
    from_below_ref,
    from_above_ref,
    mass_ref,
    w_ref,
    res_in_ref,
    cur_in_ref,
    invd_ref,
    below_ref,
    above_ref,
    coef_ref,
    res_ref,
    upd_ref,
    cur_ref,
    w_out_ref,
    up_ref,
    down_ref,
    near_ref,
):
    coarse = jnp.broadcast_to(jnp.sum(parts_ref[...], axis=0, keepdims=True), (8, NC))
    outer = jnp.concatenate(
        [from_above_ref[:, 512:1024], from_below_ref[:, 512:1024]], axis=0
    )
    both = dot_nt(coarse, jnp.concatenate([solve_ref[...], outer], axis=0), exact_mode)
    own = both[0:1, 0:128]
    beside = both[0:1, 128:256]
    near_ref[0:64] = from_below_ref[:, 1024:1152] * beside
    near_ref[64:128] = from_above_ref[:, 1024:1152] * beside
    in_plane(near_ref, 2)
    w_out_ref[...] = mass_ref[...] * own
    in_plane(w_out_ref)
    total = finish_through(
        w_ref, below_ref[...], above_ref[...]
    ) + finish_through(w_out_ref, near_ref[0:64], near_ref[64:128])
    residual = res_in_ref[...] - total
    res_ref[...] = residual
    update = residual * invd_ref[...] * STEPS[0][1]
    upd_ref[...] = update
    cur_ref[...] = cur_in_ref[...] + own + update
    emit(upd_ref, coef_ref, mass_ref, w_out_ref, up_ref, down_ref)


def last_kernel(
    w_ref,
    res_in_ref,
    upd_in_ref,
    cur_in_ref,
    invd_ref,
    below_ref,
    above_ref,
    order_ref,
    out_ref,
):
    alpha, beta = STEPS[CHEB - 1]
    residual = res_in_ref[...] - finish_through(w_ref, below_ref[...], above_ref[...])
    update = alpha * upd_in_ref[...] + beta * invd_ref[...] * residual
    out_ref[...] = take_lanes(cur_in_ref[...] + update, order_ref[...])


def call(kernel, name, outs, *args, scratch=(), smem=()):
    specs = [
        pl.BlockSpec(memory_space=pltpu.SMEM if n in smem else pltpu.VMEM)
        for n in range(len(args))
    ]
    return pl.pallas_call(
        kernel,
        name=name,
        out_shape=[jax.ShapeDtypeStruct(s, d) for s, d in outs],
        in_specs=specs,
        out_specs=[pl.BlockSpec(memory_space=pltpu.VMEM) for _ in outs],
        scratch_shapes=[pltpu.VMEM(s, f32) for s in scratch],
    )(*args)


FIELD = ((NODES, 128), f32)
PLANE = ((64, 128), f32)


def exchange(up, down):
    count = lax.axis_size("elem")
    forward = [(i, i + 1) for i in range(count - 1)]
    backward = [(b, a) for a, b in forward]
    below = lax.ppermute(up, "elem", forward)
    above = lax.ppermute(down, "elem", backward)
    return below, above


def per_device(
    pressure,
    load,
    stiffness,
    helm_mass,
    order_slots,
    recv_ids,
    donor_owner,
    donor_slot,
    interp_weights,
    live_count,
    coarse_basis,
    coarse_inverse,
):
    own_field = pressure.reshape(NODES, 128)
    order = order_slots.reshape(1, 128)
    owner = donor_owner.reshape(1, R_DEV)
    other_field = lax.ppermute(own_field, "sess", [(0, 1), (1, 0)])

    send, rank = call(
        request_kernel,
        "request",
        [((OWNERS, 2 * HALF * COMPS), f32), ((1, R_DEV), f32)],
        owner,
        donor_slot,
        interp_weights.reshape(3 * NP, R_DEV),
    )
    coef, mass, start, diag, inv, basis, solve, pack_up, pack_down = call(
        setup_kernel,
        "setup",
        [
            ((3 * NODES, 128), f32),
            FIELD,
            FIELD,
            FIELD,
            ((1, 128), jnp.int32),
            ((128, NC), f32),
            ((128, NC), f32),
            ((LAYER, 2 * NC + 128), f32),
            ((LAYER, 2 * NC + 128), f32),
        ],
        order,
        stiffness.reshape(3 * NODES, 128),
        helm_mass.reshape(NODES, 128),
        own_field,
        coarse_basis.reshape(128, NC),
        coarse_inverse.reshape(NC, NC),
        scratch=[(NODES, 128)],
    )
    from_below, from_above = exchange(pack_up, pack_down)
    received = lax.all_to_all(send, "elem", split_axis=0, concat_axis=0, tiled=True)
    (answer,) = call(
        owner_kernel, "owner", [((OWNERS, 128), f32)], received, other_field
    )
    answered = lax.all_to_all(answer, "elem", split_axis=0, concat_axis=0, tiled=True)
    w, up, down = call(
        source_kernel,
        "source",
        [FIELD, ((128, 128), f32), ((128, 128), f32)],
        answered,
        owner,
        rank,
        recv_ids,
        live_count,
        load.reshape(NODES, 128),
        inv,
        start,
        coef,
        mass,
        diag,
        smem=(4,),
    )
    below, above = exchange(up, down)
    stepped = [FIELD] * 3
    sent = [FIELD, PLANE, PLANE]
    res, upd, cur, invd, w, up, down = call(
        first_step_kernel,
        "first_step",
        stepped + [FIELD] + sent,
        w,
        diag,
        start,
        below,
        above,
        coef,
        mass,
    )
    for turn in range(1, CHEB):
        below, above = exchange(up, down)
        res, upd, cur, w, up, down = call(
            functools.partial(step_kernel, turn, True),
            f"step{turn}",
            stepped + sent,
            w,
            res,
            upd,
            cur,
            invd,
            below,
            above,
            coef,
            mass,
        )
    below, above = exchange(up, down)
    (part,) = call(
        coarse_kernel,
        "coarse",
        [((OWNERS, NC), f32)],
        res,
        w,
        basis,
        from_below,
        from_above,
    )
    parts = lax.all_to_all(part, "elem", split_axis=0, concat_axis=0, tiled=True)
    res, upd, cur, w, up, down = call(
        restart_kernel,
        "restart",
        stepped + sent,
        parts,
        solve,
        from_below,
        from_above,
        mass,
        w,
        res,
        cur,
        invd,
        below,
        above,
        coef,
        scratch=[(128, 128)],
    )
    for turn in range(1, CHEB - 1):
        below, above = exchange(up, down)
        res, upd, cur, w, up, down = call(
            functools.partial(step_kernel, turn, True),
            f"again{turn}",
            stepped + sent,
            w,
            res,
            upd,
            cur,
            invd,
            below,
            above,
            coef,
            mass,
        )
    below, above = exchange(up, down)
    (out,) = call(
        last_kernel, "last", [FIELD], w, res, upd, cur, invd, below, above, order
    )
    return out.reshape(1, NP, NP, NP, 128)


def solution(mesh):
    return jax.shard_map(
        per_device,
        mesh=mesh,
        in_specs=(
            P("sess", None, None, None, "elem"),
            P("sess", None, None, None, "elem"),
            P("sess", None, None, None, None, "elem"),
            P("sess", None, None, None, "elem"),
            P("sess", "elem", None),
            P("sess", "elem"),
            P("sess", "elem", None),
            P("sess", "elem"),
            P("sess", None, "elem"),
            P("sess", "elem"),
            P("sess", "elem", None),
            P("sess", None, None),
        ),
        out_specs=P("sess", None, None, None, "elem"),
        check_vma=False,
    )
```

time: 954 us -> 201 us (0.21)
  local copies, waits for them, and re-layouts: 440 us -> 11.9 us
  blocking collectives: 158 us -> 0 us
  other arithmetic: 119 us -> 0 us
  waiting for transfers between devices: 84.2 us -> 21.3 us
  Pallas kernels: 0 us -> 44.8 us
  matrix products: 36.7 us -> 0 us
  starting transfers between devices: 103 us -> 121 us
    psum x1 -> x0, blocking collectives: 158 us -> none  [per_device(): coarse = lax.psum(partial_coarse, 'elem')]
    scatter x50 -> x0, local copies, waits for them, and re-layouts: 136 us -> none  [the longest x12 111 us: to_grid(): return jnp.zeros_like(values).at[..., slot_grid].set(values)]
    gather x4 -> x0, local copies, waits for them, and re-layouts: 83.4 us -> none  [the longest x1 40.6 us: per_device(): gathered = other_field[..., part_slots.reshape(-1)]]
    reshape x5 -> x0, local copies, waits for them, and re-layouts: 69.5 us -> none  [the longest x1 34.6 us: per_device(): fetched = gathered.reshape(NP, NP, NP, blocks, item_count)]
    unnamed x119 -> x46, local copies, waits for them, and re-layouts: 69.6 us -> 8.38 us
    pallas_call x0 -> x13, Pallas kernels: none -> 44.8 us  [call(): pl.pallas_call(kernel, name=name, out_shape=[jax.ShapeDtypeStruct(s, d) f...]
    ppermute x23 -> x19, waiting for transfers between devices: 55.7 us -> 14.4 us  [the longest x9 13 us: exchange(): above = lax.ppermute(down, 'elem', backward)]
    dot_general x60 -> x0, matrix products: 36.7 us -> none  [the longest x9 9.5 us: local_stiffness(): jnp.einsum('ai,kjie->kjae', deriv_table, field, precision=exact_mode)]
  transfers between devices with their start and end apart: 25 -> 22, of which waited for: 12 -> 16; matrix products, arithmetic and copies ran while one was open for 19% -> 2% of each run, Pallas kernels for 0% -> 15%
where the time goes in v1:
time: 201 us; the launch traced here: 200 us
  starting transfers between devices  121 us (60%)
  Pallas kernels  44.8 us (22%)
  waiting for transfers between devices  21.3 us (11%)
  local copies, waits for them, and re-layouts  11.9 us (6%)
    ppermute x9, starting transfers between devices, exchange(): above = lax.ppermute(down, 'elem', backward)  71.1 us
    pallas_call x13, Pallas kernels, call(): pl.pallas_call(kernel, name=name, out_shape=[jax.ShapeDtypeStruct(s, d) f...  44.8 us
    ppermute x9, starting transfers between devices, exchange(): below = lax.ppermute(up, 'elem', forward)  20.7 us
    ppermute x9, waiting for transfers between devices, exchange(): above = lax.ppermute(down, 'elem', backward)  13 us
    all_to_all x1, starting transfers between devices, per_device(): lax.all_to_all(send, 'elem', split_axis=0, concat_axis=0, tiled=True)  11.6 us
    all_to_all x1, starting transfers between devices, per_device(): lax.all_to_all(part, 'elem', split_axis=0, concat_axis=0, tiled=True)  11.3 us
    unnamed x46, local copies, waits for them, and re-layouts  8.38 us
    all_to_all x1, waiting for transfers between devices, per_device(): lax.all_to_all(answer, 'elem', split_axis=0, concat_axis=0, tiled=True)  6.9 us
  transfers between devices with their start and end apart: 22, of which 16 were waited for; matrix products, arithmetic and copies ran while one was open for 2% of the time, Pallas kernels for 15%

profile of v1, /device:TPU:6, one launch (start us, length us, event | category | flops | bytes accessed | tf_op | source)
XLA Modules:
  0.0 199.7 jit_solution(2955922687969701457)
XLA Ops:
  5.0 11.6 %all-to-all-start = ((f32[64,1,768]{2,1,0:T(1,128)}), f32[64,1,768]{2,1,0:T(1,128)S(1)}, u32[]{:S(2)}, u32[]{:S(2)}) async-start(f32[64,1,768]{2,1,0:T(1,128)} %copy.13), calls=%async_computation | async-start | bytes 393216 | tf_op jit(solution)/shard_map/all_to_all | solution.py:599
  16.7 4.8 %setup.1 = (f32[1536,128]{1,0:T(8,128)}, f32[512,128]{1,0:T(8,128)}, f32[512,128]{1,0:T(8,128)}, f32[512,128]{1,0:T(8,128)}, s32[1,128]{1,0:T(1,128)}, /*index=5...) custom-call(s32[1,128]{1,0:T(1,128)} %bitcast.38, f32[1536,128]{1,0:T(8,128)} %bitcast.24, ...), custom_call_target="tpu_custom_call" | custom-call | tf_op jit(solution)/shard_map/setup/pallas_call | solution.py:526
  21.5 3.4 %collective-permute-start.9 = (f32[64,1152]{1,0:T(8,128)}, f32[64,1152]{1,0:T(8,128)S(1)}, u32[]{:S(2)}, u32[]{:S(2)}) collective-permute-start(f32[64,1152]{1,0:T(8,128)} %get-tuple-element.93), channel_id=1, source_target_pairs={{0,1},{1,2},{2,3},{3,4},{4,5},{5,6},{6,7},{7,8},{8,9},{9,10},{10,1... | collective-permute-start | bytes 884744 | tf_op jit(solution)/shard_map/ppermute | solution.py:544
  24.8 6.7 %collective-permute-start.10 = (f32[64,1152]{1,0:T(8,128)}, f32[64,1152]{1,0:T(8,128)S(1)}, u32[]{:S(2)}, u32[]{:S(2)}) collective-permute-start(f32[64,1152]{1,0:T(8,128)} %get-tuple-element.94), channel_id=1, source_target_pairs={{1,0},{2,1},{3,2},{4,3},{5,4},{6,5},{7,6},{8,7},{9,8},{10,9},{11,1... | collective-permute-start | bytes 884744 | tf_op jit(solution)/shard_map/ppermute | solution.py:545
  35.9 6.1 %all-to-all-start.1 = ((f32[64,1,128]{2,1,0:T(1,128)}), f32[64,1,128]{2,1,0:T(1,128)S(1)}, u32[]{:S(2)}, u32[]{:S(2)}) async-start(f32[64,1,128]{2,1,0:T(1,128)} %bitcast.34), calls=%async_computation.1 | async-start | bytes 65536 | tf_op jit(solution)/shard_map/all_to_all | solution.py:603
  42.6 6.9 %all-to-all-done.1 = f32[64,1,128]{2,1,0:T(1,128)S(1)} async-done(((f32[64,1,128]{2,1,0:T(1,128)}), f32[64,1,128]{2,1,0:T(1,128)S(1)}, u32[]{:S(2)}, u32[]{:S(2)}) %all-to-all-start.1) | async-done | bytes 32800 | tf_op jit(solution)/shard_map/all_to_all | solution.py:603
  50.1 4.3 %source.1 = (f32[512,128]{1,0:T(8,128)}, f32[128,128]{1,0:T(8,128)}, f32[128,128]{1,0:T(8,128)}) custom-call(f32[64,128]{1,0:T(8,128)} %bitcast.33, s32[1,1024]{1,0:T(1,128)} %bitcast.37, f32[1,1024]{1,0:T(1,128)} %get-tuple-element.62.rank_ref, s32[1,1024]{1,0:T(1,128)} %ids_ref.1, s32[1,1]{1,0:T(1,128)S(6)} %copy.22.live_ref, f32[512,128]{1,0:T(8,128)} %bitcast.27, ...), custom_call_target="tpu_custom_call" | custom-call | tf_op jit(solution)/shard_map/source/pallas_call | solution.py:526
  57.0 7.6 %collective-permute-start.2 = (f32[128,128]{1,0:T(8,128)}, f32[128,128]{1,0:T(8,128)S(1)}, u32[]{:S(2)}, u32[]{:S(2)}) collective-permute-start(f32[128,128]{1,0:T(8,128)} %get-tuple-element.70), channel_id=1, source_target_pairs={{1,0},{2,1},{3,2},{4,3},{5,4},{6,5},{7,6},{8,7},{9,8},{10,9},{11,1... | collective-permute-start | bytes 196616 | tf_op jit(solution)/shard_map/ppermute | solution.py:545
  67.4 3.4 %first_step.1 = (f32[512,128]{1,0:T(8,128)}, f32[512,128]{1,0:T(8,128)}, f32[512,128]{1,0:T(8,128)}, f32[512,128]{1,0:T(8,128)}, f32[512,128]{1,0:T(8,128)}, /*index=5*/f32[64,128]{1,0:T(8,128)}, f32[64,128]{1,0:T(8,128)}) custom-call(f32[512,128]{1,0:T(8,128)} %get-tuple-element.68.w_ref, f32[512,128]{1,0:T(8,128)} %get-tuple-element.67.diag_ref, ...), custom_call_target="tpu_custom_call" | custom-call | tf_op jit(solution)/shard_map/first_step/pallas_call | solution.py:526
  72.7 8.4 %collective-permute-start.4 = (f32[64,128]{1,0:T(8,128)}, f32[64,128]{1,0:T(8,128)S(1)}, u32[]{:S(2)}, u32[]{:S(2)}) collective-permute-start(f32[64,128]{1,0:T(8,128)} %get-tuple-element.77), channel_id=1, source_target_pairs={{1,0},{2,1},{3,2},{4,3},{5,4},{6,5},{7,6},{8,7},{9,8},{10,9},{11,1... | collective-permute-start | bytes 98312 | tf_op jit(solution)/shard_map/ppermute | solution.py:545
  83.6 3.4 %step1.1 = (f32[512,128]{1,0:T(8,128)}, f32[512,128]{1,0:T(8,128)}, f32[512,128]{1,0:T(8,128)}, f32[512,128]{1,0:T(8,128)}, f32[64,128]{1,0:T(8,128)}, /*index=5*/f32[64,128]{1,0:T(8,128)}) custom-call(f32[512,128]{1,0:T(8,128)} %get-tuple-element.71.w_ref, f32[512,128]{1,0:T(8,128)} %get-tuple-element.72.res_in_ref, ...), custom_call_target="tpu_custom_call" | custom-call | tf_op jit(solution)/shard_map/step1/pallas_call | solution.py:526
  88.9 8.3 %collective-permute-start.6 = (f32[64,128]{1,0:T(8,128)}, f32[64,128]{1,0:T(8,128)S(1)}, u32[]{:S(2)}, u32[]{:S(2)}) collective-permute-start(f32[64,128]{1,0:T(8,128)} %get-tuple-element.83), channel_id=1, source_target_pairs={{1,0},{2,1},{3,2},{4,3},{5,4},{6,5},{7,6},{8,7},{9,8},{10,9},{11,1... | collective-permute-start | bytes 98312 | tf_op jit(solution)/shard_map/ppermute | solution.py:545
  99.8 3.5 %step2.1 = (f32[512,128]{1,0:T(8,128)}, f32[512,128]{1,0:T(8,128)}, f32[512,128]{1,0:T(8,128)}, f32[512,128]{1,0:T(8,128)}, f32[64,128]{1,0:T(8,128)}, /*index=5*/f32[64,128]{1,0:T(8,128)}) custom-call(f32[512,128]{1,0:T(8,128)} %get-tuple-element.78.w_ref, f32[512,128]{1,0:T(8,128)} %get-tuple-element.79.res_in_ref, ...), custom_call_target="tpu_custom_call" | custom-call | tf_op jit(solution)/shard_map/step2/pallas_call | solution.py:526
  105.2 8.3 %collective-permute-start.8 = (f32[64,128]{1,0:T(8,128)}, f32[64,128]{1,0:T(8,128)S(1)}, u32[]{:S(2)}, u32[]{:S(2)}) collective-permute-start(f32[64,128]{1,0:T(8,128)} %get-tuple-element.89), channel_id=1, source_target_pairs={{1,0},{2,1},{3,2},{4,3},{5,4},{6,5},{7,6},{8,7},{9,8},{10,9},{11,1... | collective-permute-start | bytes 98312 | tf_op jit(solution)/shard_map/ppermute | solution.py:545
  116.0 3.4 %step3.1 = (f32[512,128]{1,0:T(8,128)}, f32[512,128]{1,0:T(8,128)}, f32[512,128]{1,0:T(8,128)}, f32[512,128]{1,0:T(8,128)}, f32[64,128]{1,0:T(8,128)}, /*index=5*/f32[64,128]{1,0:T(8,128)}) custom-call(f32[512,128]{1,0:T(8,128)} %get-tuple-element.84.w_ref, f32[512,128]{1,0:T(8,128)} %get-tuple-element.85.res_in_ref, ...), custom_call_target="tpu_custom_call" | custom-call | tf_op jit(solution)/shard_map/step3/pallas_call | solution.py:526
  124.4 11.3 %all-to-all-start.2 = ((f32[64,1,512]{2,1,0:T(1,128)}), f32[64,1,512]{2,1,0:T(1,128)S(1)}, u32[]{:S(2)}, u32[]{:S(2)}) async-start(f32[64,1,512]{2,1,0:T(1,128)} %copy.15), calls=%async_computation.2 | async-start | bytes 262144 | tf_op jit(solution)/shard_map/all_to_all | solution.py:663
  135.7 3.4 %collective-permute-start.11 = (f32[64,128]{1,0:T(8,128)S(1)}, f32[64,128]{1,0:T(8,128)S(1)}, u32[]{:S(2)}, u32[]{:S(2)}) collective-permute-start(f32[64,128]{1,0:T(8,128)S(1)} %copy-done.21), channel_id=1, source_target_pairs={{0,1},{1,2},{2,3},{3,4},{4,5},{5,6},{6,7},{7,8},{8,9},{9,10},{10,1... | collective-permute-start | bytes 98312 | tf_op jit(solution)/shard_map/ppermute | solution.py:544
  139.1 6.7 %collective-permute-start.12 = (f32[64,128]{1,0:T(8,128)S(1)}, f32[64,128]{1,0:T(8,128)S(1)}, u32[]{:S(2)}, u32[]{:S(2)}) collective-permute-start(f32[64,128]{1,0:T(8,128)S(1)} %copy-done.20), channel_id=1, source_target_pairs={{1,0},{2,1},{3,2},{4,3},{5,4},{6,5},{7,6},{8,7},{9,8},{10,9},{11,1... | collective-permute-start | bytes 98312 | tf_op jit(solution)/shard_map/ppermute | solution.py:545
  147.9 4.3 %restart.1 = (f32[512,128]{1,0:T(8,128)}, f32[512,128]{1,0:T(8,128)}, f32[512,128]{1,0:T(8,128)}, f32[512,128]{1,0:T(8,128)}, f32[64,128]{1,0:T(8,128)}, /*index=5*/f32[64,128]{1,0:T(8,128)}) custom-call(f32[64,512]{1,0:T(8,128)} %bitcast.25, f32[128,512]{1,0:T(8,128)} %get-tuple-element.95.solve_ref, f32[64,1152]{1,0:T(8,128)} %copy-done, ...), custom_call_target="tpu_custom_call" | custom-call | tf_op jit(solution)/shard_map/restart/pallas_call | solution.py:526
  154.2 8.4 %collective-permute-start.14 = (f32[64,128]{1,0:T(8,128)}, f32[64,128]{1,0:T(8,128)S(1)}, u32[]{:S(2)}, u32[]{:S(2)}) collective-permute-start(f32[64,128]{1,0:T(8,128)} %get-tuple-element.104), channel_id=1, source_target_pairs={{1,0},{2,1},{3,2},{4,3},{5,4},{6,5},{7,6},{8,7},{9,8},{10,9},{11,1... | collective-permute-start | bytes 98312 | tf_op jit(solution)/shard_map/ppermute | solution.py:545
  165.2 3.4 %again1.1 = (f32[512,128]{1,0:T(8,128)}, f32[512,128]{1,0:T(8,128)}, f32[512,128]{1,0:T(8,128)}, f32[512,128]{1,0:T(8,128)}, f32[64,128]{1,0:T(8,128)}, /*index=5*/f32[64,128]{1,0:T(8,128)}) custom-call(f32[512,128]{1,0:T(8,128)} %get-tuple-element.99.w_ref, f32[512,128]{1,0:T(8,128)} %get-tuple-element.100.res_in_ref, ...), custom_call_target="tpu_custom_call" | custom-call | tf_op jit(solution)/shard_map/again1/pallas_call | solution.py:526
  170.5 8.3 %collective-permute-start.16 = (f32[64,128]{1,0:T(8,128)}, f32[64,128]{1,0:T(8,128)S(1)}, u32[]{:S(2)}, u32[]{:S(2)}) collective-permute-start(f32[64,128]{1,0:T(8,128)} %get-tuple-element.110), channel_id=1, source_target_pairs={{1,0},{2,1},{3,2},{4,3},{5,4},{6,5},{7,6},{8,7},{9,8},{10,9},{11,1... | collective-permute-start | bytes 98312 | tf_op jit(solution)/shard_map/ppermute | solution.py:545
  181.3 3.5 %again2.1 = (f32[512,128]{1,0:T(8,128)}, f32[512,128]{1,0:T(8,128)}, f32[512,128]{1,0:T(8,128)}, f32[512,128]{1,0:T(8,128)}, f32[64,128]{1,0:T(8,128)}, /*index=5*/f32[64,128]{1,0:T(8,128)}) custom-call(f32[512,128]{1,0:T(8,128)} %get-tuple-element.105.w_ref, f32[512,128]{1,0:T(8,128)} %get-tuple-element.106.res_in_ref, ...), custom_call_target="tpu_custom_call" | custom-call | tf_op jit(solution)/shard_map/again2/pallas_call | solution.py:526
  186.7 8.3 %collective-permute-start.18 = (f32[64,128]{1,0:T(8,128)}, f32[64,128]{1,0:T(8,128)S(1)}, u32[]{:S(2)}, u32[]{:S(2)}) collective-permute-start(f32[64,128]{1,0:T(8,128)} %get-tuple-element.116), channel_id=1, source_target_pairs={{1,0},{2,1},{3,2},{4,3},{5,4},{6,5},{7,6},{8,7},{9,8},{10,9},{11,1... | collective-permute-start | bytes 98312 | tf_op jit(solution)/shard_map/ppermute | solution.py:545
  (81 shorter events, 50.9 us)
Async XLA Ops:
  0.0 32.2 %collective-permute-start = (f32[512,128]{1,0:T(8,128)}, f32[512,128]{1,0:T(8,128)S(1)}, u32[]{:S(2)}, u32[]{:S(2)}) collective-permute-start(f32[512,128]{1,0:T(8,128)} %bitcast.30), channel_id=1, source_target_pairs={{0,64},{64,0},{1,65},{65,1},{2,66},{66,2},{3,67},{67,3},{4,68},{68... | collective-permute-start | bytes 786440 | tf_op jit(solution)/shard_map/ppermute | solution.py:566
  5.0 26.5 %all-to-all-start = ((f32[64,1,768]{2,1,0:T(1,128)}), f32[64,1,768]{2,1,0:T(1,128)S(1)}, u32[]{:S(2)}, u32[]{:S(2)}) async-start(f32[64,1,768]{2,1,0:T(1,128)} %copy.13), calls=%async_computation | async-start | bytes 393216 | tf_op jit(solution)/shard_map/all_to_all | solution.py:599
  21.5 98.0 %collective-permute-start.9 = (f32[64,1152]{1,0:T(8,128)}, f32[64,1152]{1,0:T(8,128)S(1)}, u32[]{:S(2)}, u32[]{:S(2)}) collective-permute-start(f32[64,1152]{1,0:T(8,128)} %get-tuple-element.93), channel_id=1, source_target_pairs={{0,1},{1,2},{2,3},{3,4},{4,5},{5,6},{6,7},{7,8},{8,9},{9,10},{10,1... | collective-permute-start | bytes 884744 | tf_op jit(solution)/shard_map/ppermute | solution.py:544
  24.8 94.6 %collective-permute-start.10 = (f32[64,1152]{1,0:T(8,128)}, f32[64,1152]{1,0:T(8,128)S(1)}, u32[]{:S(2)}, u32[]{:S(2)}) collective-permute-start(f32[64,1152]{1,0:T(8,128)} %get-tuple-element.94), channel_id=1, source_target_pairs={{1,0},{2,1},{3,2},{4,3},{5,4},{6,5},{7,6},{8,7},{9,8},{10,9},{11,1... | collective-permute-start | bytes 884744 | tf_op jit(solution)/shard_map/ppermute | solution.py:545
  35.9 13.7 %all-to-all-start.1 = ((f32[64,1,128]{2,1,0:T(1,128)}), f32[64,1,128]{2,1,0:T(1,128)S(1)}, u32[]{:S(2)}, u32[]{:S(2)}) async-start(f32[64,1,128]{2,1,0:T(1,128)} %bitcast.34), calls=%async_computation.1 | async-start | bytes 65536 | tf_op jit(solution)/shard_map/all_to_all | solution.py:603
  54.5 10.6 %collective-permute-start.1 = (f32[128,128]{1,0:T(8,128)}, f32[128,128]{1,0:T(8,128)S(1)}, u32[]{:S(2)}, u32[]{:S(2)}) collective-permute-start(f32[128,128]{1,0:T(8,128)} %get-tuple-element.69), channel_id=1, source_target_pairs={{0,1},{1,2},{2,3},{3,4},{4,5},{5,6},{6,7},{7,8},{8,9},{9,10},{10,1... | collective-permute-start | bytes 196616 | tf_op jit(solution)/shard_map/ppermute | solution.py:544
  57.0 9.8 %collective-permute-start.2 = (f32[128,128]{1,0:T(8,128)}, f32[128,128]{1,0:T(8,128)S(1)}, u32[]{:S(2)}, u32[]{:S(2)}) collective-permute-start(f32[128,128]{1,0:T(8,128)} %get-tuple-element.70), channel_id=1, source_target_pairs={{1,0},{2,1},{3,2},{4,3},{5,4},{6,5},{7,6},{8,7},{9,8},{10,9},{11,1... | collective-permute-start | bytes 196616 | tf_op jit(solution)/shard_map/ppermute | solution.py:545
  70.8 10.5 %collective-permute-start.3 = (f32[64,128]{1,0:T(8,128)}, f32[64,128]{1,0:T(8,128)S(1)}, u32[]{:S(2)}, u32[]{:S(2)}) collective-permute-start(f32[64,128]{1,0:T(8,128)} %get-tuple-element.76), channel_id=1, source_target_pairs={{0,1},{1,2},{2,3},{3,4},{4,5},{5,6},{6,7},{7,8},{8,9},{9,10},{10,1... | collective-permute-start | bytes 98312 | tf_op jit(solution)/shard_map/ppermute | solution.py:544
  72.7 10.3 %collective-permute-start.4 = (f32[64,128]{1,0:T(8,128)}, f32[64,128]{1,0:T(8,128)S(1)}, u32[]{:S(2)}, u32[]{:S(2)}) collective-permute-start(f32[64,128]{1,0:T(8,128)} %get-tuple-element.77), channel_id=1, source_target_pairs={{1,0},{2,1},{3,2},{4,3},{5,4},{6,5},{7,6},{8,7},{9,8},{10,9},{11,1... | collective-permute-start | bytes 98312 | tf_op jit(solution)/shard_map/ppermute | solution.py:545
  87.0 10.4 %collective-permute-start.5 = (f32[64,128]{1,0:T(8,128)}, f32[64,128]{1,0:T(8,128)S(1)}, u32[]{:S(2)}, u32[]{:S(2)}) collective-permute-start(f32[64,128]{1,0:T(8,128)} %get-tuple-element.82), channel_id=1, source_target_pairs={{0,1},{1,2},{2,3},{3,4},{4,5},{5,6},{6,7},{7,8},{8,9},{9,10},{10,1... | collective-permute-start | bytes 98312 | tf_op jit(solution)/shard_map/ppermute | solution.py:544
  88.9 10.2 %collective-permute-start.6 = (f32[64,128]{1,0:T(8,128)}, f32[64,128]{1,0:T(8,128)S(1)}, u32[]{:S(2)}, u32[]{:S(2)}) collective-permute-start(f32[64,128]{1,0:T(8,128)} %get-tuple-element.83), channel_id=1, source_target_pairs={{1,0},{2,1},{3,2},{4,3},{5,4},{6,5},{7,6},{8,7},{9,8},{10,9},{11,1... | collective-permute-start | bytes 98312 | tf_op jit(solution)/shard_map/ppermute | solution.py:545
  103.2 10.4 %collective-permute-start.7 = (f32[64,128]{1,0:T(8,128)}, f32[64,128]{1,0:T(8,128)S(1)}, u32[]{:S(2)}, u32[]{:S(2)}) collective-permute-start(f32[64,128]{1,0:T(8,128)} %get-tuple-element.88), channel_id=1, source_target_pairs={{0,1},{1,2},{2,3},{3,4},{4,5},{5,6},{6,7},{7,8},{8,9},{9,10},{10,1... | collective-permute-start | bytes 98312 | tf_op jit(solution)/shard_map/ppermute | solution.py:544
  105.2 10.2 %collective-permute-start.8 = (f32[64,128]{1,0:T(8,128)}, f32[64,128]{1,0:T(8,128)S(1)}, u32[]{:S(2)}, u32[]{:S(2)}) collective-permute-start(f32[64,128]{1,0:T(8,128)} %get-tuple-element.89), channel_id=1, source_target_pairs={{1,0},{2,1},{3,2},{4,3},{5,4},{6,5},{7,6},{8,7},{9,8},{10,9},{11,1... | collective-permute-start | bytes 98312 | tf_op jit(solution)/shard_map/ppermute | solution.py:545
  124.4 11.3 %copy-start.21 = (f32[64,128]{1,0:T(8,128)S(1)}, f32[64,128]{1,0:T(8,128)}, u32[]{:S(2)}) copy-start(f32[64,128]{1,0:T(8,128)} %get-tuple-element.97) | copy-start | bytes 98308
  124.4 14.7 %copy-start.20 = (f32[64,128]{1,0:T(8,128)S(1)}, f32[64,128]{1,0:T(8,128)}, u32[]{:S(2)}) copy-start(f32[64,128]{1,0:T(8,128)} %get-tuple-element.98) | copy-start | bytes 98308
  124.4 21.4 %all-to-all-start.2 = ((f32[64,1,512]{2,1,0:T(1,128)}), f32[64,1,512]{2,1,0:T(1,128)S(1)}, u32[]{:S(2)}, u32[]{:S(2)}) async-start(f32[64,1,512]{2,1,0:T(1,128)} %copy.15), calls=%async_computation.2 | async-start | bytes 262144 | tf_op jit(solution)/shard_map/all_to_all | solution.py:663
  135.7 10.8 %collective-permute-start.11 = (f32[64,128]{1,0:T(8,128)S(1)}, f32[64,128]{1,0:T(8,128)S(1)}, u32[]{:S(2)}, u32[]{:S(2)}) collective-permute-start(f32[64,128]{1,0:T(8,128)S(1)} %copy-done.21), channel_id=1, source_target_pairs={{0,1},{1,2},{2,3},{3,4},{4,5},{5,6},{6,7},{7,8},{8,9},{9,10},{10,1... | collective-permute-start | bytes 98312 | tf_op jit(solution)/shard_map/ppermute | solution.py:544
  139.1 8.3 %collective-permute-start.12 = (f32[64,128]{1,0:T(8,128)S(1)}, f32[64,128]{1,0:T(8,128)S(1)}, u32[]{:S(2)}, u32[]{:S(2)}) collective-permute-start(f32[64,128]{1,0:T(8,128)S(1)} %copy-done.20), channel_id=1, source_target_pairs={{1,0},{2,1},{3,2},{4,3},{5,4},{6,5},{7,6},{8,7},{9,8},{10,9},{11,1... | collective-permute-start | bytes 98312 | tf_op jit(solution)/shard_map/ppermute | solution.py:545
  152.3 10.5 %collective-permute-start.13 = (f32[64,128]{1,0:T(8,128)}, f32[64,128]{1,0:T(8,128)S(1)}, u32[]{:S(2)}, u32[]{:S(2)}) collective-permute-start(f32[64,128]{1,0:T(8,128)} %get-tuple-element.103), channel_id=1, source_target_pairs={{0,1},{1,2},{2,3},{3,4},{4,5},{5,6},{6,7},{7,8},{8,9},{9,10},{10,1... | collective-permute-start | bytes 98312 | tf_op jit(solution)/shard_map/ppermute | solution.py:544
  154.2 10.3 %collective-permute-start.14 = (f32[64,128]{1,0:T(8,128)}, f32[64,128]{1,0:T(8,128)S(1)}, u32[]{:S(2)}, u32[]{:S(2)}) collective-permute-start(f32[64,128]{1,0:T(8,128)} %get-tuple-element.104), channel_id=1, source_target_pairs={{1,0},{2,1},{3,2},{4,3},{5,4},{6,5},{7,6},{8,7},{9,8},{10,9},{11,1... | collective-permute-start | bytes 98312 | tf_op jit(solution)/shard_map/ppermute | solution.py:545
  168.6 10.4 %collective-permute-start.15 = (f32[64,128]{1,0:T(8,128)}, f32[64,128]{1,0:T(8,128)S(1)}, u32[]{:S(2)}, u32[]{:S(2)}) collective-permute-start(f32[64,128]{1,0:T(8,128)} %get-tuple-element.109), channel_id=1, source_target_pairs={{0,1},{1,2},{2,3},{3,4},{4,5},{5,6},{6,7},{7,8},{8,9},{9,10},{10,1... | collective-permute-start | bytes 98312 | tf_op jit(solution)/shard_map/ppermute | solution.py:544
  170.5 10.2 %collective-permute-start.16 = (f32[64,128]{1,0:T(8,128)}, f32[64,128]{1,0:T(8,128)S(1)}, u32[]{:S(2)}, u32[]{:S(2)}) collective-permute-start(f32[64,128]{1,0:T(8,128)} %get-tuple-element.110), channel_id=1, source_target_pairs={{1,0},{2,1},{3,2},{4,3},{5,4},{6,5},{7,6},{8,7},{9,8},{10,9},{11,1... | collective-permute-start | bytes 98312 | tf_op jit(solution)/shard_map/ppermute | solution.py:545
  184.8 10.4 %collective-permute-start.17 = (f32[64,128]{1,0:T(8,128)}, f32[64,128]{1,0:T(8,128)S(1)}, u32[]{:S(2)}, u32[]{:S(2)}) collective-permute-start(f32[64,128]{1,0:T(8,128)} %get-tuple-element.115), channel_id=1, source_target_pairs={{0,1},{1,2},{2,3},{3,4},{4,5},{5,6},{6,7},{7,8},{8,9},{9,10},{10,1... | collective-permute-start | bytes 98312 | tf_op jit(solution)/shard_map/ppermute | solution.py:544
  186.7 10.2 %collective-permute-start.18 = (f32[64,128]{1,0:T(8,128)}, f32[64,128]{1,0:T(8,128)S(1)}, u32[]{:S(2)}, u32[]{:S(2)}) collective-permute-start(f32[64,128]{1,0:T(8,128)} %get-tuple-element.116), channel_id=1, source_target_pairs={{1,0},{2,1},{3,2},{4,3},{5,4},{6,5},{7,6},{8,7},{9,8},{10,9},{11,1... | collective-permute-start | bytes 98312 | tf_op jit(solution)/shard_map/ppermute | solution.py:545
  (20 other events, 20.8 us)

commit v2 on v1

--- a/solution.py
+++ b/solution.py
@@ -1,4 +1,3 @@
-import functools
 import math
 
 import jax
@@ -20,6 +19,7 @@
 OWNERS = 64
 COMPS = 32
 HALF = 12
+ASK = 8
 
 exact_mode = lax.Precision.HIGHEST
 spectrum_high = 8.0
@@ -94,7 +94,7 @@
     return lax.broadcasted_iota(jnp.int32, shape, axis)
 
 
-def request_kernel(owner_ref, slot_ref, weight_ref, send_ref, rank_ref):
+def build_requests(owner_ref, slot_ref, weight_ref, send_ref, rank_ref):
     owner = owner_ref[...]
     hits = iota((OWNERS, R_DEV), 0) == owner
     hits_f = hits.astype(f32)
@@ -125,12 +125,19 @@
         ]
         part = dot_nt(hits_b, jnp.concatenate(rows, axis=0))
         total = part if total is None else total + part
-    send_ref[...] = total
+    for c in range(ASK):
+        if c < 2 * HALF * COMPS // 128:
+            block = total[:, c * 128 : c * 128 + 128]
+        else:
+            block = jnp.zeros((OWNERS, 128), f32)
+        send_ref[pl.ds(c, OWNERS, stride=ASK), :] = block
 
 
 def owner_kernel(recv_ref, field_ref, ret_ref):
-    width = HALF * COMPS
-    packed = jnp.concatenate([recv_ref[:, :width], recv_ref[:, width:]], axis=0)
+    cols = [recv_ref[pl.ds(c, OWNERS, stride=ASK), :] for c in range(6)]
+    packed = jnp.concatenate(
+        [jnp.concatenate(cols[:3], axis=1), jnp.concatenate(cols[3:], axis=1)], axis=0
+    )
     comps = packed.T
     pieces = jnp.concatenate(split3(field_ref[...]), axis=1)
     rows = []
@@ -245,6 +252,93 @@
     return new_bottom, new_top
 
 
+def whole(bottom, ref, top):
+    return jnp.concatenate([bottom, ref[64:448], top], axis=0)
+
+
+def coupled(w_ref, below, above):
+    bottom, top = through(w_ref[0:64], w_ref[448:512], below, above)
+    return whole(bottom, w_ref, top)
+
+
+def where_am_i():
+    me = lax.axis_index("elem")
+    last = lax.axis_size("elem") - 1
+    return jnp.bitwise_and(me, 1) == 0, me > 0, me < last
+
+
+def first_layer(shape):
+    return iota(shape, 1) < LAYER
+
+
+def pack(field, a_ref, b_ref, row, even):
+    low, high = field[0:256], field[256:512]
+    first = first_layer(low.shape)
+    up = jnp.where(first, pltpu.roll(low, LAYER, 1), high)
+    down = jnp.where(first, low, pltpu.roll(high, LAYER, 1))
+    a_ref[row : row + 256] = jnp.where(even, up, down)
+    b_ref[row : row + 256] = jnp.where(even, down, up)
+
+
+def beside(a, b, place):
+    even, has_below, has_above = place
+    below = jnp.where(has_below, jnp.where(even, b, a), 0.0)
+    above = jnp.where(has_above, jnp.where(even, a, b), 0.0)
+    return below, above
+
+
+def unpack(a_ref, b_ref, row, place, out_ref):
+    below, above = beside(a_ref[row : row + 256], b_ref[row : row + 256], place)
+    first = first_layer(below.shape)
+    out_ref[0:256] = jnp.where(first, above, pltpu.roll(below, LAYER, 1))
+    out_ref[256:512] = jnp.where(first, pltpu.roll(above, LAYER, 1), below)
+
+
+def mirror(ghost_ref, bottom, top):
+    first = first_layer(bottom.shape)
+    ghost_ref[448:512] = jnp.where(first, ghost_ref[448:512], pltpu.roll(bottom, LAYER, 1))
+    ghost_ref[0:64] = jnp.where(first, pltpu.roll(top, LAYER, 1), ghost_ref[0:64])
+
+
+def message(raw_bottom, raw_top, inner_bottom, mid, inner_top):
+    first = first_layer(raw_bottom.shape)
+    return jnp.concatenate(
+        [
+            jnp.where(first, raw_bottom, inner_bottom),
+            mid,
+            jnp.where(first, inner_top, raw_top),
+        ],
+        axis=0,
+    )
+
+
+def ghost_apply(ghost_ref, third_ref, planes_ref, face_ref, out_ref):
+    first = first_layer((8, 128))
+    face_ref[...] = jnp.where(
+        first_layer((64, 128)), ghost_ref[0:64], ghost_ref[448:512]
+    )
+    lines = [face_ref[pl.ds(i, 8, stride=8), :] for i in range(8)]
+    res = apply_line(lines, lambda a: planes_ref[a * 8 : a * 8 + 8])
+    for i in range(8):
+        out_ref[pl.ds(i, 8, stride=8), :] = res[i]
+    rows = [face_ref[j * 8 : j * 8 + 8] for j in range(8)]
+    res = apply_line(rows, lambda b: planes_ref[64 + b * 8 : 72 + b * 8])
+    ends = [
+        jnp.where(first, float(DERIV[c, 0]), float(DERIV[c, 7])).astype(f32)
+        for c in range(8)
+    ]
+    for j in range(8):
+        total = out_ref[j * 8 : j * 8 + 8] + res[j]
+        total = total + planes_ref[128 + j * 8 : 136 + j * 8] * rows[j]
+        cols = [ghost_ref[k * 64 + j * 8 : k * 64 + j * 8 + 8] for k in range(8)]
+        grad = deriv8(DERIV, cols)
+        for c in range(8):
+            at = c * 64 + j * 8
+            total = total + grad[c] * third_ref[at : at + 8] * ends[c]
+        out_ref[j * 8 : j * 8 + 8] = total
+    in_plane(out_ref, 1)
+
+
 def plain8(table, v):
     out = []
     for i in range(8):
@@ -264,42 +358,7 @@
     )
 
 
-def setup_kernel(
-    order_ref,
-    stiff_ref,
-    mass_ref,
-    field_ref,
-    basis_ref,
-    inverse_ref,
-    coef_ref,
-    mass_out_ref,
-    start_ref,
-    diag_ref,
-    inv_ref,
-    basis_out_ref,
-    solve_ref,
-    pack_up_ref,
-    pack_down_ref,
-    tmp_ref,
-):
-    order = order_ref[...]
-    match = (iota((128, 128), 0) == order).astype(f32)
-    inv = jnp.sum(match.T * iota((128, 128), 0).astype(f32), axis=0, keepdims=True)
-    inv = inv.astype(jnp.int32)
-    inv_ref[...] = inv
-    tmp_ref[...] = take_lanes(stiff_ref[0:512, :], inv)
-    for k in range(8):
-        for i in range(8):
-            coef_ref[k * 64 + i * 8 : k * 64 + i * 8 + 8, :] = tmp_ref[
-                pl.ds(k * 64 + i, 8, stride=8), :
-            ]
-    coef_ref[512:1536, :] = take_lanes(stiff_ref[512:1536, :], inv)
-    mass_out_ref[...] = take_lanes(mass_ref[...], inv)
-    start_ref[...] = take_lanes(field_ref[...], inv)
-    basis = dot_nn(match, basis_ref[...], exact_mode)
-    basis_out_ref[...] = basis
-    solve = dot_nn(basis, inverse_ref[...], exact_mode)
-    solve_ref[...] = solve
+def local_diagonal(coef_ref, mass_ref, diag_ref):
     squared = DERIV * DERIV
 
     def per_k(k, carry):
@@ -310,7 +369,7 @@
         res = plain8(squared, [coef_ref[pl.ds(512 + base + b * 8, 8), :] for b in range(8)])
         for j in range(8):
             at = pl.ds(base + j * 8, 8)
-            diag_ref[at, :] = diag_ref[at, :] + res[j] + mass_out_ref[at, :]
+            diag_ref[at, :] = diag_ref[at, :] + res[j] + mass_ref[at, :]
         return carry
 
     lax.fori_loop(0, 8, per_k, 0)
@@ -324,13 +383,93 @@
         return carry
 
     lax.fori_loop(0, 8, per_j, 0)
+
+
+BASIS_ROW = 704
+GHOST_ROWS = BASIS_ROW + 256
+
+
+def prepare_kernel(
+    owner_ref,
+    slot_ref,
+    weight_ref,
+    order_ref,
+    stiff_hbm,
+    mass_hbm,
+    field_hbm,
+    basis_hbm,
+    inverse_hbm,
+    send_ref,
+    rank_ref,
+    coef_ref,
+    mass_ref,
+    start_ref,
+    diag_ref,
+    inv_ref,
+    basis_ref,
+    solve_ref,
+    a_ref,
+    b_ref,
+    stiff_in,
+    mass_in,
+    field_in,
+    basis_in,
+    inverse_in,
+    tmp_ref,
+    sems,
+):
+    copies = [
+        pltpu.make_async_copy(src, dst, sems.at[n])
+        for n, (src, dst) in enumerate(
+            [
+                (stiff_hbm, stiff_in),
+                (mass_hbm, mass_in),
+                (field_hbm, field_in),
+                (basis_hbm, basis_in),
+                (inverse_hbm, inverse_in),
+            ]
+        )
+    ]
+    for copy in copies:
+        copy.start()
+    build_requests(owner_ref, slot_ref, weight_ref, send_ref, rank_ref)
+    order = order_ref[...]
+    match = (iota((128, 128), 0) == order).astype(f32)
+    inv = jnp.sum(match.T * iota((128, 128), 0).astype(f32), axis=0, keepdims=True)
+    inv = inv.astype(jnp.int32)
+    inv_ref[...] = inv
+    for copy in copies:
+        copy.wait()
+    tmp_ref[...] = take_lanes(stiff_in[0:512, :], inv)
+    for k in range(8):
+        for i in range(8):
+            coef_ref[k * 64 + i * 8 : k * 64 + i * 8 + 8, :] = tmp_ref[
+                pl.ds(k * 64 + i, 8, stride=8), :
+            ]
+    coef_ref[512:1536, :] = take_lanes(stiff_in[512:1536, :], inv)
+    mass_ref[...] = take_lanes(mass_in[...], inv)
+    start_ref[...] = take_lanes(field_in[...], inv)
+    basis = dot_nn(match, basis_in[...], exact_mode)
+    basis_ref[...] = basis
+    solve_ref[...] = dot_nn(basis, inverse_in[...], exact_mode)
+    local_diagonal(coef_ref, mass_ref, diag_ref)
     in_plane(diag_ref)
-    pack_up_ref[:, 0:512] = basis[LAYER:]
-    pack_up_ref[:, 512:1024] = solve[LAYER:]
-    pack_up_ref[:, 1024:1152] = mass_out_ref[448:512, :]
-    pack_down_ref[:, 0:512] = basis[:LAYER]
-    pack_down_ref[:, 512:1024] = solve[:LAYER]
-    pack_down_ref[:, 1024:1152] = mass_out_ref[0:64, :]
+    even = where_am_i()[0]
+    zeros = jnp.zeros((64, 128), f32)
+    pack(coef_ref[1024:1536, :], a_ref, b_ref, 0, even)
+    pack(coupled(diag_ref, zeros, zeros), a_ref, b_ref, 256, even)
+    rows = [
+        (coef_ref[448:512], coef_ref[0:64]),
+        (coef_ref[960:1024], coef_ref[512:576]),
+        (mass_ref[448:512], mass_ref[0:64]),
+    ]
+    for c in range(NC // 128):
+        cols = slice(c * 128, c * 128 + 128)
+        rows.append((basis[LAYER:, cols], basis[:LAYER, cols]))
+    for n, (up, down) in enumerate(rows):
+        at = 512 + n * 64
+        a_ref[at : at + 64] = jnp.where(even, up, down)
+        b_ref[at : at + 64] = jnp.where(even, down, up)
 
 
 def source_kernel(
@@ -344,10 +483,9 @@
     start_ref,
     coef_ref,
     mass_ref,
-    diag_ref,
     out_ref,
-    up_ref,
-    down_ref,
+    a_ref,
+    b_ref,
 ):
     hits = (iota((OWNERS, R_DEV), 0) == owner_ref[...]).astype(f32)
     picked = dot_nn(ret_ref[...].T, hits, exact_mode)[0:32]
@@ -369,181 +507,297 @@
     stiff_apply(start_ref, coef_ref, mass_ref, out_ref)
     out_ref[...] = source - out_ref[...]
     in_plane(out_ref)
-    up_ref[0:64] = out_ref[448:512]
-    up_ref[64:128] = diag_ref[448:512]
-    down_ref[0:64] = out_ref[0:64]
-    down_ref[64:128] = diag_ref[0:64]
-
-
-def finish_through(w_ref, below, above):
-    bottom, top = through(w_ref[0:64], w_ref[448:512], below, above)
-    return jnp.concatenate([bottom, w_ref[64:448], top], axis=0)
-
-
-def emit(update_ref, coef_ref, mass_ref, w_ref, up_ref, down_ref):
-    stiff_apply(update_ref, coef_ref, mass_ref, w_ref)
-    in_plane(w_ref)
-    up_ref[...] = w_ref[448:512]
-    down_ref[...] = w_ref[0:64]
-
-
-def first_step_kernel(
-    w_ref,
-    diag_ref,
-    start_ref,
-    below_ref,
-    above_ref,
+    zeros = jnp.zeros((64, 128), f32)
+    pack(coupled(out_ref, zeros, zeros), a_ref, b_ref, 0, where_am_i()[0])
+
+
+def opening_half(
+    place,
+    base_ref,
+    y_ref,
+    cur_in_ref,
+    a_ref,
+    b_ref,
+    invd_ref,
+    third_ref,
+    ginvd_ref,
+    planes_ref,
     coef_ref,
     mass_ref,
     res_ref,
     upd_ref,
     cur_ref,
-    invd_ref,
-    w_out_ref,
-    up_ref,
-    down_ref,
+    w_ref,
+    a_out_ref,
+    b_out_ref,
+    ghost_ref,
+    face_ref,
+    side_ref,
 ):
-    residual = finish_through(w_ref, below_ref[0:64], above_ref[0:64])
-    diag = finish_through(diag_ref, below_ref[64:128], above_ref[64:128])
-    invd = 1.0 / diag
-    invd_ref[...] = invd
-    res_ref[...] = residual
+    unpack(a_ref, b_ref, 0, place, ghost_ref)
+    residual = coupled(y_ref, ghost_ref[448:512], ghost_ref[0:64])
+    if base_ref is not None:
+        residual = residual + base_ref[...]
+    mirror(ghost_ref, residual[0:64], residual[448:512])
+    invd = invd_ref[...]
     update = residual * invd * STEPS[0][1]
     upd_ref[...] = update
-    cur_ref[...] = start_ref[...] + update
-    emit(upd_ref, coef_ref, mass_ref, w_out_ref, up_ref, down_ref)
-
-
-def step_kernel(
-    turn,
-    send,
-    w_ref,
-    res_in_ref,
-    upd_in_ref,
+    ghost_ref[...] = ghost_ref[...] * ginvd_ref[...] * STEPS[0][1]
+    stiff_apply(upd_ref, coef_ref, mass_ref, w_ref)
+    in_plane(w_ref)
+    ghost_apply(ghost_ref, third_ref, planes_ref, face_ref, side_ref)
+    residual = residual - coupled(w_ref, side_ref[...], side_ref[...])
+    res_ref[...] = residual
+    alpha, beta = STEPS[1]
+    second = alpha * update + beta * invd * residual
+    upd_ref[...] = second
+    cur_ref[...] = cur_in_ref[...] + (update + second)
+    stiff_apply(upd_ref, coef_ref, mass_ref, w_ref)
+    in_plane(w_ref)
+    alpha, beta = STEPS[2]
+    zeros = jnp.zeros((64, 128), f32)
+    inner = alpha * upd_ref[...] + beta * invd_ref[...] * (
+        res_ref[...] - coupled(w_ref, zeros, zeros)
+    )
+    pack(
+        message(w_ref[0:64], w_ref[448:512], inner[0:64], inner[64:448], inner[448:512]),
+        a_out_ref,
+        b_out_ref,
+        0,
+        place[0],
+    )
+
+
+def start_kernel(
+    y_ref,
+    diag_ref,
     cur_in_ref,
-    invd_ref,
-    below_ref,
-    above_ref,
+    a_ref,
+    b_ref,
+    ga_ref,
+    gb_ref,
     coef_ref,
     mass_ref,
     res_ref,
     upd_ref,
     cur_ref,
-    *out_refs,
+    w_ref,
+    a_out_ref,
+    b_out_ref,
+    invd_ref,
+    third_ref,
+    ginvd_ref,
+    planes_ref,
+    outer_ref,
+    *scratch,
 ):
-    alpha, beta = STEPS[turn]
-    residual = res_in_ref[...] - finish_through(w_ref, below_ref[...], above_ref[...])
+    place = where_am_i()
+    unpack(ga_ref, gb_ref, 0, place, third_ref)
+    unpack(ga_ref, gb_ref, 256, place, ginvd_ref)
+    diag = coupled(diag_ref, ginvd_ref[448:512], ginvd_ref[0:64])
+    mirror(ginvd_ref, diag[0:64], diag[448:512])
+    invd_ref[...] = 1.0 / diag
+    gdiag = ginvd_ref[...]
+    there = gdiag > 0.0
+    ginvd_ref[...] = jnp.where(there, 1.0 / jnp.where(there, gdiag, 1.0), 0.0)
+    below, above = beside(ga_ref[512:704], gb_ref[512:704], place)
+    planes_ref[...] = jnp.where(first_layer(below.shape), above, below)
+    for c in range(NC // 128):
+        at = BASIS_ROW + c * 64
+        below, above = beside(ga_ref[at : at + 64], gb_ref[at : at + 64], place)
+        outer_ref[0:64, c * 128 : c * 128 + 128] = below
+        outer_ref[64:128, c * 128 : c * 128 + 128] = above
+    opening_half(
+        place,
+        None,
+        y_ref,
+        cur_in_ref,
+        a_ref,
+        b_ref,
+        invd_ref,
+        third_ref,
+        ginvd_ref,
+        planes_ref,
+        coef_ref,
+        mass_ref,
+        res_ref,
+        upd_ref,
+        cur_ref,
+        w_ref,
+        a_out_ref,
+        b_out_ref,
+        *scratch,
+    )
+
+
+def again_kernel(*refs):
+    opening_half(where_am_i(), *refs)
+
+
+def closing_half(
+    w_ref,
+    res_ref,
+    upd_ref,
+    cur_ref,
+    invd_ref,
+    a_ref,
+    b_ref,
+    third_ref,
+    planes_ref,
+    coef_ref,
+    mass_ref,
+    work_ref,
+    vec_ref,
+    ghost_ref,
+    face_ref,
+    side_ref,
+):
+    unpack(a_ref, b_ref, 0, where_am_i(), ghost_ref)
+    residual = res_ref[...] - coupled(w_ref, ghost_ref[448:512], ghost_ref[0:64])
+    alpha, beta = STEPS[2]
+    third = alpha * upd_ref[...] + beta * invd_ref[...] * residual
+    vec_ref[...] = third
+    mirror(ghost_ref, third[0:64], third[448:512])
+    stiff_apply(vec_ref, coef_ref, mass_ref, work_ref)
+    in_plane(work_ref)
+    ghost_apply(ghost_ref, third_ref, planes_ref, face_ref, side_ref)
+    residual = residual - coupled(work_ref, side_ref[...], side_ref[...])
+    alpha, beta = STEPS[3]
+    fourth = alpha * third + beta * invd_ref[...] * residual
+    vec_ref[...] = fourth
+    return residual, cur_ref[...] + (third + fourth)
+
+
+def middle_kernel(
+    w_ref,
+    res_in_ref,
+    upd_ref,
+    cur_in_ref,
+    invd_ref,
+    a_ref,
+    b_ref,
+    third_ref,
+    planes_ref,
+    coef_ref,
+    mass_ref,
+    basis_ref,
+    outer_ref,
+    res_ref,
+    cur_ref,
+    w_out_ref,
+    part_ref,
+    vec_ref,
+    *scratch,
+):
+    residual, current = closing_half(
+        w_ref,
+        res_in_ref,
+        upd_ref,
+        cur_in_ref,
+        invd_ref,
+        a_ref,
+        b_ref,
+        third_ref,
+        planes_ref,
+        coef_ref,
+        mass_ref,
+        w_out_ref,
+        vec_ref,
+        *scratch,
+    )
     res_ref[...] = residual
-    update = alpha * upd_in_ref[...] + beta * invd_ref[...] * residual
-    upd_ref[...] = update
-    cur_ref[...] = cur_in_ref[...] + update
-    if send:
-        emit(upd_ref, coef_ref, mass_ref, *out_refs)
-
-
-def coarse_kernel(res_ref, w_ref, basis_ref, from_below_ref, from_above_ref, out_ref):
+    cur_ref[...] = current
+    stiff_apply(vec_ref, coef_ref, mass_ref, w_out_ref)
+    in_plane(w_out_ref)
     zeros = jnp.zeros((64, 128), f32)
-    local = res_ref[...] - finish_through(w_ref, zeros, zeros)
+    local = res_ref[...] - coupled(w_out_ref, zeros, zeros)
     sums = jnp.sum(local, axis=0, keepdims=True)
-    bottom = -jnp.sum(w_ref[0:64], axis=0, keepdims=True)
-    top = -jnp.sum(w_ref[448:512], axis=0, keepdims=True)
-    outer = jnp.where(iota((1, 128), 1) < LAYER, bottom, top)
-    outer_basis = jnp.concatenate(
-        [from_below_ref[:, 0:512], from_above_ref[:, 0:512]], axis=0
-    )
+    bottom = -jnp.sum(w_out_ref[0:64], axis=0, keepdims=True)
+    top = -jnp.sum(w_out_ref[448:512], axis=0, keepdims=True)
+    outer = jnp.where(first_layer((1, 128)), bottom, top)
     left = jnp.broadcast_to(jnp.concatenate([sums, outer], axis=1), (8, 256))
-    right = jnp.concatenate([basis_ref[...], outer_basis], axis=0)
-    part = dot_nn(left, right, exact_mode) * (1.0 / math.sqrt(NODES))
-    out_ref[...] = jnp.broadcast_to(part[0:1], (OWNERS, NC))
+    right = jnp.concatenate([basis_ref[...], outer_ref[...]], axis=0)
+    part = dot_nn(left, right, exact_mode)[0:1] * (1.0 / math.sqrt(NODES))
+    blocks = [part[:, c * 128 : c * 128 + 128] for c in range(NC // 128)]
+    eight = jnp.concatenate(blocks + blocks, axis=0)
+    for n in range(OWNERS * NC // 1024):
+        part_ref[n * 8 : n * 8 + 8] = eight
 
 
 def restart_kernel(
     parts_ref,
     solve_ref,
-    from_below_ref,
-    from_above_ref,
     mass_ref,
     w_ref,
-    res_in_ref,
+    base_ref,
     cur_in_ref,
-    invd_ref,
-    below_ref,
-    above_ref,
-    coef_ref,
-    res_ref,
-    upd_ref,
+    y_ref,
     cur_ref,
-    w_out_ref,
-    up_ref,
-    down_ref,
-    near_ref,
+    a_ref,
+    b_ref,
 ):
-    coarse = jnp.broadcast_to(jnp.sum(parts_ref[...], axis=0, keepdims=True), (8, NC))
-    outer = jnp.concatenate(
-        [from_above_ref[:, 512:1024], from_below_ref[:, 512:1024]], axis=0
-    )
-    both = dot_nt(coarse, jnp.concatenate([solve_ref[...], outer], axis=0), exact_mode)
-    own = both[0:1, 0:128]
-    beside = both[0:1, 128:256]
-    near_ref[0:64] = from_below_ref[:, 1024:1152] * beside
-    near_ref[64:128] = from_above_ref[:, 1024:1152] * beside
-    in_plane(near_ref, 2)
-    w_out_ref[...] = mass_ref[...] * own
-    in_plane(w_out_ref)
-    total = finish_through(
-        w_ref, below_ref[...], above_ref[...]
-    ) + finish_through(w_out_ref, near_ref[0:64], near_ref[64:128])
-    residual = res_in_ref[...] - total
-    res_ref[...] = residual
-    update = residual * invd_ref[...] * STEPS[0][1]
-    upd_ref[...] = update
-    cur_ref[...] = cur_in_ref[...] + own + update
-    emit(upd_ref, coef_ref, mass_ref, w_out_ref, up_ref, down_ref)
-
-
-def last_kernel(
-    w_ref,
-    res_in_ref,
-    upd_in_ref,
-    cur_in_ref,
-    invd_ref,
-    below_ref,
-    above_ref,
-    order_ref,
-    out_ref,
-):
-    alpha, beta = STEPS[CHEB - 1]
-    residual = res_in_ref[...] - finish_through(w_ref, below_ref[...], above_ref[...])
-    update = alpha * upd_in_ref[...] + beta * invd_ref[...] * residual
-    out_ref[...] = take_lanes(cur_in_ref[...] + update, order_ref[...])
-
-
-def call(kernel, name, outs, *args, scratch=(), smem=()):
-    specs = [
-        pl.BlockSpec(memory_space=pltpu.SMEM if n in smem else pltpu.VMEM)
-        for n in range(len(args))
-    ]
+    total = parts_ref[0:8]
+    for n in range(1, OWNERS * NC // 1024):
+        total = total + parts_ref[n * 8 : n * 8 + 8]
+    total = total + pltpu.roll(total, 4, 0)
+    correction = None
+    for c in range(NC // 128):
+        row = jnp.broadcast_to(total[c : c + 1], (8, 128))
+        term = dot_nt(row, solve_ref[:, c * 128 : c * 128 + 128], exact_mode)
+        correction = term if correction is None else correction + term
+    correction = correction[0:1]
+    cur_ref[...] = cur_in_ref[...] + correction
+    y_ref[...] = mass_ref[...] * correction
+    in_plane(y_ref)
+    y_ref[...] = -(y_ref[...] + w_ref[...])
+    zeros = jnp.zeros((64, 128), f32)
+    inner = base_ref[...] + coupled(y_ref, zeros, zeros)
+    pack(
+        message(y_ref[0:64], y_ref[448:512], inner[0:64], inner[64:448], inner[448:512]),
+        a_ref,
+        b_ref,
+        0,
+        where_am_i()[0],
+    )
+
+
+def last_kernel(*refs):
+    inputs, (order_ref, out_ref), scratch = refs[:11], refs[11:13], refs[13:]
+    current = closing_half(*inputs, *scratch)[1]
+    out_ref[...] = take_lanes(current, order_ref[...])
+
+
+def call(kernel, name, outs, *args, scratch=(), smem=(), far=(), copies=0):
+    def space(n):
+        if n in smem:
+            return pltpu.SMEM
+        return pl.ANY if n in far else pltpu.VMEM
+
+    scratches = [pltpu.VMEM(s, f32) for s in scratch]
+    if copies:
+        scratches.append(pltpu.SemaphoreType.DMA((copies,)))
     return pl.pallas_call(
         kernel,
         name=name,
         out_shape=[jax.ShapeDtypeStruct(s, d) for s, d in outs],
-        in_specs=specs,
+        in_specs=[pl.BlockSpec(memory_space=space(n)) for n in range(len(args))],
         out_specs=[pl.BlockSpec(memory_space=pltpu.VMEM) for _ in outs],
-        scratch_shapes=[pltpu.VMEM(s, f32) for s in scratch],
+        scratch_shapes=scratches,
+        compiler_params=pltpu.CompilerParams(vmem_limit_bytes=20 << 20),
     )(*args)
 
 
 FIELD = ((NODES, 128), f32)
-PLANE = ((64, 128), f32)
-
-
-def exchange(up, down):
+LAYER_MSG = ((256, 128), f32)
+GHOST_MSG = ((GHOST_ROWS, 128), f32)
+GHOST_WORK = [(NODES, 128), (64, 128), (64, 128)]
+
+
+def exchange(a, b):
     count = lax.axis_size("elem")
-    forward = [(i, i + 1) for i in range(count - 1)]
-    backward = [(b, a) for a, b in forward]
-    below = lax.ppermute(up, "elem", forward)
-    above = lax.ppermute(down, "elem", backward)
-    return below, above
+    pairs_a = [(i, i ^ 1) for i in range(count)]
+    pairs_b = [(i, (i + (1 if i % 2 else -1)) % count) for i in range(count)]
+    return lax.ppermute(a, "elem", pairs_a), lax.ppermute(b, "elem", pairs_b)
 
 
 def per_device(
@@ -565,18 +819,12 @@
     owner = donor_owner.reshape(1, R_DEV)
     other_field = lax.ppermute(own_field, "sess", [(0, 1), (1, 0)])
 
-    send, rank = call(
-        request_kernel,
-        "request",
-        [((OWNERS, 2 * HALF * COMPS), f32), ((1, R_DEV), f32)],
-        owner,
-        donor_slot,
-        interp_weights.reshape(3 * NP, R_DEV),
-    )
-    coef, mass, start, diag, inv, basis, solve, pack_up, pack_down = call(
-        setup_kernel,
-        "setup",
+    send, rank, coef, mass, start, diag, inv, basis, solve, ghost_a, ghost_b = call(
+        prepare_kernel,
+        "prepare",
         [
+            ((OWNERS * ASK, 128), f32),
+            ((1, R_DEV), f32),
             ((3 * NODES, 128), f32),
             FIELD,
             FIELD,
@@ -584,27 +832,45 @@
             ((1, 128), jnp.int32),
             ((128, NC), f32),
             ((128, NC), f32),
-            ((LAYER, 2 * NC + 128), f32),
-            ((LAYER, 2 * NC + 128), f32),
+            GHOST_MSG,
+            GHOST_MSG,
         ],
+        owner,
+        donor_slot,
+        interp_weights.reshape(3 * NP, R_DEV),
         order,
         stiffness.reshape(3 * NODES, 128),
         helm_mass.reshape(NODES, 128),
         own_field,
         coarse_basis.reshape(128, NC),
         coarse_inverse.reshape(NC, NC),
-        scratch=[(NODES, 128)],
-    )
-    from_below, from_above = exchange(pack_up, pack_down)
-    received = lax.all_to_all(send, "elem", split_axis=0, concat_axis=0, tiled=True)
+        far=(4, 5, 6, 7, 8),
+        scratch=[
+            (3 * NODES, 128),
+            (NODES, 128),
+            (NODES, 128),
+            (128, NC),
+            (NC, NC),
+            (NODES, 128),
+        ],
+        copies=5,
+    )
+    ghost_a, ghost_b = exchange(ghost_a, ghost_b)
+    received = lax.all_to_all(
+        send.reshape(OWNERS, ASK, 128), "elem", split_axis=0, concat_axis=0, tiled=True
+    )
     (answer,) = call(
-        owner_kernel, "owner", [((OWNERS, 128), f32)], received, other_field
+        owner_kernel,
+        "owner",
+        [((OWNERS, 128), f32)],
+        received.reshape(OWNERS * ASK, 128),
+        other_field,
     )
     answered = lax.all_to_all(answer, "elem", split_axis=0, concat_axis=0, tiled=True)
-    w, up, down = call(
+    y, a, b = call(
         source_kernel,
         "source",
-        [FIELD, ((128, 128), f32), ((128, 128), f32)],
+        [FIELD, LAYER_MSG, LAYER_MSG],
         answered,
         owner,
         rank,
@@ -615,89 +881,99 @@
         start,
         coef,
         mass,
-        diag,
         smem=(4,),
     )
-    below, above = exchange(up, down)
-    stepped = [FIELD] * 3
-    sent = [FIELD, PLANE, PLANE]
-    res, upd, cur, invd, w, up, down = call(
-        first_step_kernel,
-        "first_step",
-        stepped + [FIELD] + sent,
-        w,
+    a, b = exchange(a, b)
+    half = [FIELD, FIELD, FIELD, FIELD, LAYER_MSG, LAYER_MSG]
+    res, upd, cur, w, a, b, invd, third, ginvd, planes, outer = call(
+        start_kernel,
+        "start",
+        half + [FIELD, FIELD, FIELD, ((192, 128), f32), ((128, NC), f32)],
+        y,
         diag,
         start,
-        below,
-        above,
+        a,
+        b,
+        ghost_a,
+        ghost_b,
         coef,
         mass,
-    )
-    for turn in range(1, CHEB):
-        below, above = exchange(up, down)
-        res, upd, cur, w, up, down = call(
-            functools.partial(step_kernel, turn, True),
-            f"step{turn}",
-            stepped + sent,
-            w,
-            res,
-            upd,
-            cur,
-            invd,
-            below,
-            above,
-            coef,
-            mass,
-        )
-    below, above = exchange(up, down)
-    (part,) = call(
-        coarse_kernel,
-        "coarse",
-        [((OWNERS, NC), f32)],
+        scratch=GHOST_WORK,
+    )
+    a, b = exchange(a, b)
+    res, cur, w, part = call(
+        middle_kernel,
+        "middle",
+        [FIELD, FIELD, FIELD, ((OWNERS * NC // 128, 128), f32)],
+        w,
         res,
-        w,
+        upd,
+        cur,
+        invd,
+        a,
+        b,
+        third,
+        planes,
+        coef,
+        mass,
         basis,
-        from_below,
-        from_above,
-    )
-    parts = lax.all_to_all(part, "elem", split_axis=0, concat_axis=0, tiled=True)
-    res, upd, cur, w, up, down = call(
+        outer,
+        scratch=[(NODES, 128)] + GHOST_WORK,
+    )
+    parts = lax.all_to_all(
+        part.reshape(OWNERS, NC // 128, 128),
+        "elem",
+        split_axis=0,
+        concat_axis=0,
+        tiled=True,
+    )
+    y, cur, a, b = call(
         restart_kernel,
         "restart",
-        stepped + sent,
-        parts,
+        [FIELD, FIELD, LAYER_MSG, LAYER_MSG],
+        parts.reshape(OWNERS * NC // 128, 128),
         solve,
-        from_below,
-        from_above,
         mass,
         w,
         res,
         cur,
+    )
+    a, b = exchange(a, b)
+    res, upd, cur, w, a, b = call(
+        again_kernel,
+        "again",
+        half,
+        res,
+        y,
+        cur,
+        a,
+        b,
         invd,
-        below,
-        above,
+        third,
+        ginvd,
+        planes,
         coef,
-        scratch=[(128, 128)],
-    )
-    for turn in range(1, CHEB - 1):
-        below, above = exchange(up, down)
-        res, upd, cur, w, up, down = call(
-            functools.partial(step_kernel, turn, True),
-            f"again{turn}",
-            stepped + sent,
-            w,
-            res,
-            upd,
-            cur,
-            invd,
-            below,
-            above,
-            coef,
-            mass,
-        )
-    below, above = exchange(up, down)
+        mass,
+        scratch=GHOST_WORK,
+    )
+    a, b = exchange(a, b)
     (out,) = call(
-        last_kernel, "last", [FIELD], w, res, upd, cur, invd, below, above, order
+        last_kernel,
+        "last",
+        [FIELD],
+        w,
+        res,
+        upd,
+        cur,
+        invd,
+        a,
+        b,
+        third,
+        planes,
+        coef,
+        mass,
+        order,
+        scratch=[(NODES, 128), (NODES, 128)] + GHOST_WORK,
     )
     return out.reshape(1, NP, NP, NP, 128)
 

time: 201 us -> 129 us (0.64)
  the two profiles are of different devices: /device:TPU:6 before, /device:TPU:0 now
where the time goes in v2:
time: 129 us; the launch traced here: 128 us
  waiting for transfers between devices  41.8 us (32%)
  blocking collectives  29.3 us (23%)
  starting transfers between devices  28.4 us (22%)
  Pallas kernels  20.4 us (16%)
  local copies, waits for them, and re-layouts  7.49 us (6%)
    ppermute x10, waiting for transfers between devices, exchange(): return (lax.ppermute(a, 'elem', pairs_a), lax.ppermute(b, 'elem', pairs_b))  32.9 us
    pallas_call x8, Pallas kernels, call(): pl.pallas_call(kernel, name=name, out_shape=[jax.ShapeDtypeStruct(s, d) f...  20.4 us
    ppermute x10, starting transfers between devices, exchange(): return (lax.ppermute(a, 'elem', pairs_a), lax.ppermute(b, 'elem', pairs_b))  19.6 us
    all_to_all x1, blocking collectives, per_device(): lax.all_to_all(send.reshape(OWNERS, ASK, 128), 'elem', split_axis=0, conc...  15.2 us
    all_to_all x1, blocking collectives, per_device(): lax.all_to_all(part.reshape(OWNERS, NC // 128, 128), 'elem', split_axis=0...  14.1 us
    all_to_all x1, waiting for transfers between devices, per_device(): lax.all_to_all(answer, 'elem', split_axis=0, concat_axis=0, tiled=True)  8.86 us
    all_to_all x1, starting transfers between devices, per_device(): lax.all_to_all(answer, 'elem', split_axis=0, concat_axis=0, tiled=True)  8.79 us
    unnamed x22, local copies, waits for them, and re-layouts  7.49 us
  transfers between devices with their start and end apart: 12, of which 9 were waited for; matrix products, arithmetic and copies ran while one was open for 0% of the time, Pallas kernels for 3%

profile of v2, /device:TPU:0, one launch (start us, length us, event | category | flops | bytes accessed | tf_op | source)
XLA Modules:
  0.0 128.0 jit_solution(16414898201848941009)
XLA Ops:
  6.8 5.6 %prepare.1 = (f32[512,128]{1,0:T(8,128)S(1)}, f32[1,1024]{1,0:T(1,128)S(1)}, f32[1536,128]{1,0:T(8,128)S(1)}, f32[512,128]{1,0:T(8,128)S(1)}, f32[512,128]{1,0:T...) custom-call(s32[1,1024]{1,0:T(1,128)S(1)} %bitcast.31, ...), custom_call_target="tpu_custom_call" | custom-call | tf_op jit(solution)/shard_map/prepare/pallas_call | solution.py:779
  12.4 2.1 %collective-permute-start.3 = (f32[960,128]{1,0:T(8,128)}, f32[960,128]{1,0:T(8,128)S(1)}, u32[]{:S(2)}, u32[]{:S(2)}) collective-permute-start(f32[960,128]{1,0:T(8,128)} %get-tuple-element.54), channel_id=1, source_target_pairs={{0,1},{1,0},{2,3},{3,2},{4,5},{5,4},{6,7},{7,6},{8,9},{9,8},{10,11... | collective-permute-start | bytes 1474568 | tf_op jit(solution)/shard_map/ppermute | solution.py:800
  14.6 7.2 %collective-permute-start.4 = (f32[960,128]{1,0:T(8,128)}, f32[960,128]{1,0:T(8,128)S(1)}, u32[]{:S(2)}, u32[]{:S(2)}) collective-permute-start(f32[960,128]{1,0:T(8,128)} %get-tuple-element.55), channel_id=1, source_target_pairs={{0,63},{1,2},{2,1},{3,4},{4,3},{5,6},{6,5},{7,8},{8,7},{9,10},{10,... | collective-permute-start | bytes 1474568 | tf_op jit(solution)/shard_map/ppermute | solution.py:800
  21.7 15.2 %all_to_all.21 = f32[64,8,128]{2,1,0:T(8,128)S(1)} all-to-all(f32[64,8,128]{2,1,0:T(8,128)S(1)} %bitcast.26), channel_id=1, replica_groups=mesh['sess'=2,'elem'=64] {'elem'}, dimensions={0} | all-to-all | bytes 524288 | tf_op jit(solution)/shard_map/all_to_all | solution.py:859
  38.8 8.8 %all-to-all-start.1 = ((f32[64,1,128]{2,1,0:T(1,128)}), f32[64,1,128]{2,1,0:T(1,128)S(1)}, u32[]{:S(2)}, u32[]{:S(2)}) async-start(f32[64,1,128]{2,1,0:T(1,128)} %bitcast.11), calls=%async_computation.1 | async-start | bytes 65536 | tf_op jit(solution)/shard_map/all_to_all | solution.py:869
  48.2 8.9 %all-to-all-done.1 = f32[64,1,128]{2,1,0:T(1,128)S(1)} async-done(((f32[64,1,128]{2,1,0:T(1,128)}), f32[64,1,128]{2,1,0:T(1,128)S(1)}, u32[]{:S(2)}, u32[]{:S(2)}) %all-to-all-start.1) | async-done | bytes 32800 | tf_op jit(solution)/shard_map/all_to_all | solution.py:869
  57.8 2.3 %source.1 = (f32[512,128]{1,0:T(8,128)S(1)}, f32[256,128]{1,0:T(8,128)S(1)}, f32[256,128]{1,0:T(8,128)S(1)}) custom-call(f32[64,128]{1,0:T(8,128)S(1)} %bitcast.28, s32[1,1024]{1,0:T(1,128)S(1)} %bitcast.32, f32[1,1024]{1,0:T(1,128)S(1)} %get-tuple-element.45.rank_ref, s32[1,1024]{1,0:T(1,128)S(1)} %copy-done.9, s32[1,1]{1,0:T(1,128)S(6)} %copy.14.live_ref, ...), custom_call_target="tpu_custom_call" | custom-call | tf_op jit(solution)/shard_map/source/pallas_call | solution.py:779
  60.7 2.2 %collective-permute-start.2 = (f32[256,128]{1,0:T(8,128)S(1)}, f32[256,128]{1,0:T(8,128)S(1)}, u32[]{:S(2)}, u32[]{:S(2)}) collective-permute-start(f32[256,128]{1,0:T(8,128)S(1)} %get-tuple-element.53), channel_id=1, source_target_pairs={{0,63},{1,2},{2,1},{3,4},{4,3},{5,6},{6,5},{7,8},{8,7},{9,10},{10,... | collective-permute-start | bytes 393224 | tf_op jit(solution)/shard_map/ppermute | solution.py:800
  63.0 2.2 %collective-permute-done.1.a_ref = f32[256,128]{1,0:T(8,128)S(1)} collective-permute-done((f32[256,128]{1,0:T(8,128)S(1)}, f32[256,128]{1,0:T(8,128)S(1)}, u32[]{:S(2)}, u32[]{:S(2)}) %collective-permute-start.1) | collective-permute-done | bytes 131104 | tf_op jit(solution)/shard_map/ppermute | solution.py:800
  65.1 6.0 %collective-permute-done.2.b_ref = f32[256,128]{1,0:T(8,128)S(1)} collective-permute-done((f32[256,128]{1,0:T(8,128)S(1)}, f32[256,128]{1,0:T(8,128)S(1)}, u32[]{:S(2)}, u32[]{:S(2)}) %collective-permute-start.2) | collective-permute-done | bytes 131104 | tf_op jit(solution)/shard_map/ppermute | solution.py:800
  71.1 2.6 %start.1 = (f32[512,128]{1,0:T(8,128)S(1)}, f32[512,128]{1,0:T(8,128)S(1)}, f32[512,128]{1,0:T(8,128)S(1)}, f32[512,128]{1,0:T(8,128)S(1)}, f32[256,128]{1,0:T(8...) custom-call(f32[512,128]{1,0:T(8,128)S(1)} %get-tuple-element.50.y_r, ...), custom_call_target="tpu_custom_call" | custom-call | tf_op jit(solution)/shard_map/start/pallas_call | solution.py:779
  73.8 2.3 %collective-permute-start.6 = (f32[256,128]{1,0:T(8,128)S(1)}, f32[256,128]{1,0:T(8,128)S(1)}, u32[]{:S(2)}, u32[]{:S(2)}) collective-permute-start(f32[256,128]{1,0:T(8,128)S(1)} %get-tuple-element.62), channel_id=1, source_target_pairs={{0,63},{1,2},{2,1},{3,4},{4,3},{5,6},{6,5},{7,8},{8,7},{9,10},{10,... | collective-permute-start | bytes 393224 | tf_op jit(solution)/shard_map/ppermute | solution.py:800
  76.1 2.6 %collective-permute-done.5.a_ref = f32[256,128]{1,0:T(8,128)S(1)} collective-permute-done((f32[256,128]{1,0:T(8,128)S(1)}, f32[256,128]{1,0:T(8,128)S(1)}, u32[]{:S(2)}, u32[]{:S(2)}) %collective-permute-start.5) | collective-permute-done | bytes 131104 | tf_op jit(solution)/shard_map/ppermute | solution.py:800
  78.7 5.5 %collective-permute-done.6.b_ref = f32[256,128]{1,0:T(8,128)S(1)} collective-permute-done((f32[256,128]{1,0:T(8,128)S(1)}, f32[256,128]{1,0:T(8,128)S(1)}, u32[]{:S(2)}, u32[]{:S(2)}) %collective-permute-start.6) | collective-permute-done | bytes 131104 | tf_op jit(solution)/shard_map/ppermute | solution.py:800
  84.3 2.6 %middle.1 = (f32[512,128]{1,0:T(8,128)S(1)}, f32[512,128]{1,0:T(8,128)S(1)}, f32[512,128]{1,0:T(8,128)S(1)}, f32[256,128]{1,0:T(8,128)S(1)}) custom-call(f32[512,128]{1,0:T(8,128)S(1)} %get-tuple-element.56.w_ref, f32[512,128]{1,0:T(8,128)S(1)} %get-tuple-element.57.res_in_ref, f32[512,128]{1,0:T(8,128)S(1)} %get-tuple-element.58.upd_ref, ...), custom_call_target="tpu_custom_call" | custom-call | tf_op jit(solution)/shard_map/middle/pallas_call | solution.py:779
  86.9 14.1 %all_to_all.22 = f32[64,4,128]{2,1,0:T(4,128)S(1)} all-to-all(f32[64,4,128]{2,1,0:T(4,128)S(1)} %bitcast.29), channel_id=1, replica_groups=mesh['sess'=2,'elem'=64] {'elem'}, dimensions={0} | all-to-all | bytes 262144 | tf_op jit(solution)/shard_map/all_to_all | solution.py:923
  102.6 2.1 %collective-permute-start.8 = (f32[256,128]{1,0:T(8,128)S(1)}, f32[256,128]{1,0:T(8,128)S(1)}, u32[]{:S(2)}, u32[]{:S(2)}) collective-permute-start(f32[256,128]{1,0:T(8,128)S(1)} %get-tuple-element.75), channel_id=1, source_target_pairs={{0,63},{1,2},{2,1},{3,4},{4,3},{5,6},{6,5},{7,8},{8,7},{9,10},{10,... | collective-permute-start | bytes 393224 | tf_op jit(solution)/shard_map/ppermute | solution.py:800
  104.8 2.2 %collective-permute-done.7.refs_3_ = f32[256,128]{1,0:T(8,128)S(1)} collective-permute-done((f32[256,128]{1,0:T(8,128)S(1)}, f32[256,128]{1,0:T(8,128)S(1)}, u32[]{:S(2)}, u32[]{:S(2)}) %collective-permute-start.7) | collective-permute-done | bytes 131104 | tf_op jit(solution)/shard_map/ppermute | solution.py:800
  106.9 6.1 %collective-permute-done.8.refs_4_ = f32[256,128]{1,0:T(8,128)S(1)} collective-permute-done((f32[256,128]{1,0:T(8,128)S(1)}, f32[256,128]{1,0:T(8,128)S(1)}, u32[]{:S(2)}, u32[]{:S(2)}) %collective-permute-start.8) | collective-permute-done | bytes 131104 | tf_op jit(solution)/shard_map/ppermute | solution.py:800
  113.0 2.3 %again.1 = (f32[512,128]{1,0:T(8,128)S(1)}, f32[512,128]{1,0:T(8,128)S(1)}, f32[512,128]{1,0:T(8,128)S(1)}, f32[512,128]{1,0:T(8,128)S(1)}, f32[256,128]{1,0:T(8,128)S(1)}, /*index=5*/f32[256,128]{1,0:T(8,128)S(1)}) custom-call(f32[512,128]{1,0:T(8,128)S(1)} %get-tuple-element.67.base_ref.refs_0_, f32[512,128]{1,0:T(8,128)S(1)} %get-tuple-element.72.refs_1_, ...), custom_call_target="tpu_custom_call" | custom-call | tf_op jit(solution)/shard_map/again/pallas_call | solution.py:779
  115.4 2.2 %collective-permute-start.10 = (f32[256,128]{1,0:T(8,128)S(1)}, f32[256,128]{1,0:T(8,128)S(1)}, u32[]{:S(2)}, u32[]{:S(2)}) collective-permute-start(f32[256,128]{1,0:T(8,128)S(1)} %get-tuple-element.82), channel_id=1, source_target_pairs={{0,63},{1,2},{2,1},{3,4},{4,3},{5,6},{6,5},{7,8},{8,7},{9,10},{10,... | collective-permute-start | bytes 393224 | tf_op jit(solution)/shard_map/ppermute | solution.py:800
  117.6 2.8 %collective-permute-done.9.refs_5_ = f32[256,128]{1,0:T(8,128)S(1)} collective-permute-done((f32[256,128]{1,0:T(8,128)S(1)}, f32[256,128]{1,0:T(8,128)S(1)}, u32[]{:S(2)}, u32[]{:S(2)}) %collective-permute-start.9) | collective-permute-done | bytes 131104 | tf_op jit(solution)/shard_map/ppermute | solution.py:800
  120.4 5.5 %collective-permute-done.10.refs_6_ = f32[256,128]{1,0:T(8,128)S(1)} collective-permute-done((f32[256,128]{1,0:T(8,128)S(1)}, f32[256,128]{1,0:T(8,128)S(1)}, u32[]{:S(2)}, u32[]{:S(2)}) %collective-permute-start.10) | collective-permute-done | bytes 131104 | tf_op jit(solution)/shard_map/ppermute | solution.py:800
  125.9 2.1 %last.1 = f32[512,128]{1,0:T(8,128)} custom-call(f32[512,128]{1,0:T(8,128)S(1)} %get-tuple-element.77.refs_0_, f32[512,128]{1,0:T(8,128)S(1)} %get-tuple-element.78.refs_1_, f32[512,128]{1,0:T(8,128)S(1)} %get-tuple-element.79.refs_2_, f32[512,128]{1,0:T(8,128)S(1)} %get-tuple-element.80.refs_3_, f32[512,128]{1,0:T(8,128)S(1)} %get-tuple-element.60.invd_ref.refs_5_.refs_4_, ...), custom_call_target="tpu_custom_call" | custom-call | tf_op jit(solution)/shard_map/last/pallas_call | solution.py:779
  (32 shorter events, 11.8 us)
Async XLA Ops:
  0.0 0.7 copy-start.8
  0.0 0.7 copy-start.7
  0.0 0.7 copy-start.10
  0.7 1.2 copy-start
  1.9 1.1 copy-start.1
  3.1 0.9 copy-start.2
  4.0 0.9 copy-start.3
  5.0 0.9 copy-start.4
  5.9 0.9 copy-start.6
  12.4 58.7 %collective-permute-start.3 = (f32[960,128]{1,0:T(8,128)}, f32[960,128]{1,0:T(8,128)S(1)}, u32[]{:S(2)}, u32[]{:S(2)}) collective-permute-start(f32[960,128]{1,0:T(8,128)} %get-tuple-element.54), channel_id=1, source_target_pairs={{0,1},{1,0},{2,3},{3,2},{4,5},{5,4},{6,7},{7,6},{8,9},{9,8},{10,11... | collective-permute-start | bytes 1474568 | tf_op jit(solution)/shard_map/ppermute | solution.py:800
  14.6 56.6 %collective-permute-start.4 = (f32[960,128]{1,0:T(8,128)}, f32[960,128]{1,0:T(8,128)S(1)}, u32[]{:S(2)}, u32[]{:S(2)}) collective-permute-start(f32[960,128]{1,0:T(8,128)} %get-tuple-element.55), channel_id=1, source_target_pairs={{0,63},{1,2},{2,1},{3,4},{4,3},{5,6},{6,5},{7,8},{8,7},{9,10},{10,... | collective-permute-start | bytes 1474568 | tf_op jit(solution)/shard_map/ppermute | solution.py:800
  21.7 15.2 %collective-permute-start = (f32[512,128]{1,0:T(8,128)S(1)}, f32[512,128]{1,0:T(8,128)S(1)}, u32[]{:S(2)}, u32[]{:S(2)}) collective-permute-start(f32[512,128]{1,0:T(8,128)S(1)} %bitcast.25), channel_id=1, source_target_pairs={{0,64},{64,0},{1,65},{65,1},{2,66},{66,2},{3,67},{67,3},{4,68},{68... | collective-permute-start | bytes 786440 | tf_op jit(solution)/shard_map/ppermute | solution.py:820
  36.9 20.2 %copy-start.5 = (f32[1,8,8,8,128]{4,3,2,1,0:T(8,128)S(1)}, f32[1,8,8,8,128]{4,3,2,1,0:T(8,128)}, u32[]{:S(2)}) copy-start(f32[1,8,8,8,128]{4,3,2,1,0:T(8,128)} %param.13) | copy-start | bytes 786436
  38.8 18.3 %all-to-all-start.1 = ((f32[64,1,128]{2,1,0:T(1,128)}), f32[64,1,128]{2,1,0:T(1,128)S(1)}, u32[]{:S(2)}, u32[]{:S(2)}) async-start(f32[64,1,128]{2,1,0:T(1,128)} %bitcast.11), calls=%async_computation.1 | async-start | bytes 65536 | tf_op jit(solution)/shard_map/all_to_all | solution.py:869
  57.1 0.7 copy-start.9
  60.1 5.0 %collective-permute-start.1 = (f32[256,128]{1,0:T(8,128)S(1)}, f32[256,128]{1,0:T(8,128)S(1)}, u32[]{:S(2)}, u32[]{:S(2)}) collective-permute-start(f32[256,128]{1,0:T(8,128)S(1)} %get-tuple-element.52), channel_id=1, source_target_pairs={{0,1},{1,0},{2,3},{3,2},{4,5},{5,4},{6,7},{7,6},{8,9},{9,8},{10,11... | collective-permute-start | bytes 393224 | tf_op jit(solution)/shard_map/ppermute | solution.py:800
  60.7 10.4 %collective-permute-start.2 = (f32[256,128]{1,0:T(8,128)S(1)}, f32[256,128]{1,0:T(8,128)S(1)}, u32[]{:S(2)}, u32[]{:S(2)}) collective-permute-start(f32[256,128]{1,0:T(8,128)S(1)} %get-tuple-element.53), channel_id=1, source_target_pairs={{0,63},{1,2},{2,1},{3,4},{4,3},{5,6},{6,5},{7,8},{8,7},{9,10},{10,... | collective-permute-start | bytes 393224 | tf_op jit(solution)/shard_map/ppermute | solution.py:800
  73.7 5.0 %collective-permute-start.5 = (f32[256,128]{1,0:T(8,128)S(1)}, f32[256,128]{1,0:T(8,128)S(1)}, u32[]{:S(2)}, u32[]{:S(2)}) collective-permute-start(f32[256,128]{1,0:T(8,128)S(1)} %get-tuple-element.61), channel_id=1, source_target_pairs={{0,1},{1,0},{2,3},{3,2},{4,5},{5,4},{6,7},{7,6},{8,9},{9,8},{10,11... | collective-permute-start | bytes 393224 | tf_op jit(solution)/shard_map/ppermute | solution.py:800
  73.8 10.5 %collective-permute-start.6 = (f32[256,128]{1,0:T(8,128)S(1)}, f32[256,128]{1,0:T(8,128)S(1)}, u32[]{:S(2)}, u32[]{:S(2)}) collective-permute-start(f32[256,128]{1,0:T(8,128)S(1)} %get-tuple-element.62), channel_id=1, source_target_pairs={{0,63},{1,2},{2,1},{3,4},{4,3},{5,6},{6,5},{7,8},{8,7},{9,10},{10,... | collective-permute-start | bytes 393224 | tf_op jit(solution)/shard_map/ppermute | solution.py:800
  101.9 5.0 %collective-permute-start.7 = (f32[256,128]{1,0:T(8,128)S(1)}, f32[256,128]{1,0:T(8,128)S(1)}, u32[]{:S(2)}, u32[]{:S(2)}) collective-permute-start(f32[256,128]{1,0:T(8,128)S(1)} %get-tuple-element.74), channel_id=1, source_target_pairs={{0,1},{1,0},{2,3},{3,2},{4,5},{5,4},{6,7},{7,6},{8,9},{9,8},{10,11... | collective-permute-start | bytes 393224 | tf_op jit(solution)/shard_map/ppermute | solution.py:800
  102.6 10.4 %collective-permute-start.8 = (f32[256,128]{1,0:T(8,128)S(1)}, f32[256,128]{1,0:T(8,128)S(1)}, u32[]{:S(2)}, u32[]{:S(2)}) collective-permute-start(f32[256,128]{1,0:T(8,128)S(1)} %get-tuple-element.75), channel_id=1, source_target_pairs={{0,63},{1,2},{2,1},{3,4},{4,3},{5,6},{6,5},{7,8},{8,7},{9,10},{10,... | collective-permute-start | bytes 393224 | tf_op jit(solution)/shard_map/ppermute | solution.py:800
  115.3 5.0 %collective-permute-start.9 = (f32[256,128]{1,0:T(8,128)S(1)}, f32[256,128]{1,0:T(8,128)S(1)}, u32[]{:S(2)}, u32[]{:S(2)}) collective-permute-start(f32[256,128]{1,0:T(8,128)S(1)} %get-tuple-element.81), channel_id=1, source_target_pairs={{0,1},{1,0},{2,3},{3,2},{4,5},{5,4},{6,7},{7,6},{8,9},{9,8},{10,11... | collective-permute-start | bytes 393224 | tf_op jit(solution)/shard_map/ppermute | solution.py:800
  115.4 10.5 %collective-permute-start.10 = (f32[256,128]{1,0:T(8,128)S(1)}, f32[256,128]{1,0:T(8,128)S(1)}, u32[]{:S(2)}, u32[]{:S(2)}) collective-permute-start(f32[256,128]{1,0:T(8,128)S(1)} %get-tuple-element.82), channel_id=1, source_target_pairs={{0,63},{1,2},{2,1},{3,4},{4,3},{5,6},{6,5},{7,8},{8,7},{9,10},{10,... | collective-permute-start | bytes 393224 | tf_op jit(solution)/shard_map/ppermute | solution.py:800

commit v3 on v2

--- a/solution.py
+++ b/solution.py
@@ -165,7 +165,12 @@
         rows.append(value[:, 128:])
     rows.append(jnp.zeros((128 - HALF, 128), f32))
     turned = jnp.concatenate(rows, axis=0).T
-    ret_ref[...] = turned[:OWNERS] + pltpu.roll(turned[OWNERS:], 16, 1)
+    mine = turned[:OWNERS] + pltpu.roll(turned[OWNERS:], 16, 1)
+    ret_ref[...] = (
+        pltpu.roll(mine, 1, 0)
+        + pltpu.roll(mine, 32, 1)
+        + pltpu.roll(pltpu.roll(mine, OWNERS - 1, 0), 64, 1)
+    )
 
 
 def deriv8(table, v):
@@ -385,8 +390,13 @@
     lax.fori_loop(0, 8, per_j, 0)
 
 
-BASIS_ROW = 704
-GHOST_ROWS = BASIS_ROW + 256
+PLANE_ROW = 512
+BASIS_ROW = PLANE_ROW + 192
+STATIC_ROW = BASIS_ROW + 256
+MASS_ROW = STATIC_ROW + 256
+SOLVE_ROW = MASS_ROW + 256
+POINT_ROW = SOLVE_ROW + 512
+GHOST_ROWS = POINT_ROW + 40
 
 
 def prepare_kernel(
@@ -394,18 +404,21 @@
     slot_ref,
     weight_ref,
     order_ref,
+    ids_ref,
+    live_ref,
     stiff_hbm,
     mass_hbm,
     field_hbm,
+    load_hbm,
     basis_hbm,
     inverse_hbm,
     send_ref,
-    rank_ref,
+    points_ref,
     coef_ref,
     mass_ref,
     start_ref,
     diag_ref,
-    inv_ref,
+    static_ref,
     basis_ref,
     solve_ref,
     a_ref,
@@ -413,9 +426,11 @@
     stiff_in,
     mass_in,
     field_in,
+    load_in,
     basis_in,
     inverse_in,
     tmp_ref,
+    rank_ref,
     sems,
 ):
     copies = [
@@ -425,6 +440,7 @@
                 (stiff_hbm, stiff_in),
                 (mass_hbm, mass_in),
                 (field_hbm, field_in),
+                (load_hbm, load_in),
                 (basis_hbm, basis_in),
                 (inverse_hbm, inverse_in),
             ]
@@ -435,9 +451,22 @@
     build_requests(owner_ref, slot_ref, weight_ref, send_ref, rank_ref)
     order = order_ref[...]
     match = (iota((128, 128), 0) == order).astype(f32)
-    inv = jnp.sum(match.T * iota((128, 128), 0).astype(f32), axis=0, keepdims=True)
-    inv = inv.astype(jnp.int32)
-    inv_ref[...] = inv
+    inv_f = jnp.sum(match.T * iota((128, 128), 0).astype(f32), axis=0, keepdims=True)
+    inv = inv_f.astype(jnp.int32)
+    rank = rank_ref[...]
+    ids = ids_ref[...]
+    live = iota((1, R_DEV), 1) < live_ref[0, 0]
+    node = jnp.where(live, lax.shift_right_logical(ids, 7), -1)
+    point_rows = [
+        owner_ref[...].astype(f32),
+        rank + jnp.where(rank >= float(HALF), float(16 - HALF), 0.0),
+        node.astype(f32),
+        jnp.bitwise_and(ids, 127).astype(f32),
+    ]
+    for n, row in enumerate(point_rows):
+        for c in range(8):
+            points_ref[n * 8 + c : n * 8 + c + 1] = row[:, c * 128 : c * 128 + 128]
+    points_ref[32:40] = jnp.broadcast_to(inv_f, (8, 128))
     for copy in copies:
         copy.wait()
     tmp_ref[...] = take_lanes(stiff_in[0:512, :], inv)
@@ -449,15 +478,21 @@
     coef_ref[512:1536, :] = take_lanes(stiff_in[512:1536, :], inv)
     mass_ref[...] = take_lanes(mass_in[...], inv)
     start_ref[...] = take_lanes(field_in[...], inv)
+    stiff_apply(start_ref, coef_ref, mass_ref, static_ref)
+    static_ref[...] = take_lanes(load_in[...], inv) - static_ref[...]
+    in_plane(static_ref)
     basis = dot_nn(match, basis_in[...], exact_mode)
     basis_ref[...] = basis
-    solve_ref[...] = dot_nn(basis, inverse_in[...], exact_mode)
+    solve = dot_nn(basis, inverse_in[...], exact_mode)
+    solve_ref[...] = solve
     local_diagonal(coef_ref, mass_ref, diag_ref)
     in_plane(diag_ref)
     even = where_am_i()[0]
     zeros = jnp.zeros((64, 128), f32)
     pack(coef_ref[1024:1536, :], a_ref, b_ref, 0, even)
     pack(coupled(diag_ref, zeros, zeros), a_ref, b_ref, 256, even)
+    pack(coupled(static_ref, zeros, zeros), a_ref, b_ref, STATIC_ROW, even)
+    pack(mass_ref[...], a_ref, b_ref, MASS_ROW, even)
     rows = [
         (coef_ref[448:512], coef_ref[0:64]),
         (coef_ref[960:1024], coef_ref[512:576]),
@@ -467,57 +502,52 @@
         cols = slice(c * 128, c * 128 + 128)
         rows.append((basis[LAYER:, cols], basis[:LAYER, cols]))
     for n, (up, down) in enumerate(rows):
-        at = 512 + n * 64
+        at = PLANE_ROW + n * 64
         a_ref[at : at + 64] = jnp.where(even, up, down)
         b_ref[at : at + 64] = jnp.where(even, down, up)
-
-
-def source_kernel(
-    ret_ref,
-    owner_ref,
-    rank_ref,
-    ids_ref,
-    live_ref,
-    load_ref,
-    inv_ref,
-    start_ref,
-    coef_ref,
-    mass_ref,
-    out_ref,
-    a_ref,
-    b_ref,
-):
-    hits = (iota((OWNERS, R_DEV), 0) == owner_ref[...]).astype(f32)
-    picked = dot_nn(ret_ref[...].T, hits, exact_mode)[0:32]
-    rank = rank_ref[...].astype(jnp.int32)
-    place = rank + jnp.where(rank >= HALF, 16 - HALF, 0)
+    for c in range(NC // 128):
+        at = SOLVE_ROW + c * 128
+        cols = solve[:, c * 128 : c * 128 + 128]
+        a_ref[at : at + 128] = cols
+        b_ref[at : at + 128] = cols
+    a_ref[POINT_ROW:GHOST_ROWS] = points_ref[...]
+    b_ref[POINT_ROW:GHOST_ROWS] = points_ref[...]
+
+
+def scatter_points(points, answers):
+    def row(n):
+        return jnp.concatenate(
+            [points[n * 8 + c : n * 8 + c + 1] for c in range(8)], axis=1
+        ).astype(jnp.int32)
+
+    owner, place, node, elem = row(0), row(1), row(2), row(3)
+    hits = (iota((OWNERS, R_DEV), 0) == owner).astype(f32)
+    picked = dot_nn(answers, hits, exact_mode)
     value = jnp.sum(
         jnp.where(iota((32, R_DEV), 0) == place, picked, 0.0), axis=0, keepdims=True
     )
-    value = jnp.where(iota((1, R_DEV), 1) < live_ref[0, 0], value, 0.0)
-    ids = ids_ref[...]
-    node = lax.shift_right_logical(ids, 7)
-    elem = jnp.bitwise_and(ids, 127)
     at_node = (iota((NODES, R_DEV), 0) == node).astype(f32).astype(bf16)
     at_elem = (iota((128, R_DEV), 0) == elem).astype(f32).astype(bf16)
     spread = jnp.concatenate([at_elem * piece for piece in split3(value)], axis=0)
     landed = dot_nt(at_node, spread)
-    source = load_ref[...] + (landed[:, 0:128] + landed[:, 128:256] + landed[:, 256:384])
-    source = take_lanes(source, inv_ref[...])
-    stiff_apply(start_ref, coef_ref, mass_ref, out_ref)
-    out_ref[...] = source - out_ref[...]
-    in_plane(out_ref)
-    zeros = jnp.zeros((64, 128), f32)
-    pack(coupled(out_ref, zeros, zeros), a_ref, b_ref, 0, where_am_i()[0])
+    landed = landed[:, 0:128] + landed[:, 128:256] + landed[:, 256:384]
+    return take_lanes(landed, points[32:33].astype(jnp.int32))
+
+
+def ghost_assemble(ghost_ref, beyond_ref):
+    in_plane(ghost_ref)
+    in_plane(beyond_ref, 1)
+    first = first_layer((64, 128))
+    turned = pltpu.roll(beyond_ref[...], LAYER, 1)
+    ghost_ref[0:64] = ghost_ref[0:64] + jnp.where(first, 0.0, turned)
+    ghost_ref[448:512] = ghost_ref[448:512] + jnp.where(first, turned, 0.0)
 
 
 def opening_half(
     place,
     base_ref,
     y_ref,
-    cur_in_ref,
-    a_ref,
-    b_ref,
+    cur_in,
     invd_ref,
     third_ref,
     ginvd_ref,
@@ -534,7 +564,6 @@
     face_ref,
     side_ref,
 ):
-    unpack(a_ref, b_ref, 0, place, ghost_ref)
     residual = coupled(y_ref, ghost_ref[448:512], ghost_ref[0:64])
     if base_ref is not None:
         residual = residual + base_ref[...]
@@ -551,7 +580,7 @@
     alpha, beta = STEPS[1]
     second = alpha * update + beta * invd * residual
     upd_ref[...] = second
-    cur_ref[...] = cur_in_ref[...] + (update + second)
+    cur_ref[...] = cur_in + (update + second)
     stiff_apply(upd_ref, coef_ref, mass_ref, w_ref)
     in_plane(w_ref)
     alpha, beta = STEPS[2]
@@ -569,11 +598,11 @@
 
 
 def start_kernel(
-    y_ref,
+    ret_ref,
+    points_ref,
+    static_ref,
     diag_ref,
     cur_in_ref,
-    a_ref,
-    b_ref,
     ga_ref,
     gb_ref,
     coef_ref,
@@ -589,31 +618,52 @@
     ginvd_ref,
     planes_ref,
     outer_ref,
-    *scratch,
+    gmass_ref,
+    beyond_mass_ref,
+    y_ref,
+    gstatic_ref,
+    ghost_ref,
+    face_ref,
+    side_ref,
 ):
     place = where_am_i()
+    even, has_below, has_above = place
     unpack(ga_ref, gb_ref, 0, place, third_ref)
     unpack(ga_ref, gb_ref, 256, place, ginvd_ref)
+    unpack(ga_ref, gb_ref, STATIC_ROW, place, gstatic_ref)
+    unpack(ga_ref, gb_ref, MASS_ROW, place, gmass_ref)
     diag = coupled(diag_ref, ginvd_ref[448:512], ginvd_ref[0:64])
     mirror(ginvd_ref, diag[0:64], diag[448:512])
     invd_ref[...] = 1.0 / diag
     gdiag = ginvd_ref[...]
     there = gdiag > 0.0
     ginvd_ref[...] = jnp.where(there, 1.0 / jnp.where(there, gdiag, 1.0), 0.0)
-    below, above = beside(ga_ref[512:704], gb_ref[512:704], place)
+    span = slice(PLANE_ROW, BASIS_ROW)
+    below, above = beside(ga_ref[span], gb_ref[span], place)
     planes_ref[...] = jnp.where(first_layer(below.shape), above, below)
+    beyond_mass_ref[...] = jnp.where(first_layer((64, 128)), below[128:], above[128:])
     for c in range(NC // 128):
         at = BASIS_ROW + c * 64
         below, above = beside(ga_ref[at : at + 64], gb_ref[at : at + 64], place)
         outer_ref[0:64, c * 128 : c * 128 + 128] = below
         outer_ref[64:128, c * 128 : c * 128 + 128] = above
+    answers = ret_ref[...].T
+    y_ref[...] = scatter_points(points_ref[...], answers[32:64])
+    in_plane(y_ref)
+    y_ref[...] = y_ref[...] + static_ref[...]
+    span = slice(POINT_ROW, GHOST_ROWS)
+    below, above = beside(ga_ref[span], gb_ref[span], place)
+    under = jnp.where(has_below, scatter_points(below, answers[0:32]), 0.0)
+    over = jnp.where(has_above, scatter_points(above, answers[64:96]), 0.0)
+    ghost_ref[...] = jnp.where(first_layer(over.shape), over, under)
+    side_ref[...] = jnp.where(first_layer((64, 128)), under[448:512], over[0:64])
+    ghost_assemble(ghost_ref, side_ref)
+    ghost_ref[...] = ghost_ref[...] + gstatic_ref[...]
     opening_half(
         place,
         None,
         y_ref,
-        cur_in_ref,
-        a_ref,
-        b_ref,
+        cur_in_ref[...],
         invd_ref,
         third_ref,
         ginvd_ref,
@@ -626,12 +676,93 @@
         w_ref,
         a_out_ref,
         b_out_ref,
-        *scratch,
-    )
-
-
-def again_kernel(*refs):
-    opening_half(where_am_i(), *refs)
+        ghost_ref,
+        face_ref,
+        side_ref,
+    )
+
+
+def again_kernel(
+    parts_ref,
+    solve_ref,
+    ga_ref,
+    gb_ref,
+    gmass_ref,
+    beyond_mass_ref,
+    y_in_ref,
+    base_ref,
+    cur_in_ref,
+    a_ref,
+    b_ref,
+    invd_ref,
+    third_ref,
+    ginvd_ref,
+    planes_ref,
+    coef_ref,
+    mass_ref,
+    res_ref,
+    upd_ref,
+    cur_ref,
+    w_ref,
+    a_out_ref,
+    b_out_ref,
+    y_ref,
+    gc_ref,
+    ghost_ref,
+    face_ref,
+    side_ref,
+):
+    place = where_am_i()
+    total = parts_ref[0:8]
+    for n in range(1, OWNERS * NC // 1024):
+        total = total + parts_ref[n * 8 : n * 8 + 8]
+    total = total + pltpu.roll(total, 4, 0)
+    both = None
+    for c in range(NC // 128):
+        row = jnp.broadcast_to(total[c : c + 1], (8, 128))
+        at = SOLVE_ROW + c * 128
+        rows = jnp.concatenate(
+            [
+                solve_ref[:, c * 128 : c * 128 + 128],
+                ga_ref[at : at + 128],
+                gb_ref[at : at + 128],
+            ],
+            axis=0,
+        )
+        term = dot_nt(row, rows, exact_mode)
+        both = term if both is None else both + term
+    correction = both[0:1, 0:128]
+    below, above = beside(both[0:1, 128:256], both[0:1, 256:384], place)
+    y_ref[...] = mass_ref[...] * correction
+    in_plane(y_ref)
+    y_ref[...] = -(y_ref[...] + y_in_ref[...])
+    unpack(a_ref, b_ref, 0, place, ghost_ref)
+    first = first_layer((1, 128))
+    gc_ref[...] = gmass_ref[...] * jnp.where(first, above, below)
+    side_ref[...] = beyond_mass_ref[...] * jnp.where(first, below, above)
+    ghost_assemble(gc_ref, side_ref)
+    ghost_ref[...] = ghost_ref[...] - gc_ref[...]
+    opening_half(
+        place,
+        base_ref,
+        y_ref,
+        cur_in_ref[...] + correction,
+        invd_ref,
+        third_ref,
+        ginvd_ref,
+        planes_ref,
+        coef_ref,
+        mass_ref,
+        res_ref,
+        upd_ref,
+        cur_ref,
+        w_ref,
+        a_out_ref,
+        b_out_ref,
+        ghost_ref,
+        face_ref,
+        side_ref,
+    )
 
 
 def closing_half(
@@ -686,6 +817,8 @@
     cur_ref,
     w_out_ref,
     part_ref,
+    a_out_ref,
+    b_out_ref,
     vec_ref,
     *scratch,
 ):
@@ -711,6 +844,15 @@
     in_plane(w_out_ref)
     zeros = jnp.zeros((64, 128), f32)
     local = res_ref[...] - coupled(w_out_ref, zeros, zeros)
+    pack(
+        message(
+            -w_out_ref[0:64], -w_out_ref[448:512], local[0:64], local[64:448], local[448:512]
+        ),
+        a_out_ref,
+        b_out_ref,
+        0,
+        where_am_i()[0],
+    )
     sums = jnp.sum(local, axis=0, keepdims=True)
     bottom = -jnp.sum(w_out_ref[0:64], axis=0, keepdims=True)
     top = -jnp.sum(w_out_ref[448:512], axis=0, keepdims=True)
@@ -724,43 +866,6 @@
         part_ref[n * 8 : n * 8 + 8] = eight
 
 
-def restart_kernel(
-    parts_ref,
-    solve_ref,
-    mass_ref,
-    w_ref,
-    base_ref,
-    cur_in_ref,
-    y_ref,
-    cur_ref,
-    a_ref,
-    b_ref,
-):
-    total = parts_ref[0:8]
-    for n in range(1, OWNERS * NC // 1024):
-        total = total + parts_ref[n * 8 : n * 8 + 8]
-    total = total + pltpu.roll(total, 4, 0)
-    correction = None
-    for c in range(NC // 128):
-        row = jnp.broadcast_to(total[c : c + 1], (8, 128))
-        term = dot_nt(row, solve_ref[:, c * 128 : c * 128 + 128], exact_mode)
-        correction = term if correction is None else correction + term
-    correction = correction[0:1]
-    cur_ref[...] = cur_in_ref[...] + correction
-    y_ref[...] = mass_ref[...] * correction
-    in_plane(y_ref)
-    y_ref[...] = -(y_ref[...] + w_ref[...])
-    zeros = jnp.zeros((64, 128), f32)
-    inner = base_ref[...] + coupled(y_ref, zeros, zeros)
-    pack(
-        message(y_ref[0:64], y_ref[448:512], inner[0:64], inner[64:448], inner[448:512]),
-        a_ref,
-        b_ref,
-        0,
-        where_am_i()[0],
-    )
-
-
 def last_kernel(*refs):
     inputs, (order_ref, out_ref), scratch = refs[:11], refs[11:13], refs[13:]
     current = closing_half(*inputs, *scratch)[1]
@@ -771,7 +876,7 @@
     def space(n):
         if n in smem:
             return pltpu.SMEM
-        return pl.ANY if n in far else pltpu.VMEM
+        return pltpu.HBM if n in far else pltpu.VMEM
 
     scratches = [pltpu.VMEM(s, f32) for s in scratch]
     if copies:
@@ -788,6 +893,7 @@
 
 
 FIELD = ((NODES, 128), f32)
+PLANE = ((64, 128), f32)
 LAYER_MSG = ((256, 128), f32)
 GHOST_MSG = ((GHOST_ROWS, 128), f32)
 GHOST_WORK = [(NODES, 128), (64, 128), (64, 128)]
@@ -819,17 +925,17 @@
     owner = donor_owner.reshape(1, R_DEV)
     other_field = lax.ppermute(own_field, "sess", [(0, 1), (1, 0)])
 
-    send, rank, coef, mass, start, diag, inv, basis, solve, ghost_a, ghost_b = call(
+    send, points, coef, mass, start, diag, static, basis, solve, ga, gb = call(
         prepare_kernel,
         "prepare",
         [
             ((OWNERS * ASK, 128), f32),
-            ((1, R_DEV), f32),
+            ((40, 128), f32),
             ((3 * NODES, 128), f32),
             FIELD,
             FIELD,
             FIELD,
-            ((1, 128), jnp.int32),
+            FIELD,
             ((128, NC), f32),
             ((128, NC), f32),
             GHOST_MSG,
@@ -839,23 +945,29 @@
         donor_slot,
         interp_weights.reshape(3 * NP, R_DEV),
         order,
+        recv_ids,
+        live_count,
         stiffness.reshape(3 * NODES, 128),
         helm_mass.reshape(NODES, 128),
         own_field,
+        load.reshape(NODES, 128),
         coarse_basis.reshape(128, NC),
         coarse_inverse.reshape(NC, NC),
-        far=(4, 5, 6, 7, 8),
+        smem=(5,),
+        far=(6, 7, 8, 9, 10, 11),
         scratch=[
             (3 * NODES, 128),
+            (NODES, 128),
             (NODES, 128),
             (NODES, 128),
             (128, NC),
             (NC, NC),
             (NODES, 128),
+            (1, R_DEV),
         ],
-        copies=5,
-    )
-    ghost_a, ghost_b = exchange(ghost_a, ghost_b)
+        copies=6,
+    )
+    ga, gb = exchange(ga, gb)
     received = lax.all_to_all(
         send.reshape(OWNERS, ASK, 128), "elem", split_axis=0, concat_axis=0, tiled=True
     )
@@ -867,44 +979,27 @@
         other_field,
     )
     answered = lax.all_to_all(answer, "elem", split_axis=0, concat_axis=0, tiled=True)
-    y, a, b = call(
-        source_kernel,
-        "source",
-        [FIELD, LAYER_MSG, LAYER_MSG],
+    half = [FIELD, FIELD, FIELD, FIELD, LAYER_MSG, LAYER_MSG]
+    res, upd, cur, w, a, b, invd, third, ginvd, planes, outer, gmass, beyond = call(
+        start_kernel,
+        "start",
+        half + [FIELD, FIELD, FIELD, ((192, 128), f32), ((128, NC), f32), FIELD, PLANE],
         answered,
-        owner,
-        rank,
-        recv_ids,
-        live_count,
-        load.reshape(NODES, 128),
-        inv,
+        points,
+        static,
+        diag,
         start,
+        ga,
+        gb,
         coef,
         mass,
-        smem=(4,),
+        scratch=[(NODES, 128), (NODES, 128)] + GHOST_WORK,
     )
     a, b = exchange(a, b)
-    half = [FIELD, FIELD, FIELD, FIELD, LAYER_MSG, LAYER_MSG]
-    res, upd, cur, w, a, b, invd, third, ginvd, planes, outer = call(
-        start_kernel,
-        "start",
-        half + [FIELD, FIELD, FIELD, ((192, 128), f32), ((128, NC), f32)],
-        y,
-        diag,
-        start,
-        a,
-        b,
-        ghost_a,
-        ghost_b,
-        coef,
-        mass,
-        scratch=GHOST_WORK,
-    )
-    a, b = exchange(a, b)
-    res, cur, w, part = call(
+    res, cur, w, part, a, b = call(
         middle_kernel,
         "middle",
-        [FIELD, FIELD, FIELD, ((OWNERS * NC // 128, 128), f32)],
+        [FIELD, FIELD, FIELD, ((OWNERS * NC // 128, 128), f32), LAYER_MSG, LAYER_MSG],
         w,
         res,
         upd,
@@ -920,6 +1015,7 @@
         outer,
         scratch=[(NODES, 128)] + GHOST_WORK,
     )
+    a, b = exchange(a, b)
     parts = lax.all_to_all(
         part.reshape(OWNERS, NC // 128, 128),
         "elem",
@@ -927,24 +1023,18 @@
         concat_axis=0,
         tiled=True,
     )
-    y, cur, a, b = call(
-        restart_kernel,
-        "restart",
-        [FIELD, FIELD, LAYER_MSG, LAYER_MSG],
-        parts.reshape(OWNERS * NC // 128, 128),
-        solve,
-        mass,
-        w,
-        res,
-        cur,
-    )
-    a, b = exchange(a, b)
     res, upd, cur, w, a, b = call(
         again_kernel,
         "again",
         half,
+        parts.reshape(OWNERS * NC // 128, 128),
+        solve,
+        ga,
+        gb,
+        gmass,
+        beyond,
+        w,
         res,
-        y,
         cur,
         a,
         b,
@@ -954,7 +1044,7 @@
         planes,
         coef,
         mass,
-        scratch=GHOST_WORK,
+        scratch=[(NODES, 128), (NODES, 128)] + GHOST_WORK,
     )
     a, b = exchange(a, b)
     (out,) = call(

time: 129 us -> 127 us (0.984)
  blocking collectives: 29.3 us -> 63.6 us
  waiting for transfers between devices: 41.8 us -> 16.4 us
  starting transfers between devices: 28.4 us -> 17.4 us
    all_to_all x0 -> x1, blocking collectives: none -> 18 us  [per_device(): lax.all_to_all(answer, 'elem', split_axis=0, concat_axis=0, tiled=True)]
    ppermute x10 -> x8, waiting for transfers between devices: 32.9 us -> 16.4 us  [exchange(): return (lax.ppermute(a, 'elem', pairs_a), lax.ppermute(b, 'elem', pairs_b))]
    all_to_all x1, blocking collectives: 15.2 us -> 28.5 us  [per_device(): lax.all_to_all(send.reshape(OWNERS, ASK, 128), 'elem', split_axis=0, conc...]
    all_to_all x1 -> x0, waiting for transfers between devices: 8.86 us -> none  [per_device(): lax.all_to_all(answer, 'elem', split_axis=0, concat_axis=0, tiled=True)]
    all_to_all x1 -> x0, starting transfers between devices: 8.79 us -> none  [per_device(): lax.all_to_all(answer, 'elem', split_axis=0, concat_axis=0, tiled=True)]
    all_to_all x1, blocking collectives: 14.1 us -> 17.1 us  [per_device(): lax.all_to_all(part.reshape(OWNERS, NC // 128, 128), 'elem', split_axis=0...]
    ppermute x10 -> x8, starting transfers between devices: 19.6 us -> 17.4 us  [exchange(): return (lax.ppermute(a, 'elem', pairs_a), lax.ppermute(b, 'elem', pairs_b))]
    pallas_call x8 -> x6, Pallas kernels: 20.4 us -> 21 us  [call(): pl.pallas_call(kernel, name=name, out_shape=[jax.ShapeDtypeStruct(s, d) f...]
  transfers between devices with their start and end apart: 12 -> 9, of which waited for: 9 -> 4; matrix products, arithmetic and copies ran while one was open for 0% -> 0% of each run, Pallas kernels for 3% -> 1%
where the time goes in v3:
time: 127 us
  blocking collectives  63.6 us (50%)
  Pallas kernels  21 us (17%)
  starting transfers between devices  17.4 us (14%)
  waiting for transfers between devices  16.4 us (13%)
  local copies, waits for them, and re-layouts  7.74 us (6%)
    all_to_all x1, blocking collectives, per_device(): lax.all_to_all(send.reshape(OWNERS, ASK, 128), 'elem', split_axis=0, conc...  28.5 us
    pallas_call x6, Pallas kernels, call(): pl.pallas_call(kernel, name=name, out_shape=[jax.ShapeDtypeStruct(s, d) f...  21 us
    all_to_all x1, blocking collectives, per_device(): lax.all_to_all(answer, 'elem', split_axis=0, concat_axis=0, tiled=True)  18 us
    ppermute x8, starting transfers between devices, exchange(): return (lax.ppermute(a, 'elem', pairs_a), lax.ppermute(b, 'elem', pairs_b))  17.4 us
    all_to_all x1, blocking collectives, per_device(): lax.all_to_all(part.reshape(OWNERS, NC // 128, 128), 'elem', split_axis=0...  17.1 us
    ppermute x8, waiting for transfers between devices, exchange(): return (lax.ppermute(a, 'elem', pairs_a), lax.ppermute(b, 'elem', pairs_b))  16.4 us
    unnamed x22, local copies, waits for them, and re-layouts  7.74 us
  transfers between devices with their start and end apart: 9, of which 4 were waited for; matrix products, arithmetic and copies ran while one was open for 0% of the time, Pallas kernels for 1%

profile of v3, /device:TPU:0, one launch (start us, length us, event | category | flops | bytes accessed | tf_op | source)
XLA Modules:
  0.0 126.9 jit_solution(6933952622973135652)
XLA Ops:
  1.4 1.2 copy-done
  2.6 1.1 copy-done.1
  3.7 0.9 copy-done.2
  4.7 0.9 copy-done.3
  5.6 0.9 copy-done.4
  6.6 0.9 copy-done.5
  8.4 6.0 %prepare.1 = (f32[512,128]{1,0:T(8,128)S(1)}, f32[40,128]{1,0:T(8,128)S(1)}, f32[1536,128]{1,0:T(8,128)S(1)}, f32[512,128]{1,0:T(8,128)S(1)}, f32[512,128]{1,0:T...) custom-call(s32[1,1024]{1,0:T(1,128)S(1)} %bitcast.32, ...), custom_call_target="tpu_custom_call" | custom-call | tf_op jit(solution)/shard_map/prepare/pallas_call | solution.py:884
  14.4 2.1 %collective-permute-start.1 = (f32[2024,128]{1,0:T(8,128)S(1)}, f32[2024,128]{1,0:T(8,128)S(1)}, u32[]{:S(2)}, u32[]{:S(2)}) collective-permute-start(f32[2024,128]{1,0:T(8,128)S(1)} %get-tuple-element.46), channel_id=1, source_target_pairs={{0,1},{1,0},{2,3},{3,2},{4,5},{5,4},{6,7},{7,6},{8,9},{9,8},{10,11... | collective-permute-start | bytes 3108872 | tf_op jit(solution)/shard_map/ppermute | solution.py:906
  16.5 7.2 %collective-permute-start.2 = (f32[2024,128]{1,0:T(8,128)S(1)}, f32[2024,128]{1,0:T(8,128)S(1)}, u32[]{:S(2)}, u32[]{:S(2)}) collective-permute-start(f32[2024,128]{1,0:T(8,128)S(1)} %get-tuple-element.47), channel_id=1, source_target_pairs={{0,63},{1,2},{2,1},{3,4},{4,3},{5,6},{6,5},{7,8},{8,7},{9,10},{10,... | collective-permute-start | bytes 3108872 | tf_op jit(solution)/shard_map/ppermute | solution.py:906
  23.7 28.5 %all_to_all.21 = f32[64,8,128]{2,1,0:T(8,128)S(1)} all-to-all(f32[64,8,128]{2,1,0:T(8,128)S(1)} %bitcast.22), channel_id=1, replica_groups=mesh['sess'=2,'elem'=64] {'elem'}, dimensions={0} | all-to-all | bytes 524288 | tf_op jit(solution)/shard_map/all_to_all | solution.py:971
  52.2 1.3 %owner.1 = f32[64,128]{1,0:T(8,128)S(1)} custom-call(f32[512,128]{1,0:T(8,128)S(1)} %bitcast.18, f32[512,128]{1,0:T(8,128)S(1)} %collective-permute-done.field_ref), custom_call_target="tpu_custom_call" | custom-call | tf_op jit(solution)/shard_map/owner/pallas_call | solution.py:884
  53.6 18.0 %all_to_all.22 = f32[64,1,128]{2,1,0:T(1,128)S(1)} all-to-all(f32[64,1,128]{2,1,0:T(1,128)S(1)} %bitcast.29), channel_id=1, replica_groups=mesh['sess'=2,'elem'=64] {'elem'}, dimensions={0} | all-to-all | bytes 65536 | tf_op jit(solution)/shard_map/all_to_all | solution.py:981
  71.5 5.4 %start.1 = (f32[512,128]{1,0:T(8,128)S(1)}, f32[512,128]{1,0:T(8,128)S(1)}, f32[512,128]{1,0:T(8,128)S(1)}, f32[512,128]{1,0:T(8,128)S(1)}, f32[256,128]{1,0:T(8...) custom-call(f32[64,128]{1,0:T(8,128)S(1)} %bitcast.28, ...), custom_call_target="tpu_custom_call" | custom-call | tf_op jit(solution)/shard_map/start/pallas_call | solution.py:884
  77.6 2.2 %collective-permute-start.4 = (f32[256,128]{1,0:T(8,128)S(1)}, f32[256,128]{1,0:T(8,128)S(1)}, u32[]{:S(2)}, u32[]{:S(2)}) collective-permute-start(f32[256,128]{1,0:T(8,128)S(1)} %get-tuple-element.56), channel_id=1, source_target_pairs={{0,63},{1,2},{2,1},{3,4},{4,3},{5,6},{6,5},{7,8},{8,7},{9,10},{10,... | collective-permute-start | bytes 393224 | tf_op jit(solution)/shard_map/ppermute | solution.py:906
  79.8 2.2 %collective-permute-done.3.a_ref = f32[256,128]{1,0:T(8,128)S(1)} collective-permute-done((f32[256,128]{1,0:T(8,128)S(1)}, f32[256,128]{1,0:T(8,128)S(1)}, u32[]{:S(2)}, u32[]{:S(2)}) %collective-permute-start.3) | collective-permute-done | bytes 131104 | tf_op jit(solution)/shard_map/ppermute | solution.py:906
  82.0 6.0 %collective-permute-done.4.b_ref = f32[256,128]{1,0:T(8,128)S(1)} collective-permute-done((f32[256,128]{1,0:T(8,128)S(1)}, f32[256,128]{1,0:T(8,128)S(1)}, u32[]{:S(2)}, u32[]{:S(2)}) %collective-permute-start.4) | collective-permute-done | bytes 131104 | tf_op jit(solution)/shard_map/ppermute | solution.py:906
  88.0 2.6 %middle.1 = (f32[512,128]{1,0:T(8,128)S(1)}, f32[512,128]{1,0:T(8,128)S(1)}, f32[512,128]{1,0:T(8,128)S(1)}, f32[256,128]{1,0:T(8,128)S(1)}, f32[256,128]{1,0:T(8,128)S(1)}, /*index=5*/f32[256,128]{1,0:T(8,128)S(1)}) custom-call(f32[512,128]{1,0:T(8,128)S(1)} %get-tuple-element.50.w_ref, f32[512,128]{1,0:T(8,128)S(1)} %get-tuple-element.51.res_in_ref, ...), custom_call_target="tpu_custom_call" | custom-call | tf_op jit(solution)/shard_map/middle/pallas_call | solution.py:884
  90.7 2.3 %collective-permute-start.6 = (f32[256,128]{1,0:T(8,128)S(1)}, f32[256,128]{1,0:T(8,128)S(1)}, u32[]{:S(2)}, u32[]{:S(2)}) collective-permute-start(f32[256,128]{1,0:T(8,128)S(1)} %get-tuple-element.69), channel_id=1, source_target_pairs={{0,63},{1,2},{2,1},{3,4},{4,3},{5,6},{6,5},{7,8},{8,7},{9,10},{10,... | collective-permute-start | bytes 393224 | tf_op jit(solution)/shard_map/ppermute | solution.py:906
  93.1 17.1 %all_to_all.23 = f32[64,4,128]{2,1,0:T(4,128)S(1)} all-to-all(f32[64,4,128]{2,1,0:T(4,128)S(1)} %bitcast.30), channel_id=1, replica_groups=mesh['sess'=2,'elem'=64] {'elem'}, dimensions={0} | all-to-all | bytes 262144 | tf_op jit(solution)/shard_map/all_to_all | solution.py:1019
  110.2 3.5 %again.1 = (f32[512,128]{1,0:T(8,128)S(1)}, f32[512,128]{1,0:T(8,128)S(1)}, f32[512,128]{1,0:T(8,128)S(1)}, f32[512,128]{1,0:T(8,128)S(1)}, f32[256,128]{1,0:T(8,128)S(1)}, /*index=5*/f32[256,128]{1,0:T(8,128)S(1)}) custom-call(f32[256,128]{1,0:T(8,128)S(1)} %bitcast.21, f32[128,512]{1,0:T(8,128)S(1)} %get-tuple-element.62.solve_ref, ...), custom_call_target="tpu_custom_call" | custom-call | tf_op jit(solution)/shard_map/again/pallas_call | solution.py:884
  114.3 2.2 %collective-permute-start.8 = (f32[256,128]{1,0:T(8,128)S(1)}, f32[256,128]{1,0:T(8,128)S(1)}, u32[]{:S(2)}, u32[]{:S(2)}) collective-permute-start(f32[256,128]{1,0:T(8,128)S(1)} %get-tuple-element.76), channel_id=1, source_target_pairs={{0,63},{1,2},{2,1},{3,4},{4,3},{5,6},{6,5},{7,8},{8,7},{9,10},{10,... | collective-permute-start | bytes 393224 | tf_op jit(solution)/shard_map/ppermute | solution.py:906
  116.5 2.2 %collective-permute-done.7.refs_5_ = f32[256,128]{1,0:T(8,128)S(1)} collective-permute-done((f32[256,128]{1,0:T(8,128)S(1)}, f32[256,128]{1,0:T(8,128)S(1)}, u32[]{:S(2)}, u32[]{:S(2)}) %collective-permute-start.7) | collective-permute-done | bytes 131104 | tf_op jit(solution)/shard_map/ppermute | solution.py:906
  118.7 6.0 %collective-permute-done.8.refs_6_ = f32[256,128]{1,0:T(8,128)S(1)} collective-permute-done((f32[256,128]{1,0:T(8,128)S(1)}, f32[256,128]{1,0:T(8,128)S(1)}, u32[]{:S(2)}, u32[]{:S(2)}) %collective-permute-start.8) | collective-permute-done | bytes 131104 | tf_op jit(solution)/shard_map/ppermute | solution.py:906
  124.7 2.1 %last.1 = f32[512,128]{1,0:T(8,128)} custom-call(f32[512,128]{1,0:T(8,128)S(1)} %get-tuple-element.71.refs_0_, f32[512,128]{1,0:T(8,128)S(1)} %get-tuple-element.72.refs_1_, f32[512,128]{1,0:T(8,128)S(1)} %get-tuple-element.73.refs_2_, f32[512,128]{1,0:T(8,128)S(1)} %get-tuple-element.74.refs_3_, f32[512,128]{1,0:T(8,128)S(1)} %get-tuple-element.54.invd_ref.refs_4_, ...), custom_call_target="tpu_custom_call" | custom-call | tf_op jit(solution)/shard_map/last/pallas_call | solution.py:884
  (25 shorter events, 3.0 us)
Async XLA Ops:
  0.7 0.7 copy-start.9
  0.7 0.7 copy-start.8
  0.7 0.7 copy-start.7
  0.7 0.7 copy-start.10
  1.4 1.2 copy-start
  2.6 1.1 copy-start.1
  3.7 0.9 copy-start.2
  4.7 0.9 copy-start.3
  5.6 0.9 copy-start.4
  6.6 0.9 copy-start.5
  7.5 0.9 copy-start.6
  14.4 57.1 %collective-permute-start.1 = (f32[2024,128]{1,0:T(8,128)S(1)}, f32[2024,128]{1,0:T(8,128)S(1)}, u32[]{:S(2)}, u32[]{:S(2)}) collective-permute-start(f32[2024,128]{1,0:T(8,128)S(1)} %get-tuple-element.46), channel_id=1, source_target_pairs={{0,1},{1,0},{2,3},{3,2},{4,5},{5,4},{6,7},{7,6},{8,9},{9,8},{10,11... | collective-permute-start | bytes 3108872 | tf_op jit(solution)/shard_map/ppermute | solution.py:906
  16.5 55.0 %collective-permute-start.2 = (f32[2024,128]{1,0:T(8,128)S(1)}, f32[2024,128]{1,0:T(8,128)S(1)}, u32[]{:S(2)}, u32[]{:S(2)}) collective-permute-start(f32[2024,128]{1,0:T(8,128)S(1)} %get-tuple-element.47), channel_id=1, source_target_pairs={{0,63},{1,2},{2,1},{3,4},{4,3},{5,6},{6,5},{7,8},{8,7},{9,10},{10,... | collective-permute-start | bytes 3108872 | tf_op jit(solution)/shard_map/ppermute | solution.py:906
  23.7 28.5 %collective-permute-start = (f32[512,128]{1,0:T(8,128)S(1)}, f32[512,128]{1,0:T(8,128)S(1)}, u32[]{:S(2)}, u32[]{:S(2)}) collective-permute-start(f32[512,128]{1,0:T(8,128)S(1)} %bitcast.27), channel_id=1, source_target_pairs={{0,64},{64,0},{1,65},{65,1},{2,66},{66,2},{3,67},{67,3},{4,68},{68... | collective-permute-start | bytes 786440 | tf_op jit(solution)/shard_map/ppermute | solution.py:926
  77.0 5.0 %collective-permute-start.3 = (f32[256,128]{1,0:T(8,128)S(1)}, f32[256,128]{1,0:T(8,128)S(1)}, u32[]{:S(2)}, u32[]{:S(2)}) collective-permute-start(f32[256,128]{1,0:T(8,128)S(1)} %get-tuple-element.55), channel_id=1, source_target_pairs={{0,1},{1,0},{2,3},{3,2},{4,5},{5,4},{6,7},{7,6},{8,9},{9,8},{10,11... | collective-permute-start | bytes 393224 | tf_op jit(solution)/shard_map/ppermute | solution.py:906
  77.6 10.4 %collective-permute-start.4 = (f32[256,128]{1,0:T(8,128)S(1)}, f32[256,128]{1,0:T(8,128)S(1)}, u32[]{:S(2)}, u32[]{:S(2)}) collective-permute-start(f32[256,128]{1,0:T(8,128)S(1)} %get-tuple-element.56), channel_id=1, source_target_pairs={{0,63},{1,2},{2,1},{3,4},{4,3},{5,6},{6,5},{7,8},{8,7},{9,10},{10,... | collective-permute-start | bytes 393224 | tf_op jit(solution)/shard_map/ppermute | solution.py:906
  90.6 19.5 %collective-permute-start.5 = (f32[256,128]{1,0:T(8,128)S(1)}, f32[256,128]{1,0:T(8,128)S(1)}, u32[]{:S(2)}, u32[]{:S(2)}) collective-permute-start(f32[256,128]{1,0:T(8,128)S(1)} %get-tuple-element.68), channel_id=1, source_target_pairs={{0,1},{1,0},{2,3},{3,2},{4,5},{5,4},{6,7},{7,6},{8,9},{9,8},{10,11... | collective-permute-start | bytes 393224 | tf_op jit(solution)/shard_map/ppermute | solution.py:906
  90.7 19.4 %collective-permute-start.6 = (f32[256,128]{1,0:T(8,128)S(1)}, f32[256,128]{1,0:T(8,128)S(1)}, u32[]{:S(2)}, u32[]{:S(2)}) collective-permute-start(f32[256,128]{1,0:T(8,128)S(1)} %get-tuple-element.69), channel_id=1, source_target_pairs={{0,63},{1,2},{2,1},{3,4},{4,3},{5,6},{6,5},{7,8},{8,7},{9,10},{10,... | collective-permute-start | bytes 393224 | tf_op jit(solution)/shard_map/ppermute | solution.py:906
  113.7 5.0 %collective-permute-start.7 = (f32[256,128]{1,0:T(8,128)S(1)}, f32[256,128]{1,0:T(8,128)S(1)}, u32[]{:S(2)}, u32[]{:S(2)}) collective-permute-start(f32[256,128]{1,0:T(8,128)S(1)} %get-tuple-element.75), channel_id=1, source_target_pairs={{0,1},{1,0},{2,3},{3,2},{4,5},{5,4},{6,7},{7,6},{8,9},{9,8},{10,11... | collective-permute-start | bytes 393224 | tf_op jit(solution)/shard_map/ppermute | solution.py:906
  114.3 10.4 %collective-permute-start.8 = (f32[256,128]{1,0:T(8,128)S(1)}, f32[256,128]{1,0:T(8,128)S(1)}, u32[]{:S(2)}, u32[]{:S(2)}) collective-permute-start(f32[256,128]{1,0:T(8,128)S(1)} %get-tuple-element.76), channel_id=1, source_target_pairs={{0,63},{1,2},{2,1},{3,4},{4,3},{5,6},{6,5},{7,8},{8,7},{9,10},{10,... | collective-permute-start | bytes 393224 | tf_op jit(solution)/shard_map/ppermute | solution.py:906

commit v4 on v2

--- a/solution.py
+++ b/solution.py
@@ -94,7 +94,9 @@
     return lax.broadcasted_iota(jnp.int32, shape, axis)
 
 
-def build_requests(owner_ref, slot_ref, weight_ref, send_ref, rank_ref):
+def request_kernel(
+    owner_ref, slot_ref, weight_ref, ids_ref, live_ref, send_ref, points_ref
+):
     owner = owner_ref[...]
     hits = iota((OWNERS, R_DEV), 0) == owner
     hits_f = hits.astype(f32)
@@ -109,7 +111,13 @@
         ranks.append(jnp.sum(block * count, axis=0, keepdims=True))
         carry = carry + jnp.sum(block, axis=1, keepdims=True)
     rank = jnp.concatenate(ranks, axis=1)
-    rank_ref[...] = rank
+    ids = ids_ref[...]
+    live = iota((1, R_DEV), 1) < live_ref[0, 0]
+    points_ref[0:1] = owner
+    points_ref[1:2] = rank.astype(jnp.int32) + jnp.where(rank >= float(HALF), 16 - HALF, 0)
+    points_ref[2:3] = jnp.where(live, lax.shift_right_logical(ids, 7), -1)
+    points_ref[3:4] = jnp.bitwise_and(ids, 127)
+    points_ref[4:8] = jnp.zeros((4, R_DEV), jnp.int32)
     payload = jnp.concatenate(
         [
             weight_ref[...],
@@ -271,13 +279,13 @@
     return iota(shape, 1) < LAYER
 
 
-def pack(field, a_ref, b_ref, row, even):
-    low, high = field[0:256], field[256:512]
-    first = first_layer(low.shape)
-    up = jnp.where(first, pltpu.roll(low, LAYER, 1), high)
-    down = jnp.where(first, low, pltpu.roll(high, LAYER, 1))
-    a_ref[row : row + 256] = jnp.where(even, up, down)
-    b_ref[row : row + 256] = jnp.where(even, down, up)
+def pack(up, down, a_ref, b_ref, row, even):
+    half = up.shape[0] // 2
+    first = first_layer((half, 128))
+    up = jnp.where(first, pltpu.roll(up[:half], LAYER, 1), up[half:])
+    down = jnp.where(first, down[:half], pltpu.roll(down[half:], LAYER, 1))
+    a_ref[row : row + half] = jnp.where(even, up, down)
+    b_ref[row : row + half] = jnp.where(even, down, up)
 
 
 def beside(a, b, place):
@@ -287,11 +295,12 @@
     return below, above
 
 
-def unpack(a_ref, b_ref, row, place, out_ref):
-    below, above = beside(a_ref[row : row + 256], b_ref[row : row + 256], place)
+def unpack(a_ref, b_ref, row, half, place):
+    below, above = beside(a_ref[row : row + half], b_ref[row : row + half], place)
     first = first_layer(below.shape)
-    out_ref[0:256] = jnp.where(first, above, pltpu.roll(below, LAYER, 1))
-    out_ref[256:512] = jnp.where(first, pltpu.roll(above, LAYER, 1), below)
+    low = jnp.where(first, above, pltpu.roll(below, LAYER, 1))
+    high = jnp.where(first, pltpu.roll(above, LAYER, 1), below)
+    return jnp.concatenate([low, high], axis=0)
 
 
 def mirror(ghost_ref, bottom, top):
@@ -385,26 +394,26 @@
     lax.fori_loop(0, 8, per_j, 0)
 
 
-BASIS_ROW = 704
+THIRD_ROW = 256
+PLANE_ROW = THIRD_ROW + 256
+BASIS_ROW = PLANE_ROW + 128
 GHOST_ROWS = BASIS_ROW + 256
 
 
-def prepare_kernel(
-    owner_ref,
-    slot_ref,
-    weight_ref,
+def setup_kernel(
     order_ref,
     stiff_hbm,
     mass_hbm,
     field_hbm,
+    load_hbm,
     basis_hbm,
     inverse_hbm,
-    send_ref,
-    rank_ref,
     coef_ref,
     mass_ref,
     start_ref,
+    static_ref,
     diag_ref,
+    invd_ref,
     inv_ref,
     basis_ref,
     solve_ref,
@@ -413,6 +422,7 @@
     stiff_in,
     mass_in,
     field_in,
+    load_in,
     basis_in,
     inverse_in,
     tmp_ref,
@@ -425,6 +435,7 @@
                 (stiff_hbm, stiff_in),
                 (mass_hbm, mass_in),
                 (field_hbm, field_in),
+                (load_hbm, load_in),
                 (basis_hbm, basis_in),
                 (inverse_hbm, inverse_in),
             ]
@@ -432,14 +443,12 @@
     ]
     for copy in copies:
         copy.start()
-    build_requests(owner_ref, slot_ref, weight_ref, send_ref, rank_ref)
     order = order_ref[...]
     match = (iota((128, 128), 0) == order).astype(f32)
     inv = jnp.sum(match.T * iota((128, 128), 0).astype(f32), axis=0, keepdims=True)
     inv = inv.astype(jnp.int32)
     inv_ref[...] = inv
-    for copy in copies:
-        copy.wait()
+    copies[0].wait()
     tmp_ref[...] = take_lanes(stiff_in[0:512, :], inv)
     for k in range(8):
         for i in range(8):
@@ -447,68 +456,85 @@
                 pl.ds(k * 64 + i, 8, stride=8), :
             ]
     coef_ref[512:1536, :] = take_lanes(stiff_in[512:1536, :], inv)
+    for copy in copies[1:]:
+        copy.wait()
     mass_ref[...] = take_lanes(mass_in[...], inv)
     start_ref[...] = take_lanes(field_in[...], inv)
+    stiff_apply(start_ref, coef_ref, mass_ref, static_ref)
+    static_ref[...] = take_lanes(load_in[...], inv) - static_ref[...]
+    in_plane(static_ref)
     basis = dot_nn(match, basis_in[...], exact_mode)
     basis_ref[...] = basis
     solve_ref[...] = dot_nn(basis, inverse_in[...], exact_mode)
     local_diagonal(coef_ref, mass_ref, diag_ref)
     in_plane(diag_ref)
+    zeros = jnp.zeros((64, 128), f32)
+    invd_ref[...] = 1.0 / coupled(diag_ref, zeros, zeros)
     even = where_am_i()[0]
-    zeros = jnp.zeros((64, 128), f32)
-    pack(coef_ref[1024:1536, :], a_ref, b_ref, 0, even)
-    pack(coupled(diag_ref, zeros, zeros), a_ref, b_ref, 256, even)
-    rows = [
-        (coef_ref[448:512], coef_ref[0:64]),
-        (coef_ref[960:1024], coef_ref[512:576]),
-        (mass_ref[448:512], mass_ref[0:64]),
-    ]
+    third = coef_ref[1024:1536, :]
+    pack(third, third, a_ref, b_ref, THIRD_ROW, even)
+    tops = [coef_ref[448:512], coef_ref[960:1024], mass_ref[448:512], diag_ref[448:512]]
+    bottoms = [coef_ref[0:64], coef_ref[512:576], mass_ref[0:64], diag_ref[0:64]]
+    pack(
+        jnp.concatenate(tops, axis=0),
+        jnp.concatenate(bottoms, axis=0),
+        a_ref,
+        b_ref,
+        PLANE_ROW,
+        even,
+    )
     for c in range(NC // 128):
-        cols = slice(c * 128, c * 128 + 128)
-        rows.append((basis[LAYER:, cols], basis[:LAYER, cols]))
-    for n, (up, down) in enumerate(rows):
-        at = 512 + n * 64
+        at = BASIS_ROW + c * 64
+        up = basis[LAYER:, c * 128 : c * 128 + 128]
+        down = basis[:LAYER, c * 128 : c * 128 + 128]
         a_ref[at : at + 64] = jnp.where(even, up, down)
         b_ref[at : at + 64] = jnp.where(even, down, up)
+    a_ref[0:THIRD_ROW] = jnp.zeros((THIRD_ROW, 128), f32)
+    b_ref[0:THIRD_ROW] = jnp.zeros((THIRD_ROW, 128), f32)
+
+
+def send_first(y_ref, base, invd, a_ref, b_ref):
+    zeros = jnp.zeros((64, 128), f32)
+    inner = coupled(y_ref, zeros, zeros)
+    if base is not None:
+        inner = inner + base
+    inner = inner * invd * STEPS[0][1]
+    out = message(
+        y_ref[0:64], y_ref[448:512], inner[0:64], inner[64:448], inner[448:512]
+    )
+    pack(out, out, a_ref, b_ref, 0, where_am_i()[0])
 
 
 def source_kernel(
     ret_ref,
-    owner_ref,
-    rank_ref,
-    ids_ref,
-    live_ref,
-    load_ref,
+    points_ref,
     inv_ref,
-    start_ref,
-    coef_ref,
-    mass_ref,
-    out_ref,
+    static_ref,
+    invd_ref,
+    a_in_ref,
+    b_in_ref,
+    y_ref,
     a_ref,
     b_ref,
 ):
-    hits = (iota((OWNERS, R_DEV), 0) == owner_ref[...]).astype(f32)
+    owner, place = points_ref[0:1], points_ref[1:2]
+    node, elem = points_ref[2:3], points_ref[3:4]
+    hits = (iota((OWNERS, R_DEV), 0) == owner).astype(f32)
     picked = dot_nn(ret_ref[...].T, hits, exact_mode)[0:32]
-    rank = rank_ref[...].astype(jnp.int32)
-    place = rank + jnp.where(rank >= HALF, 16 - HALF, 0)
     value = jnp.sum(
         jnp.where(iota((32, R_DEV), 0) == place, picked, 0.0), axis=0, keepdims=True
     )
-    value = jnp.where(iota((1, R_DEV), 1) < live_ref[0, 0], value, 0.0)
-    ids = ids_ref[...]
-    node = lax.shift_right_logical(ids, 7)
-    elem = jnp.bitwise_and(ids, 127)
     at_node = (iota((NODES, R_DEV), 0) == node).astype(f32).astype(bf16)
     at_elem = (iota((128, R_DEV), 0) == elem).astype(f32).astype(bf16)
     spread = jnp.concatenate([at_elem * piece for piece in split3(value)], axis=0)
     landed = dot_nt(at_node, spread)
-    source = load_ref[...] + (landed[:, 0:128] + landed[:, 128:256] + landed[:, 256:384])
-    source = take_lanes(source, inv_ref[...])
-    stiff_apply(start_ref, coef_ref, mass_ref, out_ref)
-    out_ref[...] = source - out_ref[...]
-    in_plane(out_ref)
-    zeros = jnp.zeros((64, 128), f32)
-    pack(coupled(out_ref, zeros, zeros), a_ref, b_ref, 0, where_am_i()[0])
+    landed = landed[:, 0:128] + landed[:, 128:256] + landed[:, 256:384]
+    y_ref[...] = take_lanes(landed, inv_ref[...])
+    in_plane(y_ref)
+    y_ref[...] = y_ref[...] + static_ref[...]
+    send_first(y_ref, None, invd_ref[...], a_ref, b_ref)
+    a_ref[THIRD_ROW:] = a_in_ref[THIRD_ROW:]
+    b_ref[THIRD_ROW:] = b_in_ref[THIRD_ROW:]
 
 
 def opening_half(
@@ -520,7 +546,6 @@
     b_ref,
     invd_ref,
     third_ref,
-    ginvd_ref,
     planes_ref,
     coef_ref,
     mass_ref,
@@ -534,15 +559,14 @@
     face_ref,
     side_ref,
 ):
-    unpack(a_ref, b_ref, 0, place, ghost_ref)
+    ghost_ref[...] = unpack(a_ref, b_ref, 0, 256, place)
     residual = coupled(y_ref, ghost_ref[448:512], ghost_ref[0:64])
     if base_ref is not None:
         residual = residual + base_ref[...]
-    mirror(ghost_ref, residual[0:64], residual[448:512])
     invd = invd_ref[...]
     update = residual * invd * STEPS[0][1]
     upd_ref[...] = update
-    ghost_ref[...] = ghost_ref[...] * ginvd_ref[...] * STEPS[0][1]
+    mirror(ghost_ref, update[0:64], update[448:512])
     stiff_apply(upd_ref, coef_ref, mass_ref, w_ref)
     in_plane(w_ref)
     ghost_apply(ghost_ref, third_ref, planes_ref, face_ref, side_ref)
@@ -559,23 +583,19 @@
     inner = alpha * upd_ref[...] + beta * invd_ref[...] * (
         res_ref[...] - coupled(w_ref, zeros, zeros)
     )
-    pack(
-        message(w_ref[0:64], w_ref[448:512], inner[0:64], inner[64:448], inner[448:512]),
-        a_out_ref,
-        b_out_ref,
-        0,
-        place[0],
-    )
+    out = message(
+        w_ref[0:64], w_ref[448:512], inner[0:64], inner[64:448], inner[448:512]
+    )
+    pack(out, out, a_out_ref, b_out_ref, 0, place[0])
 
 
 def start_kernel(
     y_ref,
     diag_ref,
+    invd_in_ref,
     cur_in_ref,
     a_ref,
     b_ref,
-    ga_ref,
-    gb_ref,
     coef_ref,
     mass_ref,
     res_ref,
@@ -586,25 +606,21 @@
     b_out_ref,
     invd_ref,
     third_ref,
-    ginvd_ref,
     planes_ref,
     outer_ref,
     *scratch,
 ):
     place = where_am_i()
-    unpack(ga_ref, gb_ref, 0, place, third_ref)
-    unpack(ga_ref, gb_ref, 256, place, ginvd_ref)
-    diag = coupled(diag_ref, ginvd_ref[448:512], ginvd_ref[0:64])
-    mirror(ginvd_ref, diag[0:64], diag[448:512])
-    invd_ref[...] = 1.0 / diag
-    gdiag = ginvd_ref[...]
-    there = gdiag > 0.0
-    ginvd_ref[...] = jnp.where(there, 1.0 / jnp.where(there, gdiag, 1.0), 0.0)
-    below, above = beside(ga_ref[512:704], gb_ref[512:704], place)
-    planes_ref[...] = jnp.where(first_layer(below.shape), above, below)
+    third_ref[...] = unpack(a_ref, b_ref, THIRD_ROW, 256, place)
+    planes = unpack(a_ref, b_ref, PLANE_ROW, 128, place)
+    planes_ref[...] = planes[0:192]
+    bottom, top = through(
+        diag_ref[0:64], diag_ref[448:512], planes[192:256], planes[192:256]
+    )
+    invd_ref[...] = whole(1.0 / bottom, invd_in_ref, 1.0 / top)
     for c in range(NC // 128):
         at = BASIS_ROW + c * 64
-        below, above = beside(ga_ref[at : at + 64], gb_ref[at : at + 64], place)
+        below, above = beside(a_ref[at : at + 64], b_ref[at : at + 64], place)
         outer_ref[0:64, c * 128 : c * 128 + 128] = below
         outer_ref[64:128, c * 128 : c * 128 + 128] = above
     opening_half(
@@ -616,7 +632,6 @@
         b_ref,
         invd_ref,
         third_ref,
-        ginvd_ref,
         planes_ref,
         coef_ref,
         mass_ref,
@@ -652,7 +667,7 @@
     face_ref,
     side_ref,
 ):
-    unpack(a_ref, b_ref, 0, where_am_i(), ghost_ref)
+    ghost_ref[...] = unpack(a_ref, b_ref, 0, 256, where_am_i())
     residual = res_ref[...] - coupled(w_ref, ghost_ref[448:512], ghost_ref[0:64])
     alpha, beta = STEPS[2]
     third = alpha * upd_ref[...] + beta * invd_ref[...] * residual
@@ -731,6 +746,7 @@
     w_ref,
     base_ref,
     cur_in_ref,
+    invd_ref,
     y_ref,
     cur_ref,
     a_ref,
@@ -750,15 +766,7 @@
     y_ref[...] = mass_ref[...] * correction
     in_plane(y_ref)
     y_ref[...] = -(y_ref[...] + w_ref[...])
-    zeros = jnp.zeros((64, 128), f32)
-    inner = base_ref[...] + coupled(y_ref, zeros, zeros)
-    pack(
-        message(y_ref[0:64], y_ref[448:512], inner[0:64], inner[64:448], inner[448:512]),
-        a_ref,
-        b_ref,
-        0,
-        where_am_i()[0],
-    )
+    send_first(y_ref, base_ref[...], invd_ref[...], a_ref, b_ref)
 
 
 def last_kernel(*refs):
@@ -767,11 +775,14 @@
     out_ref[...] = take_lanes(current, order_ref[...])
 
 
-def call(kernel, name, outs, *args, scratch=(), smem=(), far=(), copies=0):
+def call(kernel, name, outs, *args, scratch=(), smem=(), far=(), near=(), copies=0):
+    def stay(x):
+        return pltpu.with_memory_space_constraint(x, pltpu.HBM)
+
     def space(n):
         if n in smem:
             return pltpu.SMEM
-        return pl.ANY if n in far else pltpu.VMEM
+        return pltpu.HBM if n in far else pltpu.VMEM
 
     scratches = [pltpu.VMEM(s, f32) for s in scratch]
     if copies:
@@ -784,7 +795,7 @@
         out_specs=[pl.BlockSpec(memory_space=pltpu.VMEM) for _ in outs],
         scratch_shapes=scratches,
         compiler_params=pltpu.CompilerParams(vmem_limit_bytes=20 << 20),
-    )(*args)
+    )(*[stay(x) if n in far + near else x for n, x in enumerate(args)])
 
 
 FIELD = ((NODES, 128), f32)
@@ -795,9 +806,15 @@
 
 def exchange(a, b):
     count = lax.axis_size("elem")
-    pairs_a = [(i, i ^ 1) for i in range(count)]
-    pairs_b = [(i, (i + (1 if i % 2 else -1)) % count) for i in range(count)]
-    return lax.ppermute(a, "elem", pairs_a), lax.ppermute(b, "elem", pairs_b)
+    pairs_a, pairs_b = [], []
+    for d in range(2 * count):
+        base, slab = d - d % count, d % count
+        pairs_a.append((d, base + (slab ^ 1)))
+        other = slab + (1 if slab % 2 else -1)
+        inside = 0 <= other < count
+        pairs_b.append((d, base + other if inside else (d + count) % (2 * count)))
+    axes = ("sess", "elem")
+    return lax.ppermute(a, axes, pairs_a), lax.ppermute(b, axes, pairs_b)
 
 
 def per_device(
@@ -819,13 +836,28 @@
     owner = donor_owner.reshape(1, R_DEV)
     other_field = lax.ppermute(own_field, "sess", [(0, 1), (1, 0)])
 
-    send, rank, coef, mass, start, diag, inv, basis, solve, ghost_a, ghost_b = call(
-        prepare_kernel,
-        "prepare",
+    send, points = call(
+        request_kernel,
+        "request",
+        [((OWNERS * ASK, 128), f32), ((8, R_DEV), jnp.int32)],
+        owner,
+        donor_slot,
+        interp_weights.reshape(3 * NP, R_DEV),
+        recv_ids,
+        live_count,
+        smem=(4,),
+        near=(0, 1, 2, 3),
+    )
+    received = lax.all_to_all(
+        send.reshape(OWNERS, ASK, 128), "elem", split_axis=0, concat_axis=0, tiled=True
+    )
+    coef, mass, start, static, diag, invd, inv, basis, solve, ga, gb = call(
+        setup_kernel,
+        "setup",
         [
-            ((OWNERS * ASK, 128), f32),
-            ((1, R_DEV), f32),
             ((3 * NODES, 128), f32),
+            FIELD,
+            FIELD,
             FIELD,
             FIELD,
             FIELD,
@@ -835,29 +867,25 @@
             GHOST_MSG,
             GHOST_MSG,
         ],
-        owner,
-        donor_slot,
-        interp_weights.reshape(3 * NP, R_DEV),
         order,
         stiffness.reshape(3 * NODES, 128),
         helm_mass.reshape(NODES, 128),
         own_field,
+        load.reshape(NODES, 128),
         coarse_basis.reshape(128, NC),
         coarse_inverse.reshape(NC, NC),
-        far=(4, 5, 6, 7, 8),
+        near=(0,),
+        far=(1, 2, 3, 4, 5, 6),
         scratch=[
             (3 * NODES, 128),
+            (NODES, 128),
             (NODES, 128),
             (NODES, 128),
             (128, NC),
             (NC, NC),
             (NODES, 128),
         ],
-        copies=5,
-    )
-    ghost_a, ghost_b = exchange(ghost_a, ghost_b)
-    received = lax.all_to_all(
-        send.reshape(OWNERS, ASK, 128), "elem", split_axis=0, concat_axis=0, tiled=True
+        copies=6,
     )
     (answer,) = call(
         owner_kernel,
@@ -870,32 +898,27 @@
     y, a, b = call(
         source_kernel,
         "source",
-        [FIELD, LAYER_MSG, LAYER_MSG],
+        [FIELD, GHOST_MSG, GHOST_MSG],
         answered,
-        owner,
-        rank,
-        recv_ids,
-        live_count,
-        load.reshape(NODES, 128),
+        points,
         inv,
-        start,
-        coef,
-        mass,
-        smem=(4,),
+        static,
+        invd,
+        ga,
+        gb,
     )
     a, b = exchange(a, b)
     half = [FIELD, FIELD, FIELD, FIELD, LAYER_MSG, LAYER_MSG]
-    res, upd, cur, w, a, b, invd, third, ginvd, planes, outer = call(
+    res, upd, cur, w, a, b, invd, third, planes, outer = call(
         start_kernel,
         "start",
-        half + [FIELD, FIELD, FIELD, ((192, 128), f32), ((128, NC), f32)],
+        half + [FIELD, FIELD, ((192, 128), f32), ((128, NC), f32)],
         y,
         diag,
+        invd,
         start,
         a,
         b,
-        ghost_a,
-        ghost_b,
         coef,
         mass,
         scratch=GHOST_WORK,
@@ -937,6 +960,7 @@
         w,
         res,
         cur,
+        invd,
     )
     a, b = exchange(a, b)
     res, upd, cur, w, a, b = call(
@@ -950,7 +974,6 @@
         b,
         invd,
         third,
-        ginvd,
         planes,
         coef,
         mass,

time: 129 us -> 117 us (0.907)
  the two profiles are of different devices: /device:TPU:0 before, /device:TPU:6 now
where the time goes in v4:
time: 117 us; the launch traced here: 115 us
  blocking collectives  36.8 us (31%)
  waiting for transfers between devices  33 us (28%)
  Pallas kernels  22.6 us (19%)
  starting transfers between devices  20.3 us (17%)
  local copies, waits for them, and re-layouts  2.01 us (2%)
    ppermute x8, waiting for transfers between devices, exchange(): return (lax.ppermute(a, axes, pairs_a), lax.ppermute(b, axes, pairs_b))  30.6 us
    pallas_call x9, Pallas kernels, call(): pl.pallas_call(kernel, name=name, out_shape=[jax.ShapeDtypeStruct(s, d) f...  22.6 us
    all_to_all x1, blocking collectives, per_device(): lax.all_to_all(send.reshape(OWNERS, ASK, 128), 'elem', split_axis=0, conc...  20.6 us
    all_to_all x1, blocking collectives, per_device(): lax.all_to_all(part.reshape(OWNERS, NC // 128, 128), 'elem', split_axis=0...  16.2 us
    ppermute x8, starting transfers between devices, exchange(): return (lax.ppermute(a, axes, pairs_a), lax.ppermute(b, axes, pairs_b))  13 us
    all_to_all x1, starting transfers between devices, per_device(): lax.all_to_all(answer, 'elem', split_axis=0, concat_axis=0, tiled=True)  7.26 us
    all_to_all x1, waiting for transfers between devices, per_device(): lax.all_to_all(answer, 'elem', split_axis=0, concat_axis=0, tiled=True)  2.38 us
  transfers between devices with their start and end apart: 10, of which 9 were waited for; matrix products, arithmetic and copies ran while one was open for 0% of the time, Pallas kernels for 7%

profile of v4, /device:TPU:6, one launch (start us, length us, event | category | flops | bytes accessed | tf_op | source)
XLA Modules:
  0.0 115.4 jit_solution(11843643677000359946)
XLA Ops:
  0.7 2.6 %request.1 = (f32[512,128]{1,0:T(8,128)S(1)}, s32[8,1024]{1,0:T(8,128)S(1)}) custom-call(s32[1,1024]{1,0:T(1,128)} %bitcast.32, s32[1,1024]{1,0:T(1,128)} %slot_ref.1, f32[24,1024]{1,0:T(8,128)} %bitcast.31, s32[1,1024]{1,0:T(1,128)} %ids_ref.1, s32[1,1]{1,0:T(1,128)S(6)} %copy.14.live_ref), custom_call_target="tpu_custom_call" | custom-call | tf_op jit(solution)/shard_map/request/pallas_call | solution.py:790
  3.9 20.6 %all_to_all.21 = f32[64,8,128]{2,1,0:T(8,128)S(1)} all-to-all(f32[64,8,128]{2,1,0:T(8,128)S(1)} %bitcast.20), channel_id=1, replica_groups=mesh['sess'=2,'elem'=64] {'elem'}, dimensions={0} | all-to-all | bytes 524288 | tf_op jit(solution)/shard_map/all_to_all | solution.py:851
  24.4 1.9 %owner.1 = f32[64,128]{1,0:T(8,128)} custom-call(f32[512,128]{1,0:T(8,128)S(1)} %bitcast.18, f32[512,128]{1,0:T(8,128)S(1)} %collective-permute-done.field_ref), custom_call_target="tpu_custom_call" | custom-call | tf_op jit(solution)/shard_map/owner/pallas_call | solution.py:790
  26.3 7.3 %all-to-all-start.1 = ((f32[64,1,128]{2,1,0:T(1,128)}), f32[64,1,128]{2,1,0:T(1,128)}, u32[]{:S(2)}, u32[]{:S(2)}) async-start(f32[64,1,128]{2,1,0:T(1,128)} %bitcast.6), calls=%async_computation.1 | async-start | bytes 65536 | tf_op jit(solution)/shard_map/all_to_all | solution.py:897
  33.6 5.2 %setup.1 = (f32[1536,128]{1,0:T(8,128)S(1)}, f32[512,128]{1,0:T(8,128)S(1)}, f32[512,128]{1,0:T(8,128)S(1)}, f32[512,128]{1,0:T(8,128)S(1)}, f32[512,128]{1,0:T(...) custom-call(s32[1,128]{1,0:T(1,128)} %bitcast.22, ...), custom_call_target="tpu_custom_call" | custom-call | tf_op jit(solution)/shard_map/setup/pallas_call | solution.py:790
  38.7 2.4 %all-to-all-done.1 = f32[64,1,128]{2,1,0:T(1,128)} async-done(((f32[64,1,128]{2,1,0:T(1,128)}), f32[64,1,128]{2,1,0:T(1,128)}, u32[]{:S(2)}, u32[]{:S(2)}) %all-to-all-start.1) | async-done | bytes 32800 | tf_op jit(solution)/shard_map/all_to_all | solution.py:897
  41.9 2.5 %source.1 = (f32[512,128]{1,0:T(8,128)S(1)}, f32[896,128]{1,0:T(8,128)S(1)}, f32[896,128]{1,0:T(8,128)S(1)}) custom-call(f32[64,128]{1,0:T(8,128)} %bitcast.7.ret_ref, s32[8,1024]{1,0:T(8,128)S(1)} %copy-done.1, s32[1,128]{1,0:T(1,128)S(1)} %get-tuple-element.47.inv_ref, f32[512,128]{1,0:T(8,128)S(1)} %get-tuple-element.48.static_ref, ...), custom_call_target="tpu_custom_call" | custom-call | tf_op jit(solution)/shard_map/source/pallas_call | solution.py:790
  44.9 3.1 %collective-permute-start.2 = (f32[896,128]{1,0:T(8,128)S(1)}, f32[896,128]{1,0:T(8,128)S(1)}, u32[]{:S(2)}, u32[]{:S(2)}) collective-permute-start(f32[896,128]{1,0:T(8,128)S(1)} %get-tuple-element.56), channel_id=1, source_target_pairs={{0,64},{1,2},{2,1},{3,4},{4,3},{5,6},{6,5},{7,8},{8,7},{9,10},{10,... | collective-permute-start | bytes 1376264 | tf_op jit(solution)/shard_map/ppermute | solution.py:817
  48.0 6.7 %collective-permute-done.1.a_ref = f32[896,128]{1,0:T(8,128)S(1)} collective-permute-done((f32[896,128]{1,0:T(8,128)S(1)}, f32[896,128]{1,0:T(8,128)S(1)}, u32[]{:S(2)}, u32[]{:S(2)}) %collective-permute-start.1) | collective-permute-done | bytes 458784 | tf_op jit(solution)/shard_map/ppermute | solution.py:817
  54.7 4.7 %collective-permute-done.2.b_ref = f32[896,128]{1,0:T(8,128)S(1)} collective-permute-done((f32[896,128]{1,0:T(8,128)S(1)}, f32[896,128]{1,0:T(8,128)S(1)}, u32[]{:S(2)}, u32[]{:S(2)}) %collective-permute-start.2) | collective-permute-done | bytes 458784 | tf_op jit(solution)/shard_map/ppermute | solution.py:817
  59.4 2.5 %start.1 = (f32[512,128]{1,0:T(8,128)S(1)}, f32[512,128]{1,0:T(8,128)S(1)}, f32[512,128]{1,0:T(8,128)S(1)}, f32[512,128]{1,0:T(8,128)S(1)}, f32[256,128]{1,0:T(8...) custom-call(f32[512,128]{1,0:T(8,128)S(1)} %get-tuple-element.52.y_r, ...), custom_call_target="tpu_custom_call" | custom-call | tf_op jit(solution)/shard_map/start/pallas_call | solution.py:790
  61.9 3.9 %collective-permute-start.4 = (f32[256,128]{1,0:T(8,128)S(1)}, f32[256,128]{1,0:T(8,128)S(1)}, u32[]{:S(2)}, u32[]{:S(2)}) collective-permute-start(f32[256,128]{1,0:T(8,128)S(1)} %get-tuple-element.65), channel_id=1, source_target_pairs={{0,64},{1,2},{2,1},{3,4},{4,3},{5,6},{6,5},{7,8},{8,7},{9,10},{10,... | collective-permute-start | bytes 393224 | tf_op jit(solution)/shard_map/ppermute | solution.py:817
  65.9 1.0 collective-permute-done.3.a_ref
  66.9 4.3 %collective-permute-done.4.b_ref = f32[256,128]{1,0:T(8,128)S(1)} collective-permute-done((f32[256,128]{1,0:T(8,128)S(1)}, f32[256,128]{1,0:T(8,128)S(1)}, u32[]{:S(2)}, u32[]{:S(2)}) %collective-permute-start.4) | collective-permute-done | bytes 131104 | tf_op jit(solution)/shard_map/ppermute | solution.py:817
  71.2 2.6 %middle.1 = (f32[512,128]{1,0:T(8,128)S(1)}, f32[512,128]{1,0:T(8,128)S(1)}, f32[512,128]{1,0:T(8,128)S(1)}, f32[256,128]{1,0:T(8,128)S(1)}) custom-call(f32[512,128]{1,0:T(8,128)S(1)} %get-tuple-element.59.w_ref, f32[512,128]{1,0:T(8,128)S(1)} %get-tuple-element.60.res_in_ref, f32[512,128]{1,0:T(8,128)S(1)} %get-tuple-element.61.upd_ref, ...), custom_call_target="tpu_custom_call" | custom-call | tf_op jit(solution)/shard_map/middle/pallas_call | solution.py:790
  73.9 16.2 %all_to_all.22 = f32[64,4,128]{2,1,0:T(4,128)S(1)} all-to-all(f32[64,4,128]{2,1,0:T(4,128)S(1)} %bitcast.21), channel_id=1, replica_groups=mesh['sess'=2,'elem'=64] {'elem'}, dimensions={0} | all-to-all | bytes 262144 | tf_op jit(solution)/shard_map/all_to_all | solution.py:946
  91.8 2.2 %collective-permute-start.6 = (f32[256,128]{1,0:T(8,128)S(1)}, f32[256,128]{1,0:T(8,128)S(1)}, u32[]{:S(2)}, u32[]{:S(2)}) collective-permute-start(f32[256,128]{1,0:T(8,128)S(1)} %get-tuple-element.78), channel_id=1, source_target_pairs={{0,64},{1,2},{2,1},{3,4},{4,3},{5,6},{6,5},{7,8},{8,7},{9,10},{10,... | collective-permute-start | bytes 393224 | tf_op jit(solution)/shard_map/ppermute | solution.py:817
  94.0 2.2 %collective-permute-done.5.refs_3_ = f32[256,128]{1,0:T(8,128)S(1)} collective-permute-done((f32[256,128]{1,0:T(8,128)S(1)}, f32[256,128]{1,0:T(8,128)S(1)}, u32[]{:S(2)}, u32[]{:S(2)}) %collective-permute-start.5) | collective-permute-done | bytes 131104 | tf_op jit(solution)/shard_map/ppermute | solution.py:817
  96.2 4.8 %collective-permute-done.6.refs_4_ = f32[256,128]{1,0:T(8,128)S(1)} collective-permute-done((f32[256,128]{1,0:T(8,128)S(1)}, f32[256,128]{1,0:T(8,128)S(1)}, u32[]{:S(2)}, u32[]{:S(2)}) %collective-permute-start.6) | collective-permute-done | bytes 131104 | tf_op jit(solution)/shard_map/ppermute | solution.py:817
  101.0 2.3 %again.1 = (f32[512,128]{1,0:T(8,128)S(1)}, f32[512,128]{1,0:T(8,128)S(1)}, f32[512,128]{1,0:T(8,128)S(1)}, f32[512,128]{1,0:T(8,128)S(1)}, f32[256,128]{1,0:T(8,128)S(1)}, /*index=5*/f32[256,128]{1,0:T(8,128)S(1)}) custom-call(f32[512,128]{1,0:T(8,128)S(1)} %get-tuple-element.70.base_ref.refs_0_, f32[512,128]{1,0:T(8,128)S(1)} %get-tuple-element.75.refs_1_, ...), custom_call_target="tpu_custom_call" | custom-call | tf_op jit(solution)/shard_map/again/pallas_call | solution.py:790
  103.3 2.3 %collective-permute-start.8 = (f32[256,128]{1,0:T(8,128)S(1)}, f32[256,128]{1,0:T(8,128)S(1)}, u32[]{:S(2)}, u32[]{:S(2)}) collective-permute-start(f32[256,128]{1,0:T(8,128)S(1)} %get-tuple-element.84), channel_id=1, source_target_pairs={{0,64},{1,2},{2,1},{3,4},{4,3},{5,6},{6,5},{7,8},{8,7},{9,10},{10,... | collective-permute-start | bytes 393224 | tf_op jit(solution)/shard_map/ppermute | solution.py:817
  105.7 2.6 %collective-permute-done.7.refs_5_ = f32[256,128]{1,0:T(8,128)S(1)} collective-permute-done((f32[256,128]{1,0:T(8,128)S(1)}, f32[256,128]{1,0:T(8,128)S(1)}, u32[]{:S(2)}, u32[]{:S(2)}) %collective-permute-start.7) | collective-permute-done | bytes 131104 | tf_op jit(solution)/shard_map/ppermute | solution.py:817
  108.3 4.3 %collective-permute-done.8.refs_6_ = f32[256,128]{1,0:T(8,128)S(1)} collective-permute-done((f32[256,128]{1,0:T(8,128)S(1)}, f32[256,128]{1,0:T(8,128)S(1)}, u32[]{:S(2)}, u32[]{:S(2)}) %collective-permute-start.8) | collective-permute-done | bytes 131104 | tf_op jit(solution)/shard_map/ppermute | solution.py:817
  113.3 2.1 %last.1 = f32[512,128]{1,0:T(8,128)} custom-call(f32[512,128]{1,0:T(8,128)S(1)} %get-tuple-element.79.refs_0_, f32[512,128]{1,0:T(8,128)S(1)} %get-tuple-element.80.refs_1_, f32[512,128]{1,0:T(8,128)S(1)} %get-tuple-element.81.refs_2_, f32[512,128]{1,0:T(8,128)S(1)} %get-tuple-element.82.refs_3_, f32[512,128]{1,0:T(8,128)S(1)} %get-tuple-element.63.invd_ref.refs_5_.refs_4_, ...), custom_call_target="tpu_custom_call" | custom-call | tf_op jit(solution)/shard_map/last/pallas_call | solution.py:790
  (13 shorter events, 4.3 us)
Async XLA Ops:
  0.0 24.4 %collective-permute-start = (f32[512,128]{1,0:T(8,128)}, f32[512,128]{1,0:T(8,128)S(1)}, u32[]{:S(2)}, u32[]{:S(2)}) collective-permute-start(f32[512,128]{1,0:T(8,128)} %bitcast.26), channel_id=1, source_target_pairs={{0,64},{64,0},{1,65},{65,1},{2,66},{66,2},{3,67},{67,3},{4,68},{68... | collective-permute-start | bytes 786440 | tf_op jit(solution)/shard_map/ppermute | solution.py:837
  3.2 0.6 copy-start
  26.3 14.8 %all-to-all-start.1 = ((f32[64,1,128]{2,1,0:T(1,128)}), f32[64,1,128]{2,1,0:T(1,128)}, u32[]{:S(2)}, u32[]{:S(2)}) async-start(f32[64,1,128]{2,1,0:T(1,128)} %bitcast.6), calls=%async_computation.1 | async-start | bytes 65536 | tf_op jit(solution)/shard_map/all_to_all | solution.py:897
  41.1 0.8 copy-start.1
  44.4 10.3 %collective-permute-start.1 = (f32[896,128]{1,0:T(8,128)S(1)}, f32[896,128]{1,0:T(8,128)S(1)}, u32[]{:S(2)}, u32[]{:S(2)}) collective-permute-start(f32[896,128]{1,0:T(8,128)S(1)} %get-tuple-element.55), channel_id=1, source_target_pairs={{0,1},{1,0},{2,3},{3,2},{4,5},{5,4},{6,7},{7,6},{8,9},{9,8},{10,11... | collective-permute-start | bytes 1376264 | tf_op jit(solution)/shard_map/ppermute | solution.py:817
  44.9 14.5 %collective-permute-start.2 = (f32[896,128]{1,0:T(8,128)S(1)}, f32[896,128]{1,0:T(8,128)S(1)}, u32[]{:S(2)}, u32[]{:S(2)}) collective-permute-start(f32[896,128]{1,0:T(8,128)S(1)} %get-tuple-element.56), channel_id=1, source_target_pairs={{0,64},{1,2},{2,1},{3,4},{4,3},{5,6},{6,5},{7,8},{8,7},{9,10},{10,... | collective-permute-start | bytes 1376264 | tf_op jit(solution)/shard_map/ppermute | solution.py:817
  61.9 5.0 %collective-permute-start.3 = (f32[256,128]{1,0:T(8,128)S(1)}, f32[256,128]{1,0:T(8,128)S(1)}, u32[]{:S(2)}, u32[]{:S(2)}) collective-permute-start(f32[256,128]{1,0:T(8,128)S(1)} %get-tuple-element.64), channel_id=1, source_target_pairs={{0,1},{1,0},{2,3},{3,2},{4,5},{5,4},{6,7},{7,6},{8,9},{9,8},{10,11... | collective-permute-start | bytes 393224 | tf_op jit(solution)/shard_map/ppermute | solution.py:817
  61.9 9.3 %collective-permute-start.4 = (f32[256,128]{1,0:T(8,128)S(1)}, f32[256,128]{1,0:T(8,128)S(1)}, u32[]{:S(2)}, u32[]{:S(2)}) collective-permute-start(f32[256,128]{1,0:T(8,128)S(1)} %get-tuple-element.65), channel_id=1, source_target_pairs={{0,64},{1,2},{2,1},{3,4},{4,3},{5,6},{6,5},{7,8},{8,7},{9,10},{10,... | collective-permute-start | bytes 393224 | tf_op jit(solution)/shard_map/ppermute | solution.py:817
  91.0 5.2 %collective-permute-start.5 = (f32[256,128]{1,0:T(8,128)S(1)}, f32[256,128]{1,0:T(8,128)S(1)}, u32[]{:S(2)}, u32[]{:S(2)}) collective-permute-start(f32[256,128]{1,0:T(8,128)S(1)} %get-tuple-element.77), channel_id=1, source_target_pairs={{0,1},{1,0},{2,3},{3,2},{4,5},{5,4},{6,7},{7,6},{8,9},{9,8},{10,11... | collective-permute-start | bytes 393224 | tf_op jit(solution)/shard_map/ppermute | solution.py:817
  91.8 9.2 %collective-permute-start.6 = (f32[256,128]{1,0:T(8,128)S(1)}, f32[256,128]{1,0:T(8,128)S(1)}, u32[]{:S(2)}, u32[]{:S(2)}) collective-permute-start(f32[256,128]{1,0:T(8,128)S(1)} %get-tuple-element.78), channel_id=1, source_target_pairs={{0,64},{1,2},{2,1},{3,4},{4,3},{5,6},{6,5},{7,8},{8,7},{9,10},{10,... | collective-permute-start | bytes 393224 | tf_op jit(solution)/shard_map/ppermute | solution.py:817
  103.3 5.0 %collective-permute-start.7 = (f32[256,128]{1,0:T(8,128)S(1)}, f32[256,128]{1,0:T(8,128)S(1)}, u32[]{:S(2)}, u32[]{:S(2)}) collective-permute-start(f32[256,128]{1,0:T(8,128)S(1)} %get-tuple-element.83), channel_id=1, source_target_pairs={{0,1},{1,0},{2,3},{3,2},{4,5},{5,4},{6,7},{7,6},{8,9},{9,8},{10,11... | collective-permute-start | bytes 393224 | tf_op jit(solution)/shard_map/ppermute | solution.py:817
  103.3 9.3 %collective-permute-start.8 = (f32[256,128]{1,0:T(8,128)S(1)}, f32[256,128]{1,0:T(8,128)S(1)}, u32[]{:S(2)}, u32[]{:S(2)}) collective-permute-start(f32[256,128]{1,0:T(8,128)S(1)} %get-tuple-element.84), channel_id=1, source_target_pairs={{0,64},{1,2},{2,1},{3,4},{4,3},{5,6},{6,5},{7,8},{8,7},{9,10},{10,... | collective-permute-start | bytes 393224 | tf_op jit(solution)/shard_map/ppermute | solution.py:817
  112.6 0.7 copy-start.2

commit v5 on v4

--- a/solution.py
+++ b/solution.py
@@ -94,9 +94,7 @@
     return lax.broadcasted_iota(jnp.int32, shape, axis)
 
 
-def request_kernel(
-    owner_ref, slot_ref, weight_ref, ids_ref, live_ref, send_ref, points_ref
-):
+def request_kernel(owner_ref, slot_ref, weight_ref, send_ref, rank_ref):
     owner = owner_ref[...]
     hits = iota((OWNERS, R_DEV), 0) == owner
     hits_f = hits.astype(f32)
@@ -111,13 +109,7 @@
         ranks.append(jnp.sum(block * count, axis=0, keepdims=True))
         carry = carry + jnp.sum(block, axis=1, keepdims=True)
     rank = jnp.concatenate(ranks, axis=1)
-    ids = ids_ref[...]
-    live = iota((1, R_DEV), 1) < live_ref[0, 0]
-    points_ref[0:1] = owner
-    points_ref[1:2] = rank.astype(jnp.int32) + jnp.where(rank >= float(HALF), 16 - HALF, 0)
-    points_ref[2:3] = jnp.where(live, lax.shift_right_logical(ids, 7), -1)
-    points_ref[3:4] = jnp.bitwise_and(ids, 127)
-    points_ref[4:8] = jnp.zeros((4, R_DEV), jnp.int32)
+    rank_ref[...] = rank
     payload = jnp.concatenate(
         [
             weight_ref[...],
@@ -141,7 +133,7 @@
         send_ref[pl.ds(c, OWNERS, stride=ASK), :] = block
 
 
-def owner_kernel(recv_ref, field_ref, ret_ref):
+def owner_kernel(recv_ref, field_ref, before_ref, ret_ref, after_ref):
     cols = [recv_ref[pl.ds(c, OWNERS, stride=ASK), :] for c in range(6)]
     packed = jnp.concatenate(
         [jnp.concatenate(cols[:3], axis=1), jnp.concatenate(cols[3:], axis=1)], axis=0
@@ -174,6 +166,7 @@
     rows.append(jnp.zeros((128 - HALF, 128), f32))
     turned = jnp.concatenate(rows, axis=0).T
     ret_ref[...] = turned[:OWNERS] + pltpu.roll(turned[OWNERS:], 16, 1)
+    after_ref[...] = before_ref[...]
 
 
 def deriv8(table, v):
@@ -303,49 +296,54 @@
     return jnp.concatenate([low, high], axis=0)
 
 
-def mirror(ghost_ref, bottom, top):
-    first = first_layer(bottom.shape)
-    ghost_ref[448:512] = jnp.where(first, ghost_ref[448:512], pltpu.roll(bottom, LAYER, 1))
-    ghost_ref[0:64] = jnp.where(first, pltpu.roll(top, LAYER, 1), ghost_ref[0:64])
-
-
-def message(raw_bottom, raw_top, inner_bottom, mid, inner_top):
-    first = first_layer(raw_bottom.shape)
-    return jnp.concatenate(
-        [
-            jnp.where(first, raw_bottom, inner_bottom),
-            mid,
-            jnp.where(first, inner_top, raw_top),
-        ],
-        axis=0,
-    )
-
-
-def ghost_apply(ghost_ref, third_ref, planes_ref, face_ref, out_ref):
+def blend(bottom, top):
+    return jnp.where(first_layer(bottom.shape), bottom, top)
+
+
+def end_rows():
     first = first_layer((8, 128))
-    face_ref[...] = jnp.where(
-        first_layer((64, 128)), ghost_ref[0:64], ghost_ref[448:512]
-    )
+    return [
+        jnp.where(first, float(DERIV[c, 0]), float(DERIV[c, 7])).astype(f32)
+        for c in range(8)
+    ]
+
+
+def send_planes(w_ref, next_ref, coef_ref, work_ref, a_ref, b_ref, even):
+    first = first_layer((8, 128))
+    ends = end_rows()
+    work_ref[0:64] = blend(w_ref[0:64], w_ref[448:512])
+    for j in range(8):
+        cols = [next_ref[k * 64 + j * 8 : k * 64 + j * 8 + 8] for k in range(8)]
+        cols[0] = jnp.where(first, 0.0, cols[0])
+        cols[7] = jnp.where(first, cols[7], 0.0)
+        grad = deriv8(DERIV, cols)
+        total = None
+        for c in range(8):
+            at = 1024 + c * 64 + j * 8
+            term = grad[c] * coef_ref[at : at + 8] * ends[c]
+            total = term if total is None else total + term
+        work_ref[64 + j * 8 : 72 + j * 8] = total
+    both = work_ref[...]
+    pack(both, both, a_ref, b_ref, 0, even)
+
+
+def ghost_side(update_ref, inner, planes_ref, face_ref, side_ref):
+    face_ref[...] = pltpu.roll(blend(update_ref[0:64], update_ref[448:512]), LAYER, 1)
     lines = [face_ref[pl.ds(i, 8, stride=8), :] for i in range(8)]
     res = apply_line(lines, lambda a: planes_ref[a * 8 : a * 8 + 8])
     for i in range(8):
-        out_ref[pl.ds(i, 8, stride=8), :] = res[i]
+        side_ref[pl.ds(i, 8, stride=8), :] = res[i]
     rows = [face_ref[j * 8 : j * 8 + 8] for j in range(8)]
     res = apply_line(rows, lambda b: planes_ref[64 + b * 8 : 72 + b * 8])
-    ends = [
-        jnp.where(first, float(DERIV[c, 0]), float(DERIV[c, 7])).astype(f32)
-        for c in range(8)
-    ]
     for j in range(8):
-        total = out_ref[j * 8 : j * 8 + 8] + res[j]
-        total = total + planes_ref[128 + j * 8 : 136 + j * 8] * rows[j]
-        cols = [ghost_ref[k * 64 + j * 8 : k * 64 + j * 8 + 8] for k in range(8)]
-        grad = deriv8(DERIV, cols)
-        for c in range(8):
-            at = c * 64 + j * 8
-            total = total + grad[c] * third_ref[at : at + 8] * ends[c]
-        out_ref[j * 8 : j * 8 + 8] = total
-    in_plane(out_ref, 1)
+        at = slice(j * 8, j * 8 + 8)
+        side_ref[at] = (
+            side_ref[at]
+            + res[j]
+            + planes_ref[128 + j * 8 : 136 + j * 8] * rows[j]
+            + inner[at]
+        )
+    in_plane(side_ref, 1)
 
 
 def plain8(table, v):
@@ -394,8 +392,7 @@
     lax.fori_loop(0, 8, per_j, 0)
 
 
-THIRD_ROW = 256
-PLANE_ROW = THIRD_ROW + 256
+PLANE_ROW = 64
 BASIS_ROW = PLANE_ROW + 128
 GHOST_ROWS = BASIS_ROW + 256
 
@@ -417,8 +414,7 @@
     inv_ref,
     basis_ref,
     solve_ref,
-    a_ref,
-    b_ref,
+    ends_ref,
     stiff_in,
     mass_in,
     field_in,
@@ -470,56 +466,54 @@
     in_plane(diag_ref)
     zeros = jnp.zeros((64, 128), f32)
     invd_ref[...] = 1.0 / coupled(diag_ref, zeros, zeros)
-    even = where_am_i()[0]
-    third = coef_ref[1024:1536, :]
-    pack(third, third, a_ref, b_ref, THIRD_ROW, even)
-    tops = [coef_ref[448:512], coef_ref[960:1024], mass_ref[448:512], diag_ref[448:512]]
-    bottoms = [coef_ref[0:64], coef_ref[512:576], mass_ref[0:64], diag_ref[0:64]]
-    pack(
-        jnp.concatenate(tops, axis=0),
-        jnp.concatenate(bottoms, axis=0),
-        a_ref,
-        b_ref,
-        PLANE_ROW,
-        even,
-    )
-    for c in range(NC // 128):
-        at = BASIS_ROW + c * 64
-        up = basis[LAYER:, c * 128 : c * 128 + 128]
-        down = basis[:LAYER, c * 128 : c * 128 + 128]
-        a_ref[at : at + 64] = jnp.where(even, up, down)
-        b_ref[at : at + 64] = jnp.where(even, down, up)
-    a_ref[0:THIRD_ROW] = jnp.zeros((THIRD_ROW, 128), f32)
-    b_ref[0:THIRD_ROW] = jnp.zeros((THIRD_ROW, 128), f32)
-
-
-def send_first(y_ref, base, invd, a_ref, b_ref):
+    ends = end_rows()
+    for j in range(8):
+        total = None
+        for c in range(8):
+            at = 1024 + c * 64 + j * 8
+            term = coef_ref[at : at + 8] * (ends[c] * ends[c])
+            total = term if total is None else total + term
+        tmp_ref[j * 8 : j * 8 + 8] = total
+    ends_ref[0:64] = blend(coef_ref[0:64], coef_ref[448:512])
+    ends_ref[64:128] = blend(coef_ref[512:576], coef_ref[960:1024])
+    ends_ref[128:192] = blend(mass_ref[0:64], mass_ref[448:512]) + tmp_ref[0:64]
+    ends_ref[192:256] = blend(diag_ref[0:64], diag_ref[448:512])
+
+
+def send_first(y_ref, base, invd, coef_ref, next_ref, work_ref, a_ref, b_ref):
     zeros = jnp.zeros((64, 128), f32)
     inner = coupled(y_ref, zeros, zeros)
     if base is not None:
         inner = inner + base
-    inner = inner * invd * STEPS[0][1]
-    out = message(
-        y_ref[0:64], y_ref[448:512], inner[0:64], inner[64:448], inner[448:512]
-    )
-    pack(out, out, a_ref, b_ref, 0, where_am_i()[0])
+    next_ref[...] = inner * invd * STEPS[0][1]
+    send_planes(y_ref, next_ref, coef_ref, work_ref, a_ref, b_ref, where_am_i()[0])
 
 
 def source_kernel(
     ret_ref,
-    points_ref,
+    owner_ref,
+    rank_ref,
+    ids_ref,
+    live_ref,
     inv_ref,
     static_ref,
     invd_ref,
-    a_in_ref,
-    b_in_ref,
+    coef_ref,
+    ends_ref,
+    basis_ref,
     y_ref,
     a_ref,
     b_ref,
+    next_ref,
+    work_ref,
 ):
-    owner, place = points_ref[0:1], points_ref[1:2]
-    node, elem = points_ref[2:3], points_ref[3:4]
-    hits = (iota((OWNERS, R_DEV), 0) == owner).astype(f32)
+    rank = rank_ref[...].astype(jnp.int32)
+    place = rank + jnp.where(rank >= HALF, 16 - HALF, 0)
+    ids = ids_ref[...]
+    live = iota((1, R_DEV), 1) < live_ref[0, 0]
+    node = jnp.where(live, lax.shift_right_logical(ids, 7), -1)
+    elem = jnp.bitwise_and(ids, 127)
+    hits = (iota((OWNERS, R_DEV), 0) == owner_ref[...]).astype(f32)
     picked = dot_nn(ret_ref[...].T, hits, exact_mode)[0:32]
     value = jnp.sum(
         jnp.where(iota((32, R_DEV), 0) == place, picked, 0.0), axis=0, keepdims=True
@@ -532,9 +526,16 @@
     y_ref[...] = take_lanes(landed, inv_ref[...])
     in_plane(y_ref)
     y_ref[...] = y_ref[...] + static_ref[...]
-    send_first(y_ref, None, invd_ref[...], a_ref, b_ref)
-    a_ref[THIRD_ROW:] = a_in_ref[THIRD_ROW:]
-    b_ref[THIRD_ROW:] = b_in_ref[THIRD_ROW:]
+    send_first(y_ref, None, invd_ref[...], coef_ref, next_ref, work_ref, a_ref, b_ref)
+    even = where_am_i()[0]
+    ends = ends_ref[...]
+    pack(ends, ends, a_ref, b_ref, PLANE_ROW, even)
+    for c in range(NC // 128):
+        at = BASIS_ROW + c * 64
+        up = basis_ref[LAYER:, c * 128 : c * 128 + 128]
+        down = basis_ref[:LAYER, c * 128 : c * 128 + 128]
+        a_ref[at : at + 64] = jnp.where(even, up, down)
+        b_ref[at : at + 64] = jnp.where(even, down, up)
 
 
 def opening_half(
@@ -545,7 +546,6 @@
     a_ref,
     b_ref,
     invd_ref,
-    third_ref,
     planes_ref,
     coef_ref,
     mass_ref,
@@ -555,38 +555,34 @@
     w_ref,
     a_out_ref,
     b_out_ref,
-    ghost_ref,
+    next_ref,
+    work_ref,
     face_ref,
     side_ref,
 ):
-    ghost_ref[...] = unpack(a_ref, b_ref, 0, 256, place)
-    residual = coupled(y_ref, ghost_ref[448:512], ghost_ref[0:64])
+    came = unpack(a_ref, b_ref, 0, 64, place)
+    residual = coupled(y_ref, came[0:64], came[0:64])
     if base_ref is not None:
         residual = residual + base_ref[...]
-    invd = invd_ref[...]
-    update = residual * invd * STEPS[0][1]
+    update = residual * invd_ref[...] * STEPS[0][1]
     upd_ref[...] = update
-    mirror(ghost_ref, update[0:64], update[448:512])
+    ghost_side(upd_ref, came[64:128], planes_ref, face_ref, side_ref)
     stiff_apply(upd_ref, coef_ref, mass_ref, w_ref)
     in_plane(w_ref)
-    ghost_apply(ghost_ref, third_ref, planes_ref, face_ref, side_ref)
     residual = residual - coupled(w_ref, side_ref[...], side_ref[...])
     res_ref[...] = residual
     alpha, beta = STEPS[1]
-    second = alpha * update + beta * invd * residual
+    second = alpha * update + beta * invd_ref[...] * residual
     upd_ref[...] = second
     cur_ref[...] = cur_in_ref[...] + (update + second)
     stiff_apply(upd_ref, coef_ref, mass_ref, w_ref)
     in_plane(w_ref)
     alpha, beta = STEPS[2]
     zeros = jnp.zeros((64, 128), f32)
-    inner = alpha * upd_ref[...] + beta * invd_ref[...] * (
+    next_ref[...] = alpha * upd_ref[...] + beta * invd_ref[...] * (
         res_ref[...] - coupled(w_ref, zeros, zeros)
     )
-    out = message(
-        w_ref[0:64], w_ref[448:512], inner[0:64], inner[64:448], inner[448:512]
-    )
-    pack(out, out, a_out_ref, b_out_ref, 0, place[0])
+    send_planes(w_ref, next_ref, coef_ref, work_ref, a_out_ref, b_out_ref, place[0])
 
 
 def start_kernel(
@@ -605,13 +601,11 @@
     a_out_ref,
     b_out_ref,
     invd_ref,
-    third_ref,
     planes_ref,
     outer_ref,
     *scratch,
 ):
     place = where_am_i()
-    third_ref[...] = unpack(a_ref, b_ref, THIRD_ROW, 256, place)
     planes = unpack(a_ref, b_ref, PLANE_ROW, 128, place)
     planes_ref[...] = planes[0:192]
     bottom, top = through(
@@ -631,7 +625,6 @@
         a_ref,
         b_ref,
         invd_ref,
-        third_ref,
         planes_ref,
         coef_ref,
         mass_ref,
@@ -657,25 +650,22 @@
     invd_ref,
     a_ref,
     b_ref,
-    third_ref,
     planes_ref,
     coef_ref,
     mass_ref,
     work_ref,
     vec_ref,
-    ghost_ref,
     face_ref,
     side_ref,
 ):
-    ghost_ref[...] = unpack(a_ref, b_ref, 0, 256, where_am_i())
-    residual = res_ref[...] - coupled(w_ref, ghost_ref[448:512], ghost_ref[0:64])
+    came = unpack(a_ref, b_ref, 0, 64, where_am_i())
+    residual = res_ref[...] - coupled(w_ref, came[0:64], came[0:64])
     alpha, beta = STEPS[2]
     third = alpha * upd_ref[...] + beta * invd_ref[...] * residual
     vec_ref[...] = third
-    mirror(ghost_ref, third[0:64], third[448:512])
+    ghost_side(vec_ref, came[64:128], planes_ref, face_ref, side_ref)
     stiff_apply(vec_ref, coef_ref, mass_ref, work_ref)
     in_plane(work_ref)
-    ghost_apply(ghost_ref, third_ref, planes_ref, face_ref, side_ref)
     residual = residual - coupled(work_ref, side_ref[...], side_ref[...])
     alpha, beta = STEPS[3]
     fourth = alpha * third + beta * invd_ref[...] * residual
@@ -691,7 +681,6 @@
     invd_ref,
     a_ref,
     b_ref,
-    third_ref,
     planes_ref,
     coef_ref,
     mass_ref,
@@ -712,8 +701,7 @@
         invd_ref,
         a_ref,
         b_ref,
-        third_ref,
-        planes_ref,
+            planes_ref,
         coef_ref,
         mass_ref,
         w_out_ref,
@@ -747,10 +735,13 @@
     base_ref,
     cur_in_ref,
     invd_ref,
+    coef_ref,
     y_ref,
     cur_ref,
     a_ref,
     b_ref,
+    next_ref,
+    work_ref,
 ):
     total = parts_ref[0:8]
     for n in range(1, OWNERS * NC // 1024):
@@ -766,11 +757,13 @@
     y_ref[...] = mass_ref[...] * correction
     in_plane(y_ref)
     y_ref[...] = -(y_ref[...] + w_ref[...])
-    send_first(y_ref, base_ref[...], invd_ref[...], a_ref, b_ref)
+    send_first(
+        y_ref, base_ref[...], invd_ref[...], coef_ref, next_ref, work_ref, a_ref, b_ref
+    )
 
 
 def last_kernel(*refs):
-    inputs, (order_ref, out_ref), scratch = refs[:11], refs[11:13], refs[13:]
+    inputs, (order_ref, out_ref), scratch = refs[:10], refs[10:12], refs[12:]
     current = closing_half(*inputs, *scratch)[1]
     out_ref[...] = take_lanes(current, order_ref[...])
 
@@ -799,9 +792,10 @@
 
 
 FIELD = ((NODES, 128), f32)
-LAYER_MSG = ((256, 128), f32)
+SIDE_MSG = ((64, 128), f32)
 GHOST_MSG = ((GHOST_ROWS, 128), f32)
-GHOST_WORK = [(NODES, 128), (64, 128), (64, 128)]
+SIDE_WORK = [(64, 128), (64, 128)]
+SEND_WORK = [(NODES, 128), (128, 128)]
 
 
 def exchange(a, b):
@@ -836,22 +830,19 @@
     owner = donor_owner.reshape(1, R_DEV)
     other_field = lax.ppermute(own_field, "sess", [(0, 1), (1, 0)])
 
-    send, points = call(
+    send, rank = call(
         request_kernel,
         "request",
-        [((OWNERS * ASK, 128), f32), ((8, R_DEV), jnp.int32)],
+        [((OWNERS * ASK, 128), f32), ((1, R_DEV), f32)],
         owner,
         donor_slot,
         interp_weights.reshape(3 * NP, R_DEV),
-        recv_ids,
-        live_count,
-        smem=(4,),
-        near=(0, 1, 2, 3),
+        near=(0, 1, 2),
     )
     received = lax.all_to_all(
         send.reshape(OWNERS, ASK, 128), "elem", split_axis=0, concat_axis=0, tiled=True
     )
-    coef, mass, start, static, diag, invd, inv, basis, solve, ga, gb = call(
+    coef, mass, start, static, diag, invd, inv, basis, solve, ends = call(
         setup_kernel,
         "setup",
         [
@@ -864,8 +855,7 @@
             ((1, 128), jnp.int32),
             ((128, NC), f32),
             ((128, NC), f32),
-            GHOST_MSG,
-            GHOST_MSG,
+            ((256, 128), f32),
         ],
         order,
         stiffness.reshape(3 * NODES, 128),
@@ -887,12 +877,13 @@
         ],
         copies=6,
     )
-    (answer,) = call(
+    answer, inv = call(
         owner_kernel,
         "owner",
-        [((OWNERS, 128), f32)],
+        [((OWNERS, 128), f32), ((1, 128), jnp.int32)],
         received.reshape(OWNERS * ASK, 128),
         other_field,
+        inv,
     )
     answered = lax.all_to_all(answer, "elem", split_axis=0, concat_axis=0, tiled=True)
     y, a, b = call(
@@ -900,19 +891,26 @@
         "source",
         [FIELD, GHOST_MSG, GHOST_MSG],
         answered,
-        points,
+        owner,
+        rank,
+        recv_ids,
+        live_count,
         inv,
         static,
         invd,
-        ga,
-        gb,
+        coef,
+        ends,
+        basis,
+        smem=(4,),
+        near=(1, 3),
+        scratch=SEND_WORK,
     )
     a, b = exchange(a, b)
-    half = [FIELD, FIELD, FIELD, FIELD, LAYER_MSG, LAYER_MSG]
-    res, upd, cur, w, a, b, invd, third, planes, outer = call(
+    half = [FIELD, FIELD, FIELD, FIELD, SIDE_MSG, SIDE_MSG]
+    res, upd, cur, w, a, b, invd, planes, outer = call(
         start_kernel,
         "start",
-        half + [FIELD, FIELD, ((192, 128), f32), ((128, NC), f32)],
+        half + [FIELD, ((192, 128), f32), ((128, NC), f32)],
         y,
         diag,
         invd,
@@ -921,7 +919,7 @@
         b,
         coef,
         mass,
-        scratch=GHOST_WORK,
+        scratch=SEND_WORK + SIDE_WORK,
     )
     a, b = exchange(a, b)
     res, cur, w, part = call(
@@ -935,13 +933,12 @@
         invd,
         a,
         b,
-        third,
         planes,
         coef,
         mass,
         basis,
         outer,
-        scratch=[(NODES, 128)] + GHOST_WORK,
+        scratch=[(NODES, 128)] + SIDE_WORK,
     )
     parts = lax.all_to_all(
         part.reshape(OWNERS, NC // 128, 128),
@@ -953,7 +950,7 @@
     y, cur, a, b = call(
         restart_kernel,
         "restart",
-        [FIELD, FIELD, LAYER_MSG, LAYER_MSG],
+        [FIELD, FIELD, SIDE_MSG, SIDE_MSG],
         parts.reshape(OWNERS * NC // 128, 128),
         solve,
         mass,
@@ -961,6 +958,8 @@
         res,
         cur,
         invd,
+        coef,
+        scratch=SEND_WORK,
     )
     a, b = exchange(a, b)
     res, upd, cur, w, a, b = call(
@@ -973,11 +972,10 @@
         a,
         b,
         invd,
-        third,
         planes,
         coef,
         mass,
-        scratch=GHOST_WORK,
+        scratch=SEND_WORK + SIDE_WORK,
     )
     a, b = exchange(a, b)
     (out,) = call(
@@ -991,12 +989,12 @@
         invd,
         a,
         b,
-        third,
         planes,
         coef,
         mass,
         order,
-        scratch=[(NODES, 128), (NODES, 128)] + GHOST_WORK,
+        near=(10,),
+        scratch=[(NODES, 128), (NODES, 128)] + SIDE_WORK,
     )
     return out.reshape(1, NP, NP, NP, 128)
 

time: 117 us -> 106 us (0.906)
  blocking collectives: 36.8 us -> 14.6 us
  starting transfers between devices: 20.3 us -> 28.9 us
  waiting for transfers between devices: 33 us -> 36.7 us
  local copies, waits for them, and re-layouts: 2.01 us -> 0 us
  Pallas kernels: 22.6 us -> 23.9 us
    all_to_all x1 -> x0, blocking collectives: 20.6 us -> none  [per_device(): lax.all_to_all(send.reshape(OWNERS, ASK, 128), 'elem', split_axis=0, conc...]
    all_to_all x0 -> x1, starting transfers between devices: none -> 11.6 us  [per_device(): lax.all_to_all(send.reshape(OWNERS, ASK, 128), 'elem', split_axis=0, conc...]
    ppermute x8, waiting for transfers between devices: 30.6 us -> 25.9 us  [exchange(): return (lax.ppermute(a, axes, pairs_a), lax.ppermute(b, axes, pairs_b))]
    all_to_all x1, waiting for transfers between devices: 2.38 us -> 6.82 us  [per_device(): lax.all_to_all(answer, 'elem', split_axis=0, concat_axis=0, tiled=True)]
    all_to_all x0 -> x1, waiting for transfers between devices: none -> 4.01 us  [per_device(): lax.all_to_all(send.reshape(OWNERS, ASK, 128), 'elem', split_axis=0, conc...]
    ppermute x8, starting transfers between devices: 13 us -> 10.3 us  [exchange(): return (lax.ppermute(a, axes, pairs_a), lax.ppermute(b, axes, pairs_b))]
    unnamed x6 -> x0, local copies, waits for them, and re-layouts: 2.01 us -> none
    all_to_all x1, blocking collectives: 16.2 us -> 14.6 us  [per_device(): lax.all_to_all(part.reshape(OWNERS, NC // 128, 128), 'elem', split_axis=0...]
  transfers between devices with their start and end apart: 10 -> 11, of which waited for: 9 -> 10; matrix products, arithmetic and copies ran while one was open for 0% -> 0% of each run, Pallas kernels for 7% -> 8%
where the time goes in v5:
time: 106 us; the launch traced here: 105 us
  waiting for transfers between devices  36.7 us (35%)
  starting transfers between devices  28.9 us (27%)
  Pallas kernels  23.9 us (23%)
  blocking collectives  14.6 us (14%)
    ppermute x8, waiting for transfers between devices, exchange(): return (lax.ppermute(a, axes, pairs_a), lax.ppermute(b, axes, pairs_b))  25.9 us
    pallas_call x9, Pallas kernels, call(): pl.pallas_call(kernel, name=name, out_shape=[jax.ShapeDtypeStruct(s, d) f...  23.9 us
    all_to_all x1, blocking collectives, per_device(): lax.all_to_all(part.reshape(OWNERS, NC // 128, 128), 'elem', split_axis=0...  14.6 us
    all_to_all x1, starting transfers between devices, per_device(): lax.all_to_all(send.reshape(OWNERS, ASK, 128), 'elem', split_axis=0, conc...  11.6 us
    ppermute x8, starting transfers between devices, exchange(): return (lax.ppermute(a, axes, pairs_a), lax.ppermute(b, axes, pairs_b))  10.3 us
    all_to_all x1, starting transfers between devices, per_device(): lax.all_to_all(answer, 'elem', split_axis=0, concat_axis=0, tiled=True)  6.96 us
    all_to_all x1, waiting for transfers between devices, per_device(): lax.all_to_all(answer, 'elem', split_axis=0, concat_axis=0, tiled=True)  6.82 us
    all_to_all x1, waiting for transfers between devices, per_device(): lax.all_to_all(send.reshape(OWNERS, ASK, 128), 'elem', split_axis=0, conc...  4.01 us
  transfers between devices with their start and end apart: 11, of which 10 were waited for; matrix products, arithmetic and copies ran while one was open for 0% of the time, Pallas kernels for 8%

profile of v5, /device:TPU:6, one launch (start us, length us, event | category | flops | bytes accessed | tf_op | source)
XLA Modules:
  0.0 104.7 jit_solution(1172284236137694884)
XLA Ops:
  0.0 3.3 %request.1 = (f32[512,128]{1,0:T(8,128)}, f32[1,1024]{1,0:T(1,128)S(1)}) custom-call(s32[1,1024]{1,0:T(1,128)} %bitcast.30, s32[1,1024]{1,0:T(1,128)} %slot_ref.1, f32[24,1024]{1,0:T(8,128)} %bitcast.29), custom_call_target="tpu_custom_call" | custom-call | tf_op jit(solution)/shard_map/request/pallas_call | solution.py:783
  3.3 11.6 %all-to-all-start = ((f32[64,8,128]{2,1,0:T(8,128)}), f32[64,8,128]{2,1,0:T(8,128)S(1)}, u32[]{:S(2)}, u32[]{:S(2)}) async-start(f32[64,8,128]{2,1,0:T(8,128)} %bitcast.2), calls=%async_computation | async-start | bytes 524288 | tf_op jit(solution)/shard_map/all_to_all | solution.py:842
  14.9 5.1 %setup.1 = (f32[1536,128]{1,0:T(8,128)S(1)}, f32[512,128]{1,0:T(8,128)S(1)}, f32[512,128]{1,0:T(8,128)S(1)}, f32[512,128]{1,0:T(8,128)S(1)}, f32[512,128]{1,0:T(...) custom-call(s32[1,128]{1,0:T(1,128)} %bitcast.32, ...), custom_call_target="tpu_custom_call" | custom-call | tf_op jit(solution)/shard_map/setup/pallas_call | solution.py:783
  20.0 4.0 %all-to-all-done = f32[64,8,128]{2,1,0:T(8,128)S(1)} async-done(((f32[64,8,128]{2,1,0:T(8,128)}), f32[64,8,128]{2,1,0:T(8,128)S(1)}, u32[]{:S(2)}, u32[]{:S(2)}) %all-to-all-start) | async-done | bytes 262176 | tf_op jit(solution)/shard_map/all_to_all | solution.py:842
  24.0 1.9 %owner.1 = (f32[64,128]{1,0:T(8,128)}, s32[1,128]{1,0:T(1,128)S(1)}) custom-call(f32[512,128]{1,0:T(8,128)S(1)} %bitcast.18, f32[512,128]{1,0:T(8,128)S(1)} %collective-permute-done.field_ref, s32[1,128]{1,0:T(1,128)S(1)} %get-tuple-element.46.before_ref), custom_call_target="tpu_custom_call" | custom-call | tf_op jit(solution)/shard_map/owner/pallas_call | solution.py:783
  25.9 7.0 %all-to-all-start.1 = ((f32[64,1,128]{2,1,0:T(1,128)}), f32[64,1,128]{2,1,0:T(1,128)S(1)}, u32[]{:S(2)}, u32[]{:S(2)}) async-start(f32[64,1,128]{2,1,0:T(1,128)} %bitcast.12), calls=%async_computation.1 | async-start | bytes 65536 | tf_op jit(solution)/shard_map/all_to_all | solution.py:888
  33.6 6.8 %all-to-all-done.1 = f32[64,1,128]{2,1,0:T(1,128)S(1)} async-done(((f32[64,1,128]{2,1,0:T(1,128)}), f32[64,1,128]{2,1,0:T(1,128)S(1)}, u32[]{:S(2)}, u32[]{:S(2)}) %all-to-all-start.1) | async-done | bytes 32800 | tf_op jit(solution)/shard_map/all_to_all | solution.py:888
  40.4 2.4 %source.1 = (f32[512,128]{1,0:T(8,128)S(1)}, f32[448,128]{1,0:T(8,128)S(1)}, f32[448,128]{1,0:T(8,128)S(1)}) custom-call(f32[64,128]{1,0:T(8,128)S(1)} %bitcast.20, s32[1,1024]{1,0:T(1,128)} %bitcast.31, f32[1,1024]{1,0:T(1,128)S(1)} %get-tuple-element.48.rank_ref, s32[1,1024]{1,0:T(1,128)} %ids_ref.1, s32[1,1]{1,0:T(1,128)S(6)} %copy.14.live_ref, ...), custom_call_target="tpu_custom_call" | custom-call | tf_op jit(solution)/shard_map/source/pallas_call | solution.py:783
  43.4 2.2 %collective-permute-start.2 = (f32[448,128]{1,0:T(8,128)S(1)}, f32[448,128]{1,0:T(8,128)S(1)}, u32[]{:S(2)}, u32[]{:S(2)}) collective-permute-start(f32[448,128]{1,0:T(8,128)S(1)} %get-tuple-element.59), channel_id=1, source_target_pairs={{0,64},{1,2},{2,1},{3,4},{4,3},{5,6},{6,5},{7,8},{8,7},{9,10},{10,... | collective-permute-start | bytes 688136 | tf_op jit(solution)/shard_map/ppermute | solution.py:811
  45.6 3.3 %collective-permute-done.1.a_ref = f32[448,128]{1,0:T(8,128)S(1)} collective-permute-done((f32[448,128]{1,0:T(8,128)S(1)}, f32[448,128]{1,0:T(8,128)S(1)}, u32[]{:S(2)}, u32[]{:S(2)}) %collective-permute-start.1) | collective-permute-done | bytes 229408 | tf_op jit(solution)/shard_map/ppermute | solution.py:811
  48.9 4.8 %collective-permute-done.2.b_ref = f32[448,128]{1,0:T(8,128)S(1)} collective-permute-done((f32[448,128]{1,0:T(8,128)S(1)}, f32[448,128]{1,0:T(8,128)S(1)}, u32[]{:S(2)}, u32[]{:S(2)}) %collective-permute-start.2) | collective-permute-done | bytes 229408 | tf_op jit(solution)/shard_map/ppermute | solution.py:811
  53.7 2.4 %start.1 = (f32[512,128]{1,0:T(8,128)S(1)}, f32[512,128]{1,0:T(8,128)S(1)}, f32[512,128]{1,0:T(8,128)S(1)}, f32[512,128]{1,0:T(8,128)S(1)}, f32[64,128]{1,0:T(8,...) custom-call(f32[512,128]{1,0:T(8,128)S(1)} %get-tuple-element.55.y_r, ...), custom_call_target="tpu_custom_call" | custom-call | tf_op jit(solution)/shard_map/start/pallas_call | solution.py:783
  56.1 2.3 %collective-permute-start.4 = (f32[64,128]{1,0:T(8,128)S(1)}, f32[64,128]{1,0:T(8,128)S(1)}, u32[]{:S(2)}, u32[]{:S(2)}) collective-permute-start(f32[64,128]{1,0:T(8,128)S(1)} %get-tuple-element.67), channel_id=1, source_target_pairs={{0,64},{1,2},{2,1},{3,4},{4,3},{5,6},{6,5},{7,8},{8,7},{9,10},{10,... | collective-permute-start | bytes 98312 | tf_op jit(solution)/shard_map/ppermute | solution.py:811
  58.4 1.6 %collective-permute-done.3.a_ref = f32[64,128]{1,0:T(8,128)S(1)} collective-permute-done((f32[64,128]{1,0:T(8,128)S(1)}, f32[64,128]{1,0:T(8,128)S(1)}, u32[]{:S(2)}, u32[]{:S(2)}) %collective-permute-start.3) | collective-permute-done | bytes 32800 | tf_op jit(solution)/shard_map/ppermute | solution.py:811
  60.0 4.3 %collective-permute-done.4.b_ref = f32[64,128]{1,0:T(8,128)S(1)} collective-permute-done((f32[64,128]{1,0:T(8,128)S(1)}, f32[64,128]{1,0:T(8,128)S(1)}, u32[]{:S(2)}, u32[]{:S(2)}) %collective-permute-start.4) | collective-permute-done | bytes 32800 | tf_op jit(solution)/shard_map/ppermute | solution.py:811
  64.4 2.7 %middle.1 = (f32[512,128]{1,0:T(8,128)S(1)}, f32[512,128]{1,0:T(8,128)S(1)}, f32[512,128]{1,0:T(8,128)S(1)}, f32[256,128]{1,0:T(8,128)S(1)}) custom-call(f32[512,128]{1,0:T(8,128)S(1)} %get-tuple-element.61.w_ref, f32[512,128]{1,0:T(8,128)S(1)} %get-tuple-element.62.res_in_ref, f32[512,128]{1,0:T(8,128)S(1)} %get-tuple-element.63.upd_ref, ...), custom_call_target="tpu_custom_call" | custom-call | tf_op jit(solution)/shard_map/middle/pallas_call | solution.py:783
  67.0 14.6 %all_to_all.21 = f32[64,4,128]{2,1,0:T(4,128)S(1)} all-to-all(f32[64,4,128]{2,1,0:T(4,128)S(1)} %bitcast.21), channel_id=1, replica_groups=mesh['sess'=2,'elem'=64] {'elem'}, dimensions={0} | all-to-all | bytes 262144 | tf_op jit(solution)/shard_map/all_to_all | solution.py:943
  83.1 2.2 %collective-permute-start.6 = (f32[64,128]{1,0:T(8,128)S(1)}, f32[64,128]{1,0:T(8,128)S(1)}, u32[]{:S(2)}, u32[]{:S(2)}) collective-permute-start(f32[64,128]{1,0:T(8,128)S(1)} %get-tuple-element.78), channel_id=1, source_target_pairs={{0,64},{1,2},{2,1},{3,4},{4,3},{5,6},{6,5},{7,8},{8,7},{9,10},{10,... | collective-permute-start | bytes 98312 | tf_op jit(solution)/shard_map/ppermute | solution.py:811
  86.5 4.8 %collective-permute-done.6.refs_4_ = f32[64,128]{1,0:T(8,128)S(1)} collective-permute-done((f32[64,128]{1,0:T(8,128)S(1)}, f32[64,128]{1,0:T(8,128)S(1)}, u32[]{:S(2)}, u32[]{:S(2)}) %collective-permute-start.6) | collective-permute-done | bytes 32800 | tf_op jit(solution)/shard_map/ppermute | solution.py:811
  91.3 2.4 %again.1 = (f32[512,128]{1,0:T(8,128)S(1)}, f32[512,128]{1,0:T(8,128)S(1)}, f32[512,128]{1,0:T(8,128)S(1)}, f32[512,128]{1,0:T(8,128)S(1)}, f32[64,128]{1,0:T(8,128)S(1)}, /*index=5*/f32[64,128]{1,0:T(8,128)S(1)}) custom-call(f32[512,128]{1,0:T(8,128)S(1)} %get-tuple-element.70.base_ref.refs_0_, f32[512,128]{1,0:T(8,128)S(1)} %get-tuple-element.75.refs_1_, ...), custom_call_target="tpu_custom_call" | custom-call | tf_op jit(solution)/shard_map/again/pallas_call | solution.py:783
  93.7 2.3 %collective-permute-start.8 = (f32[64,128]{1,0:T(8,128)S(1)}, f32[64,128]{1,0:T(8,128)S(1)}, u32[]{:S(2)}, u32[]{:S(2)}) collective-permute-start(f32[64,128]{1,0:T(8,128)S(1)} %get-tuple-element.84), channel_id=1, source_target_pairs={{0,64},{1,2},{2,1},{3,4},{4,3},{5,6},{6,5},{7,8},{8,7},{9,10},{10,... | collective-permute-start | bytes 98312 | tf_op jit(solution)/shard_map/ppermute | solution.py:811
  95.9 1.6 %collective-permute-done.7.refs_5_ = f32[64,128]{1,0:T(8,128)S(1)} collective-permute-done((f32[64,128]{1,0:T(8,128)S(1)}, f32[64,128]{1,0:T(8,128)S(1)}, u32[]{:S(2)}, u32[]{:S(2)}) %collective-permute-start.7) | collective-permute-done | bytes 32800 | tf_op jit(solution)/shard_map/ppermute | solution.py:811
  97.6 4.3 %collective-permute-done.8.refs_6_ = f32[64,128]{1,0:T(8,128)S(1)} collective-permute-done((f32[64,128]{1,0:T(8,128)S(1)}, f32[64,128]{1,0:T(8,128)S(1)}, u32[]{:S(2)}, u32[]{:S(2)}) %collective-permute-start.8) | collective-permute-done | bytes 32800 | tf_op jit(solution)/shard_map/ppermute | solution.py:811
  101.9 2.8 %last.1 = f32[512,128]{1,0:T(8,128)} custom-call(f32[512,128]{1,0:T(8,128)S(1)} %get-tuple-element.79.refs_0_, f32[512,128]{1,0:T(8,128)S(1)} %get-tuple-element.80.refs_1_, f32[512,128]{1,0:T(8,128)S(1)} %get-tuple-element.81.refs_2_, f32[512,128]{1,0:T(8,128)S(1)} %get-tuple-element.82.refs_3_, f32[512,128]{1,0:T(8,128)S(1)} %get-tuple-element.65.invd_ref.refs_5_.refs_4_, ...), custom_call_target="tpu_custom_call" | custom-call | tf_op jit(solution)/shard_map/last/pallas_call | solution.py:783
  (8 shorter events, 3.4 us)
Async XLA Ops:
  0.0 24.0 %collective-permute-start = (f32[512,128]{1,0:T(8,128)}, f32[512,128]{1,0:T(8,128)S(1)}, u32[]{:S(2)}, u32[]{:S(2)}) collective-permute-start(f32[512,128]{1,0:T(8,128)} %bitcast.27), channel_id=1, source_target_pairs={{0,64},{64,0},{1,65},{65,1},{2,66},{66,2},{3,67},{67,3},{4,68},{68... | collective-permute-start | bytes 786440 | tf_op jit(solution)/shard_map/ppermute | solution.py:831
  3.3 20.8 %all-to-all-start = ((f32[64,8,128]{2,1,0:T(8,128)}), f32[64,8,128]{2,1,0:T(8,128)S(1)}, u32[]{:S(2)}, u32[]{:S(2)}) async-start(f32[64,8,128]{2,1,0:T(8,128)} %bitcast.2), calls=%async_computation | async-start | bytes 524288 | tf_op jit(solution)/shard_map/all_to_all | solution.py:842
  25.9 14.4 %all-to-all-start.1 = ((f32[64,1,128]{2,1,0:T(1,128)}), f32[64,1,128]{2,1,0:T(1,128)S(1)}, u32[]{:S(2)}, u32[]{:S(2)}) async-start(f32[64,1,128]{2,1,0:T(1,128)} %bitcast.12), calls=%async_computation.1 | async-start | bytes 65536 | tf_op jit(solution)/shard_map/all_to_all | solution.py:888
  42.8 6.1 %collective-permute-start.1 = (f32[448,128]{1,0:T(8,128)S(1)}, f32[448,128]{1,0:T(8,128)S(1)}, u32[]{:S(2)}, u32[]{:S(2)}) collective-permute-start(f32[448,128]{1,0:T(8,128)S(1)} %get-tuple-element.58), channel_id=1, source_target_pairs={{0,1},{1,0},{2,3},{3,2},{4,5},{5,4},{6,7},{7,6},{8,9},{9,8},{10,11... | collective-permute-start | bytes 688136 | tf_op jit(solution)/shard_map/ppermute | solution.py:811
  43.4 10.2 %collective-permute-start.2 = (f32[448,128]{1,0:T(8,128)S(1)}, f32[448,128]{1,0:T(8,128)S(1)}, u32[]{:S(2)}, u32[]{:S(2)}) collective-permute-start(f32[448,128]{1,0:T(8,128)S(1)} %get-tuple-element.59), channel_id=1, source_target_pairs={{0,64},{1,2},{2,1},{3,4},{4,3},{5,6},{6,5},{7,8},{8,7},{9,10},{10,... | collective-permute-start | bytes 688136 | tf_op jit(solution)/shard_map/ppermute | solution.py:811
  56.1 4.0 %collective-permute-start.3 = (f32[64,128]{1,0:T(8,128)S(1)}, f32[64,128]{1,0:T(8,128)S(1)}, u32[]{:S(2)}, u32[]{:S(2)}) collective-permute-start(f32[64,128]{1,0:T(8,128)S(1)} %get-tuple-element.66), channel_id=1, source_target_pairs={{0,1},{1,0},{2,3},{3,2},{4,5},{5,4},{6,7},{7,6},{8,9},{9,8},{10,11... | collective-permute-start | bytes 98312 | tf_op jit(solution)/shard_map/ppermute | solution.py:811
  56.1 8.2 %collective-permute-start.4 = (f32[64,128]{1,0:T(8,128)S(1)}, f32[64,128]{1,0:T(8,128)S(1)}, u32[]{:S(2)}, u32[]{:S(2)}) collective-permute-start(f32[64,128]{1,0:T(8,128)S(1)} %get-tuple-element.67), channel_id=1, source_target_pairs={{0,64},{1,2},{2,1},{3,4},{4,3},{5,6},{6,5},{7,8},{8,7},{9,10},{10,... | collective-permute-start | bytes 98312 | tf_op jit(solution)/shard_map/ppermute | solution.py:811
  82.5 4.0 %collective-permute-start.5 = (f32[64,128]{1,0:T(8,128)S(1)}, f32[64,128]{1,0:T(8,128)S(1)}, u32[]{:S(2)}, u32[]{:S(2)}) collective-permute-start(f32[64,128]{1,0:T(8,128)S(1)} %get-tuple-element.77), channel_id=1, source_target_pairs={{0,1},{1,0},{2,3},{3,2},{4,5},{5,4},{6,7},{7,6},{8,9},{9,8},{10,11... | collective-permute-start | bytes 98312 | tf_op jit(solution)/shard_map/ppermute | solution.py:811
  83.1 8.1 %collective-permute-start.6 = (f32[64,128]{1,0:T(8,128)S(1)}, f32[64,128]{1,0:T(8,128)S(1)}, u32[]{:S(2)}, u32[]{:S(2)}) collective-permute-start(f32[64,128]{1,0:T(8,128)S(1)} %get-tuple-element.78), channel_id=1, source_target_pairs={{0,64},{1,2},{2,1},{3,4},{4,3},{5,6},{6,5},{7,8},{8,7},{9,10},{10,... | collective-permute-start | bytes 98312 | tf_op jit(solution)/shard_map/ppermute | solution.py:811
  93.6 4.0 %collective-permute-start.7 = (f32[64,128]{1,0:T(8,128)S(1)}, f32[64,128]{1,0:T(8,128)S(1)}, u32[]{:S(2)}, u32[]{:S(2)}) collective-permute-start(f32[64,128]{1,0:T(8,128)S(1)} %get-tuple-element.83), channel_id=1, source_target_pairs={{0,1},{1,0},{2,3},{3,2},{4,5},{5,4},{6,7},{7,6},{8,9},{9,8},{10,11... | collective-permute-start | bytes 98312 | tf_op jit(solution)/shard_map/ppermute | solution.py:811
  93.7 8.2 %collective-permute-start.8 = (f32[64,128]{1,0:T(8,128)S(1)}, f32[64,128]{1,0:T(8,128)S(1)}, u32[]{:S(2)}, u32[]{:S(2)}) collective-permute-start(f32[64,128]{1,0:T(8,128)S(1)} %get-tuple-element.84), channel_id=1, source_target_pairs={{0,64},{1,2},{2,1},{3,4},{4,3},{5,6},{6,5},{7,8},{8,7},{9,10},{10,... | collective-permute-start | bytes 98312 | tf_op jit(solution)/shard_map/ppermute | solution.py:811

commit v6 on v5

--- a/solution.py
+++ b/solution.py
@@ -7,6 +7,7 @@
 from jax.experimental import pallas as pl
 from jax.experimental.pallas import tpu as pltpu
 from jax.sharding import PartitionSpec as P
+
 
 NP = 8
 EX = 8
@@ -94,7 +95,9 @@
     return lax.broadcasted_iota(jnp.int32, shape, axis)
 
 
-def request_kernel(owner_ref, slot_ref, weight_ref, send_ref, rank_ref):
+def request_kernel(
+    owner_ref, slot_ref, weight_ref, ids_ref, send_ref, rank_ref, owner_out_ref, ids_out_ref
+):
     owner = owner_ref[...]
     hits = iota((OWNERS, R_DEV), 0) == owner
     hits_f = hits.astype(f32)
@@ -110,6 +113,8 @@
         carry = carry + jnp.sum(block, axis=1, keepdims=True)
     rank = jnp.concatenate(ranks, axis=1)
     rank_ref[...] = rank
+    owner_out_ref[...] = owner
+    ids_out_ref[...] = ids_ref[...]
     payload = jnp.concatenate(
         [
             weight_ref[...],
@@ -392,8 +397,7 @@
     lax.fori_loop(0, 8, per_j, 0)
 
 
-PLANE_ROW = 64
-BASIS_ROW = PLANE_ROW + 128
+BASIS_ROW = 128
 GHOST_ROWS = BASIS_ROW + 256
 
 
@@ -414,7 +418,9 @@
     inv_ref,
     basis_ref,
     solve_ref,
-    ends_ref,
+    order_out_ref,
+    a_ref,
+    b_ref,
     stiff_in,
     mass_in,
     field_in,
@@ -444,6 +450,7 @@
     inv = jnp.sum(match.T * iota((128, 128), 0).astype(f32), axis=0, keepdims=True)
     inv = inv.astype(jnp.int32)
     inv_ref[...] = inv
+    order_out_ref[...] = order
     copies[0].wait()
     tmp_ref[...] = take_lanes(stiff_in[0:512, :], inv)
     for k in range(8):
@@ -474,10 +481,23 @@
             term = coef_ref[at : at + 8] * (ends[c] * ends[c])
             total = term if total is None else total + term
         tmp_ref[j * 8 : j * 8 + 8] = total
-    ends_ref[0:64] = blend(coef_ref[0:64], coef_ref[448:512])
-    ends_ref[64:128] = blend(coef_ref[512:576], coef_ref[960:1024])
-    ends_ref[128:192] = blend(mass_ref[0:64], mass_ref[448:512]) + tmp_ref[0:64]
-    ends_ref[192:256] = blend(diag_ref[0:64], diag_ref[448:512])
+    planes = jnp.concatenate(
+        [
+            blend(coef_ref[0:64], coef_ref[448:512]),
+            blend(coef_ref[512:576], coef_ref[960:1024]),
+            blend(mass_ref[0:64], mass_ref[448:512]) + tmp_ref[0:64],
+            blend(diag_ref[0:64], diag_ref[448:512]),
+        ],
+        axis=0,
+    )
+    even = where_am_i()[0]
+    pack(planes, planes, a_ref, b_ref, 0, even)
+    for c in range(NC // 128):
+        at = BASIS_ROW + c * 64
+        up = basis[LAYER:, c * 128 : c * 128 + 128]
+        down = basis[:LAYER, c * 128 : c * 128 + 128]
+        a_ref[at : at + 64] = jnp.where(even, up, down)
+        b_ref[at : at + 64] = jnp.where(even, down, up)
 
 
 def send_first(y_ref, base, invd, coef_ref, next_ref, work_ref, a_ref, b_ref):
@@ -499,8 +519,6 @@
     static_ref,
     invd_ref,
     coef_ref,
-    ends_ref,
-    basis_ref,
     y_ref,
     a_ref,
     b_ref,
@@ -527,15 +545,6 @@
     in_plane(y_ref)
     y_ref[...] = y_ref[...] + static_ref[...]
     send_first(y_ref, None, invd_ref[...], coef_ref, next_ref, work_ref, a_ref, b_ref)
-    even = where_am_i()[0]
-    ends = ends_ref[...]
-    pack(ends, ends, a_ref, b_ref, PLANE_ROW, even)
-    for c in range(NC // 128):
-        at = BASIS_ROW + c * 64
-        up = basis_ref[LAYER:, c * 128 : c * 128 + 128]
-        down = basis_ref[:LAYER, c * 128 : c * 128 + 128]
-        a_ref[at : at + 64] = jnp.where(even, up, down)
-        b_ref[at : at + 64] = jnp.where(even, down, up)
 
 
 def opening_half(
@@ -592,6 +601,8 @@
     cur_in_ref,
     a_ref,
     b_ref,
+    ga_ref,
+    gb_ref,
     coef_ref,
     mass_ref,
     res_ref,
@@ -602,21 +613,15 @@
     b_out_ref,
     invd_ref,
     planes_ref,
-    outer_ref,
     *scratch,
 ):
     place = where_am_i()
-    planes = unpack(a_ref, b_ref, PLANE_ROW, 128, place)
+    planes = unpack(ga_ref, gb_ref, 0, 128, place)
     planes_ref[...] = planes[0:192]
     bottom, top = through(
         diag_ref[0:64], diag_ref[448:512], planes[192:256], planes[192:256]
     )
     invd_ref[...] = whole(1.0 / bottom, invd_in_ref, 1.0 / top)
-    for c in range(NC // 128):
-        at = BASIS_ROW + c * 64
-        below, above = beside(a_ref[at : at + 64], b_ref[at : at + 64], place)
-        outer_ref[0:64, c * 128 : c * 128 + 128] = below
-        outer_ref[64:128, c * 128 : c * 128 + 128] = above
     opening_half(
         place,
         None,
@@ -685,7 +690,8 @@
     coef_ref,
     mass_ref,
     basis_ref,
-    outer_ref,
+    ga_ref,
+    gb_ref,
     res_ref,
     cur_ref,
     w_out_ref,
@@ -719,9 +725,15 @@
     top = -jnp.sum(w_out_ref[448:512], axis=0, keepdims=True)
     outer = jnp.where(first_layer((1, 128)), bottom, top)
     left = jnp.broadcast_to(jnp.concatenate([sums, outer], axis=1), (8, 256))
-    right = jnp.concatenate([basis_ref[...], outer_ref[...]], axis=0)
-    part = dot_nn(left, right, exact_mode)[0:1] * (1.0 / math.sqrt(NODES))
-    blocks = [part[:, c * 128 : c * 128 + 128] for c in range(NC // 128)]
+    place = where_am_i()
+    blocks = []
+    for c in range(NC // 128):
+        at = BASIS_ROW + c * 64
+        below, above = beside(ga_ref[at : at + 64], gb_ref[at : at + 64], place)
+        own = basis_ref[:, c * 128 : c * 128 + 128]
+        right = jnp.concatenate([own, below, above], axis=0)
+        part = dot_nn(left, right, exact_mode)[0:1]
+        blocks.append(part * (1.0 / math.sqrt(NODES)))
     eight = jnp.concatenate(blocks + blocks, axis=0)
     for n in range(OWNERS * NC // 1024):
         part_ref[n * 8 : n * 8 + 8] = eight
@@ -768,7 +780,7 @@
     out_ref[...] = take_lanes(current, order_ref[...])
 
 
-def call(kernel, name, outs, *args, scratch=(), smem=(), far=(), near=(), copies=0):
+def call(kernel, outs, *args, scratch=(), smem=(), far=(), near=(), copies=0):
     def stay(x):
         return pltpu.with_memory_space_constraint(x, pltpu.HBM)
 
@@ -782,7 +794,6 @@
         scratches.append(pltpu.SemaphoreType.DMA((copies,)))
     return pl.pallas_call(
         kernel,
-        name=name,
         out_shape=[jax.ShapeDtypeStruct(s, d) for s, d in outs],
         in_specs=[pl.BlockSpec(memory_space=space(n)) for n in range(len(args))],
         out_specs=[pl.BlockSpec(memory_space=pltpu.VMEM) for _ in outs],
@@ -811,7 +822,7 @@
     return lax.ppermute(a, axes, pairs_a), lax.ppermute(b, axes, pairs_b)
 
 
-def per_device(
+def one_device(
     pressure,
     load,
     stiffness,
@@ -830,21 +841,25 @@
     owner = donor_owner.reshape(1, R_DEV)
     other_field = lax.ppermute(own_field, "sess", [(0, 1), (1, 0)])
 
-    send, rank = call(
+    send, rank, owner, ids = call(
         request_kernel,
-        "request",
-        [((OWNERS * ASK, 128), f32), ((1, R_DEV), f32)],
+        [
+            ((OWNERS * ASK, 128), f32),
+            ((1, R_DEV), f32),
+            ((1, R_DEV), jnp.int32),
+            ((1, R_DEV), jnp.int32),
+        ],
         owner,
         donor_slot,
         interp_weights.reshape(3 * NP, R_DEV),
-        near=(0, 1, 2),
+        recv_ids,
+        near=(0, 1, 2, 3),
     )
     received = lax.all_to_all(
         send.reshape(OWNERS, ASK, 128), "elem", split_axis=0, concat_axis=0, tiled=True
     )
-    coef, mass, start, static, diag, invd, inv, basis, solve, ends = call(
+    coef, mass, start, static, diag, invd, inv, basis, solve, order, ga, gb = call(
         setup_kernel,
-        "setup",
         [
             ((3 * NODES, 128), f32),
             FIELD,
@@ -855,7 +870,9 @@
             ((1, 128), jnp.int32),
             ((128, NC), f32),
             ((128, NC), f32),
-            ((256, 128), f32),
+            ((1, 128), jnp.int32),
+            GHOST_MSG,
+            GHOST_MSG,
         ],
         order,
         stiffness.reshape(3 * NODES, 128),
@@ -879,44 +896,41 @@
     )
     answer, inv = call(
         owner_kernel,
-        "owner",
         [((OWNERS, 128), f32), ((1, 128), jnp.int32)],
         received.reshape(OWNERS * ASK, 128),
         other_field,
         inv,
     )
     answered = lax.all_to_all(answer, "elem", split_axis=0, concat_axis=0, tiled=True)
+    ga, gb = exchange(ga, gb)
     y, a, b = call(
         source_kernel,
-        "source",
-        [FIELD, GHOST_MSG, GHOST_MSG],
+        [FIELD, SIDE_MSG, SIDE_MSG],
         answered,
         owner,
         rank,
-        recv_ids,
+        ids,
         live_count,
         inv,
         static,
         invd,
         coef,
-        ends,
-        basis,
         smem=(4,),
-        near=(1, 3),
         scratch=SEND_WORK,
     )
     a, b = exchange(a, b)
     half = [FIELD, FIELD, FIELD, FIELD, SIDE_MSG, SIDE_MSG]
-    res, upd, cur, w, a, b, invd, planes, outer = call(
+    res, upd, cur, w, a, b, invd, planes = call(
         start_kernel,
-        "start",
-        half + [FIELD, ((192, 128), f32), ((128, NC), f32)],
+        half + [FIELD, ((192, 128), f32)],
         y,
         diag,
         invd,
         start,
         a,
         b,
+        ga,
+        gb,
         coef,
         mass,
         scratch=SEND_WORK + SIDE_WORK,
@@ -924,7 +938,6 @@
     a, b = exchange(a, b)
     res, cur, w, part = call(
         middle_kernel,
-        "middle",
         [FIELD, FIELD, FIELD, ((OWNERS * NC // 128, 128), f32)],
         w,
         res,
@@ -937,7 +950,8 @@
         coef,
         mass,
         basis,
-        outer,
+        ga,
+        gb,
         scratch=[(NODES, 128)] + SIDE_WORK,
     )
     parts = lax.all_to_all(
@@ -949,7 +963,6 @@
     )
     y, cur, a, b = call(
         restart_kernel,
-        "restart",
         [FIELD, FIELD, SIDE_MSG, SIDE_MSG],
         parts.reshape(OWNERS * NC // 128, 128),
         solve,
@@ -964,7 +977,6 @@
     a, b = exchange(a, b)
     res, upd, cur, w, a, b = call(
         again_kernel,
-        "again",
         half,
         res,
         y,
@@ -980,7 +992,6 @@
     a, b = exchange(a, b)
     (out,) = call(
         last_kernel,
-        "last",
         [FIELD],
         w,
         res,
@@ -993,7 +1004,6 @@
         coef,
         mass,
         order,
-        near=(10,),
         scratch=[(NODES, 128), (NODES, 128)] + SIDE_WORK,
     )
     return out.reshape(1, NP, NP, NP, 128)
@@ -1001,7 +1011,7 @@
 
 def solution(mesh):
     return jax.shard_map(
-        per_device,
+        one_device,
         mesh=mesh,
         in_specs=(
             P("sess", None, None, None, "elem"),

time: 106 us -> 107 us (level)
  waiting for transfers between devices: 36.7 us -> 30.6 us
  starting transfers between devices: 28.9 us -> 34.6 us
  local copies, waits for them, and re-layouts: 0 us -> 2.9 us
  Pallas kernels: 23.9 us -> 22.5 us
    ppermute x8 -> x10, starting transfers between devices: 10.3 us -> 16.2 us  [exchange(): return (lax.ppermute(a, axes, pairs_a), lax.ppermute(b, axes, pairs_b))]
    all_to_all x2, waiting for transfers between devices: 10.8 us -> 6.82 us  [the longest x1 6.82 us: one_device(): lax.all_to_all(answer, 'elem', split_axis=0, concat_axis=0, tiled=True)]
    unnamed x0 -> x10, local copies, waits for them, and re-layouts: none -> 2.9 us
    ppermute x8 -> x10, waiting for transfers between devices: 25.9 us -> 23.8 us  [exchange(): return (lax.ppermute(a, axes, pairs_a), lax.ppermute(b, axes, pairs_b))]
    pallas_call x9, Pallas kernels: 23.9 us -> 22.5 us  [call(): pl.pallas_call(kernel, out_shape=[jax.ShapeDtypeStruct(s, d) for s, d in...]
  transfers between devices with their start and end apart: 11 -> 13, of which waited for: 10 -> 9; matrix products, arithmetic and copies ran while one was open for 0% -> 0% of each run, Pallas kernels for 8% -> 11%
where the time goes in v6:
time: 107 us; the launch traced here: 106 us
  starting transfers between devices  34.6 us (32%)
  waiting for transfers between devices  30.6 us (29%)
  Pallas kernels  22.5 us (21%)
  blocking collectives  14.6 us (14%)
  local copies, waits for them, and re-layouts  2.9 us (3%)
    ppermute x10, waiting for transfers between devices, exchange(): return (lax.ppermute(a, axes, pairs_a), lax.ppermute(b, axes, pairs_b))  23.8 us
    pallas_call x9, Pallas kernels, call(): pl.pallas_call(kernel, out_shape=[jax.ShapeDtypeStruct(s, d) for s, d in...  22.5 us
    ppermute x10, starting transfers between devices, exchange(): return (lax.ppermute(a, axes, pairs_a), lax.ppermute(b, axes, pairs_b))  16.2 us
    all_to_all x1, blocking collectives, one_device(): lax.all_to_all(part.reshape(OWNERS, NC // 128, 128), 'elem', split_axis=0...  14.6 us
    all_to_all x1, starting transfers between devices, one_device(): lax.all_to_all(send.reshape(OWNERS, ASK, 128), 'elem', split_axis=0, conc...  11.6 us
    all_to_all x1, waiting for transfers between devices, one_device(): lax.all_to_all(answer, 'elem', split_axis=0, concat_axis=0, tiled=True)  6.82 us
    all_to_all x1, starting transfers between devices, one_device(): lax.all_to_all(answer, 'elem', split_axis=0, concat_axis=0, tiled=True)  6.78 us
    unnamed x10, local copies, waits for them, and re-layouts  2.9 us
  transfers between devices with their start and end apart: 13, of which 9 were waited for; matrix products, arithmetic and copies ran while one was open for 0% of the time, Pallas kernels for 11%

profile of v6, /device:TPU:6, one launch (start us, length us, event | category | flops | bytes accessed | tf_op | source)
XLA Modules:
  0.0 105.9 jit_solution(3359680137910086774)
XLA Ops:
  0.0 3.3 %shard_map.118 = (f32[512,128]{1,0:T(8,128)}, f32[1,1024]{1,0:T(1,128)S(1)}, s32[1,1024]{1,0:T(1,128)S(1)}, s32[1,1024]{1,0:T(1,128)S(1)}) custom-call(s32[1,1024]{1,0:T(1,128)} %bitcast.31, s32[1,1024]{1,0:T(1,128)} %slot_ref.1, f32[24,1024]{1,0:T(8,128)} %bitcast.30, s32[1,1024]{1,0:T(1,128)} %ids_ref.1), custom_call_target="tpu_custom_call" | custom-call | tf_op jit(solution)/shard_map/pallas_call | solution.py:795
  3.3 11.6 %all-to-all-start = ((f32[64,8,128]{2,1,0:T(8,128)}), f32[64,8,128]{2,1,0:T(8,128)S(1)}, u32[]{:S(2)}, u32[]{:S(2)}) async-start(f32[64,8,128]{2,1,0:T(8,128)} %bitcast.2), calls=%async_computation | async-start | bytes 524288 | tf_op jit(solution)/shard_map/all_to_all | solution.py:858
  14.9 5.9 %shard_map.119 = (f32[1536,128]{1,0:T(8,128)S(1)}, f32[512,128]{1,0:T(8,128)S(1)}, f32[512,128]{1,0:T(8,128)S(1)}, f32[512,128]{1,0:T(8,128)S(1)}, f32[512,128]{...) custom-call(s32[1,128]{1,0:T(1,128)} %bitcast.32, ...), custom_call_target="tpu_custom_call" | custom-call | tf_op jit(solution)/shard_map/pallas_call | solution.py:795
  21.3 1.5 %collective-permute-start.3 = (f32[384,128]{1,0:T(8,128)}, f32[384,128]{1,0:T(8,128)S(1)}, u32[]{:S(2)}, u32[]{:S(2)}) collective-permute-start(f32[384,128]{1,0:T(8,128)} %get-tuple-element.63), channel_id=1, source_target_pairs={{0,1},{1,0},{2,3},{3,2},{4,5},{5,4},{6,7},{7,6},{8,9},{9,8},{10,11... | collective-permute-start | bytes 589832 | tf_op jit(solution)/shard_map/ppermute | solution.py:822
  22.8 4.4 %collective-permute-start.4 = (f32[384,128]{1,0:T(8,128)}, f32[384,128]{1,0:T(8,128)S(1)}, u32[]{:S(2)}, u32[]{:S(2)}) collective-permute-start(f32[384,128]{1,0:T(8,128)} %get-tuple-element.64), channel_id=1, source_target_pairs={{0,64},{1,2},{2,1},{3,4},{4,3},{5,6},{6,5},{7,8},{8,7},{9,10},{10,... | collective-permute-start | bytes 589832 | tf_op jit(solution)/shard_map/ppermute | solution.py:822
  27.9 1.3 %shard_map.120 = (f32[64,128]{1,0:T(8,128)S(1)}, s32[1,128]{1,0:T(1,128)S(1)}) custom-call(f32[512,128]{1,0:T(8,128)S(1)} %bitcast.18, f32[512,128]{1,0:T(8,128)S(1)} %collective-permute-done.field_ref, s32[1,128]{1,0:T(1,128)S(1)} %copy-done.2), custom_call_target="tpu_custom_call" | custom-call | tf_op jit(solution)/shard_map/pallas_call | solution.py:795
  30.3 6.8 %all-to-all-start.1 = ((f32[64,1,128]{2,1,0:T(1,128)}), f32[64,1,128]{2,1,0:T(1,128)S(1)}, u32[]{:S(2)}, u32[]{:S(2)}) async-start(f32[64,1,128]{2,1,0:T(1,128)} %bitcast.22), calls=%async_computation.1 | async-start | bytes 65536 | tf_op jit(solution)/shard_map/all_to_all | solution.py:904
  37.7 6.8 %all-to-all-done.1 = f32[64,1,128]{2,1,0:T(1,128)S(1)} async-done(((f32[64,1,128]{2,1,0:T(1,128)}), f32[64,1,128]{2,1,0:T(1,128)S(1)}, u32[]{:S(2)}, u32[]{:S(2)}) %all-to-all-start.1) | async-done | bytes 32800 | tf_op jit(solution)/shard_map/all_to_all | solution.py:904
  45.2 1.7 %shard_map.121 = (f32[512,128]{1,0:T(8,128)S(1)}, f32[64,128]{1,0:T(8,128)S(1)}, f32[64,128]{1,0:T(8,128)S(1)}) custom-call(f32[64,128]{1,0:T(8,128)S(1)} %bitcast.20, s32[1,1024]{1,0:T(1,128)S(1)} %get-tuple-element.51.owner_ref, f32[1,1024]{1,0:T(1,128)S(1)} %get-tuple-element.52.rank_ref, s32[1,1024]{1,0:T(1,128)S(1)} %get-tuple-element.53.ids_ref, ...), custom_call_target="tpu_custom_call" | custom-call | tf_op jit(solution)/shard_map/pallas_call | solution.py:795
  47.5 2.2 %collective-permute-start.2 = (f32[64,128]{1,0:T(8,128)S(1)}, f32[64,128]{1,0:T(8,128)S(1)}, u32[]{:S(2)}, u32[]{:S(2)}) collective-permute-start(f32[64,128]{1,0:T(8,128)S(1)} %get-tuple-element.62), channel_id=1, source_target_pairs={{0,64},{1,2},{2,1},{3,4},{4,3},{5,6},{6,5},{7,8},{8,7},{9,10},{10,... | collective-permute-start | bytes 98312 | tf_op jit(solution)/shard_map/ppermute | solution.py:822
  50.8 4.8 %collective-permute-done.2.b_ref = f32[64,128]{1,0:T(8,128)S(1)} collective-permute-done((f32[64,128]{1,0:T(8,128)S(1)}, f32[64,128]{1,0:T(8,128)S(1)}, u32[]{:S(2)}, u32[]{:S(2)}) %collective-permute-start.2) | collective-permute-done | bytes 32800 | tf_op jit(solution)/shard_map/ppermute | solution.py:822
  55.6 2.4 %shard_map.122 = (f32[512,128]{1,0:T(8,128)S(1)}, f32[512,128]{1,0:T(8,128)S(1)}, f32[512,128]{1,0:T(8,128)S(1)}, f32[512,128]{1,0:T(8,128)S(1)}, f32[64,128]{1,...) custom-call(f32[512,128]{1,0:T(8,128)S(1)} %get-tuple-element.58.y_ref, ...), custom_call_target="tpu_custom_call" | custom-call | tf_op jit(solution)/shard_map/pallas_call | solution.py:795
  58.0 2.3 %collective-permute-start.6 = (f32[64,128]{1,0:T(8,128)S(1)}, f32[64,128]{1,0:T(8,128)S(1)}, u32[]{:S(2)}, u32[]{:S(2)}) collective-permute-start(f32[64,128]{1,0:T(8,128)S(1)} %get-tuple-element.72), channel_id=1, source_target_pairs={{0,64},{1,2},{2,1},{3,4},{4,3},{5,6},{6,5},{7,8},{8,7},{9,10},{10,... | collective-permute-start | bytes 98312 | tf_op jit(solution)/shard_map/ppermute | solution.py:822
  60.3 1.6 %collective-permute-done.5.a_ref = f32[64,128]{1,0:T(8,128)S(1)} collective-permute-done((f32[64,128]{1,0:T(8,128)S(1)}, f32[64,128]{1,0:T(8,128)S(1)}, u32[]{:S(2)}, u32[]{:S(2)}) %collective-permute-start.5) | collective-permute-done | bytes 32800 | tf_op jit(solution)/shard_map/ppermute | solution.py:822
  62.0 4.3 %collective-permute-done.6.b_ref = f32[64,128]{1,0:T(8,128)S(1)} collective-permute-done((f32[64,128]{1,0:T(8,128)S(1)}, f32[64,128]{1,0:T(8,128)S(1)}, u32[]{:S(2)}, u32[]{:S(2)}) %collective-permute-start.6) | collective-permute-done | bytes 32800 | tf_op jit(solution)/shard_map/ppermute | solution.py:822
  66.3 2.7 %shard_map.123 = (f32[512,128]{1,0:T(8,128)S(1)}, f32[512,128]{1,0:T(8,128)S(1)}, f32[512,128]{1,0:T(8,128)S(1)}, f32[256,128]{1,0:T(8,128)S(1)}) custom-call(f32[512,128]{1,0:T(8,128)S(1)} %get-tuple-element.66.w_ref, f32[512,128]{1,0:T(8,128)S(1)} %get-tuple-element.67.res_in_ref, f32[512,128]{1,0:T(8,128)S(1)} %get-tuple-element.68.upd_ref, ...), custom_call_target="tpu_custom_call" | custom-call | tf_op jit(solution)/shard_map/pallas_call | solution.py:795
  68.9 14.6 %all_to_all.21 = f32[64,4,128]{2,1,0:T(4,128)S(1)} all-to-all(f32[64,4,128]{2,1,0:T(4,128)S(1)} %bitcast.21), channel_id=1, replica_groups=mesh['sess'=2,'elem'=64] {'elem'}, dimensions={0} | all-to-all | bytes 262144 | tf_op jit(solution)/shard_map/all_to_all | solution.py:957
  85.0 2.2 %collective-permute-start.8 = (f32[64,128]{1,0:T(8,128)S(1)}, f32[64,128]{1,0:T(8,128)S(1)}, u32[]{:S(2)}, u32[]{:S(2)}) collective-permute-start(f32[64,128]{1,0:T(8,128)S(1)} %get-tuple-element.83), channel_id=1, source_target_pairs={{0,64},{1,2},{2,1},{3,4},{4,3},{5,6},{6,5},{7,8},{8,7},{9,10},{10,... | collective-permute-start | bytes 98312 | tf_op jit(solution)/shard_map/ppermute | solution.py:822
  88.4 4.8 %collective-permute-done.8.refs_4_ = f32[64,128]{1,0:T(8,128)S(1)} collective-permute-done((f32[64,128]{1,0:T(8,128)S(1)}, f32[64,128]{1,0:T(8,128)S(1)}, u32[]{:S(2)}, u32[]{:S(2)}) %collective-permute-start.8) | collective-permute-done | bytes 32800 | tf_op jit(solution)/shard_map/ppermute | solution.py:822
  93.1 2.4 %shard_map.125 = (f32[512,128]{1,0:T(8,128)S(1)}, f32[512,128]{1,0:T(8,128)S(1)}, f32[512,128]{1,0:T(8,128)S(1)}, f32[512,128]{1,0:T(8,128)S(1)}, f32[64,128]{1,0:T(8,128)S(1)}, /*index=5*/f32[64,128]{1,0:T(8,128)S(1)}) custom-call(f32[512,128]{1,0:T(8,128)S(1)} %get-tuple-element.75.base_ref.refs_0_, f32[512,128]{1,0:T(8,128)S(1)} %get-tuple-element.80.refs_1_, ...), custom_call_target="tpu_custom_call" | custom-call | tf_op jit(solution)/shard_map/pallas_call | solution.py:795
  95.6 2.3 %collective-permute-start.10 = (f32[64,128]{1,0:T(8,128)S(1)}, f32[64,128]{1,0:T(8,128)S(1)}, u32[]{:S(2)}, u32[]{:S(2)}) collective-permute-start(f32[64,128]{1,0:T(8,128)S(1)} %get-tuple-element.89), channel_id=1, source_target_pairs={{0,64},{1,2},{2,1},{3,4},{4,3},{5,6},{6,5},{7,8},{8,7},{9,10},{10,... | collective-permute-start | bytes 98312 | tf_op jit(solution)/shard_map/ppermute | solution.py:822
  97.8 1.6 %collective-permute-done.9.refs_5_ = f32[64,128]{1,0:T(8,128)S(1)} collective-permute-done((f32[64,128]{1,0:T(8,128)S(1)}, f32[64,128]{1,0:T(8,128)S(1)}, u32[]{:S(2)}, u32[]{:S(2)}) %collective-permute-start.9) | collective-permute-done | bytes 32800 | tf_op jit(solution)/shard_map/ppermute | solution.py:822
  99.5 4.3 %collective-permute-done.10.refs_6_ = f32[64,128]{1,0:T(8,128)S(1)} collective-permute-done((f32[64,128]{1,0:T(8,128)S(1)}, f32[64,128]{1,0:T(8,128)S(1)}, u32[]{:S(2)}, u32[]{:S(2)}) %collective-permute-start.10) | collective-permute-done | bytes 32800 | tf_op jit(solution)/shard_map/ppermute | solution.py:822
  103.8 2.1 %shard_map.126 = f32[512,128]{1,0:T(8,128)} custom-call(f32[512,128]{1,0:T(8,128)S(1)} %get-tuple-element.84.refs_0_, f32[512,128]{1,0:T(8,128)S(1)} %get-tuple-element.85.refs_1_, f32[512,128]{1,0:T(8,128)S(1)} %get-tuple-element.86.refs_2_, f32[512,128]{1,0:T(8,128)S(1)} %get-tuple-element.87.refs_3_, ...), custom_call_target="tpu_custom_call" | custom-call | tf_op jit(solution)/shard_map/pallas_call | solution.py:795
  (22 shorter events, 7.5 us)
Async XLA Ops:
  0.0 27.3 %collective-permute-start = (f32[512,128]{1,0:T(8,128)}, f32[512,128]{1,0:T(8,128)S(1)}, u32[]{:S(2)}, u32[]{:S(2)}) collective-permute-start(f32[512,128]{1,0:T(8,128)} %bitcast.28), channel_id=1, source_target_pairs={{0,64},{64,0},{1,65},{65,1},{2,66},{66,2},{3,67},{67,3},{4,68},{68... | collective-permute-start | bytes 786440 | tf_op jit(solution)/shard_map/ppermute | solution.py:842
  3.3 24.0 %all-to-all-start = ((f32[64,8,128]{2,1,0:T(8,128)}), f32[64,8,128]{2,1,0:T(8,128)S(1)}, u32[]{:S(2)}, u32[]{:S(2)}) async-start(f32[64,8,128]{2,1,0:T(8,128)} %bitcast.2), calls=%async_computation | async-start | bytes 524288 | tf_op jit(solution)/shard_map/all_to_all | solution.py:858
  20.8 0.5 copy-start.1
  21.3 28.3 %collective-permute-start.3 = (f32[384,128]{1,0:T(8,128)}, f32[384,128]{1,0:T(8,128)S(1)}, u32[]{:S(2)}, u32[]{:S(2)}) collective-permute-start(f32[384,128]{1,0:T(8,128)} %get-tuple-element.63), channel_id=1, source_target_pairs={{0,1},{1,0},{2,3},{3,2},{4,5},{5,4},{6,7},{7,6},{8,9},{9,8},{10,11... | collective-permute-start | bytes 589832 | tf_op jit(solution)/shard_map/ppermute | solution.py:822
  22.8 26.9 %collective-permute-start.4 = (f32[384,128]{1,0:T(8,128)}, f32[384,128]{1,0:T(8,128)S(1)}, u32[]{:S(2)}, u32[]{:S(2)}) collective-permute-start(f32[384,128]{1,0:T(8,128)} %get-tuple-element.64), channel_id=1, source_target_pairs={{0,64},{1,2},{2,1},{3,4},{4,3},{5,6},{6,5},{7,8},{8,7},{9,10},{10,... | collective-permute-start | bytes 589832 | tf_op jit(solution)/shard_map/ppermute | solution.py:822
  27.3 0.6 copy-start.2
  29.1 0.6 copy-start
  29.8 0.5 copy-start.3
  30.3 14.3 %all-to-all-start.1 = ((f32[64,1,128]{2,1,0:T(1,128)}), f32[64,1,128]{2,1,0:T(1,128)S(1)}, u32[]{:S(2)}, u32[]{:S(2)}) async-start(f32[64,1,128]{2,1,0:T(1,128)} %bitcast.22), calls=%async_computation.1 | async-start | bytes 65536 | tf_op jit(solution)/shard_map/all_to_all | solution.py:904
  44.6 0.6 copy-start.4
  46.8 4.0 %collective-permute-start.1 = (f32[64,128]{1,0:T(8,128)S(1)}, f32[64,128]{1,0:T(8,128)S(1)}, u32[]{:S(2)}, u32[]{:S(2)}) collective-permute-start(f32[64,128]{1,0:T(8,128)S(1)} %get-tuple-element.61), channel_id=1, source_target_pairs={{0,1},{1,0},{2,3},{3,2},{4,5},{5,4},{6,7},{7,6},{8,9},{9,8},{10,11... | collective-permute-start | bytes 98312 | tf_op jit(solution)/shard_map/ppermute | solution.py:822
  47.5 8.1 %collective-permute-start.2 = (f32[64,128]{1,0:T(8,128)S(1)}, f32[64,128]{1,0:T(8,128)S(1)}, u32[]{:S(2)}, u32[]{:S(2)}) collective-permute-start(f32[64,128]{1,0:T(8,128)S(1)} %get-tuple-element.62), channel_id=1, source_target_pairs={{0,64},{1,2},{2,1},{3,4},{4,3},{5,6},{6,5},{7,8},{8,7},{9,10},{10,... | collective-permute-start | bytes 98312 | tf_op jit(solution)/shard_map/ppermute | solution.py:822
  58.0 4.0 %collective-permute-start.5 = (f32[64,128]{1,0:T(8,128)S(1)}, f32[64,128]{1,0:T(8,128)S(1)}, u32[]{:S(2)}, u32[]{:S(2)}) collective-permute-start(f32[64,128]{1,0:T(8,128)S(1)} %get-tuple-element.71), channel_id=1, source_target_pairs={{0,1},{1,0},{2,3},{3,2},{4,5},{5,4},{6,7},{7,6},{8,9},{9,8},{10,11... | collective-permute-start | bytes 98312 | tf_op jit(solution)/shard_map/ppermute | solution.py:822
  58.0 8.2 %collective-permute-start.6 = (f32[64,128]{1,0:T(8,128)S(1)}, f32[64,128]{1,0:T(8,128)S(1)}, u32[]{:S(2)}, u32[]{:S(2)}) collective-permute-start(f32[64,128]{1,0:T(8,128)S(1)} %get-tuple-element.72), channel_id=1, source_target_pairs={{0,64},{1,2},{2,1},{3,4},{4,3},{5,6},{6,5},{7,8},{8,7},{9,10},{10,... | collective-permute-start | bytes 98312 | tf_op jit(solution)/shard_map/ppermute | solution.py:822
  84.4 4.0 %collective-permute-start.7 = (f32[64,128]{1,0:T(8,128)S(1)}, f32[64,128]{1,0:T(8,128)S(1)}, u32[]{:S(2)}, u32[]{:S(2)}) collective-permute-start(f32[64,128]{1,0:T(8,128)S(1)} %get-tuple-element.82), channel_id=1, source_target_pairs={{0,1},{1,0},{2,3},{3,2},{4,5},{5,4},{6,7},{7,6},{8,9},{9,8},{10,11... | collective-permute-start | bytes 98312 | tf_op jit(solution)/shard_map/ppermute | solution.py:822
  85.0 8.1 %collective-permute-start.8 = (f32[64,128]{1,0:T(8,128)S(1)}, f32[64,128]{1,0:T(8,128)S(1)}, u32[]{:S(2)}, u32[]{:S(2)}) collective-permute-start(f32[64,128]{1,0:T(8,128)S(1)} %get-tuple-element.83), channel_id=1, source_target_pairs={{0,64},{1,2},{2,1},{3,4},{4,3},{5,6},{6,5},{7,8},{8,7},{9,10},{10,... | collective-permute-start | bytes 98312 | tf_op jit(solution)/shard_map/ppermute | solution.py:822
  95.5 4.0 %collective-permute-start.9 = (f32[64,128]{1,0:T(8,128)S(1)}, f32[64,128]{1,0:T(8,128)S(1)}, u32[]{:S(2)}, u32[]{:S(2)}) collective-permute-start(f32[64,128]{1,0:T(8,128)S(1)} %get-tuple-element.88), channel_id=1, source_target_pairs={{0,1},{1,0},{2,3},{3,2},{4,5},{5,4},{6,7},{7,6},{8,9},{9,8},{10,11... | collective-permute-start | bytes 98312 | tf_op jit(solution)/shard_map/ppermute | solution.py:822
  95.6 8.2 %collective-permute-start.10 = (f32[64,128]{1,0:T(8,128)S(1)}, f32[64,128]{1,0:T(8,128)S(1)}, u32[]{:S(2)}, u32[]{:S(2)}) collective-permute-start(f32[64,128]{1,0:T(8,128)S(1)} %get-tuple-element.89), channel_id=1, source_target_pairs={{0,64},{1,2},{2,1},{3,4},{4,3},{5,6},{6,5},{7,8},{8,7},{9,10},{10,... | collective-permute-start | bytes 98312 | tf_op jit(solution)/shard_map/ppermute | solution.py:822

commit v7 on v6

--- a/solution.py
+++ b/solution.py
@@ -313,10 +313,9 @@
     ]
 
 
-def send_planes(w_ref, next_ref, coef_ref, work_ref, a_ref, b_ref, even):
+def inner_planes(next_ref, coef_ref, out_ref, row):
     first = first_layer((8, 128))
     ends = end_rows()
-    work_ref[0:64] = blend(w_ref[0:64], w_ref[448:512])
     for j in range(8):
         cols = [next_ref[k * 64 + j * 8 : k * 64 + j * 8 + 8] for k in range(8)]
         cols[0] = jnp.where(first, 0.0, cols[0])
@@ -327,9 +326,100 @@
             at = 1024 + c * 64 + j * 8
             term = grad[c] * coef_ref[at : at + 8] * ends[c]
             total = term if total is None else total + term
-        work_ref[64 + j * 8 : 72 + j * 8] = total
+        out_ref[row + j * 8 : row + j * 8 + 8] = total
+
+
+def send_planes(w_ref, next_ref, coef_ref, work_ref, a_ref, b_ref, even):
+    work_ref[0:64] = blend(w_ref[0:64], w_ref[448:512])
+    inner_planes(next_ref, coef_ref, work_ref, 64)
     both = work_ref[...]
     pack(both, both, a_ref, b_ref, 0, even)
+
+
+def shift_x(src_ref, dst_ref, count):
+    rows = count * NP
+    col = iota((rows, 128), 1) % EX
+    dst_ref[...] = jnp.zeros(dst_ref.shape, f32)
+    low = pltpu.roll(src_ref[pl.ds(7, rows, stride=8), :], 1, 1)
+    high = pltpu.roll(src_ref[pl.ds(0, rows, stride=8), :], 127, 1)
+    dst_ref[pl.ds(0, rows, stride=8), :] = jnp.where(col > 0, low, 0.0)
+    dst_ref[pl.ds(7, rows, stride=8), :] = jnp.where(col < EX - 1, high, 0.0)
+
+
+def shift_y(src_ref, dst_ref, count):
+    line = (iota((8, 128), 1) // EX) % EY
+    dst_ref[...] = jnp.zeros(dst_ref.shape, f32)
+    for k in range(count):
+        low = pltpu.roll(src_ref[k * 64 + 56 : k * 64 + 64], EX, 1)
+        high = pltpu.roll(src_ref[k * 64 : k * 64 + 8], 128 - EX, 1)
+        dst_ref[k * 64 : k * 64 + 8] = jnp.where(line > 0, low, 0.0)
+        dst_ref[k * 64 + 56 : k * 64 + 64] = jnp.where(line < EY - 1, high, 0.0)
+
+
+def correction_shares(coef_ref, mass_ref, invd_ref, out_ref, next_ref, x_ref, y_ref, face_ref, side_ref):
+    scaled = STEPS[0][1]
+    next_ref[...] = mass_ref[...] * invd_ref[...] * scaled
+    inner_planes(next_ref, coef_ref, out_ref, 0)
+    shift_x(mass_ref, x_ref, NP)
+    next_ref[...] = x_ref[...] * invd_ref[...] * scaled
+    inner_planes(next_ref, coef_ref, out_ref, 64)
+    shift_y(mass_ref, y_ref, NP)
+    next_ref[...] = y_ref[...] * invd_ref[...] * scaled
+    inner_planes(next_ref, coef_ref, out_ref, 128)
+    shift_y(x_ref, y_ref, NP)
+    next_ref[...] = y_ref[...] * invd_ref[...] * scaled
+    inner_planes(next_ref, coef_ref, out_ref, 192)
+    first = first_layer((8, 128))
+    ends = end_rows()
+    weights = [
+        ends[c] * jnp.where(first, float(DERIV[c, 7]), float(DERIV[c, 0]))
+        for c in range(8)
+    ]
+    for j in range(8):
+        total = None
+        for c in range(8):
+            at = 1024 + c * 64 + j * 8
+            term = coef_ref[at : at + 8] * weights[c]
+            total = term if total is None else total + term
+        at = slice(j * 8, j * 8 + 8)
+        inv = blend(invd_ref[448 + j * 8 : 456 + j * 8], invd_ref[at])
+        next_ref[at] = total * inv * scaled
+    share = next_ref[0:64]
+    face_ref[...] = pltpu.roll(blend(mass_ref[448:512], mass_ref[0:64]), LAYER, 1)
+    out_ref[256:320] = share * face_ref[...]
+    shift_x(face_ref, side_ref, 1)
+    out_ref[320:384] = share * side_ref[...]
+    shift_y(face_ref, next_ref.at[64:128], 1)
+    out_ref[384:448] = share * next_ref[64:128]
+    shift_y(side_ref, next_ref.at[64:128], 1)
+    out_ref[448:512] = share * next_ref[64:128]
+
+
+def correction_inner(shares, near, behind):
+    node = iota((64, 128), 0)
+    left, front = node % 8 == 0, node < 8
+    total = None
+    for base, row in ((0, near), (256, behind)):
+        row = jnp.broadcast_to(row, (64, 128))
+
+        def turn(count):
+            return pltpu.roll(row, count % 128, 1)
+
+        values = [
+            row,
+            jnp.where(left, turn(1), turn(-1)),
+            jnp.where(front, turn(8), turn(-8)),
+            jnp.where(
+                front,
+                jnp.where(left, turn(9), turn(7)),
+                jnp.where(left, turn(-7), turn(-9)),
+            ),
+        ]
+        for n, value in enumerate(values):
+            at = base + n * 64
+            term = shares[at : at + 64] * value
+            total = term if total is None else total + term
+    return total
 
 
 def ghost_side(update_ref, inner, planes_ref, face_ref, side_ref):
@@ -397,8 +487,9 @@
     lax.fori_loop(0, 8, per_j, 0)
 
 
-BASIS_ROW = 128
-GHOST_ROWS = BASIS_ROW + 256
+SHARE_ROW = 192
+BASIS_ROW = SHARE_ROW + 256
+GHOST_ROWS = BASIS_ROW + 512
 
 
 def setup_kernel(
@@ -411,9 +502,8 @@
     inverse_hbm,
     coef_ref,
     mass_ref,
-    start_ref,
     static_ref,
-    diag_ref,
+    faces_ref,
     invd_ref,
     inv_ref,
     basis_ref,
@@ -428,6 +518,13 @@
     basis_in,
     inverse_in,
     tmp_ref,
+    start_ref,
+    diag_ref,
+    share_ref,
+    x_ref,
+    y_ref,
+    face_ref,
+    side_ref,
     sems,
 ):
     copies = [
@@ -487,17 +584,25 @@
             blend(coef_ref[512:576], coef_ref[960:1024]),
             blend(mass_ref[0:64], mass_ref[448:512]) + tmp_ref[0:64],
             blend(diag_ref[0:64], diag_ref[448:512]),
+            blend(mass_ref[0:64], mass_ref[448:512]),
+            zeros,
         ],
         axis=0,
     )
+    faces_ref[0:64] = diag_ref[0:64]
+    faces_ref[64:128] = diag_ref[448:512]
     even = where_am_i()[0]
     pack(planes, planes, a_ref, b_ref, 0, even)
+    correction_shares(
+        coef_ref, mass_ref, invd_ref, share_ref, tmp_ref, x_ref, y_ref, face_ref, side_ref
+    )
+    shares = share_ref[...]
+    pack(shares, shares, a_ref, b_ref, SHARE_ROW, even)
     for c in range(NC // 128):
-        at = BASIS_ROW + c * 64
-        up = basis[LAYER:, c * 128 : c * 128 + 128]
-        down = basis[:LAYER, c * 128 : c * 128 + 128]
-        a_ref[at : at + 64] = jnp.where(even, up, down)
-        b_ref[at : at + 64] = jnp.where(even, down, up)
+        at = BASIS_ROW + c * 128
+        cols = basis[:, c * 128 : c * 128 + 128]
+        a_ref[at : at + 128] = cols
+        b_ref[at : at + 128] = cols
 
 
 def send_first(y_ref, base, invd, coef_ref, next_ref, work_ref, a_ref, b_ref):
@@ -551,9 +656,9 @@
     place,
     base_ref,
     y_ref,
-    cur_in_ref,
-    a_ref,
-    b_ref,
+    cur_in,
+    raw,
+    inner,
     invd_ref,
     planes_ref,
     coef_ref,
@@ -569,13 +674,12 @@
     face_ref,
     side_ref,
 ):
-    came = unpack(a_ref, b_ref, 0, 64, place)
-    residual = coupled(y_ref, came[0:64], came[0:64])
+    residual = coupled(y_ref, raw, raw)
     if base_ref is not None:
         residual = residual + base_ref[...]
     update = residual * invd_ref[...] * STEPS[0][1]
     upd_ref[...] = update
-    ghost_side(upd_ref, came[64:128], planes_ref, face_ref, side_ref)
+    ghost_side(upd_ref, inner, planes_ref, face_ref, side_ref)
     stiff_apply(upd_ref, coef_ref, mass_ref, w_ref)
     in_plane(w_ref)
     residual = residual - coupled(w_ref, side_ref[...], side_ref[...])
@@ -583,7 +687,8 @@
     alpha, beta = STEPS[1]
     second = alpha * update + beta * invd_ref[...] * residual
     upd_ref[...] = second
-    cur_ref[...] = cur_in_ref[...] + (update + second)
+    done = update + second
+    cur_ref[...] = done if cur_in is None else cur_in + done
     stiff_apply(upd_ref, coef_ref, mass_ref, w_ref)
     in_plane(w_ref)
     alpha, beta = STEPS[2]
@@ -596,9 +701,8 @@
 
 def start_kernel(
     y_ref,
-    diag_ref,
+    faces_ref,
     invd_in_ref,
-    cur_in_ref,
     a_ref,
     b_ref,
     ga_ref,
@@ -616,19 +720,20 @@
     *scratch,
 ):
     place = where_am_i()
-    planes = unpack(ga_ref, gb_ref, 0, 128, place)
-    planes_ref[...] = planes[0:192]
+    planes = unpack(ga_ref, gb_ref, 0, SHARE_ROW, place)
+    planes_ref[...] = planes[0:320]
+    came = unpack(a_ref, b_ref, 0, 64, place)
     bottom, top = through(
-        diag_ref[0:64], diag_ref[448:512], planes[192:256], planes[192:256]
+        faces_ref[0:64], faces_ref[64:128], planes[192:256], planes[192:256]
     )
     invd_ref[...] = whole(1.0 / bottom, invd_in_ref, 1.0 / top)
     opening_half(
         place,
         None,
         y_ref,
-        cur_in_ref,
-        a_ref,
-        b_ref,
+        None,
+        came[0:64],
+        came[64:128],
         invd_ref,
         planes_ref,
         coef_ref,
@@ -643,8 +748,104 @@
     )
 
 
-def again_kernel(*refs):
-    opening_half(where_am_i(), *refs)
+def near_kernel(
+    ga_ref, gb_ref, inverse_ref, after_ref, out_ref, shares_hbm, shares_ref, sems
+):
+    place = where_am_i()
+    blocks = []
+    for c in range(NC // 128):
+        at = BASIS_ROW + c * 128
+        below, above = beside(ga_ref[at : at + 128], gb_ref[at : at + 128], place)
+        blocks.append(jnp.concatenate([above, below], axis=0))
+    rows = jnp.concatenate(blocks, axis=1)
+    shares_ref[...] = unpack(ga_ref, gb_ref, SHARE_ROW, 256, place)
+    copy = pltpu.make_async_copy(shares_ref, shares_hbm, sems.at[0])
+    copy.start()
+    out_ref[...] = dot_nn(rows, inverse_ref[...], exact_mode)
+    copy.wait()
+
+
+def again_kernel(
+    parts_ref,
+    solve_ref,
+    near_ref,
+    shares_hbm,
+    base_hbm,
+    a_ref,
+    b_ref,
+    invd_ref,
+    planes_ref,
+    coef_ref,
+    mass_ref,
+    res_ref,
+    upd_ref,
+    cur_ref,
+    w_ref,
+    a_out_ref,
+    b_out_ref,
+    y_ref,
+    next_ref,
+    work_ref,
+    face_ref,
+    side_ref,
+    shares_ref,
+    base_ref,
+    sems,
+):
+    copies = [
+        pltpu.make_async_copy(shares_hbm, shares_ref, sems.at[0]),
+        pltpu.make_async_copy(base_hbm, base_ref, sems.at[1]),
+    ]
+    for copy in copies:
+        copy.start()
+    place = where_am_i()
+    total = parts_ref[0:8]
+    for n in range(1, OWNERS * NC // 1024):
+        total = total + parts_ref[n * 8 : n * 8 + 8]
+    total = total + pltpu.roll(total, 4, 0)
+    both = None
+    for c in range(NC // 128):
+        row = jnp.broadcast_to(total[c : c + 1], (8, 128))
+        cols = slice(c * 128, c * 128 + 128)
+        rows = jnp.concatenate([solve_ref[:, cols], near_ref[:, cols]], axis=0)
+        term = dot_nt(row, rows, exact_mode)
+        both = term if both is None else both + term
+    correction = both[0:1, 0:128]
+    above, below = both[0:1, 128:256], both[0:1, 256:384]
+    first = first_layer((1, 128))
+    near = jnp.where(first, above, below)
+    behind = pltpu.roll(jnp.broadcast_to(jnp.where(first, below, above), (8, 128)), LAYER, 1)
+    y_ref[...] = mass_ref[...] * (-correction)
+    in_plane(y_ref)
+    came = unpack(a_ref, b_ref, 0, 64, place)
+    side_ref[...] = planes_ref[256:320] * near
+    in_plane(side_ref, 1)
+    raw = -(came[0:64] + side_ref[...])
+    for copy in copies:
+        copy.wait()
+    inner = came[64:128] - correction_inner(shares_ref, near, behind[0:1])
+    opening_half(
+        place,
+        base_ref,
+        y_ref,
+        correction,
+        raw,
+        inner,
+        invd_ref,
+        planes_ref,
+        coef_ref,
+        mass_ref,
+        res_ref,
+        upd_ref,
+        cur_ref,
+        w_ref,
+        a_out_ref,
+        b_out_ref,
+        next_ref,
+        work_ref,
+        face_ref,
+        side_ref,
+    )
 
 
 def closing_half(
@@ -692,12 +893,20 @@
     basis_ref,
     ga_ref,
     gb_ref,
-    res_ref,
+    local_hbm,
+    cur_hbm,
+    part_ref,
+    a_out_ref,
+    b_out_ref,
+    w_out_ref,
+    vec_ref,
     cur_ref,
-    w_out_ref,
-    part_ref,
-    vec_ref,
-    *scratch,
+    local_ref,
+    next_ref,
+    work_ref,
+    face_ref,
+    side_ref,
+    sems,
 ):
     residual, current = closing_half(
         w_ref,
@@ -712,75 +921,64 @@
         mass_ref,
         w_out_ref,
         vec_ref,
-        *scratch,
-    )
-    res_ref[...] = residual
+        face_ref,
+        side_ref,
+    )
+    local_ref[...] = residual
     cur_ref[...] = current
+    copy = pltpu.make_async_copy(cur_ref, cur_hbm, sems.at[0])
+    copy.start()
     stiff_apply(vec_ref, coef_ref, mass_ref, w_out_ref)
     in_plane(w_out_ref)
     zeros = jnp.zeros((64, 128), f32)
-    local = res_ref[...] - coupled(w_out_ref, zeros, zeros)
+    local = local_ref[...] - coupled(w_out_ref, zeros, zeros)
+    local_ref[...] = local
+    second = pltpu.make_async_copy(local_ref, local_hbm, sems.at[1])
+    second.start()
+    next_ref[...] = local * invd_ref[...] * STEPS[0][1]
+    place = where_am_i()
+    send_planes(w_out_ref, next_ref, coef_ref, work_ref, a_out_ref, b_out_ref, place[0])
     sums = jnp.sum(local, axis=0, keepdims=True)
     bottom = -jnp.sum(w_out_ref[0:64], axis=0, keepdims=True)
     top = -jnp.sum(w_out_ref[448:512], axis=0, keepdims=True)
     outer = jnp.where(first_layer((1, 128)), bottom, top)
     left = jnp.broadcast_to(jnp.concatenate([sums, outer], axis=1), (8, 256))
-    place = where_am_i()
     blocks = []
     for c in range(NC // 128):
-        at = BASIS_ROW + c * 64
-        below, above = beside(ga_ref[at : at + 64], gb_ref[at : at + 64], place)
+        at = BASIS_ROW + c * 128
+        below, above = beside(ga_ref[at : at + 128], gb_ref[at : at + 128], place)
         own = basis_ref[:, c * 128 : c * 128 + 128]
-        right = jnp.concatenate([own, below, above], axis=0)
+        right = jnp.concatenate([own, below[LAYER:], above[:LAYER]], axis=0)
         part = dot_nn(left, right, exact_mode)[0:1]
         blocks.append(part * (1.0 / math.sqrt(NODES)))
     eight = jnp.concatenate(blocks + blocks, axis=0)
     for n in range(OWNERS * NC // 1024):
         part_ref[n * 8 : n * 8 + 8] = eight
-
-
-def restart_kernel(
-    parts_ref,
-    solve_ref,
-    mass_ref,
-    w_ref,
-    base_ref,
-    cur_in_ref,
-    invd_ref,
-    coef_ref,
-    y_ref,
-    cur_ref,
-    a_ref,
-    b_ref,
-    next_ref,
-    work_ref,
-):
-    total = parts_ref[0:8]
-    for n in range(1, OWNERS * NC // 1024):
-        total = total + parts_ref[n * 8 : n * 8 + 8]
-    total = total + pltpu.roll(total, 4, 0)
-    correction = None
-    for c in range(NC // 128):
-        row = jnp.broadcast_to(total[c : c + 1], (8, 128))
-        term = dot_nt(row, solve_ref[:, c * 128 : c * 128 + 128], exact_mode)
-        correction = term if correction is None else correction + term
-    correction = correction[0:1]
-    cur_ref[...] = cur_in_ref[...] + correction
-    y_ref[...] = mass_ref[...] * correction
-    in_plane(y_ref)
-    y_ref[...] = -(y_ref[...] + w_ref[...])
-    send_first(
-        y_ref, base_ref[...], invd_ref[...], coef_ref, next_ref, work_ref, a_ref, b_ref
-    )
+    copy.wait()
+    second.wait()
 
 
 def last_kernel(*refs):
-    inputs, (order_ref, out_ref), scratch = refs[:10], refs[10:12], refs[12:]
+    inputs, (order_ref, field_hbm, first_hbm, out_ref), rest = (
+        refs[:10],
+        refs[10:14],
+        refs[14:],
+    )
+    scratch, (field_in, first_in, sems) = rest[:-3], rest[-3:]
+    copies = [
+        pltpu.make_async_copy(field_hbm, field_in, sems.at[0]),
+        pltpu.make_async_copy(first_hbm, first_in, sems.at[1]),
+    ]
+    for copy in copies:
+        copy.start()
     current = closing_half(*inputs, *scratch)[1]
-    out_ref[...] = take_lanes(current, order_ref[...])
-
-
-def call(kernel, outs, *args, scratch=(), smem=(), far=(), near=(), copies=0):
+    for copy in copies:
+        copy.wait()
+    moved = take_lanes(first_in[...] + current, order_ref[...])
+    out_ref[...] = field_in[...] + moved
+
+
+def call(kernel, outs, *args, scratch=(), smem=(), far=(), near=(), copies=0, away=()):
     def stay(x):
         return pltpu.with_memory_space_constraint(x, pltpu.HBM)
 
@@ -794,9 +992,15 @@
         scratches.append(pltpu.SemaphoreType.DMA((copies,)))
     return pl.pallas_call(
         kernel,
-        out_shape=[jax.ShapeDtypeStruct(s, d) for s, d in outs],
+        out_shape=[
+            pltpu.HBM(s, d) if n in away else jax.ShapeDtypeStruct(s, d)
+            for n, (s, d) in enumerate(outs)
+        ],
         in_specs=[pl.BlockSpec(memory_space=space(n)) for n in range(len(args))],
-        out_specs=[pl.BlockSpec(memory_space=pltpu.VMEM) for _ in outs],
+        out_specs=[
+            pl.BlockSpec(memory_space=pltpu.HBM if n in away else pltpu.VMEM)
+            for n in range(len(outs))
+        ],
         scratch_shapes=scratches,
         compiler_params=pltpu.CompilerParams(vmem_limit_bytes=20 << 20),
     )(*[stay(x) if n in far + near else x for n, x in enumerate(args)])
@@ -858,14 +1062,13 @@
     received = lax.all_to_all(
         send.reshape(OWNERS, ASK, 128), "elem", split_axis=0, concat_axis=0, tiled=True
     )
-    coef, mass, start, static, diag, invd, inv, basis, solve, order, ga, gb = call(
+    coef, mass, static, faces, invd, inv, basis, solve, order, ga, gb = call(
         setup_kernel,
         [
             ((3 * NODES, 128), f32),
             FIELD,
             FIELD,
-            FIELD,
-            FIELD,
+            ((128, 128), f32),
             FIELD,
             ((1, 128), jnp.int32),
             ((128, NC), f32),
@@ -891,6 +1094,13 @@
             (128, NC),
             (NC, NC),
             (NODES, 128),
+            (NODES, 128),
+            (NODES, 128),
+            (NODES, 128),
+            (NODES, 128),
+            (NODES, 128),
+            (64, 128),
+            (64, 128),
         ],
         copies=6,
     )
@@ -922,11 +1132,10 @@
     half = [FIELD, FIELD, FIELD, FIELD, SIDE_MSG, SIDE_MSG]
     res, upd, cur, w, a, b, invd, planes = call(
         start_kernel,
-        half + [FIELD, ((192, 128), f32)],
+        half + [FIELD, ((320, 128), f32)],
         y,
-        diag,
+        faces,
         invd,
-        start,
         a,
         b,
         ga,
@@ -936,9 +1145,9 @@
         scratch=SEND_WORK + SIDE_WORK,
     )
     a, b = exchange(a, b)
-    res, cur, w, part = call(
+    res, total, part, a, b = call(
         middle_kernel,
-        [FIELD, FIELD, FIELD, ((OWNERS * NC // 128, 128), f32)],
+        [FIELD, FIELD, ((OWNERS * NC // 128, 128), f32), SIDE_MSG, SIDE_MSG],
         w,
         res,
         upd,
@@ -952,7 +1161,21 @@
         basis,
         ga,
         gb,
-        scratch=[(NODES, 128)] + SIDE_WORK,
+        scratch=[(NODES, 128)] * 4 + SEND_WORK + SIDE_WORK,
+        copies=2,
+        away=(0, 1),
+    )
+    near, shares = call(
+        near_kernel,
+        [((256, NC), f32), FIELD],
+        ga,
+        gb,
+        coarse_inverse.reshape(NC, NC),
+        a,
+        near=(2,),
+        scratch=[(NODES, 128)],
+        copies=1,
+        away=(1,),
     )
     parts = lax.all_to_all(
         part.reshape(OWNERS, NC // 128, 128),
@@ -961,33 +1184,24 @@
         concat_axis=0,
         tiled=True,
     )
-    y, cur, a, b = call(
-        restart_kernel,
-        [FIELD, FIELD, SIDE_MSG, SIDE_MSG],
-        parts.reshape(OWNERS * NC // 128, 128),
-        solve,
-        mass,
-        w,
-        res,
-        cur,
-        invd,
-        coef,
-        scratch=SEND_WORK,
-    )
     a, b = exchange(a, b)
     res, upd, cur, w, a, b = call(
         again_kernel,
         half,
+        parts.reshape(OWNERS * NC // 128, 128),
+        solve,
+        near,
+        shares,
         res,
-        y,
-        cur,
         a,
         b,
         invd,
         planes,
         coef,
         mass,
-        scratch=SEND_WORK + SIDE_WORK,
+        far=(3, 4),
+        scratch=[(NODES, 128)] + SEND_WORK + SIDE_WORK + [(NODES, 128)] * 2,
+        copies=2,
     )
     a, b = exchange(a, b)
     (out,) = call(
@@ -1004,7 +1218,11 @@
         coef,
         mass,
         order,
-        scratch=[(NODES, 128), (NODES, 128)] + SIDE_WORK,
+        own_field,
+        total,
+        far=(11, 12),
+        scratch=[(NODES, 128)] * 2 + SIDE_WORK + [(NODES, 128)] * 2,
+        copies=2,
     )
     return out.reshape(1, NP, NP, NP, 128)
 

time: 107 us -> 106 us (level)
  waiting for transfers between devices: 30.6 us -> 24.6 us
  Pallas kernels: 22.5 us -> 27.9 us
  local copies, waits for them, and re-layouts: 2.9 us -> 0.7 us
  starting transfers between devices: 34.6 us -> 35.9 us
    ppermute x10, waiting for transfers between devices: 23.8 us -> 17.7 us  [exchange(): return (lax.ppermute(a, axes, pairs_a), lax.ppermute(b, axes, pairs_b))]
    ppermute x10, starting transfers between devices: 16.2 us -> 21.9 us  [exchange(): return (lax.ppermute(a, axes, pairs_a), lax.ppermute(b, axes, pairs_b))]
    pallas_call x9, Pallas kernels: 22.5 us -> 27.9 us  [call(): pl.pallas_call(kernel, out_shape=[pltpu.HBM(s, d) if n in away else jax.S...]
    all_to_all x1, starting transfers between devices: 11.6 us -> 6.93 us  [one_device(): lax.all_to_all(part.reshape(OWNERS, NC // 128, 128), 'elem', split_axis=0...]
    unnamed x10, local copies, waits for them, and re-layouts: 2.9 us -> 0.7 us
  transfers between devices with their start and end apart: 13 -> 13, of which waited for: 9 -> 8; matrix products, arithmetic and copies ran while one was open for 0% -> 0% of each run, Pallas kernels for 11% -> 9%
where the time goes in v7:
time: 106 us; the launch traced here: 105 us
  starting transfers between devices  35.9 us (34%)
  Pallas kernels  27.9 us (26%)
  waiting for transfers between devices  24.6 us (23%)
  blocking collectives  15.3 us (14%)
    pallas_call x9, Pallas kernels, call(): pl.pallas_call(kernel, out_shape=[pltpu.HBM(s, d) if n in away else jax.S...  27.9 us
    ppermute x10, starting transfers between devices, exchange(): return (lax.ppermute(a, axes, pairs_a), lax.ppermute(b, axes, pairs_b))  21.9 us
    ppermute x10, waiting for transfers between devices, exchange(): return (lax.ppermute(a, axes, pairs_a), lax.ppermute(b, axes, pairs_b))  17.7 us
    all_to_all x1, blocking collectives, one_device(): lax.all_to_all(send.reshape(OWNERS, ASK, 128), 'elem', split_axis=0, conc...  15.3 us
    all_to_all x1, starting transfers between devices, one_device(): lax.all_to_all(answer, 'elem', split_axis=0, concat_axis=0, tiled=True)  7.06 us
    all_to_all x1, starting transfers between devices, one_device(): lax.all_to_all(part.reshape(OWNERS, NC // 128, 128), 'elem', split_axis=0...  6.93 us
    all_to_all x1, waiting for transfers between devices, one_device(): lax.all_to_all(answer, 'elem', split_axis=0, concat_axis=0, tiled=True)  6.9 us
  transfers between devices with their start and end apart: 13, of which 8 were waited for; matrix products, arithmetic and copies ran while one was open for 0% of the time, Pallas kernels for 9%

profile of v7, /device:TPU:6, one launch (start us, length us, event | category | flops | bytes accessed | tf_op | source)
XLA Modules:
  0.0 105.2 jit_solution(7194448888868045582)
XLA Ops:
  0.0 6.7 %shard_map.119 = (f32[1536,128]{1,0:T(8,128)S(1)}, f32[512,128]{1,0:T(8,128)S(1)}, f32[512,128]{1,0:T(8,128)S(1)}, f32[128,128]{1,0:T(8,128)S(1)}, f32[512,128]{...) custom-call(s32[1,128]{1,0:T(1,128)} %bitcast.33, ...), custom_call_target="tpu_custom_call" | custom-call | tf_op jit(solution)/shard_map/pallas_call | solution.py:993
  7.5 1.9 %collective-permute-start.3 = (f32[960,128]{1,0:T(8,128)}, f32[960,128]{1,0:T(8,128)S(1)}, u32[]{:S(2)}, u32[]{:S(2)}) collective-permute-start(f32[960,128]{1,0:T(8,128)} %get-tuple-element.60), channel_id=1, source_target_pairs={{0,1},{1,0},{2,3},{3,2},{4,5},{5,4},{6,7},{7,6},{8,9},{9,8},{10,11... | collective-permute-start | bytes 1474568 | tf_op jit(solution)/shard_map/ppermute | solution.py:1026
  9.4 5.2 %collective-permute-start.4 = (f32[960,128]{1,0:T(8,128)}, f32[960,128]{1,0:T(8,128)S(1)}, u32[]{:S(2)}, u32[]{:S(2)}) collective-permute-start(f32[960,128]{1,0:T(8,128)} %get-tuple-element.61), channel_id=1, source_target_pairs={{0,64},{1,2},{2,1},{3,4},{4,3},{5,6},{6,5},{7,8},{8,7},{9,10},{10,... | collective-permute-start | bytes 1474568 | tf_op jit(solution)/shard_map/ppermute | solution.py:1026
  14.6 2.6 %shard_map.118 = (f32[512,128]{1,0:T(8,128)S(1)}, f32[1,1024]{1,0:T(1,128)S(1)}, s32[1,1024]{1,0:T(1,128)S(1)}, s32[1,1024]{1,0:T(1,128)S(1)}) custom-call(s32[1,1024]{1,0:T(1,128)} %bitcast.32, s32[1,1024]{1,0:T(1,128)} %slot_ref.1, f32[24,1024]{1,0:T(8,128)} %bitcast.31, s32[1,1024]{1,0:T(1,128)} %ids_ref.1), custom_call_target="tpu_custom_call" | custom-call | tf_op jit(solution)/shard_map/pallas_call | solution.py:993
  17.2 15.3 %all_to_all.21 = f32[64,8,128]{2,1,0:T(8,128)S(1)} all-to-all(f32[64,8,128]{2,1,0:T(8,128)S(1)} %bitcast.20), channel_id=1, replica_groups=mesh['sess'=2,'elem'=64] {'elem'}, dimensions={0} | all-to-all | bytes 524288 | tf_op jit(solution)/shard_map/all_to_all | solution.py:1062
  32.4 1.9 %shard_map.120 = (f32[64,128]{1,0:T(8,128)}, s32[1,128]{1,0:T(1,128)S(1)}) custom-call(f32[512,128]{1,0:T(8,128)S(1)} %bitcast.18, f32[512,128]{1,0:T(8,128)S(1)} %collective-permute-done.field_ref, s32[1,128]{1,0:T(1,128)S(1)} %get-tuple-element.47.before_ref), custom_call_target="tpu_custom_call" | custom-call | tf_op jit(solution)/shard_map/pallas_call | solution.py:993
  34.3 7.1 %all-to-all-start.1 = ((f32[64,1,128]{2,1,0:T(1,128)}), f32[64,1,128]{2,1,0:T(1,128)S(1)}, u32[]{:S(2)}, u32[]{:S(2)}) async-start(f32[64,1,128]{2,1,0:T(1,128)} %bitcast.12), calls=%async_computation.1 | async-start | bytes 65536 | tf_op jit(solution)/shard_map/all_to_all | solution.py:1114
  42.0 6.9 %all-to-all-done.1 = f32[64,1,128]{2,1,0:T(1,128)S(1)} async-done(((f32[64,1,128]{2,1,0:T(1,128)}), f32[64,1,128]{2,1,0:T(1,128)S(1)}, u32[]{:S(2)}, u32[]{:S(2)}) %all-to-all-start.1) | async-done | bytes 32800 | tf_op jit(solution)/shard_map/all_to_all | solution.py:1114
  48.9 1.7 %shard_map.121 = (f32[512,128]{1,0:T(8,128)S(1)}, f32[64,128]{1,0:T(8,128)S(1)}, f32[64,128]{1,0:T(8,128)S(1)}) custom-call(f32[64,128]{1,0:T(8,128)S(1)} %bitcast.21, s32[1,1024]{1,0:T(1,128)S(1)} %get-tuple-element.49.owner_ref, f32[1,1024]{1,0:T(1,128)S(1)} %get-tuple-element.50.rank_ref, s32[1,1024]{1,0:T(1,128)S(1)} %get-tuple-element.51.ids_ref, ...), custom_call_target="tpu_custom_call" | custom-call | tf_op jit(solution)/shard_map/pallas_call | solution.py:993
  51.2 2.2 %collective-permute-start.2 = (f32[64,128]{1,0:T(8,128)S(1)}, f32[64,128]{1,0:T(8,128)S(1)}, u32[]{:S(2)}, u32[]{:S(2)}) collective-permute-start(f32[64,128]{1,0:T(8,128)S(1)} %get-tuple-element.59), channel_id=1, source_target_pairs={{0,64},{1,2},{2,1},{3,4},{4,3},{5,6},{6,5},{7,8},{8,7},{9,10},{10,... | collective-permute-start | bytes 98312 | tf_op jit(solution)/shard_map/ppermute | solution.py:1026
  54.6 4.8 %collective-permute-done.2.b_ref = f32[64,128]{1,0:T(8,128)S(1)} collective-permute-done((f32[64,128]{1,0:T(8,128)S(1)}, f32[64,128]{1,0:T(8,128)S(1)}, u32[]{:S(2)}, u32[]{:S(2)}) %collective-permute-start.2) | collective-permute-done | bytes 32800 | tf_op jit(solution)/shard_map/ppermute | solution.py:1026
  59.4 2.4 %shard_map.122 = (f32[512,128]{1,0:T(8,128)S(1)}, f32[512,128]{1,0:T(8,128)S(1)}, f32[512,128]{1,0:T(8,128)S(1)}, f32[512,128]{1,0:T(8,128)S(1)}, f32[64,128]{1,...) custom-call(f32[512,128]{1,0:T(8,128)S(1)} %get-tuple-element.56.y_ref, ...), custom_call_target="tpu_custom_call" | custom-call | tf_op jit(solution)/shard_map/pallas_call | solution.py:993
  61.8 2.3 %collective-permute-start.6 = (f32[64,128]{1,0:T(8,128)S(1)}, f32[64,128]{1,0:T(8,128)S(1)}, u32[]{:S(2)}, u32[]{:S(2)}) collective-permute-start(f32[64,128]{1,0:T(8,128)S(1)} %get-tuple-element.69), channel_id=1, source_target_pairs={{0,64},{1,2},{2,1},{3,4},{4,3},{5,6},{6,5},{7,8},{8,7},{9,10},{10,... | collective-permute-start | bytes 98312 | tf_op jit(solution)/shard_map/ppermute | solution.py:1026
  64.1 1.6 %collective-permute-done.5.a_ref = f32[64,128]{1,0:T(8,128)S(1)} collective-permute-done((f32[64,128]{1,0:T(8,128)S(1)}, f32[64,128]{1,0:T(8,128)S(1)}, u32[]{:S(2)}, u32[]{:S(2)}) %collective-permute-start.5) | collective-permute-done | bytes 32800 | tf_op jit(solution)/shard_map/ppermute | solution.py:1026
  65.7 4.3 %collective-permute-done.6.b_ref = f32[64,128]{1,0:T(8,128)S(1)} collective-permute-done((f32[64,128]{1,0:T(8,128)S(1)}, f32[64,128]{1,0:T(8,128)S(1)}, u32[]{:S(2)}, u32[]{:S(2)}) %collective-permute-start.6) | collective-permute-done | bytes 32800 | tf_op jit(solution)/shard_map/ppermute | solution.py:1026
  70.0 3.9 %shard_map.123 = (f32[512,128]{1,0:T(8,128)}, f32[512,128]{1,0:T(8,128)}, f32[256,128]{1,0:T(8,128)}, f32[64,128]{1,0:T(8,128)S(1)}, f32[64,128]{1,0:T(8,128)S(1)}) custom-call(f32[512,128]{1,0:T(8,128)S(1)} %get-tuple-element.63.w_ref, f32[512,128]{1,0:T(8,128)S(1)} %get-tuple-element.64.res_in_ref, f32[512,128]{1,0:T(8,128)S(1)} %get-tuple-element.65.upd_ref, ...), custom_call_target="tpu_custom_call" | custom-call | tf_op jit(solution)/shard_map/pallas_call | solution.py:993
  74.0 6.9 %all-to-all-start.2 = ((f32[64,4,128]{2,1,0:T(4,128)}), f32[64,4,128]{2,1,0:T(4,128)S(1)}, u32[]{:S(2)}, u32[]{:S(2)}) async-start(f32[64,4,128]{2,1,0:T(4,128)} %bitcast.14), calls=%async_computation.2 | async-start | bytes 262144 | tf_op jit(solution)/shard_map/all_to_all | solution.py:1180
  80.9 5.1 %collective-permute-start.8 = (f32[64,128]{1,0:T(8,128)S(1)}, f32[64,128]{1,0:T(8,128)S(1)}, u32[]{:S(2)}, u32[]{:S(2)}) collective-permute-start(f32[64,128]{1,0:T(8,128)S(1)} %get-tuple-element.78), channel_id=1, source_target_pairs={{0,64},{1,2},{2,1},{3,4},{4,3},{5,6},{6,5},{7,8},{8,7},{9,10},{10,... | collective-permute-start | bytes 98312 | tf_op jit(solution)/shard_map/ppermute | solution.py:1026
  86.1 2.9 %shard_map.124 = (f32[256,512]{1,0:T(8,128)S(1)}, f32[512,128]{1,0:T(8,128)}) custom-call(f32[960,128]{1,0:T(8,128)S(1)} %collective-permute-done.3.ga_ref, f32[960,128]{1,0:T(8,128)S(1)} %collective-permute-done.4.gb_ref, f32[512,512]{1,0:T(8,128)} %bitcast.23, f32[64,128]{1,0:T(8,128)S(1)} %get-tuple-element.74.after_ref), custom_call_target="tpu_custom_call" | custom-call | tf_op jit(solution)/shard_map/pallas_call | solution.py:993
  90.0 3.5 %shard_map.125 = (f32[512,128]{1,0:T(8,128)S(1)}, f32[512,128]{1,0:T(8,128)S(1)}, f32[512,128]{1,0:T(8,128)S(1)}, f32[512,128]{1,0:T(8,128)S(1)}, f32[64,128]{1,0:T(8,128)S(1)}, /*index=5*/f32[64,128]{1,0:T(8,128)S(1)}) custom-call(f32[256,128]{1,0:T(8,128)S(1)} %bitcast.19, f32[128,512]{1,0:T(8,128)S(1)} %get-tuple-element.73.solve_ref, ...), custom_call_target="tpu_custom_call" | custom-call | tf_op jit(solution)/shard_map/pallas_call | solution.py:993
  93.6 1.2 %collective-permute-start.9 = (f32[64,128]{1,0:T(8,128)S(1)}, f32[64,128]{1,0:T(8,128)S(1)}, u32[]{:S(2)}, u32[]{:S(2)}) collective-permute-start(f32[64,128]{1,0:T(8,128)S(1)} %get-tuple-element.83), channel_id=1, source_target_pairs={{0,1},{1,0},{2,3},{3,2},{4,5},{5,4},{6,7},{7,6},{8,9},{9,8},{10,11... | collective-permute-start | bytes 98312 | tf_op jit(solution)/shard_map/ppermute | solution.py:1026
  94.7 3.2 %collective-permute-start.10 = (f32[64,128]{1,0:T(8,128)S(1)}, f32[64,128]{1,0:T(8,128)S(1)}, u32[]{:S(2)}, u32[]{:S(2)}) collective-permute-start(f32[64,128]{1,0:T(8,128)S(1)} %get-tuple-element.84), channel_id=1, source_target_pairs={{0,64},{1,2},{2,1},{3,4},{4,3},{5,6},{6,5},{7,8},{8,7},{9,10},{10,... | collective-permute-start | bytes 98312 | tf_op jit(solution)/shard_map/ppermute | solution.py:1026
  98.0 4.9 %collective-permute-done.10.refs_6_ = f32[64,128]{1,0:T(8,128)S(1)} collective-permute-done((f32[64,128]{1,0:T(8,128)S(1)}, f32[64,128]{1,0:T(8,128)S(1)}, u32[]{:S(2)}, u32[]{:S(2)}) %collective-permute-start.10) | collective-permute-done | bytes 32800 | tf_op jit(solution)/shard_map/ppermute | solution.py:1026
  102.9 2.2 %shard_map.126 = f32[512,128]{1,0:T(8,128)} custom-call(f32[512,128]{1,0:T(8,128)S(1)} %get-tuple-element.79.refs_0_, f32[512,128]{1,0:T(8,128)S(1)} %get-tuple-element.80.refs_1_, f32[512,128]{1,0:T(8,128)S(1)} %get-tuple-element.81.refs_2_, f32[512,128]{1,0:T(8,128)S(1)} %get-tuple-element.82.refs_3_, f32[512,128]{1,0:T(8,128)S(1)} %get-tuple-element.67.invd_ref.refs_4_, ...), custom_call_target="tpu_custom_call" | custom-call | tf_op jit(solution)/shard_map/pallas_call | solution.py:993
  (22 shorter events, 3.5 us)
Async XLA Ops:
  0.0 14.6 %copy-start.4 = (f32[1,8,8,8,128]{4,3,2,1,0:T(8,128)S(1)}, f32[1,8,8,8,128]{4,3,2,1,0:T(8,128)}, u32[]{:S(2)}) copy-start(f32[1,8,8,8,128]{4,3,2,1,0:T(8,128)} %param.12) | copy-start | bytes 786436
  6.8 0.7 copy-start.2
  7.5 25.0 %copy-start = (f32[512,128]{1,0:T(8,128)}, f32[512,128]{1,0:T(8,128)S(1)}, u32[]{:S(2)}) copy-start(f32[512,128]{1,0:T(8,128)S(1)} %get-tuple-element.53.static_ref) | copy-start | bytes 786436
  7.5 51.9 %collective-permute-start.3 = (f32[960,128]{1,0:T(8,128)}, f32[960,128]{1,0:T(8,128)S(1)}, u32[]{:S(2)}, u32[]{:S(2)}) collective-permute-start(f32[960,128]{1,0:T(8,128)} %get-tuple-element.60), channel_id=1, source_target_pairs={{0,1},{1,0},{2,3},{3,2},{4,5},{5,4},{6,7},{7,6},{8,9},{9,8},{10,11... | collective-permute-start | bytes 1474568 | tf_op jit(solution)/shard_map/ppermute | solution.py:1026
  9.4 50.0 %collective-permute-start.4 = (f32[960,128]{1,0:T(8,128)}, f32[960,128]{1,0:T(8,128)S(1)}, u32[]{:S(2)}, u32[]{:S(2)}) collective-permute-start(f32[960,128]{1,0:T(8,128)} %get-tuple-element.61), channel_id=1, source_target_pairs={{0,64},{1,2},{2,1},{3,4},{4,3},{5,6},{6,5},{7,8},{8,7},{9,10},{10,... | collective-permute-start | bytes 1474568 | tf_op jit(solution)/shard_map/ppermute | solution.py:1026
  14.6 17.8 %collective-permute-start = (f32[512,128]{1,0:T(8,128)S(1)}, f32[512,128]{1,0:T(8,128)S(1)}, u32[]{:S(2)}, u32[]{:S(2)}) collective-permute-start(f32[512,128]{1,0:T(8,128)S(1)} %bitcast.26), channel_id=1, source_target_pairs={{0,64},{64,0},{1,65},{65,1},{2,66},{66,2},{3,67},{67,3},{4,68},{68... | collective-permute-start | bytes 786440 | tf_op jit(solution)/shard_map/ppermute | solution.py:1046
  32.4 16.5 %copy-start.1 = (f32[512,128]{1,0:T(8,128)S(1)}, f32[512,128]{1,0:T(8,128)}, u32[]{:S(2)}) copy-start(f32[512,128]{1,0:T(8,128)} %copy-done) | copy-start | bytes 786436
  34.3 14.6 %all-to-all-start.1 = ((f32[64,1,128]{2,1,0:T(1,128)}), f32[64,1,128]{2,1,0:T(1,128)S(1)}, u32[]{:S(2)}, u32[]{:S(2)}) async-start(f32[64,1,128]{2,1,0:T(1,128)} %bitcast.12), calls=%async_computation.1 | async-start | bytes 65536 | tf_op jit(solution)/shard_map/all_to_all | solution.py:1114
  50.6 4.0 %collective-permute-start.1 = (f32[64,128]{1,0:T(8,128)S(1)}, f32[64,128]{1,0:T(8,128)S(1)}, u32[]{:S(2)}, u32[]{:S(2)}) collective-permute-start(f32[64,128]{1,0:T(8,128)S(1)} %get-tuple-element.58), channel_id=1, source_target_pairs={{0,1},{1,0},{2,3},{3,2},{4,5},{5,4},{6,7},{7,6},{8,9},{9,8},{10,11... | collective-permute-start | bytes 98312 | tf_op jit(solution)/shard_map/ppermute | solution.py:1026
  51.2 8.1 %collective-permute-start.2 = (f32[64,128]{1,0:T(8,128)S(1)}, f32[64,128]{1,0:T(8,128)S(1)}, u32[]{:S(2)}, u32[]{:S(2)}) collective-permute-start(f32[64,128]{1,0:T(8,128)S(1)} %get-tuple-element.59), channel_id=1, source_target_pairs={{0,64},{1,2},{2,1},{3,4},{4,3},{5,6},{6,5},{7,8},{8,7},{9,10},{10,... | collective-permute-start | bytes 98312 | tf_op jit(solution)/shard_map/ppermute | solution.py:1026
  59.4 10.7 %copy-start.3 = (f32[128,512]{1,0:T(8,128)S(1)}, f32[128,512]{1,0:T(8,128)}, u32[]{:S(2)}) copy-start(f32[128,512]{1,0:T(8,128)} %copy-done.2) | copy-start | bytes 786436
  61.8 4.0 %collective-permute-start.5 = (f32[64,128]{1,0:T(8,128)S(1)}, f32[64,128]{1,0:T(8,128)S(1)}, u32[]{:S(2)}, u32[]{:S(2)}) collective-permute-start(f32[64,128]{1,0:T(8,128)S(1)} %get-tuple-element.68), channel_id=1, source_target_pairs={{0,1},{1,0},{2,3},{3,2},{4,5},{5,4},{6,7},{7,6},{8,9},{9,8},{10,11... | collective-permute-start | bytes 98312 | tf_op jit(solution)/shard_map/ppermute | solution.py:1026
  61.8 8.2 %collective-permute-start.6 = (f32[64,128]{1,0:T(8,128)S(1)}, f32[64,128]{1,0:T(8,128)S(1)}, u32[]{:S(2)}, u32[]{:S(2)}) collective-permute-start(f32[64,128]{1,0:T(8,128)S(1)} %get-tuple-element.69), channel_id=1, source_target_pairs={{0,64},{1,2},{2,1},{3,4},{4,3},{5,6},{6,5},{7,8},{8,7},{9,10},{10,... | collective-permute-start | bytes 98312 | tf_op jit(solution)/shard_map/ppermute | solution.py:1026
  74.0 16.0 %all-to-all-start.2 = ((f32[64,4,128]{2,1,0:T(4,128)}), f32[64,4,128]{2,1,0:T(4,128)S(1)}, u32[]{:S(2)}, u32[]{:S(2)}) async-start(f32[64,4,128]{2,1,0:T(4,128)} %bitcast.14), calls=%async_computation.2 | async-start | bytes 262144 | tf_op jit(solution)/shard_map/all_to_all | solution.py:1180
  80.9 8.2 %collective-permute-start.8 = (f32[64,128]{1,0:T(8,128)S(1)}, f32[64,128]{1,0:T(8,128)S(1)}, u32[]{:S(2)}, u32[]{:S(2)}) collective-permute-start(f32[64,128]{1,0:T(8,128)S(1)} %get-tuple-element.78), channel_id=1, source_target_pairs={{0,64},{1,2},{2,1},{3,4},{4,3},{5,6},{6,5},{7,8},{8,7},{9,10},{10,... | collective-permute-start | bytes 98312 | tf_op jit(solution)/shard_map/ppermute | solution.py:1026
  86.1 3.9 %collective-permute-start.7 = (f32[64,128]{1,0:T(8,128)S(1)}, f32[64,128]{1,0:T(8,128)S(1)}, u32[]{:S(2)}, u32[]{:S(2)}) collective-permute-start(f32[64,128]{1,0:T(8,128)S(1)} %get-tuple-element.74.after_ref), channel_id=1, source_target_pairs={{0,1},{1,0},{2,3},{3,2},{4,5},{5,4},{6,7},{7,6},{8,9},{9,8},{10,11... | collective-permute-start | bytes 98312 | tf_op jit(solution)/shard_map/ppermute | solution.py:1026
  93.6 4.4 %collective-permute-start.9 = (f32[64,128]{1,0:T(8,128)S(1)}, f32[64,128]{1,0:T(8,128)S(1)}, u32[]{:S(2)}, u32[]{:S(2)}) collective-permute-start(f32[64,128]{1,0:T(8,128)S(1)} %get-tuple-element.83), channel_id=1, source_target_pairs={{0,1},{1,0},{2,3},{3,2},{4,5},{5,4},{6,7},{7,6},{8,9},{9,8},{10,11... | collective-permute-start | bytes 98312 | tf_op jit(solution)/shard_map/ppermute | solution.py:1026
  94.7 8.1 %collective-permute-start.10 = (f32[64,128]{1,0:T(8,128)S(1)}, f32[64,128]{1,0:T(8,128)S(1)}, u32[]{:S(2)}, u32[]{:S(2)}) collective-permute-start(f32[64,128]{1,0:T(8,128)S(1)} %get-tuple-element.84), channel_id=1, source_target_pairs={{0,64},{1,2},{2,1},{3,4},{4,3},{5,6},{6,5},{7,8},{8,7},{9,10},{10,... | collective-permute-start | bytes 98312 | tf_op jit(solution)/shard_map/ppermute | solution.py:1026

commit v8 on v7

--- a/solution.py
+++ b/solution.py
@@ -770,7 +770,7 @@
     solve_ref,
     near_ref,
     shares_hbm,
-    base_hbm,
+    base_ref,
     a_ref,
     b_ref,
     invd_ref,
@@ -789,15 +789,10 @@
     face_ref,
     side_ref,
     shares_ref,
-    base_ref,
     sems,
 ):
-    copies = [
-        pltpu.make_async_copy(shares_hbm, shares_ref, sems.at[0]),
-        pltpu.make_async_copy(base_hbm, base_ref, sems.at[1]),
-    ]
-    for copy in copies:
-        copy.start()
+    copy = pltpu.make_async_copy(shares_hbm, shares_ref, sems.at[0])
+    copy.start()
     place = where_am_i()
     total = parts_ref[0:8]
     for n in range(1, OWNERS * NC // 1024):
@@ -821,8 +816,7 @@
     side_ref[...] = planes_ref[256:320] * near
     in_plane(side_ref, 1)
     raw = -(came[0:64] + side_ref[...])
-    for copy in copies:
-        copy.wait()
+    copy.wait()
     inner = came[64:128] - correction_inner(shares_ref, near, behind[0:1])
     opening_half(
         place,
@@ -893,7 +887,7 @@
     basis_ref,
     ga_ref,
     gb_ref,
-    local_hbm,
+    local_ref,
     cur_hbm,
     part_ref,
     a_out_ref,
@@ -901,7 +895,6 @@
     w_out_ref,
     vec_ref,
     cur_ref,
-    local_ref,
     next_ref,
     work_ref,
     face_ref,
@@ -933,8 +926,6 @@
     zeros = jnp.zeros((64, 128), f32)
     local = local_ref[...] - coupled(w_out_ref, zeros, zeros)
     local_ref[...] = local
-    second = pltpu.make_async_copy(local_ref, local_hbm, sems.at[1])
-    second.start()
     next_ref[...] = local * invd_ref[...] * STEPS[0][1]
     place = where_am_i()
     send_planes(w_out_ref, next_ref, coef_ref, work_ref, a_out_ref, b_out_ref, place[0])
@@ -955,7 +946,6 @@
     for n in range(OWNERS * NC // 1024):
         part_ref[n * 8 : n * 8 + 8] = eight
     copy.wait()
-    second.wait()
 
 
 def last_kernel(*refs):
@@ -1023,7 +1013,9 @@
         inside = 0 <= other < count
         pairs_b.append((d, base + other if inside else (d + count) % (2 * count)))
     axes = ("sess", "elem")
-    return lax.ppermute(a, axes, pairs_a), lax.ppermute(b, axes, pairs_b)
+    b = lax.ppermute(b, axes, pairs_b)
+    a = lax.ppermute(a, axes, pairs_a)
+    return a, b
 
 
 def one_device(
@@ -1144,6 +1136,18 @@
         mass,
         scratch=SEND_WORK + SIDE_WORK,
     )
+    near, shares = call(
+        near_kernel,
+        [((256, NC), f32), FIELD],
+        ga,
+        gb,
+        coarse_inverse.reshape(NC, NC),
+        a,
+        near=(2,),
+        scratch=[(NODES, 128)],
+        copies=1,
+        away=(1,),
+    )
     a, b = exchange(a, b)
     res, total, part, a, b = call(
         middle_kernel,
@@ -1161,19 +1165,7 @@
         basis,
         ga,
         gb,
-        scratch=[(NODES, 128)] * 4 + SEND_WORK + SIDE_WORK,
-        copies=2,
-        away=(0, 1),
-    )
-    near, shares = call(
-        near_kernel,
-        [((256, NC), f32), FIELD],
-        ga,
-        gb,
-        coarse_inverse.reshape(NC, NC),
-        a,
-        near=(2,),
-        scratch=[(NODES, 128)],
+        scratch=[(NODES, 128)] * 3 + SEND_WORK + SIDE_WORK,
         copies=1,
         away=(1,),
     )
@@ -1199,9 +1191,9 @@
         planes,
         coef,
         mass,
-        far=(3, 4),
-        scratch=[(NODES, 128)] + SEND_WORK + SIDE_WORK + [(NODES, 128)] * 2,
-        copies=2,
+        far=(3,),
+        scratch=[(NODES, 128)] + SEND_WORK + SIDE_WORK + [(NODES, 128)],
+        copies=1,
     )
     a, b = exchange(a, b)
     (out,) = call(

time: 106 us -> 106 us (level)
  local copies, waits for them, and re-layouts: 0.7 us -> 2.35 us
  waiting for transfers between devices: 24.6 us -> 23.2 us
    unnamed x10 -> x14, local copies, waits for them, and re-layouts: 0.7 us -> 2.35 us
    ppermute x10, waiting for transfers between devices: 17.7 us -> 16.3 us  [the longest x5 15.2 us: exchange(): b = lax.ppermute(b, axes, pairs_b)]
  transfers between devices with their start and end apart: 13 -> 13, of which waited for: 8 -> 6; matrix products, arithmetic and copies ran while one was open for 0% -> 0% of each run, Pallas kernels for 9% -> 9%
where the time goes in v8:
time: 106 us
  starting transfers between devices  36.8 us (35%)
  Pallas kernels  27.3 us (26%)
  waiting for transfers between devices  23.2 us (22%)
  blocking collectives  15.3 us (14%)
  local copies, waits for them, and re-layouts  2.35 us (2%)
    pallas_call x9, Pallas kernels, call(): pl.pallas_call(kernel, out_shape=[pltpu.HBM(s, d) if n in away else jax.S...  27.3 us
    ppermute x5, starting transfers between devices, exchange(): b = lax.ppermute(b, axes, pairs_b)  18.6 us
    all_to_all x1, blocking collectives, one_device(): lax.all_to_all(send.reshape(OWNERS, ASK, 128), 'elem', split_axis=0, conc...  15.3 us
    ppermute x5, waiting for transfers between devices, exchange(): b = lax.ppermute(b, axes, pairs_b)  15.2 us
    all_to_all x1, starting transfers between devices, one_device(): lax.all_to_all(answer, 'elem', split_axis=0, concat_axis=0, tiled=True)  7.06 us
    all_to_all x1, starting transfers between devices, one_device(): lax.all_to_all(part.reshape(OWNERS, NC // 128, 128), 'elem', split_axis=0...  6.89 us
    all_to_all x1, waiting for transfers between devices, one_device(): lax.all_to_all(answer, 'elem', split_axis=0, concat_axis=0, tiled=True)  6.89 us
    ppermute x5, starting transfers between devices, exchange(): a = lax.ppermute(a, axes, pairs_a)  4.19 us
  transfers between devices with their start and end apart: 13, of which 6 were waited for; matrix products, arithmetic and copies ran while one was open for 0% of the time, Pallas kernels for 9%

profile of v8, /device:TPU:6, one launch (start us, length us, event | category | flops | bytes accessed | tf_op | source)
XLA Modules:
  0.0 105.8 jit_solution(14943777406738305890)
XLA Ops:
  0.0 6.7 %shard_map.119 = (f32[1536,128]{1,0:T(8,128)S(1)}, f32[512,128]{1,0:T(8,128)S(1)}, f32[512,128]{1,0:T(8,128)S(1)}, f32[128,128]{1,0:T(8,128)S(1)}, f32[512,128]{...) custom-call(s32[1,128]{1,0:T(1,128)} %bitcast.33, ...), custom_call_target="tpu_custom_call" | custom-call | tf_op jit(solution)/shard_map/pallas_call | solution.py:983
  7.5 1.9 %collective-permute-start.3 = (f32[960,128]{1,0:T(8,128)}, f32[960,128]{1,0:T(8,128)S(1)}, u32[]{:S(2)}, u32[]{:S(2)}) collective-permute-start(f32[960,128]{1,0:T(8,128)} %get-tuple-element.60), channel_id=1, source_target_pairs={{0,1},{1,0},{2,3},{3,2},{4,5},{5,4},{6,7},{7,6},{8,9},{9,8},{10,11... | collective-permute-start | bytes 1474568 | tf_op jit(solution)/shard_map/ppermute | solution.py:1017
  9.4 5.2 %collective-permute-start.4 = (f32[960,128]{1,0:T(8,128)}, f32[960,128]{1,0:T(8,128)S(1)}, u32[]{:S(2)}, u32[]{:S(2)}) collective-permute-start(f32[960,128]{1,0:T(8,128)} %get-tuple-element.61), channel_id=1, source_target_pairs={{0,64},{1,2},{2,1},{3,4},{4,3},{5,6},{6,5},{7,8},{8,7},{9,10},{10,... | collective-permute-start | bytes 1474568 | tf_op jit(solution)/shard_map/ppermute | solution.py:1016
  14.6 2.6 %shard_map.118 = (f32[512,128]{1,0:T(8,128)S(1)}, f32[1,1024]{1,0:T(1,128)S(1)}, s32[1,1024]{1,0:T(1,128)S(1)}, s32[1,1024]{1,0:T(1,128)S(1)}) custom-call(s32[1,1024]{1,0:T(1,128)} %bitcast.32, s32[1,1024]{1,0:T(1,128)} %slot_ref.1, f32[24,1024]{1,0:T(8,128)} %bitcast.31, s32[1,1024]{1,0:T(1,128)} %ids_ref.1), custom_call_target="tpu_custom_call" | custom-call | tf_op jit(solution)/shard_map/pallas_call | solution.py:983
  17.2 15.3 %all_to_all.21 = f32[64,8,128]{2,1,0:T(8,128)S(1)} all-to-all(f32[64,8,128]{2,1,0:T(8,128)S(1)} %bitcast.20), channel_id=1, replica_groups=mesh['sess'=2,'elem'=64] {'elem'}, dimensions={0} | all-to-all | bytes 524288 | tf_op jit(solution)/shard_map/all_to_all | solution.py:1054
  32.4 1.9 %shard_map.120 = (f32[64,128]{1,0:T(8,128)}, s32[1,128]{1,0:T(1,128)S(1)}) custom-call(f32[512,128]{1,0:T(8,128)S(1)} %bitcast.18, f32[512,128]{1,0:T(8,128)S(1)} %collective-permute-done.field_ref, s32[1,128]{1,0:T(1,128)S(1)} %get-tuple-element.47.before_ref), custom_call_target="tpu_custom_call" | custom-call | tf_op jit(solution)/shard_map/pallas_call | solution.py:983
  34.3 7.1 %all-to-all-start.1 = ((f32[64,1,128]{2,1,0:T(1,128)}), f32[64,1,128]{2,1,0:T(1,128)S(1)}, u32[]{:S(2)}, u32[]{:S(2)}) async-start(f32[64,1,128]{2,1,0:T(1,128)} %bitcast.12), calls=%async_computation.1 | async-start | bytes 65536 | tf_op jit(solution)/shard_map/all_to_all | solution.py:1106
  42.0 6.9 %all-to-all-done.1 = f32[64,1,128]{2,1,0:T(1,128)S(1)} async-done(((f32[64,1,128]{2,1,0:T(1,128)}), f32[64,1,128]{2,1,0:T(1,128)S(1)}, u32[]{:S(2)}, u32[]{:S(2)}) %all-to-all-start.1) | async-done | bytes 32800 | tf_op jit(solution)/shard_map/all_to_all | solution.py:1106
  48.9 1.7 %shard_map.121 = (f32[512,128]{1,0:T(8,128)S(1)}, f32[64,128]{1,0:T(8,128)S(1)}, f32[64,128]{1,0:T(8,128)S(1)}) custom-call(f32[64,128]{1,0:T(8,128)S(1)} %bitcast.21, s32[1,1024]{1,0:T(1,128)S(1)} %get-tuple-element.49.owner_ref, f32[1,1024]{1,0:T(1,128)S(1)} %get-tuple-element.50.rank_ref, s32[1,1024]{1,0:T(1,128)S(1)} %get-tuple-element.51.ids_ref, ...), custom_call_target="tpu_custom_call" | custom-call | tf_op jit(solution)/shard_map/pallas_call | solution.py:983
  51.2 2.2 %collective-permute-start.2 = (f32[64,128]{1,0:T(8,128)S(1)}, f32[64,128]{1,0:T(8,128)S(1)}, u32[]{:S(2)}, u32[]{:S(2)}) collective-permute-start(f32[64,128]{1,0:T(8,128)S(1)} %get-tuple-element.59), channel_id=1, source_target_pairs={{0,64},{1,2},{2,1},{3,4},{4,3},{5,6},{6,5},{7,8},{8,7},{9,10},{10,... | collective-permute-start | bytes 98312 | tf_op jit(solution)/shard_map/ppermute | solution.py:1016
  53.4 1.2 %collective-permute-done.1.a_ref = f32[64,128]{1,0:T(8,128)S(1)} collective-permute-done((f32[64,128]{1,0:T(8,128)S(1)}, f32[64,128]{1,0:T(8,128)S(1)}, u32[]{:S(2)}, u32[]{:S(2)}) %collective-permute-start.1) | collective-permute-done | bytes 32800 | tf_op jit(solution)/shard_map/ppermute | solution.py:1017
  54.6 4.8 %collective-permute-done.2.b_ref = f32[64,128]{1,0:T(8,128)S(1)} collective-permute-done((f32[64,128]{1,0:T(8,128)S(1)}, f32[64,128]{1,0:T(8,128)S(1)}, u32[]{:S(2)}, u32[]{:S(2)}) %collective-permute-start.2) | collective-permute-done | bytes 32800 | tf_op jit(solution)/shard_map/ppermute | solution.py:1016
  59.4 2.4 %shard_map.122 = (f32[512,128]{1,0:T(8,128)S(1)}, f32[512,128]{1,0:T(8,128)S(1)}, f32[512,128]{1,0:T(8,128)S(1)}, f32[512,128]{1,0:T(8,128)S(1)}, f32[64,128]{1,...) custom-call(f32[512,128]{1,0:T(8,128)S(1)} %get-tuple-element.56.y_ref, ...), custom_call_target="tpu_custom_call" | custom-call | tf_op jit(solution)/shard_map/pallas_call | solution.py:983
  61.8 2.2 %collective-permute-start.6 = (f32[64,128]{1,0:T(8,128)S(1)}, f32[64,128]{1,0:T(8,128)S(1)}, u32[]{:S(2)}, u32[]{:S(2)}) collective-permute-start(f32[64,128]{1,0:T(8,128)S(1)} %get-tuple-element.69), channel_id=1, source_target_pairs={{0,64},{1,2},{2,1},{3,4},{4,3},{5,6},{6,5},{7,8},{8,7},{9,10},{10,... | collective-permute-start | bytes 98312 | tf_op jit(solution)/shard_map/ppermute | solution.py:1016
  64.0 6.0 %collective-permute-done.6.b_ref = f32[64,128]{1,0:T(8,128)S(1)} collective-permute-done((f32[64,128]{1,0:T(8,128)S(1)}, f32[64,128]{1,0:T(8,128)S(1)}, u32[]{:S(2)}, u32[]{:S(2)}) %collective-permute-start.6) | collective-permute-done | bytes 32800 | tf_op jit(solution)/shard_map/ppermute | solution.py:1016
  70.0 3.4 %shard_map.123 = (f32[512,128]{1,0:T(8,128)S(1)}, f32[512,128]{1,0:T(8,128)}, f32[256,128]{1,0:T(8,128)}, f32[64,128]{1,0:T(8,128)S(1)}, f32[64,128]{1,0:T(8,128)S(1)}) custom-call(f32[512,128]{1,0:T(8,128)S(1)} %get-tuple-element.63.w_ref, f32[512,128]{1,0:T(8,128)S(1)} %get-tuple-element.64.res_in_ref, f32[512,128]{1,0:T(8,128)S(1)} %get-tuple-element.65.upd_ref, ...), custom_call_target="tpu_custom_call" | custom-call | tf_op jit(solution)/shard_map/pallas_call | solution.py:983
  74.1 6.9 %all-to-all-start.2 = ((f32[64,4,128]{2,1,0:T(4,128)}), f32[64,4,128]{2,1,0:T(4,128)S(1)}, u32[]{:S(2)}, u32[]{:S(2)}) async-start(f32[64,4,128]{2,1,0:T(4,128)} %bitcast.14), calls=%async_computation.2 | async-start | bytes 262144 | tf_op jit(solution)/shard_map/all_to_all | solution.py:1172
  81.0 1.5 %collective-permute-start.7 = (f32[64,128]{1,0:T(8,128)S(1)}, f32[64,128]{1,0:T(8,128)S(1)}, u32[]{:S(2)}, u32[]{:S(2)}) collective-permute-start(f32[64,128]{1,0:T(8,128)S(1)} %get-tuple-element.77), channel_id=1, source_target_pairs={{0,1},{1,0},{2,3},{3,2},{4,5},{5,4},{6,7},{7,6},{8,9},{9,8},{10,11... | collective-permute-start | bytes 98312 | tf_op jit(solution)/shard_map/ppermute | solution.py:1017
  82.6 4.5 %collective-permute-start.8 = (f32[64,128]{1,0:T(8,128)S(1)}, f32[64,128]{1,0:T(8,128)S(1)}, u32[]{:S(2)}, u32[]{:S(2)}) collective-permute-start(f32[64,128]{1,0:T(8,128)S(1)} %get-tuple-element.78), channel_id=1, source_target_pairs={{0,64},{1,2},{2,1},{3,4},{4,3},{5,6},{6,5},{7,8},{8,7},{9,10},{10,... | collective-permute-start | bytes 98312 | tf_op jit(solution)/shard_map/ppermute | solution.py:1016
  87.0 2.9 %shard_map.124 = (f32[256,512]{1,0:T(8,128)S(1)}, f32[512,128]{1,0:T(8,128)}) custom-call(f32[960,128]{1,0:T(8,128)S(1)} %collective-permute-done.3.ga_ref, f32[960,128]{1,0:T(8,128)S(1)} %collective-permute-done.4.gb_ref, f32[512,512]{1,0:T(8,128)} %bitcast.23, f32[64,128]{1,0:T(8,128)S(1)} %get-tuple-element.68.after_ref), custom_call_target="tpu_custom_call" | custom-call | tf_op jit(solution)/shard_map/pallas_call | solution.py:983
  91.7 3.5 %shard_map.125 = (f32[512,128]{1,0:T(8,128)S(1)}, f32[512,128]{1,0:T(8,128)S(1)}, f32[512,128]{1,0:T(8,128)S(1)}, f32[512,128]{1,0:T(8,128)S(1)}, f32[64,128]{1,0:T(8,128)S(1)}, /*index=5*/f32[64,128]{1,0:T(8,128)S(1)}) custom-call(f32[256,128]{1,0:T(8,128)S(1)} %bitcast.19, f32[128,512]{1,0:T(8,128)S(1)} %get-tuple-element.73.solve_ref, ...), custom_call_target="tpu_custom_call" | custom-call | tf_op jit(solution)/shard_map/pallas_call | solution.py:983
  95.3 4.5 %collective-permute-start.10 = (f32[64,128]{1,0:T(8,128)S(1)}, f32[64,128]{1,0:T(8,128)S(1)}, u32[]{:S(2)}, u32[]{:S(2)}) collective-permute-start(f32[64,128]{1,0:T(8,128)S(1)} %get-tuple-element.84), channel_id=1, source_target_pairs={{0,64},{1,2},{2,1},{3,4},{4,3},{5,6},{6,5},{7,8},{8,7},{9,10},{10,... | collective-permute-start | bytes 98312 | tf_op jit(solution)/shard_map/ppermute | solution.py:1016
  99.8 3.7 %collective-permute-done.10.refs_6_ = f32[64,128]{1,0:T(8,128)S(1)} collective-permute-done((f32[64,128]{1,0:T(8,128)S(1)}, f32[64,128]{1,0:T(8,128)S(1)}, u32[]{:S(2)}, u32[]{:S(2)}) %collective-permute-start.10) | collective-permute-done | bytes 32800 | tf_op jit(solution)/shard_map/ppermute | solution.py:1016
  103.5 2.2 %shard_map.126 = f32[512,128]{1,0:T(8,128)} custom-call(f32[512,128]{1,0:T(8,128)S(1)} %get-tuple-element.79.refs_0_, f32[512,128]{1,0:T(8,128)S(1)} %get-tuple-element.80.refs_1_, f32[512,128]{1,0:T(8,128)S(1)} %get-tuple-element.81.refs_2_, f32[512,128]{1,0:T(8,128)S(1)} %get-tuple-element.82.refs_3_, f32[512,128]{1,0:T(8,128)S(1)} %get-tuple-element.67.invd_ref.refs_4_, ...), custom_call_target="tpu_custom_call" | custom-call | tf_op jit(solution)/shard_map/pallas_call | solution.py:983
  (26 shorter events, 3.8 us)
Async XLA Ops:
  0.0 14.6 %copy-start.6 = (f32[1,8,8,8,128]{4,3,2,1,0:T(8,128)S(1)}, f32[1,8,8,8,128]{4,3,2,1,0:T(8,128)}, u32[]{:S(2)}) copy-start(f32[1,8,8,8,128]{4,3,2,1,0:T(8,128)} %param.12) | copy-start | bytes 786436
  6.8 0.7 copy-start.4
  7.5 25.0 %copy-start.2 = (f32[512,128]{1,0:T(8,128)}, f32[512,128]{1,0:T(8,128)S(1)}, u32[]{:S(2)}) copy-start(f32[512,128]{1,0:T(8,128)S(1)} %get-tuple-element.53.static_ref) | copy-start | bytes 786436
  7.5 51.9 %collective-permute-start.3 = (f32[960,128]{1,0:T(8,128)}, f32[960,128]{1,0:T(8,128)S(1)}, u32[]{:S(2)}, u32[]{:S(2)}) collective-permute-start(f32[960,128]{1,0:T(8,128)} %get-tuple-element.60), channel_id=1, source_target_pairs={{0,1},{1,0},{2,3},{3,2},{4,5},{5,4},{6,7},{7,6},{8,9},{9,8},{10,11... | collective-permute-start | bytes 1474568 | tf_op jit(solution)/shard_map/ppermute | solution.py:1017
  9.4 50.0 %collective-permute-start.4 = (f32[960,128]{1,0:T(8,128)}, f32[960,128]{1,0:T(8,128)S(1)}, u32[]{:S(2)}, u32[]{:S(2)}) collective-permute-start(f32[960,128]{1,0:T(8,128)} %get-tuple-element.61), channel_id=1, source_target_pairs={{0,64},{1,2},{2,1},{3,4},{4,3},{5,6},{6,5},{7,8},{8,7},{9,10},{10,... | collective-permute-start | bytes 1474568 | tf_op jit(solution)/shard_map/ppermute | solution.py:1016
  14.6 17.8 %collective-permute-start = (f32[512,128]{1,0:T(8,128)S(1)}, f32[512,128]{1,0:T(8,128)S(1)}, u32[]{:S(2)}, u32[]{:S(2)}) collective-permute-start(f32[512,128]{1,0:T(8,128)S(1)} %bitcast.26), channel_id=1, source_target_pairs={{0,64},{64,0},{1,65},{65,1},{2,66},{66,2},{3,67},{67,3},{4,68},{68... | collective-permute-start | bytes 786440 | tf_op jit(solution)/shard_map/ppermute | solution.py:1038
  32.4 16.5 %copy-start.3 = (f32[512,128]{1,0:T(8,128)S(1)}, f32[512,128]{1,0:T(8,128)}, u32[]{:S(2)}) copy-start(f32[512,128]{1,0:T(8,128)} %copy-done.2) | copy-start | bytes 786436
  34.3 14.6 %all-to-all-start.1 = ((f32[64,1,128]{2,1,0:T(1,128)}), f32[64,1,128]{2,1,0:T(1,128)S(1)}, u32[]{:S(2)}, u32[]{:S(2)}) async-start(f32[64,1,128]{2,1,0:T(1,128)} %bitcast.12), calls=%async_computation.1 | async-start | bytes 65536 | tf_op jit(solution)/shard_map/all_to_all | solution.py:1106
  50.6 4.0 %collective-permute-start.1 = (f32[64,128]{1,0:T(8,128)S(1)}, f32[64,128]{1,0:T(8,128)S(1)}, u32[]{:S(2)}, u32[]{:S(2)}) collective-permute-start(f32[64,128]{1,0:T(8,128)S(1)} %get-tuple-element.58), channel_id=1, source_target_pairs={{0,1},{1,0},{2,3},{3,2},{4,5},{5,4},{6,7},{7,6},{8,9},{9,8},{10,11... | collective-permute-start | bytes 98312 | tf_op jit(solution)/shard_map/ppermute | solution.py:1017
  51.2 8.1 %collective-permute-start.2 = (f32[64,128]{1,0:T(8,128)S(1)}, f32[64,128]{1,0:T(8,128)S(1)}, u32[]{:S(2)}, u32[]{:S(2)}) collective-permute-start(f32[64,128]{1,0:T(8,128)S(1)} %get-tuple-element.59), channel_id=1, source_target_pairs={{0,64},{1,2},{2,1},{3,4},{4,3},{5,6},{6,5},{7,8},{8,7},{9,10},{10,... | collective-permute-start | bytes 98312 | tf_op jit(solution)/shard_map/ppermute | solution.py:1016
  59.4 10.6 %copy-start.5 = (f32[128,512]{1,0:T(8,128)S(1)}, f32[128,512]{1,0:T(8,128)}, u32[]{:S(2)}) copy-start(f32[128,512]{1,0:T(8,128)} %copy-done.4) | copy-start | bytes 786436
  61.8 8.2 %collective-permute-start.6 = (f32[64,128]{1,0:T(8,128)S(1)}, f32[64,128]{1,0:T(8,128)S(1)}, u32[]{:S(2)}, u32[]{:S(2)}) collective-permute-start(f32[64,128]{1,0:T(8,128)S(1)} %get-tuple-element.69), channel_id=1, source_target_pairs={{0,64},{1,2},{2,1},{3,4},{4,3},{5,6},{6,5},{7,8},{8,7},{9,10},{10,... | collective-permute-start | bytes 98312 | tf_op jit(solution)/shard_map/ppermute | solution.py:1016
  64.0 6.0 %collective-permute-start.5 = (f32[64,128]{1,0:T(8,128)S(1)}, f32[64,128]{1,0:T(8,128)S(1)}, u32[]{:S(2)}, u32[]{:S(2)}) collective-permute-start(f32[64,128]{1,0:T(8,128)S(1)} %get-tuple-element.68.after_ref), channel_id=1, source_target_pairs={{0,1},{1,0},{2,3},{3,2},{4,5},{5,4},{6,7},{7,6},{8,9},{9,8},{10,11... | collective-permute-start | bytes 98312 | tf_op jit(solution)/shard_map/ppermute | solution.py:1017
  73.4 0.7 copy-start
  74.1 16.6 %all-to-all-start.2 = ((f32[64,4,128]{2,1,0:T(4,128)}), f32[64,4,128]{2,1,0:T(4,128)S(1)}, u32[]{:S(2)}, u32[]{:S(2)}) async-start(f32[64,4,128]{2,1,0:T(4,128)} %bitcast.14), calls=%async_computation.2 | async-start | bytes 262144 | tf_op jit(solution)/shard_map/all_to_all | solution.py:1172
  81.0 9.0 %collective-permute-start.7 = (f32[64,128]{1,0:T(8,128)S(1)}, f32[64,128]{1,0:T(8,128)S(1)}, u32[]{:S(2)}, u32[]{:S(2)}) collective-permute-start(f32[64,128]{1,0:T(8,128)S(1)} %get-tuple-element.77), channel_id=1, source_target_pairs={{0,1},{1,0},{2,3},{3,2},{4,5},{5,4},{6,7},{7,6},{8,9},{9,8},{10,11... | collective-permute-start | bytes 98312 | tf_op jit(solution)/shard_map/ppermute | solution.py:1017
  82.6 8.1 %collective-permute-start.8 = (f32[64,128]{1,0:T(8,128)S(1)}, f32[64,128]{1,0:T(8,128)S(1)}, u32[]{:S(2)}, u32[]{:S(2)}) collective-permute-start(f32[64,128]{1,0:T(8,128)S(1)} %get-tuple-element.78), channel_id=1, source_target_pairs={{0,64},{1,2},{2,1},{3,4},{4,3},{5,6},{6,5},{7,8},{8,7},{9,10},{10,... | collective-permute-start | bytes 98312 | tf_op jit(solution)/shard_map/ppermute | solution.py:1016
  90.7 1.0 copy-start.1
  95.2 4.6 %collective-permute-start.9 = (f32[64,128]{1,0:T(8,128)S(1)}, f32[64,128]{1,0:T(8,128)S(1)}, u32[]{:S(2)}, u32[]{:S(2)}) collective-permute-start(f32[64,128]{1,0:T(8,128)S(1)} %get-tuple-element.83), channel_id=1, source_target_pairs={{0,1},{1,0},{2,3},{3,2},{4,5},{5,4},{6,7},{7,6},{8,9},{9,8},{10,11... | collective-permute-start | bytes 98312 | tf_op jit(solution)/shard_map/ppermute | solution.py:1017
  95.3 8.2 %collective-permute-start.10 = (f32[64,128]{1,0:T(8,128)S(1)}, f32[64,128]{1,0:T(8,128)S(1)}, u32[]{:S(2)}, u32[]{:S(2)}) collective-permute-start(f32[64,128]{1,0:T(8,128)S(1)} %get-tuple-element.84), channel_id=1, source_target_pairs={{0,64},{1,2},{2,1},{3,4},{4,3},{5,6},{6,5},{7,8},{8,7},{9,10},{10,... | collective-permute-start | bytes 98312 | tf_op jit(solution)/shard_map/ppermute | solution.py:1016

commit v9 on v8

--- a/solution.py
+++ b/solution.py
@@ -20,7 +20,7 @@
 OWNERS = 64
 COMPS = 32
 HALF = 12
-ASK = 8
+ASK = 6
 
 exact_mode = lax.Precision.HIGHEST
 spectrum_high = 8.0
@@ -499,7 +499,6 @@
     field_hbm,
     load_hbm,
     basis_hbm,
-    inverse_hbm,
     coef_ref,
     mass_ref,
     static_ref,
@@ -507,7 +506,6 @@
     invd_ref,
     inv_ref,
     basis_ref,
-    solve_ref,
     order_out_ref,
     a_ref,
     b_ref,
@@ -516,7 +514,6 @@
     field_in,
     load_in,
     basis_in,
-    inverse_in,
     tmp_ref,
     start_ref,
     diag_ref,
@@ -536,7 +533,6 @@
                 (field_hbm, field_in),
                 (load_hbm, load_in),
                 (basis_hbm, basis_in),
-                (inverse_hbm, inverse_in),
             ]
         )
     ]
@@ -565,7 +561,6 @@
     in_plane(static_ref)
     basis = dot_nn(match, basis_in[...], exact_mode)
     basis_ref[...] = basis
-    solve_ref[...] = dot_nn(basis, inverse_in[...], exact_mode)
     local_diagonal(coef_ref, mass_ref, diag_ref)
     in_plane(diag_ref)
     zeros = jnp.zeros((64, 128), f32)
@@ -636,8 +631,10 @@
     live = iota((1, R_DEV), 1) < live_ref[0, 0]
     node = jnp.where(live, lax.shift_right_logical(ids, 7), -1)
     elem = jnp.bitwise_and(ids, 127)
-    hits = (iota((OWNERS, R_DEV), 0) == owner_ref[...]).astype(f32)
-    picked = dot_nn(ret_ref[...].T, hits, exact_mode)[0:32]
+    hits = (iota((OWNERS, R_DEV), 0) == owner_ref[...]).astype(f32).astype(bf16)
+    answers = jnp.concatenate(split3(ret_ref[...].T[0:32]), axis=0)
+    picked = dot_nn(answers, hits)
+    picked = picked[0:32] + picked[32:64] + picked[64:96]
     value = jnp.sum(
         jnp.where(iota((32, R_DEV), 0) == place, picked, 0.0), axis=0, keepdims=True
     )
@@ -749,26 +746,30 @@
 
 
 def near_kernel(
-    ga_ref, gb_ref, inverse_ref, after_ref, out_ref, shares_hbm, shares_ref, sems
+    basis_ref, ga_ref, gb_ref, inverse_ref, after_ref,
+    out_hbm, shares_hbm, out_ref, shares_ref, sems
 ):
     place = where_am_i()
     blocks = []
     for c in range(NC // 128):
         at = BASIS_ROW + c * 128
         below, above = beside(ga_ref[at : at + 128], gb_ref[at : at + 128], place)
-        blocks.append(jnp.concatenate([above, below], axis=0))
+        own = basis_ref[:, c * 128 : c * 128 + 128]
+        blocks.append(jnp.concatenate([own, above, below], axis=0))
     rows = jnp.concatenate(blocks, axis=1)
     shares_ref[...] = unpack(ga_ref, gb_ref, SHARE_ROW, 256, place)
     copy = pltpu.make_async_copy(shares_ref, shares_hbm, sems.at[0])
     copy.start()
     out_ref[...] = dot_nn(rows, inverse_ref[...], exact_mode)
+    second = pltpu.make_async_copy(out_ref, out_hbm, sems.at[1])
+    second.start()
     copy.wait()
+    second.wait()
 
 
 def again_kernel(
     parts_ref,
-    solve_ref,
-    near_ref,
+    near_hbm,
     shares_hbm,
     base_ref,
     a_ref,
@@ -789,34 +790,45 @@
     face_ref,
     side_ref,
     shares_ref,
+    near_ref,
     sems,
 ):
-    copy = pltpu.make_async_copy(shares_hbm, shares_ref, sems.at[0])
-    copy.start()
+    mine, others = pl.ds(0, 128), pl.ds(128, 256)
+    copies = [
+        pltpu.make_async_copy(near_hbm.at[mine], near_ref.at[mine], sems.at[0]),
+        pltpu.make_async_copy(near_hbm.at[others], near_ref.at[others], sems.at[1]),
+        pltpu.make_async_copy(shares_hbm, shares_ref, sems.at[2]),
+    ]
+    for copy in copies:
+        copy.start()
     place = where_am_i()
     total = parts_ref[0:8]
     for n in range(1, OWNERS * NC // 1024):
         total = total + parts_ref[n * 8 : n * 8 + 8]
     total = total + pltpu.roll(total, 4, 0)
-    both = None
-    for c in range(NC // 128):
-        row = jnp.broadcast_to(total[c : c + 1], (8, 128))
-        cols = slice(c * 128, c * 128 + 128)
-        rows = jnp.concatenate([solve_ref[:, cols], near_ref[:, cols]], axis=0)
-        term = dot_nt(row, rows, exact_mode)
-        both = term if both is None else both + term
-    correction = both[0:1, 0:128]
-    above, below = both[0:1, 128:256], both[0:1, 256:384]
+
+    def solved(g):
+        acc = None
+        for c in range(NC // 128):
+            cols = slice(c * 128, c * 128 + 128)
+            term = near_ref[g * 128 : g * 128 + 128, cols] * total[c : c + 1]
+            acc = term if acc is None else acc + term
+        return jnp.sum(acc.T, axis=0, keepdims=True)
+
+    copies[0].wait()
+    correction = solved(0)
+    y_ref[...] = mass_ref[...] * (-correction)
+    in_plane(y_ref)
+    copies[1].wait()
+    above, below = solved(1), solved(2)
     first = first_layer((1, 128))
     near = jnp.where(first, above, below)
     behind = pltpu.roll(jnp.broadcast_to(jnp.where(first, below, above), (8, 128)), LAYER, 1)
-    y_ref[...] = mass_ref[...] * (-correction)
-    in_plane(y_ref)
     came = unpack(a_ref, b_ref, 0, 64, place)
     side_ref[...] = planes_ref[256:320] * near
     in_plane(side_ref, 1)
     raw = -(came[0:64] + side_ref[...])
-    copy.wait()
+    copies[2].wait()
     inner = came[64:128] - correction_inner(shares_ref, near, behind[0:1])
     opening_half(
         place,
@@ -933,14 +945,15 @@
     bottom = -jnp.sum(w_out_ref[0:64], axis=0, keepdims=True)
     top = -jnp.sum(w_out_ref[448:512], axis=0, keepdims=True)
     outer = jnp.where(first_layer((1, 128)), bottom, top)
-    left = jnp.broadcast_to(jnp.concatenate([sums, outer], axis=1), (8, 256))
+    sums = jnp.broadcast_to(sums, (128, 128)).T
+    outer = jnp.broadcast_to(outer, (128, 128)).T
     blocks = []
     for c in range(NC // 128):
         at = BASIS_ROW + c * 128
         below, above = beside(ga_ref[at : at + 128], gb_ref[at : at + 128], place)
         own = basis_ref[:, c * 128 : c * 128 + 128]
-        right = jnp.concatenate([own, below[LAYER:], above[:LAYER]], axis=0)
-        part = dot_nn(left, right, exact_mode)[0:1]
+        other = jnp.concatenate([below[LAYER:], above[:LAYER]], axis=0)
+        part = jnp.sum(own * sums + other * outer, axis=0, keepdims=True)
         blocks.append(part * (1.0 / math.sqrt(NODES)))
     eight = jnp.concatenate(blocks + blocks, axis=0)
     for n in range(OWNERS * NC // 1024):
@@ -1052,9 +1065,9 @@
         near=(0, 1, 2, 3),
     )
     received = lax.all_to_all(
-        send.reshape(OWNERS, ASK, 128), "elem", split_axis=0, concat_axis=0, tiled=True
-    )
-    coef, mass, static, faces, invd, inv, basis, solve, order, ga, gb = call(
+        send.reshape(OWNERS, 1, ASK * 128), "elem", split_axis=0, concat_axis=0, tiled=True
+    )
+    coef, mass, static, faces, invd, inv, basis, order, ga, gb = call(
         setup_kernel,
         [
             ((3 * NODES, 128), f32),
@@ -1063,7 +1076,6 @@
             ((128, 128), f32),
             FIELD,
             ((1, 128), jnp.int32),
-            ((128, NC), f32),
             ((128, NC), f32),
             ((1, 128), jnp.int32),
             GHOST_MSG,
@@ -1075,16 +1087,14 @@
         own_field,
         load.reshape(NODES, 128),
         coarse_basis.reshape(128, NC),
-        coarse_inverse.reshape(NC, NC),
         near=(0,),
-        far=(1, 2, 3, 4, 5, 6),
+        far=(1, 2, 3, 4, 5),
         scratch=[
             (3 * NODES, 128),
             (NODES, 128),
             (NODES, 128),
             (NODES, 128),
             (128, NC),
-            (NC, NC),
             (NODES, 128),
             (NODES, 128),
             (NODES, 128),
@@ -1094,7 +1104,7 @@
             (64, 128),
             (64, 128),
         ],
-        copies=6,
+        copies=5,
     )
     answer, inv = call(
         owner_kernel,
@@ -1138,15 +1148,16 @@
     )
     near, shares = call(
         near_kernel,
-        [((256, NC), f32), FIELD],
+        [((384, NC), f32), FIELD],
+        basis,
         ga,
         gb,
         coarse_inverse.reshape(NC, NC),
         a,
-        near=(2,),
-        scratch=[(NODES, 128)],
-        copies=1,
-        away=(1,),
+        near=(3,),
+        scratch=[(384, NC), (NODES, 128)],
+        copies=2,
+        away=(0, 1),
     )
     a, b = exchange(a, b)
     res, total, part, a, b = call(
@@ -1181,7 +1192,6 @@
         again_kernel,
         half,
         parts.reshape(OWNERS * NC // 128, 128),
-        solve,
         near,
         shares,
         res,
@@ -1191,9 +1201,9 @@
         planes,
         coef,
         mass,
-        far=(3,),
-        scratch=[(NODES, 128)] + SEND_WORK + SIDE_WORK + [(NODES, 128)],
-        copies=1,
+        far=(1, 2),
+        scratch=[(NODES, 128)] + SEND_WORK + SIDE_WORK + [(NODES, 128), (384, NC)],
+        copies=3,
     )
     a, b = exchange(a, b)
     (out,) = call(

time: 106 us -> 102 us (0.962)
  local copies, waits for them, and re-layouts: 2.35 us -> 0.01 us
    unnamed x14 -> x2, local copies, waits for them, and re-layouts: 2.35 us -> 0.01 us
where the time goes in v9:
time: 102 us
  starting transfers between devices  36.9 us (36%)
  Pallas kernels  27 us (26%)
  waiting for transfers between devices  22.4 us (22%)
  blocking collectives  14.6 us (14%)
    pallas_call x9, Pallas kernels, call(): pl.pallas_call(kernel, out_shape=[pltpu.HBM(s, d) if n in away else jax.S...  27 us
    ppermute x5, starting transfers between devices, exchange(): b = lax.ppermute(b, axes, pairs_b)  18.7 us
    all_to_all x1, blocking collectives, one_device(): lax.all_to_all(send.reshape(OWNERS, 1, ASK * 128), 'elem', split_axis=0,...  14.6 us
    ppermute x5, waiting for transfers between devices, exchange(): b = lax.ppermute(b, axes, pairs_b)  14.5 us
    all_to_all x1, starting transfers between devices, one_device(): lax.all_to_all(answer, 'elem', split_axis=0, concat_axis=0, tiled=True)  7.05 us
    all_to_all x1, starting transfers between devices, one_device(): lax.all_to_all(part.reshape(OWNERS, NC // 128, 128), 'elem', split_axis=0...  6.92 us
    all_to_all x1, waiting for transfers between devices, one_device(): lax.all_to_all(answer, 'elem', split_axis=0, concat_axis=0, tiled=True)  6.82 us
    ppermute x5, starting transfers between devices, exchange(): a = lax.ppermute(a, axes, pairs_a)  4.26 us
  transfers between devices with their start and end apart: 13, of which 6 were waited for; matrix products, arithmetic and copies ran while one was open for 0% of the time, Pallas kernels for 9%

profile of v9, /device:TPU:6, one launch (start us, length us, event | category | flops | bytes accessed | tf_op | source)
XLA Modules:
  0.0 101.8 jit_solution(4863180123017419287)
XLA Ops:
  0.0 5.8 %shard_map.119 = (f32[1536,128]{1,0:T(8,128)S(1)}, f32[512,128]{1,0:T(8,128)S(1)}, f32[512,128]{1,0:T(8,128)S(1)}, f32[128,128]{1,0:T(8,128)S(1)}, f32[512,128]{...) custom-call(s32[1,128]{1,0:T(1,128)} %bitcast.32, ...), custom_call_target="tpu_custom_call" | custom-call | tf_op jit(solution)/shard_map/pallas_call | solution.py:996
  5.8 2.0 %collective-permute-start.3 = (f32[960,128]{1,0:T(8,128)}, f32[960,128]{1,0:T(8,128)S(1)}, u32[]{:S(2)}, u32[]{:S(2)}) collective-permute-start(f32[960,128]{1,0:T(8,128)} %get-tuple-element.59), channel_id=1, source_target_pairs={{0,1},{1,0},{2,3},{3,2},{4,5},{5,4},{6,7},{7,6},{8,9},{9,8},{10,11... | collective-permute-start | bytes 1474568 | tf_op jit(solution)/shard_map/ppermute | solution.py:1030
  7.8 5.2 %collective-permute-start.4 = (f32[960,128]{1,0:T(8,128)}, f32[960,128]{1,0:T(8,128)S(1)}, u32[]{:S(2)}, u32[]{:S(2)}) collective-permute-start(f32[960,128]{1,0:T(8,128)} %get-tuple-element.60), channel_id=1, source_target_pairs={{0,64},{1,2},{2,1},{3,4},{4,3},{5,6},{6,5},{7,8},{8,7},{9,10},{10,... | collective-permute-start | bytes 1474568 | tf_op jit(solution)/shard_map/ppermute | solution.py:1029
  13.0 2.5 %shard_map.118 = (f32[384,128]{1,0:T(8,128)S(1)}, f32[1,1024]{1,0:T(1,128)S(1)}, s32[1,1024]{1,0:T(1,128)S(1)}, s32[1,1024]{1,0:T(1,128)S(1)}) custom-call(s32[1,1024]{1,0:T(1,128)} %bitcast.31, s32[1,1024]{1,0:T(1,128)} %slot_ref.1, f32[24,1024]{1,0:T(8,128)} %bitcast.30, s32[1,1024]{1,0:T(1,128)} %ids_ref.1), custom_call_target="tpu_custom_call" | custom-call | tf_op jit(solution)/shard_map/pallas_call | solution.py:996
  15.6 14.6 %all_to_all.21 = f32[64,1,768]{2,1,0:T(1,128)S(1)} all-to-all(f32[64,1,768]{2,1,0:T(1,128)S(1)} %bitcast.20), channel_id=1, replica_groups=mesh['sess'=2,'elem'=64] {'elem'}, dimensions={0} | all-to-all | bytes 393216 | tf_op jit(solution)/shard_map/all_to_all | solution.py:1067
  30.2 1.9 %shard_map.120 = (f32[64,128]{1,0:T(8,128)}, s32[1,128]{1,0:T(1,128)S(1)}) custom-call(f32[384,128]{1,0:T(8,128)S(1)} %bitcast.18, f32[512,128]{1,0:T(8,128)S(1)} %collective-permute-done.field_ref, s32[1,128]{1,0:T(1,128)S(1)} %get-tuple-element.46.before_ref), custom_call_target="tpu_custom_call" | custom-call | tf_op jit(solution)/shard_map/pallas_call | solution.py:996
  32.0 7.0 %all-to-all-start.1 = ((f32[64,1,128]{2,1,0:T(1,128)}), f32[64,1,128]{2,1,0:T(1,128)S(1)}, u32[]{:S(2)}, u32[]{:S(2)}) async-start(f32[64,1,128]{2,1,0:T(1,128)} %bitcast.11), calls=%async_computation.1 | async-start | bytes 65536 | tf_op jit(solution)/shard_map/all_to_all | solution.py:1116
  39.7 6.8 %all-to-all-done.1 = f32[64,1,128]{2,1,0:T(1,128)S(1)} async-done(((f32[64,1,128]{2,1,0:T(1,128)}), f32[64,1,128]{2,1,0:T(1,128)S(1)}, u32[]{:S(2)}, u32[]{:S(2)}) %all-to-all-start.1) | async-done | bytes 32800 | tf_op jit(solution)/shard_map/all_to_all | solution.py:1116
  46.6 1.4 %shard_map.121 = (f32[512,128]{1,0:T(8,128)S(1)}, f32[64,128]{1,0:T(8,128)S(1)}, f32[64,128]{1,0:T(8,128)S(1)}) custom-call(f32[64,128]{1,0:T(8,128)S(1)} %bitcast.21, s32[1,1024]{1,0:T(1,128)S(1)} %get-tuple-element.48.owner_ref, f32[1,1024]{1,0:T(1,128)S(1)} %get-tuple-element.49.rank_ref, s32[1,1024]{1,0:T(1,128)S(1)} %get-tuple-element.50.ids_ref, ...), custom_call_target="tpu_custom_call" | custom-call | tf_op jit(solution)/shard_map/pallas_call | solution.py:996
  48.6 2.2 %collective-permute-start.2 = (f32[64,128]{1,0:T(8,128)S(1)}, f32[64,128]{1,0:T(8,128)S(1)}, u32[]{:S(2)}, u32[]{:S(2)}) collective-permute-start(f32[64,128]{1,0:T(8,128)S(1)} %get-tuple-element.58), channel_id=1, source_target_pairs={{0,64},{1,2},{2,1},{3,4},{4,3},{5,6},{6,5},{7,8},{8,7},{9,10},{10,... | collective-permute-start | bytes 98312 | tf_op jit(solution)/shard_map/ppermute | solution.py:1029
  50.8 1.1 %collective-permute-done.1.a_ref = f32[64,128]{1,0:T(8,128)S(1)} collective-permute-done((f32[64,128]{1,0:T(8,128)S(1)}, f32[64,128]{1,0:T(8,128)S(1)}, u32[]{:S(2)}, u32[]{:S(2)}) %collective-permute-start.1) | collective-permute-done | bytes 32800 | tf_op jit(solution)/shard_map/ppermute | solution.py:1030
  52.0 4.8 %collective-permute-done.2.b_ref = f32[64,128]{1,0:T(8,128)S(1)} collective-permute-done((f32[64,128]{1,0:T(8,128)S(1)}, f32[64,128]{1,0:T(8,128)S(1)}, u32[]{:S(2)}, u32[]{:S(2)}) %collective-permute-start.2) | collective-permute-done | bytes 32800 | tf_op jit(solution)/shard_map/ppermute | solution.py:1029
  56.8 2.4 %shard_map.122 = (f32[512,128]{1,0:T(8,128)S(1)}, f32[512,128]{1,0:T(8,128)S(1)}, f32[512,128]{1,0:T(8,128)S(1)}, f32[512,128]{1,0:T(8,128)S(1)}, f32[64,128]{1,...) custom-call(f32[512,128]{1,0:T(8,128)S(1)} %get-tuple-element.55.y_ref, ...), custom_call_target="tpu_custom_call" | custom-call | tf_op jit(solution)/shard_map/pallas_call | solution.py:996
  59.2 2.2 %collective-permute-start.6 = (f32[64,128]{1,0:T(8,128)S(1)}, f32[64,128]{1,0:T(8,128)S(1)}, u32[]{:S(2)}, u32[]{:S(2)}) collective-permute-start(f32[64,128]{1,0:T(8,128)S(1)} %get-tuple-element.68), channel_id=1, source_target_pairs={{0,64},{1,2},{2,1},{3,4},{4,3},{5,6},{6,5},{7,8},{8,7},{9,10},{10,... | collective-permute-start | bytes 98312 | tf_op jit(solution)/shard_map/ppermute | solution.py:1029
  61.4 5.9 %collective-permute-done.6.b_ref = f32[64,128]{1,0:T(8,128)S(1)} collective-permute-done((f32[64,128]{1,0:T(8,128)S(1)}, f32[64,128]{1,0:T(8,128)S(1)}, u32[]{:S(2)}, u32[]{:S(2)}) %collective-permute-start.6) | collective-permute-done | bytes 32800 | tf_op jit(solution)/shard_map/ppermute | solution.py:1029
  67.3 3.2 %shard_map.123 = (f32[512,128]{1,0:T(8,128)S(1)}, f32[512,128]{1,0:T(8,128)}, f32[256,128]{1,0:T(8,128)}, f32[64,128]{1,0:T(8,128)S(1)}, f32[64,128]{1,0:T(8,128)S(1)}) custom-call(f32[512,128]{1,0:T(8,128)S(1)} %get-tuple-element.62.w_ref, f32[512,128]{1,0:T(8,128)S(1)} %get-tuple-element.63.res_in_ref, f32[512,128]{1,0:T(8,128)S(1)} %get-tuple-element.64.upd_ref, ...), custom_call_target="tpu_custom_call" | custom-call | tf_op jit(solution)/shard_map/pallas_call | solution.py:996
  70.6 6.9 %all-to-all-start.2 = ((f32[64,4,128]{2,1,0:T(4,128)}), f32[64,4,128]{2,1,0:T(4,128)S(1)}, u32[]{:S(2)}, u32[]{:S(2)}) async-start(f32[64,4,128]{2,1,0:T(4,128)} %bitcast.13), calls=%async_computation.2 | async-start | bytes 262144 | tf_op jit(solution)/shard_map/all_to_all | solution.py:1183
  77.5 1.5 %collective-permute-start.7 = (f32[64,128]{1,0:T(8,128)S(1)}, f32[64,128]{1,0:T(8,128)S(1)}, u32[]{:S(2)}, u32[]{:S(2)}) collective-permute-start(f32[64,128]{1,0:T(8,128)S(1)} %get-tuple-element.75), channel_id=1, source_target_pairs={{0,1},{1,0},{2,3},{3,2},{4,5},{5,4},{6,7},{7,6},{8,9},{9,8},{10,11... | collective-permute-start | bytes 98312 | tf_op jit(solution)/shard_map/ppermute | solution.py:1030
  79.0 4.5 %collective-permute-start.8 = (f32[64,128]{1,0:T(8,128)S(1)}, f32[64,128]{1,0:T(8,128)S(1)}, u32[]{:S(2)}, u32[]{:S(2)}) collective-permute-start(f32[64,128]{1,0:T(8,128)S(1)} %get-tuple-element.76), channel_id=1, source_target_pairs={{0,64},{1,2},{2,1},{3,4},{4,3},{5,6},{6,5},{7,8},{8,7},{9,10},{10,... | collective-permute-start | bytes 98312 | tf_op jit(solution)/shard_map/ppermute | solution.py:1029
  83.5 3.6 %shard_map.124 = (f32[384,512]{1,0:T(8,128)}, f32[512,128]{1,0:T(8,128)}) custom-call(f32[128,512]{1,0:T(8,128)S(1)} %get-tuple-element.70.basis_ref, f32[960,128]{1,0:T(8,128)S(1)} %collective-permute-done.3.ga_ref, f32[960,128]{1,0:T(8,128)S(1)} %collective-permute-done.4.gb_ref, f32[512,512]{1,0:T(8,128)} %bitcast.22, ...), custom_call_target="tpu_custom_call" | custom-call | tf_op jit(solution)/shard_map/pallas_call | solution.py:996
  87.2 3.9 %shard_map.125 = (f32[512,128]{1,0:T(8,128)S(1)}, f32[512,128]{1,0:T(8,128)S(1)}, f32[512,128]{1,0:T(8,128)S(1)}, f32[512,128]{1,0:T(8,128)S(1)}, f32[64,128]{1,0:T(8,128)S(1)}, /*index=5*/f32[64,128]{1,0:T(8,128)S(1)}) custom-call(f32[256,128]{1,0:T(8,128)S(1)} %bitcast.19, f32[384,512]{1,0:T(8,128)} %get-tuple-element.72.near_hbm, ...), custom_call_target="tpu_custom_call" | custom-call | tf_op jit(solution)/shard_map/pallas_call | solution.py:996
  91.2 4.5 %collective-permute-start.10 = (f32[64,128]{1,0:T(8,128)S(1)}, f32[64,128]{1,0:T(8,128)S(1)}, u32[]{:S(2)}, u32[]{:S(2)}) collective-permute-start(f32[64,128]{1,0:T(8,128)S(1)} %get-tuple-element.82), channel_id=1, source_target_pairs={{0,64},{1,2},{2,1},{3,4},{4,3},{5,6},{6,5},{7,8},{8,7},{9,10},{10,... | collective-permute-start | bytes 98312 | tf_op jit(solution)/shard_map/ppermute | solution.py:1029
  95.8 3.7 %collective-permute-done.10.refs_6_ = f32[64,128]{1,0:T(8,128)S(1)} collective-permute-done((f32[64,128]{1,0:T(8,128)S(1)}, f32[64,128]{1,0:T(8,128)S(1)}, u32[]{:S(2)}, u32[]{:S(2)}) %collective-permute-start.10) | collective-permute-done | bytes 32800 | tf_op jit(solution)/shard_map/ppermute | solution.py:1029
  99.4 2.2 %shard_map.126 = f32[512,128]{1,0:T(8,128)} custom-call(f32[512,128]{1,0:T(8,128)S(1)} %get-tuple-element.77.refs_0_, f32[512,128]{1,0:T(8,128)S(1)} %get-tuple-element.78.refs_1_, f32[512,128]{1,0:T(8,128)S(1)} %get-tuple-element.79.refs_2_, f32[512,128]{1,0:T(8,128)S(1)} %get-tuple-element.80.refs_3_, f32[512,128]{1,0:T(8,128)S(1)} %get-tuple-element.66.invd_ref.refs_4_, ...), custom_call_target="tpu_custom_call" | custom-call | tf_op jit(solution)/shard_map/pallas_call | solution.py:996
  (14 shorter events, 0.8 us)
Async XLA Ops:
  0.0 13.0 %copy-start = (f32[1,8,8,8,128]{4,3,2,1,0:T(8,128)S(1)}, f32[1,8,8,8,128]{4,3,2,1,0:T(8,128)}, u32[]{:S(2)}) copy-start(f32[1,8,8,8,128]{4,3,2,1,0:T(8,128)} %param.12) | copy-start | bytes 786436
  5.8 51.0 %collective-permute-start.3 = (f32[960,128]{1,0:T(8,128)}, f32[960,128]{1,0:T(8,128)S(1)}, u32[]{:S(2)}, u32[]{:S(2)}) collective-permute-start(f32[960,128]{1,0:T(8,128)} %get-tuple-element.59), channel_id=1, source_target_pairs={{0,1},{1,0},{2,3},{3,2},{4,5},{5,4},{6,7},{7,6},{8,9},{9,8},{10,11... | collective-permute-start | bytes 1474568 | tf_op jit(solution)/shard_map/ppermute | solution.py:1030
  7.8 49.0 %collective-permute-start.4 = (f32[960,128]{1,0:T(8,128)}, f32[960,128]{1,0:T(8,128)S(1)}, u32[]{:S(2)}, u32[]{:S(2)}) collective-permute-start(f32[960,128]{1,0:T(8,128)} %get-tuple-element.60), channel_id=1, source_target_pairs={{0,64},{1,2},{2,1},{3,4},{4,3},{5,6},{6,5},{7,8},{8,7},{9,10},{10,... | collective-permute-start | bytes 1474568 | tf_op jit(solution)/shard_map/ppermute | solution.py:1029
  13.0 17.1 %collective-permute-start = (f32[512,128]{1,0:T(8,128)S(1)}, f32[512,128]{1,0:T(8,128)S(1)}, u32[]{:S(2)}, u32[]{:S(2)}) collective-permute-start(f32[512,128]{1,0:T(8,128)S(1)} %bitcast.25), channel_id=1, source_target_pairs={{0,64},{64,0},{1,65},{65,1},{2,66},{66,2},{3,67},{67,3},{4,68},{68... | collective-permute-start | bytes 786440 | tf_op jit(solution)/shard_map/ppermute | solution.py:1051
  32.0 14.5 %all-to-all-start.1 = ((f32[64,1,128]{2,1,0:T(1,128)}), f32[64,1,128]{2,1,0:T(1,128)S(1)}, u32[]{:S(2)}, u32[]{:S(2)}) async-start(f32[64,1,128]{2,1,0:T(1,128)} %bitcast.11), calls=%async_computation.1 | async-start | bytes 65536 | tf_op jit(solution)/shard_map/all_to_all | solution.py:1116
  48.0 4.0 %collective-permute-start.1 = (f32[64,128]{1,0:T(8,128)S(1)}, f32[64,128]{1,0:T(8,128)S(1)}, u32[]{:S(2)}, u32[]{:S(2)}) collective-permute-start(f32[64,128]{1,0:T(8,128)S(1)} %get-tuple-element.57), channel_id=1, source_target_pairs={{0,1},{1,0},{2,3},{3,2},{4,5},{5,4},{6,7},{7,6},{8,9},{9,8},{10,11... | collective-permute-start | bytes 98312 | tf_op jit(solution)/shard_map/ppermute | solution.py:1030
  48.6 8.1 %collective-permute-start.2 = (f32[64,128]{1,0:T(8,128)S(1)}, f32[64,128]{1,0:T(8,128)S(1)}, u32[]{:S(2)}, u32[]{:S(2)}) collective-permute-start(f32[64,128]{1,0:T(8,128)S(1)} %get-tuple-element.58), channel_id=1, source_target_pairs={{0,64},{1,2},{2,1},{3,4},{4,3},{5,6},{6,5},{7,8},{8,7},{9,10},{10,... | collective-permute-start | bytes 98312 | tf_op jit(solution)/shard_map/ppermute | solution.py:1029
  59.2 8.2 %collective-permute-start.6 = (f32[64,128]{1,0:T(8,128)S(1)}, f32[64,128]{1,0:T(8,128)S(1)}, u32[]{:S(2)}, u32[]{:S(2)}) collective-permute-start(f32[64,128]{1,0:T(8,128)S(1)} %get-tuple-element.68), channel_id=1, source_target_pairs={{0,64},{1,2},{2,1},{3,4},{4,3},{5,6},{6,5},{7,8},{8,7},{9,10},{10,... | collective-permute-start | bytes 98312 | tf_op jit(solution)/shard_map/ppermute | solution.py:1029
  61.4 5.9 %collective-permute-start.5 = (f32[64,128]{1,0:T(8,128)S(1)}, f32[64,128]{1,0:T(8,128)S(1)}, u32[]{:S(2)}, u32[]{:S(2)}) collective-permute-start(f32[64,128]{1,0:T(8,128)S(1)} %get-tuple-element.67.after_ref), channel_id=1, source_target_pairs={{0,1},{1,0},{2,3},{3,2},{4,5},{5,4},{6,7},{7,6},{8,9},{9,8},{10,11... | collective-permute-start | bytes 98312 | tf_op jit(solution)/shard_map/ppermute | solution.py:1030
  70.6 16.6 %all-to-all-start.2 = ((f32[64,4,128]{2,1,0:T(4,128)}), f32[64,4,128]{2,1,0:T(4,128)S(1)}, u32[]{:S(2)}, u32[]{:S(2)}) async-start(f32[64,4,128]{2,1,0:T(4,128)} %bitcast.13), calls=%async_computation.2 | async-start | bytes 262144 | tf_op jit(solution)/shard_map/all_to_all | solution.py:1183
  77.5 9.6 %collective-permute-start.7 = (f32[64,128]{1,0:T(8,128)S(1)}, f32[64,128]{1,0:T(8,128)S(1)}, u32[]{:S(2)}, u32[]{:S(2)}) collective-permute-start(f32[64,128]{1,0:T(8,128)S(1)} %get-tuple-element.75), channel_id=1, source_target_pairs={{0,1},{1,0},{2,3},{3,2},{4,5},{5,4},{6,7},{7,6},{8,9},{9,8},{10,11... | collective-permute-start | bytes 98312 | tf_op jit(solution)/shard_map/ppermute | solution.py:1030
  79.0 8.1 %collective-permute-start.8 = (f32[64,128]{1,0:T(8,128)S(1)}, f32[64,128]{1,0:T(8,128)S(1)}, u32[]{:S(2)}, u32[]{:S(2)}) collective-permute-start(f32[64,128]{1,0:T(8,128)S(1)} %get-tuple-element.76), channel_id=1, source_target_pairs={{0,64},{1,2},{2,1},{3,4},{4,3},{5,6},{6,5},{7,8},{8,7},{9,10},{10,... | collective-permute-start | bytes 98312 | tf_op jit(solution)/shard_map/ppermute | solution.py:1029
  91.1 4.6 %collective-permute-start.9 = (f32[64,128]{1,0:T(8,128)S(1)}, f32[64,128]{1,0:T(8,128)S(1)}, u32[]{:S(2)}, u32[]{:S(2)}) collective-permute-start(f32[64,128]{1,0:T(8,128)S(1)} %get-tuple-element.81), channel_id=1, source_target_pairs={{0,1},{1,0},{2,3},{3,2},{4,5},{5,4},{6,7},{7,6},{8,9},{9,8},{10,11... | collective-permute-start | bytes 98312 | tf_op jit(solution)/shard_map/ppermute | solution.py:1030
  91.2 8.2 %collective-permute-start.10 = (f32[64,128]{1,0:T(8,128)S(1)}, f32[64,128]{1,0:T(8,128)S(1)}, u32[]{:S(2)}, u32[]{:S(2)}) collective-permute-start(f32[64,128]{1,0:T(8,128)S(1)} %get-tuple-element.82), channel_id=1, source_target_pairs={{0,64},{1,2},{2,1},{3,4},{4,3},{5,6},{6,5},{7,8},{8,7},{9,10},{10,... | collective-permute-start | bytes 98312 | tf_op jit(solution)/shard_map/ppermute | solution.py:1029

commit v10 on v9

--- a/solution.py
+++ b/solution.py
@@ -211,7 +211,7 @@
             out_ref[at, :] = out_ref[at, :] + res[j] + mass_ref[at, :] * rows[j]
         return carry
 
-    lax.fori_loop(0, 8, per_k, 0)
+    lax.fori_loop(0, 8, per_k, 0, unroll=2)
 
     def per_j(j, carry):
         base = pl.multiple_of(j * 8, 8)
@@ -222,7 +222,7 @@
             out_ref[at, :] = out_ref[at, :] + res[k]
         return carry
 
-    lax.fori_loop(0, 8, per_j, 0)
+    lax.fori_loop(0, 8, per_j, 0, unroll=2)
 
 
 def couple(high, low, shift, pos, count):
@@ -474,7 +474,7 @@
             diag_ref[at, :] = diag_ref[at, :] + res[j] + mass_ref[at, :]
         return carry
 
-    lax.fori_loop(0, 8, per_k, 0)
+    lax.fori_loop(0, 8, per_k, 0, unroll=2)
 
     def per_j(j, carry):
         base = pl.multiple_of(j * 8, 8)
@@ -484,7 +484,7 @@
             diag_ref[at, :] = diag_ref[at, :] + res[k]
         return carry
 
-    lax.fori_loop(0, 8, per_j, 0)
+    lax.fori_loop(0, 8, per_j, 0, unroll=2)
 
 
 SHARE_ROW = 192

time: 102 us -> 102 us (level)
  no operation moved by 1% of the time
where the time goes in v10:
time: 102 us; the launch traced here: 101 us
  starting transfers between devices  36.9 us (36%)
  Pallas kernels  26.4 us (26%)
  waiting for transfers between devices  22.4 us (22%)
  blocking collectives  14.6 us (14%)
    pallas_call x9, Pallas kernels, call(): pl.pallas_call(kernel, out_shape=[pltpu.HBM(s, d) if n in away else jax.S...  26.4 us
    ppermute x5, starting transfers between devices, exchange(): b = lax.ppermute(b, axes, pairs_b)  18.7 us
    all_to_all x1, blocking collectives, one_device(): lax.all_to_all(send.reshape(OWNERS, 1, ASK * 128), 'elem', split_axis=0,...  14.6 us
    ppermute x5, waiting for transfers between devices, exchange(): b = lax.ppermute(b, axes, pairs_b)  14.5 us
    all_to_all x1, starting transfers between devices, one_device(): lax.all_to_all(answer, 'elem', split_axis=0, concat_axis=0, tiled=True)  7.04 us
    all_to_all x1, starting transfers between devices, one_device(): lax.all_to_all(part.reshape(OWNERS, NC // 128, 128), 'elem', split_axis=0...  6.92 us
    all_to_all x1, waiting for transfers between devices, one_device(): lax.all_to_all(answer, 'elem', split_axis=0, concat_axis=0, tiled=True)  6.82 us
    ppermute x5, starting transfers between devices, exchange(): a = lax.ppermute(a, axes, pairs_a)  4.26 us
  transfers between devices with their start and end apart: 13, of which 6 were waited for; matrix products, arithmetic and copies ran while one was open for 0% of the time, Pallas kernels for 9%

profile of v10, /device:TPU:6, one launch (start us, length us, event | category | flops | bytes accessed | tf_op | source)
XLA Modules:
  0.0 101.3 jit_solution(17540832798771661216)
XLA Ops:
  0.0 5.6 %shard_map.119 = (f32[1536,128]{1,0:T(8,128)S(1)}, f32[512,128]{1,0:T(8,128)S(1)}, f32[512,128]{1,0:T(8,128)S(1)}, f32[128,128]{1,0:T(8,128)S(1)}, f32[512,128]{...) custom-call(s32[1,128]{1,0:T(1,128)} %bitcast.32, ...), custom_call_target="tpu_custom_call" | custom-call | tf_op jit(solution)/shard_map/pallas_call | solution.py:996
  5.6 2.0 %collective-permute-start.3 = (f32[960,128]{1,0:T(8,128)}, f32[960,128]{1,0:T(8,128)S(1)}, u32[]{:S(2)}, u32[]{:S(2)}) collective-permute-start(f32[960,128]{1,0:T(8,128)} %get-tuple-element.59), channel_id=1, source_target_pairs={{0,1},{1,0},{2,3},{3,2},{4,5},{5,4},{6,7},{7,6},{8,9},{9,8},{10,11... | collective-permute-start | bytes 1474568 | tf_op jit(solution)/shard_map/ppermute | solution.py:1030
  7.6 5.2 %collective-permute-start.4 = (f32[960,128]{1,0:T(8,128)}, f32[960,128]{1,0:T(8,128)S(1)}, u32[]{:S(2)}, u32[]{:S(2)}) collective-permute-start(f32[960,128]{1,0:T(8,128)} %get-tuple-element.60), channel_id=1, source_target_pairs={{0,64},{1,2},{2,1},{3,4},{4,3},{5,6},{6,5},{7,8},{8,7},{9,10},{10,... | collective-permute-start | bytes 1474568 | tf_op jit(solution)/shard_map/ppermute | solution.py:1029
  12.9 2.5 %shard_map.118 = (f32[384,128]{1,0:T(8,128)S(1)}, f32[1,1024]{1,0:T(1,128)S(1)}, s32[1,1024]{1,0:T(1,128)S(1)}, s32[1,1024]{1,0:T(1,128)S(1)}) custom-call(s32[1,1024]{1,0:T(1,128)} %bitcast.31, s32[1,1024]{1,0:T(1,128)} %slot_ref.1, f32[24,1024]{1,0:T(8,128)} %bitcast.30, s32[1,1024]{1,0:T(1,128)} %ids_ref.1), custom_call_target="tpu_custom_call" | custom-call | tf_op jit(solution)/shard_map/pallas_call | solution.py:996
  15.4 14.6 %all_to_all.21 = f32[64,1,768]{2,1,0:T(1,128)S(1)} all-to-all(f32[64,1,768]{2,1,0:T(1,128)S(1)} %bitcast.20), channel_id=1, replica_groups=mesh['sess'=2,'elem'=64] {'elem'}, dimensions={0} | all-to-all | bytes 393216 | tf_op jit(solution)/shard_map/all_to_all | solution.py:1067
  30.0 1.9 %shard_map.120 = (f32[64,128]{1,0:T(8,128)}, s32[1,128]{1,0:T(1,128)S(1)}) custom-call(f32[384,128]{1,0:T(8,128)S(1)} %bitcast.18, f32[512,128]{1,0:T(8,128)S(1)} %collective-permute-done.field_ref, s32[1,128]{1,0:T(1,128)S(1)} %get-tuple-element.46.before_ref), custom_call_target="tpu_custom_call" | custom-call | tf_op jit(solution)/shard_map/pallas_call | solution.py:996
  31.9 7.0 %all-to-all-start.1 = ((f32[64,1,128]{2,1,0:T(1,128)}), f32[64,1,128]{2,1,0:T(1,128)S(1)}, u32[]{:S(2)}, u32[]{:S(2)}) async-start(f32[64,1,128]{2,1,0:T(1,128)} %bitcast.11), calls=%async_computation.1 | async-start | bytes 65536 | tf_op jit(solution)/shard_map/all_to_all | solution.py:1116
  39.6 6.8 %all-to-all-done.1 = f32[64,1,128]{2,1,0:T(1,128)S(1)} async-done(((f32[64,1,128]{2,1,0:T(1,128)}), f32[64,1,128]{2,1,0:T(1,128)S(1)}, u32[]{:S(2)}, u32[]{:S(2)}) %all-to-all-start.1) | async-done | bytes 32800 | tf_op jit(solution)/shard_map/all_to_all | solution.py:1116
  46.4 1.4 %shard_map.121 = (f32[512,128]{1,0:T(8,128)S(1)}, f32[64,128]{1,0:T(8,128)S(1)}, f32[64,128]{1,0:T(8,128)S(1)}) custom-call(f32[64,128]{1,0:T(8,128)S(1)} %bitcast.21, s32[1,1024]{1,0:T(1,128)S(1)} %get-tuple-element.48.owner_ref, f32[1,1024]{1,0:T(1,128)S(1)} %get-tuple-element.49.rank_ref, s32[1,1024]{1,0:T(1,128)S(1)} %get-tuple-element.50.ids_ref, ...), custom_call_target="tpu_custom_call" | custom-call | tf_op jit(solution)/shard_map/pallas_call | solution.py:996
  48.5 2.2 %collective-permute-start.2 = (f32[64,128]{1,0:T(8,128)S(1)}, f32[64,128]{1,0:T(8,128)S(1)}, u32[]{:S(2)}, u32[]{:S(2)}) collective-permute-start(f32[64,128]{1,0:T(8,128)S(1)} %get-tuple-element.58), channel_id=1, source_target_pairs={{0,64},{1,2},{2,1},{3,4},{4,3},{5,6},{6,5},{7,8},{8,7},{9,10},{10,... | collective-permute-start | bytes 98312 | tf_op jit(solution)/shard_map/ppermute | solution.py:1029
  50.7 1.1 %collective-permute-done.1.a_ref = f32[64,128]{1,0:T(8,128)S(1)} collective-permute-done((f32[64,128]{1,0:T(8,128)S(1)}, f32[64,128]{1,0:T(8,128)S(1)}, u32[]{:S(2)}, u32[]{:S(2)}) %collective-permute-start.1) | collective-permute-done | bytes 32800 | tf_op jit(solution)/shard_map/ppermute | solution.py:1030
  51.8 4.8 %collective-permute-done.2.b_ref = f32[64,128]{1,0:T(8,128)S(1)} collective-permute-done((f32[64,128]{1,0:T(8,128)S(1)}, f32[64,128]{1,0:T(8,128)S(1)}, u32[]{:S(2)}, u32[]{:S(2)}) %collective-permute-start.2) | collective-permute-done | bytes 32800 | tf_op jit(solution)/shard_map/ppermute | solution.py:1029
  56.6 2.3 %shard_map.122 = (f32[512,128]{1,0:T(8,128)S(1)}, f32[512,128]{1,0:T(8,128)S(1)}, f32[512,128]{1,0:T(8,128)S(1)}, f32[512,128]{1,0:T(8,128)S(1)}, f32[64,128]{1,...) custom-call(f32[512,128]{1,0:T(8,128)S(1)} %get-tuple-element.55.y_ref, ...), custom_call_target="tpu_custom_call" | custom-call | tf_op jit(solution)/shard_map/pallas_call | solution.py:996
  58.9 2.2 %collective-permute-start.6 = (f32[64,128]{1,0:T(8,128)S(1)}, f32[64,128]{1,0:T(8,128)S(1)}, u32[]{:S(2)}, u32[]{:S(2)}) collective-permute-start(f32[64,128]{1,0:T(8,128)S(1)} %get-tuple-element.68), channel_id=1, source_target_pairs={{0,64},{1,2},{2,1},{3,4},{4,3},{5,6},{6,5},{7,8},{8,7},{9,10},{10,... | collective-permute-start | bytes 98312 | tf_op jit(solution)/shard_map/ppermute | solution.py:1029
  61.2 5.9 %collective-permute-done.6.b_ref = f32[64,128]{1,0:T(8,128)S(1)} collective-permute-done((f32[64,128]{1,0:T(8,128)S(1)}, f32[64,128]{1,0:T(8,128)S(1)}, u32[]{:S(2)}, u32[]{:S(2)}) %collective-permute-start.6) | collective-permute-done | bytes 32800 | tf_op jit(solution)/shard_map/ppermute | solution.py:1029
  67.1 3.1 %shard_map.123 = (f32[512,128]{1,0:T(8,128)S(1)}, f32[512,128]{1,0:T(8,128)}, f32[256,128]{1,0:T(8,128)}, f32[64,128]{1,0:T(8,128)S(1)}, f32[64,128]{1,0:T(8,128)S(1)}) custom-call(f32[512,128]{1,0:T(8,128)S(1)} %get-tuple-element.62.w_ref, f32[512,128]{1,0:T(8,128)S(1)} %get-tuple-element.63.res_in_ref, f32[512,128]{1,0:T(8,128)S(1)} %get-tuple-element.64.upd_ref, ...), custom_call_target="tpu_custom_call" | custom-call | tf_op jit(solution)/shard_map/pallas_call | solution.py:996
  70.2 6.9 %all-to-all-start.2 = ((f32[64,4,128]{2,1,0:T(4,128)}), f32[64,4,128]{2,1,0:T(4,128)S(1)}, u32[]{:S(2)}, u32[]{:S(2)}) async-start(f32[64,4,128]{2,1,0:T(4,128)} %bitcast.13), calls=%async_computation.2 | async-start | bytes 262144 | tf_op jit(solution)/shard_map/all_to_all | solution.py:1183
  77.1 1.5 %collective-permute-start.7 = (f32[64,128]{1,0:T(8,128)S(1)}, f32[64,128]{1,0:T(8,128)S(1)}, u32[]{:S(2)}, u32[]{:S(2)}) collective-permute-start(f32[64,128]{1,0:T(8,128)S(1)} %get-tuple-element.75), channel_id=1, source_target_pairs={{0,1},{1,0},{2,3},{3,2},{4,5},{5,4},{6,7},{7,6},{8,9},{9,8},{10,11... | collective-permute-start | bytes 98312 | tf_op jit(solution)/shard_map/ppermute | solution.py:1030
  78.7 4.5 %collective-permute-start.8 = (f32[64,128]{1,0:T(8,128)S(1)}, f32[64,128]{1,0:T(8,128)S(1)}, u32[]{:S(2)}, u32[]{:S(2)}) collective-permute-start(f32[64,128]{1,0:T(8,128)S(1)} %get-tuple-element.76), channel_id=1, source_target_pairs={{0,64},{1,2},{2,1},{3,4},{4,3},{5,6},{6,5},{7,8},{8,7},{9,10},{10,... | collective-permute-start | bytes 98312 | tf_op jit(solution)/shard_map/ppermute | solution.py:1029
  83.1 3.6 %shard_map.124 = (f32[384,512]{1,0:T(8,128)}, f32[512,128]{1,0:T(8,128)}) custom-call(f32[128,512]{1,0:T(8,128)S(1)} %get-tuple-element.70.basis_ref, f32[960,128]{1,0:T(8,128)S(1)} %collective-permute-done.3.ga_ref, f32[960,128]{1,0:T(8,128)S(1)} %collective-permute-done.4.gb_ref, f32[512,512]{1,0:T(8,128)} %bitcast.22, ...), custom_call_target="tpu_custom_call" | custom-call | tf_op jit(solution)/shard_map/pallas_call | solution.py:996
  86.8 3.8 %shard_map.125 = (f32[512,128]{1,0:T(8,128)S(1)}, f32[512,128]{1,0:T(8,128)S(1)}, f32[512,128]{1,0:T(8,128)S(1)}, f32[512,128]{1,0:T(8,128)S(1)}, f32[64,128]{1,0:T(8,128)S(1)}, /*index=5*/f32[64,128]{1,0:T(8,128)S(1)}) custom-call(f32[256,128]{1,0:T(8,128)S(1)} %bitcast.19, f32[384,512]{1,0:T(8,128)} %get-tuple-element.72.near_hbm, ...), custom_call_target="tpu_custom_call" | custom-call | tf_op jit(solution)/shard_map/pallas_call | solution.py:996
  90.7 4.5 %collective-permute-start.10 = (f32[64,128]{1,0:T(8,128)S(1)}, f32[64,128]{1,0:T(8,128)S(1)}, u32[]{:S(2)}, u32[]{:S(2)}) collective-permute-start(f32[64,128]{1,0:T(8,128)S(1)} %get-tuple-element.82), channel_id=1, source_target_pairs={{0,64},{1,2},{2,1},{3,4},{4,3},{5,6},{6,5},{7,8},{8,7},{9,10},{10,... | collective-permute-start | bytes 98312 | tf_op jit(solution)/shard_map/ppermute | solution.py:1029
  95.3 3.7 %collective-permute-done.10.refs_6_ = f32[64,128]{1,0:T(8,128)S(1)} collective-permute-done((f32[64,128]{1,0:T(8,128)S(1)}, f32[64,128]{1,0:T(8,128)S(1)}, u32[]{:S(2)}, u32[]{:S(2)}) %collective-permute-start.10) | collective-permute-done | bytes 32800 | tf_op jit(solution)/shard_map/ppermute | solution.py:1029
  99.0 2.1 %shard_map.126 = f32[512,128]{1,0:T(8,128)} custom-call(f32[512,128]{1,0:T(8,128)S(1)} %get-tuple-element.77.refs_0_, f32[512,128]{1,0:T(8,128)S(1)} %get-tuple-element.78.refs_1_, f32[512,128]{1,0:T(8,128)S(1)} %get-tuple-element.79.refs_2_, f32[512,128]{1,0:T(8,128)S(1)} %get-tuple-element.80.refs_3_, f32[512,128]{1,0:T(8,128)S(1)} %get-tuple-element.66.invd_ref.refs_4_, ...), custom_call_target="tpu_custom_call" | custom-call | tf_op jit(solution)/shard_map/pallas_call | solution.py:996
  (14 shorter events, 0.8 us)
Async XLA Ops:
  0.0 12.9 %copy-start = (f32[1,8,8,8,128]{4,3,2,1,0:T(8,128)S(1)}, f32[1,8,8,8,128]{4,3,2,1,0:T(8,128)}, u32[]{:S(2)}) copy-start(f32[1,8,8,8,128]{4,3,2,1,0:T(8,128)} %param.12) | copy-start | bytes 786436
  5.6 51.0 %collective-permute-start.3 = (f32[960,128]{1,0:T(8,128)}, f32[960,128]{1,0:T(8,128)S(1)}, u32[]{:S(2)}, u32[]{:S(2)}) collective-permute-start(f32[960,128]{1,0:T(8,128)} %get-tuple-element.59), channel_id=1, source_target_pairs={{0,1},{1,0},{2,3},{3,2},{4,5},{5,4},{6,7},{7,6},{8,9},{9,8},{10,11... | collective-permute-start | bytes 1474568 | tf_op jit(solution)/shard_map/ppermute | solution.py:1030
  7.6 49.0 %collective-permute-start.4 = (f32[960,128]{1,0:T(8,128)}, f32[960,128]{1,0:T(8,128)S(1)}, u32[]{:S(2)}, u32[]{:S(2)}) collective-permute-start(f32[960,128]{1,0:T(8,128)} %get-tuple-element.60), channel_id=1, source_target_pairs={{0,64},{1,2},{2,1},{3,4},{4,3},{5,6},{6,5},{7,8},{8,7},{9,10},{10,... | collective-permute-start | bytes 1474568 | tf_op jit(solution)/shard_map/ppermute | solution.py:1029
  12.9 17.1 %collective-permute-start = (f32[512,128]{1,0:T(8,128)S(1)}, f32[512,128]{1,0:T(8,128)S(1)}, u32[]{:S(2)}, u32[]{:S(2)}) collective-permute-start(f32[512,128]{1,0:T(8,128)S(1)} %bitcast.25), channel_id=1, source_target_pairs={{0,64},{64,0},{1,65},{65,1},{2,66},{66,2},{3,67},{67,3},{4,68},{68... | collective-permute-start | bytes 786440 | tf_op jit(solution)/shard_map/ppermute | solution.py:1051
  31.9 14.5 %all-to-all-start.1 = ((f32[64,1,128]{2,1,0:T(1,128)}), f32[64,1,128]{2,1,0:T(1,128)S(1)}, u32[]{:S(2)}, u32[]{:S(2)}) async-start(f32[64,1,128]{2,1,0:T(1,128)} %bitcast.11), calls=%async_computation.1 | async-start | bytes 65536 | tf_op jit(solution)/shard_map/all_to_all | solution.py:1116
  47.9 4.0 %collective-permute-start.1 = (f32[64,128]{1,0:T(8,128)S(1)}, f32[64,128]{1,0:T(8,128)S(1)}, u32[]{:S(2)}, u32[]{:S(2)}) collective-permute-start(f32[64,128]{1,0:T(8,128)S(1)} %get-tuple-element.57), channel_id=1, source_target_pairs={{0,1},{1,0},{2,3},{3,2},{4,5},{5,4},{6,7},{7,6},{8,9},{9,8},{10,11... | collective-permute-start | bytes 98312 | tf_op jit(solution)/shard_map/ppermute | solution.py:1030
  48.5 8.1 %collective-permute-start.2 = (f32[64,128]{1,0:T(8,128)S(1)}, f32[64,128]{1,0:T(8,128)S(1)}, u32[]{:S(2)}, u32[]{:S(2)}) collective-permute-start(f32[64,128]{1,0:T(8,128)S(1)} %get-tuple-element.58), channel_id=1, source_target_pairs={{0,64},{1,2},{2,1},{3,4},{4,3},{5,6},{6,5},{7,8},{8,7},{9,10},{10,... | collective-permute-start | bytes 98312 | tf_op jit(solution)/shard_map/ppermute | solution.py:1029
  58.9 8.2 %collective-permute-start.6 = (f32[64,128]{1,0:T(8,128)S(1)}, f32[64,128]{1,0:T(8,128)S(1)}, u32[]{:S(2)}, u32[]{:S(2)}) collective-permute-start(f32[64,128]{1,0:T(8,128)S(1)} %get-tuple-element.68), channel_id=1, source_target_pairs={{0,64},{1,2},{2,1},{3,4},{4,3},{5,6},{6,5},{7,8},{8,7},{9,10},{10,... | collective-permute-start | bytes 98312 | tf_op jit(solution)/shard_map/ppermute | solution.py:1029
  61.2 5.9 %collective-permute-start.5 = (f32[64,128]{1,0:T(8,128)S(1)}, f32[64,128]{1,0:T(8,128)S(1)}, u32[]{:S(2)}, u32[]{:S(2)}) collective-permute-start(f32[64,128]{1,0:T(8,128)S(1)} %get-tuple-element.67.after_ref), channel_id=1, source_target_pairs={{0,1},{1,0},{2,3},{3,2},{4,5},{5,4},{6,7},{7,6},{8,9},{9,8},{10,11... | collective-permute-start | bytes 98312 | tf_op jit(solution)/shard_map/ppermute | solution.py:1030
  70.2 16.6 %all-to-all-start.2 = ((f32[64,4,128]{2,1,0:T(4,128)}), f32[64,4,128]{2,1,0:T(4,128)S(1)}, u32[]{:S(2)}, u32[]{:S(2)}) async-start(f32[64,4,128]{2,1,0:T(4,128)} %bitcast.13), calls=%async_computation.2 | async-start | bytes 262144 | tf_op jit(solution)/shard_map/all_to_all | solution.py:1183
  77.1 9.6 %collective-permute-start.7 = (f32[64,128]{1,0:T(8,128)S(1)}, f32[64,128]{1,0:T(8,128)S(1)}, u32[]{:S(2)}, u32[]{:S(2)}) collective-permute-start(f32[64,128]{1,0:T(8,128)S(1)} %get-tuple-element.75), channel_id=1, source_target_pairs={{0,1},{1,0},{2,3},{3,2},{4,5},{5,4},{6,7},{7,6},{8,9},{9,8},{10,11... | collective-permute-start | bytes 98312 | tf_op jit(solution)/shard_map/ppermute | solution.py:1030
  78.7 8.1 %collective-permute-start.8 = (f32[64,128]{1,0:T(8,128)S(1)}, f32[64,128]{1,0:T(8,128)S(1)}, u32[]{:S(2)}, u32[]{:S(2)}) collective-permute-start(f32[64,128]{1,0:T(8,128)S(1)} %get-tuple-element.76), channel_id=1, source_target_pairs={{0,64},{1,2},{2,1},{3,4},{4,3},{5,6},{6,5},{7,8},{8,7},{9,10},{10,... | collective-permute-start | bytes 98312 | tf_op jit(solution)/shard_map/ppermute | solution.py:1029
  90.7 4.6 %collective-permute-start.9 = (f32[64,128]{1,0:T(8,128)S(1)}, f32[64,128]{1,0:T(8,128)S(1)}, u32[]{:S(2)}, u32[]{:S(2)}) collective-permute-start(f32[64,128]{1,0:T(8,128)S(1)} %get-tuple-element.81), channel_id=1, source_target_pairs={{0,1},{1,0},{2,3},{3,2},{4,5},{5,4},{6,7},{7,6},{8,9},{9,8},{10,11... | collective-permute-start | bytes 98312 | tf_op jit(solution)/shard_map/ppermute | solution.py:1030
  90.7 8.2 %collective-permute-start.10 = (f32[64,128]{1,0:T(8,128)S(1)}, f32[64,128]{1,0:T(8,128)S(1)}, u32[]{:S(2)}, u32[]{:S(2)}) collective-permute-start(f32[64,128]{1,0:T(8,128)S(1)} %get-tuple-element.82), channel_id=1, source_target_pairs={{0,64},{1,2},{2,1},{3,4},{4,3},{5,6},{6,5},{7,8},{8,7},{9,10},{10,... | collective-permute-start | bytes 98312 | tf_op jit(solution)/shard_map/ppermute | solution.py:1029
